TPU v7x, 256 devices: a whole 4x4x8 slice. The times are simulated.
256 devices in a mesh: az: 8 (over z), rng: 8 (over y_lo, x), dp: 4 (over y_hi, core).
Axes of the slice: x: 4, y: 4 (y_hi: 2, y_lo: 2; y = y_hi * 2 + y_lo), z: 8, core: 2. Of those that a mesh axis runs over, the one named last changes fastest.
Arguments:
- tokens: bfloat16 [4, 128, 128, 512], P('dp', 'az', 'rng'), may hold values from -6 to 6
- qkv_weight: bfloat16 [512, 1536], replicated, may hold values from -0.25 to 0.25
- out_weight: bfloat16 [512, 512], replicated, may hold values from -0.25 to 0.25
- relative_bias: float32 [8, 17, 17], replicated, may hold values from -4 to 260
- cotangent: bfloat16 [4, 128, 128, 512], P('dp', 'az', 'rng'), may hold values from -6 to 6
Outputs:
- grad_tokens: bfloat16 [4, 128, 128, 512], P('dp', 'az', 'rng')
- grad_qkv_weight: float32 [512, 1536], P(('az', 'rng'))
- grad_out_weight: float32 [512, 512], P(('az', 'rng'))
- grad_bias: float32 [8, 17, 17], replicated
All inputs are finite; a program needn't handle non-finite values.
Results may differ from a plain program's by a relative error of at most 0.012.
Values may be sent and summed in bfloat16 or wider, within the bound.
No kernel may reach another device: no remote copies, remote signals or barrier semaphores. Data moves between devices by JAX's collectives and lax.ppermute only.
A program may use at most 128 MiB of HBM per device.

v0:
```python
import math

import jax
import jax.numpy as jnp
from jax import lax
from jax.sharding import PartitionSpec as P


def extended(cells, sides, width, closed):
    for axis, dim in sides:
        count = lax.axis_size(axis)
        ends = count if closed else count - 1
        head = lax.slice_in_dim(cells, 0, width, axis=dim)
        tail = lax.slice_in_dim(cells, cells.shape[dim] - width, cells.shape[dim], axis=dim)
        cells = jnp.concatenate(
            [
                lax.ppermute(tail, axis, [(i, (i + 1) % count) for i in range(ends)]),
                cells,
                lax.ppermute(head, axis, [((i + 1) % count, i) for i in range(ends)]),
            ],
            axis=dim,
        )
    return cells


def starts(*values):
    return tuple((jnp.asarray(value).astype(jnp.int32) for value in values))


def selector(length, radius, present):
    span = 2 * radius + 1
    inner = jnp.arange(length)[:, None, None]
    outer = jnp.arange(length + 2 * radius)[None, :, None]
    offset = jnp.arange(span)[None, None, :]
    return ((outer - inner == offset) & present[None, :, None]).astype(jnp.float32)


def window(table, along, across):
    heads = table.shape[0]
    part_bias = jnp.einsum("hxy,jly->hxjl", table, across, precision=lax.Precision.HIGHEST)
    full_bias = jnp.einsum("ikx,hxjl->hijkl", along, part_bias, precision=lax.Precision.HIGHEST)
    row_total = along.shape[0] * across.shape[0]
    col_total = along.shape[1] * across.shape[1]
    inside = (
        jnp.sum(along, axis=2)[:, None, :, None] * jnp.sum(across, axis=2)[None, :, None, :] > 0.5
    )
    return (full_bias.reshape(heads, row_total, col_total), inside.reshape(row_total, col_total))


def bias_grad(d_score, along, across):
    heads = d_score.shape[0]
    shaped = d_score.reshape(
        heads, along.shape[0], across.shape[0], along.shape[1], across.shape[1]
    )
    folded = jnp.einsum("hijkl,ikx->hxjl", shaped, along, precision=lax.Precision.HIGHEST)
    return jnp.einsum("hxjl,jly->hxy", folded, across, precision=lax.Precision.HIGHEST)


def query_side(queries, d_attended, key_rows, value_rows, bias, inside, scale):
    score = (
        jnp.einsum("qhc,khc->hqk", queries, key_rows, preferred_element_type=jnp.float32) * scale
        + bias
    )
    score = jnp.where(inside[None], score, -jnp.inf)
    top = jnp.max(score, axis=2, keepdims=True)
    log_total = top + jnp.log(jnp.sum(jnp.exp(score - top), axis=2, keepdims=True))
    soft_prob = jnp.exp(score - log_total)
    prob_low = soft_prob.astype(jnp.bfloat16)
    attended = jnp.einsum(
        "hqk,khc->qhc", prob_low, value_rows, preferred_element_type=jnp.float32
    ).astype(jnp.bfloat16)
    delta = jnp.einsum("qhc,qhc->hq", d_attended, attended, preferred_element_type=jnp.float32)
    d_prob = jnp.einsum("qhc,khc->hqk", d_attended, value_rows, preferred_element_type=jnp.float32)
    d_score = soft_prob * (d_prob - delta[:, :, None])
    score_low = d_score.astype(jnp.bfloat16)
    d_query = (
        jnp.einsum("hqk,khc->qhc", score_low, key_rows, preferred_element_type=jnp.float32) * scale
    ).astype(jnp.bfloat16)
    return (attended, log_total[:, :, 0], delta, d_query, d_score, score_low, prob_low)


def shards(tokens, qkv_weight, out_weight, relative_bias, cotangent):
    sweeps, azimuth, radial, width = tokens.shape
    heads = relative_bias.shape[0]
    radius = relative_bias.shape[1] // 2
    head_dim = width // heads
    scale = 1.0 / math.sqrt(head_dim)
    local_count = sweeps * azimuth * radial
    flat_tokens = tokens.reshape(local_count, width)
    flat_cot = cotangent.reshape(local_count, width)
    projected = jnp.dot(flat_tokens, qkv_weight, preferred_element_type=jnp.float32).astype(
        jnp.bfloat16
    )
    projected = projected.reshape(sweeps, azimuth, radial, 3 * width)
    queries = projected[..., :width]
    key_value = projected[..., width:]
    d_attended = lax.dot_general(
        flat_cot, out_weight, (((1,), (1,)), ((), ())), preferred_element_type=jnp.float32
    )
    d_attended = d_attended.astype(jnp.bfloat16).reshape(sweeps, azimuth, radial, width)
    key_ext = extended(key_value, (("az", 1), ("rng", 2)), radius, True)
    tile_side = 8
    tiles_az = azimuth // tile_side
    tiles_rg = radial // tile_side
    tile_count = sweeps * tiles_az * tiles_rg
    group = math.gcd(tile_count, 8)
    turns = tile_count // group
    ext_side = tile_side + 2 * radius
    tile_cells = tile_side * tile_side
    ext_cells = ext_side * ext_side
    first_col = lax.axis_index("rng") * radial
    total_cols = lax.axis_size("rng") * radial
    every_col = jnp.ones((ext_side,), dtype=bool)
    along = selector(tile_side, radius, every_col)
    bias_fixed, inside_fixed = window(relative_bias, along, along)

    def locate(counter):
        sweep_at = counter // (tiles_az * tiles_rg)
        leftover = counter % (tiles_az * tiles_rg)
        return (sweep_at, leftover // tiles_rg * tile_side, leftover % tiles_rg * tile_side)

    def inside_of(col_at):
        column = first_col + col_at - radius + jnp.arange(ext_side)
        present = (column >= 0) & (column < total_cols)
        present_cells = jnp.broadcast_to(present[None, :], (ext_side, ext_side)).reshape(ext_cells)
        return inside_fixed & present_cells[None, :]

    def untile(leaf):
        last = leaf.shape[-1]
        shaped = leaf.reshape(sweeps, tiles_az, tiles_rg, tile_side, tile_side, last)
        return shaped.transpose(0, 1, 3, 2, 4, 5).reshape(sweeps, azimuth, radial, last)

    def query_tile(counter):
        sweep_at, row_at, col_at = locate(counter)
        place = starts(sweep_at, row_at, col_at, 0)
        query_block = lax.dynamic_slice(queries, place, (1, tile_side, tile_side, width)).reshape(
            tile_cells, heads, head_dim
        )
        cot_block = lax.dynamic_slice(d_attended, place, (1, tile_side, tile_side, width)).reshape(
            tile_cells, heads, head_dim
        )
        pair_block = lax.dynamic_slice(key_ext, place, (1, ext_side, ext_side, 2 * width)).reshape(
            ext_cells, 2, heads, head_dim
        )
        inside = inside_of(col_at)
        attended, log_total, delta, d_query, d_score, score_low, prob_low = query_side(
            query_block, cot_block, pair_block[:, 0], pair_block[:, 1], bias_fixed, inside, scale
        )
        d_key = (
            jnp.einsum("hqk,qhc->khc", score_low, query_block, preferred_element_type=jnp.float32)
            * scale
        )
        d_value = jnp.einsum(
            "hqk,qhc->khc", prob_low, cot_block, preferred_element_type=jnp.float32
        )
        term = jnp.stack([d_key, d_value], axis=1).reshape(1, ext_side, ext_side, 2 * width)
        return (
            attended.reshape(tile_cells, width),
            log_total.T,
            delta.T,
            d_query.reshape(tile_cells, width),
            d_score,
            term,
        )

    sums_init = jnp.zeros(
        (sweeps, azimuth + 2 * radius, radial + 2 * radius, 2 * width), jnp.float32
    )

    def query_turn(carry, counter):
        part_sums, score_sum = carry
        lanes = counter * group + jnp.arange(group, dtype=jnp.int32)
        attended, log_total, delta, d_query, d_scores, terms = jax.vmap(query_tile)(lanes)
        score_sum = score_sum + jnp.sum(d_scores, axis=0)
        for member in range(group):
            sweep_at, row_at, col_at = locate(lanes[member])
            place = starts(sweep_at, row_at, col_at, 0)
            current = lax.dynamic_slice(part_sums, place, terms[member].shape)
            part_sums = lax.dynamic_update_slice(part_sums, current + terms[member], place)
        return ((part_sums, score_sum), (attended, log_total, delta, d_query))

    init = (sums_init, jnp.zeros((heads, tile_cells, ext_cells), jnp.float32))
    (part_sums, score_total), outputs = lax.scan(
        query_turn, init, jnp.arange(turns, dtype=jnp.int32)
    )
    bias_local = bias_grad(score_total, along, along)
    attended_all, log_all, delta_all, dquery_all = [
        untile(leaf.reshape((tile_count,) + leaf.shape[2:])) for leaf in outputs
    ]
    edge_terms = jnp.concatenate(
        [part_sums[:, :, :radius], part_sums[:, :, radial + radius :]], axis=2
    )
    arrived = extended(edge_terms.astype(jnp.bfloat16), (("rng", 2),), radius, False).astype(
        edge_terms.dtype
    )
    inner = part_sums[:, :, radius : radius + radial]
    inner = inner.at[:, :, :radius].add(arrived[:, :, :radius])
    inner = inner.at[:, :, radial - radius :].add(arrived[:, :, 3 * radius :])
    cycle_terms = jnp.concatenate([inner[:, :radius], inner[:, azimuth + radius :]], axis=1)
    arrived_cycle = extended(cycle_terms.astype(jnp.bfloat16), (("az", 1),), radius, True).astype(
        cycle_terms.dtype
    )
    owned = inner[:, radius : radius + azimuth]
    owned = owned.at[:, :radius].add(arrived_cycle[:, :radius])
    owned = owned.at[:, azimuth - radius :].add(arrived_cycle[:, 3 * radius :])
    grad_pair = owned.astype(jnp.bfloat16)
    grad_qkv = jnp.concatenate([dquery_all, grad_pair], axis=3)
    grad_flat = grad_qkv.reshape(local_count, 3 * width)
    grad_tokens = lax.dot_general(
        grad_flat, qkv_weight, (((1,), (1,)), ((), ())), preferred_element_type=jnp.float32
    )
    grad_tokens = grad_tokens.astype(jnp.bfloat16).reshape(sweeps, azimuth, radial, width)
    local_qkv = lax.dot_general(
        flat_tokens, grad_flat, (((0,), (0,)), ((), ())), preferred_element_type=jnp.float32
    )
    local_out = lax.dot_general(
        attended_all.reshape(local_count, width),
        flat_cot,
        (((0,), (0,)), ((), ())),
        preferred_element_type=jnp.float32,
    )
    share = width // (lax.axis_size("az") * lax.axis_size("rng"))
    total_qkv, total_out, total_bias = lax.psum(
        (local_qkv, local_out, bias_local), ("az", "rng", "dp")
    )
    first_row = lax.axis_index(("az", "rng")) * share
    rows_qkv = lax.dynamic_slice_in_dim(total_qkv, first_row, share, 0)
    rows_out = lax.dynamic_slice_in_dim(total_out, first_row, share, 0)
    return (grad_tokens, rows_qkv, rows_out, total_bias)


def solution(mesh):
    placed = (P("dp", "az", "rng", None), P(), P(), P(), P("dp", "az", "rng", None))
    return jax.shard_map(
        shards,
        mesh=mesh,
        in_specs=placed,
        out_specs=(P("dp", "az", "rng", None), P(("az", "rng"), None), P(("az", "rng"), None), P()),
        check_vma=False,
    )
```

profile of v0, /device:TPU:1, one launch (start us, length us, event | category | flops | bytes accessed | tf_op | source)
XLA Modules:
  0.0 516.2 jit_solution(8498767762918409143)
XLA Ops:
  7.2 1.3 copy-done
  8.6 1.5 convolution_convert_fusion
  11.0 2.5 collective-permute-start
  13.4 3.9 collective-permute-start.1
  26.8 1.4 convolution_convert_fusion.2
  28.3 8.0 %while.16 = (s32[]{:T(128)}, bf16[1,16,16,512]{3,2,1,0:T(8,128)(2,1)S(1)}, s32[4,4]{1,0:T(4,128)S(1)}, bf16[4,1,8,8,512]{4,3,2,1,0:T(8,128)(2,1)S(1)}, s32[]{:T(128)}) while((s32[]{:T(128)}, bf16[1,16,16,512]{3,2,1,0:T(8,128)(2,1)S(1)}, s32[4,4]{1,0:T(4,128)S(1)}, bf16[4,1,8,8,512]{4,3,2,1,0:T(8,128)(2,1)S(1)}, s32[]{:T(128)}) %tuple.101), condition=%wide.while_cond.6, body=%wide.while_body.6.sunk | while | flops 2 | bytes 131205 | solution.py:139
  29.0 1.3 bitcast_dynamic-update-slice_fusion.8
  31.0 1.3 bitcast_dynamic-update-slice_fusion.8
  33.0 1.3 bitcast_dynamic-update-slice_fusion.8
  35.0 1.3 bitcast_dynamic-update-slice_fusion.8
  37.8 8.3 %while.15 = (s32[]{:T(128)}, bf16[1,16,16,512]{3,2,1,0:T(8,128)(2,1)S(1)}, s32[4,4]{1,0:T(4,128)S(1)}, bf16[4,1,8,8,512]{4,3,2,1,0:T(8,128)(2,1)S(1)}, s32[]{:T(128)}) while((s32[]{:T(128)}, bf16[1,16,16,512]{3,2,1,0:T(8,128)(2,1)S(1)}, s32[4,4]{1,0:T(4,128)S(1)}, bf16[4,1,8,8,512]{4,3,2,1,0:T(8,128)(2,1)S(1)}, s32[]{:T(128)}) %tuple.102), condition=%wide.while_cond.5, body=%wide.while_body.5.sunk | while | flops 2 | bytes 131205 | solution.py:136
  38.5 1.4 bitcast_dynamic-update-slice_fusion.7
  40.5 1.4 bitcast_dynamic-update-slice_fusion.7
  42.6 1.4 bitcast_dynamic-update-slice_fusion.7
  44.7 1.4 bitcast_dynamic-update-slice_fusion.7
  47.1 2.6 copy.46
  54.4 2.8 collective-permute-start.3
  57.2 4.6 convolution_bitcast_fusion.1
  61.8 6.6 %copy.22 = f32[8,8,8,24,24]{4,3,2,1,0:T(8,128)} copy(f32[8,8,8,24,24]{3,4,1,2,0:T(8,128)} %convolution_bitcast_fusion.1) | data formatting | bytes 2359296 | tf_op jit(solution)/shard_map/ikx,hxjl->hijkl/transpose | solution.py:41
  68.4 4.3 add.387
  73.5 2.8 pad_maximum_fusion.1
  76.3 19.3 %while.14 = (s32[]{:T(128)}, bf16[1,32,32,1024]{3,2,1,0:T(8,128)(2,1)}, s32[4,4]{1,0:T(4,128)S(1)}, bf16[4,1,24,24,1024]{4,3,2,1,0:T(8,128)(2,1)}, s32[]{:T(128)}) while((s32[]{:T(128)}, bf16[1,32,32,1024]{3,2,1,0:T(8,128)(2,1)}, s32[4,4]{1,0:T(4,128)S(1)}, bf16[4,1,24,24,1024]{4,3,2,1,0:T(8,128)(2,1)}, s32[]{:T(128)}) %tuple.95), condition=%wide.while_cond.4, body=%wide.while_body.4.sunk | while | flops 2 | bytes 2360445 | solution.py:142
  76.9 4.3 bitcast_dynamic-update-slice_fusion.6
  81.8 4.2 bitcast_dynamic-update-slice_fusion.6
  86.6 4.3 bitcast_dynamic-update-slice_fusion.6
  91.5 4.2 bitcast_dynamic-update-slice_fusion.6
  95.6 13.1 %reshape.627 = bf16[4,576,2,8,64]{4,3,2,1,0:T(8,128)(2,1)} reshape(bf16[4,1,24,24,1024]{4,3,2,1,0:T(8,128)(2,1)} %get-tuple-element.92) | data formatting | bytes 9437184 | tf_op jit(solution)/shard_map/while/body/eval_jaxpr/vmap()/reshape | solution.py:142
  108.7 8.1 %fusion.80 = (bf16[4,576,1,8,64]{4,3,2,1,0:T(8,128)(2,1)}, bf16[4,576,1,8,64]{4,3,2,1,0:T(8,128)(2,1)}) fusion(bf16[4,576,2,8,64]{4,3,2,1,0:T(8,128)(2,1)} %reshape.627), kind=kLoop, calls=%fused_computation.139 | loop fusion | bytes 9437184 | tf_op jit(solution)/shard_map/while/body/eval_jaxpr/vmap()/slice | solution.py:147
  116.9 6.2 %copy.51 = bf16[4,576,1,8,64]{1,4,3,0,2:T(8,128)(2,1)} copy(bf16[4,576,1,8,64]{4,3,2,1,0:T(8,128)(2,1)} %get-tuple-element.153) | data formatting | bytes 4718592
  123.1 6.2 %copy.50 = bf16[4,576,1,8,64]{1,4,3,0,2:T(8,128)(2,1)} copy(bf16[4,576,1,8,64]{4,3,2,1,0:T(8,128)(2,1)} %get-tuple-element.154) | data formatting | bytes 4718592
  129.3 3.1 fusion.86
  132.5 1.5 exponential_reduce_fusion
  136.0 2.1 multiply_reduce_fusion
  138.1 2.1 fusion.87
  141.7 4.6 pad_maximum_fusion
  146.3 5.8 %copy.32 = f32[1,576,2,8,64]{4,3,2,1,0:T(8,128)} copy(f32[1,576,2,8,64]{1,4,3,0,2:T(8,128)} %get-tuple-element.149) | data formatting | bytes 4718592 | tf_op jit(solution)/shard_map/while/body/eval_jaxpr/slice | solution.py:179
  152.1 5.0 squeeze.52
  157.1 5.8 %copy.29 = f32[1,576,2,8,64]{4,3,2,1,0:T(8,128)} copy(f32[1,576,2,8,64]{1,4,3,0,2:T(8,128)} %get-tuple-element.150) | data formatting | bytes 4718592 | tf_op jit(solution)/shard_map/while/body/eval_jaxpr/slice | solution.py:179
  162.9 5.0 squeeze.45
  167.9 5.8 %copy.30 = f32[1,576,2,8,64]{4,3,2,1,0:T(8,128)} copy(f32[1,576,2,8,64]{1,4,3,0,2:T(8,128)} %get-tuple-element.151) | data formatting | bytes 4718592 | tf_op jit(solution)/shard_map/while/body/eval_jaxpr/slice | solution.py:179
  173.7 5.0 squeeze.48
  178.7 5.8 %copy.31 = f32[1,576,2,8,64]{4,3,2,1,0:T(8,128)} copy(f32[1,576,2,8,64]{1,4,3,0,2:T(8,128)} %get-tuple-element.152) | data formatting | bytes 4718592 | tf_op jit(solution)/shard_map/while/body/eval_jaxpr/slice | solution.py:179
  184.5 5.0 squeeze.50
  191.5 1.4 copy-done.7
  197.9 2.1 collective-permute-start.4
  201.3 1.4 slice.323
  203.8 1.4 reshape_reshape.10
  206.0 4.3 fusion.29
  210.2 1.4 copy.25
  213.6 1.4 maximum_bitcast_fusion
  215.0 2.5 fusion.35
  217.5 2.6 fusion.34
  220.1 1.4 fusion.82
  221.7 2.9 collective-permute-start.7
  224.5 1.3 fusion.88
  226.0 3.2 collective-permute-done.6
  229.5 2.3 convolution_bitcast_fusion
  231.8 4.0 reshape.636
  235.8 5.0 convolution_bitcast_fusion.3
  241.4 83.8 %psum.23 = f32[8,17,17]{2,1,0:T(8,128)S(1)} all-reduce(f32[8,17,17]{2,1,0:T(8,128)S(1)} %convolution_bitcast_fusion.5), channel_id=1, replica_groups=mesh['az'=8,'rng'=8,'dp'=4] {'az','rng','dp'}, use_global_device_ids=true, to_apply=%region_6.7 | all-reduce | flops 2312 | bytes 18496 | tf_op jit(solution)/shard_map/psum | solution.py:223
  325.8 1.3 convolution_convert_fusion.1
  327.1 178.4 %all-reduce.3.cloned.1.call-done = (f32[512,1536]{0,1:T(8,128)}, f32[512,512]{1,0:T(8,128)}) async-done(((f32[512,1536]{0,1:T(8,128)}, f32[512,512]{1,0:T(8,128)}), (f32[512,1536]{0,1:T(8,128)}, f32[512,512]{1,0:T(8,128)})) %all-reduce.3.cloned.1.call-update) | async-done | bytes 4194320 | tf_op jit(solution)/shard_map/psum | solution.py:223
  505.5 1.4 constant_dynamic-slice_fusion.4
  506.9 1.3 constant_dynamic-slice_fusion.3
  (125 shorter events, 36.5 us)
Async XLA Ops:
  7.2 1.4 copy-start
  7.2 19.6 %copy-start.14 = (bf16[1,16,16,512]{3,2,1,0:T(8,128)(2,1)S(1)}, bf16[1,16,16,512]{3,2,1,0:T(8,128)(2,1)}, u32[]{:S(2)}) copy-start(bf16[1,16,16,512]{3,2,1,0:T(8,128)(2,1)} %param.17) | copy-start | bytes 786436
  7.2 498.3 %all-reduce.3.cloned.1.call-start = ((), (), s32[]{:S(2)}) async-start(), calls=%async_computation | async-start | bytes 8388608 | tf_op jit(solution)/shard_map/psum | solution.py:223
  11.0 40.0 %collective-permute-start = (bf16[1,8,16,1024]{3,2,1,0:T(8,128)(2,1)}, bf16[1,8,16,1024]{3,2,1,0:T(8,128)(2,1)}, u32[]{:S(2)}, u32[]{:S(2)}) collective-permute-start(bf16[1,8,16,1024]{3,2,1,0:T(8,128)(2,1)} %get-tuple-element.161), channel_id=1, source_target_pairs={{0,32},{32,64},{64,96},{96,128},{128,160},{160,192},{192,224},{224... | collective-permute-start | bytes 786440 | tf_op jit(solution)/shard_map/ppermute | solution.py:17
  13.4 37.5 %collective-permute-start.1 = (bf16[1,8,16,1024]{3,2,1,0:T(8,128)(2,1)}, bf16[1,8,16,1024]{3,2,1,0:T(8,128)(2,1)}, u32[]{:S(2)}, u32[]{:S(2)}) collective-permute-start(bf16[1,8,16,1024]{3,2,1,0:T(8,128)(2,1)} %get-tuple-element.162), channel_id=1, source_target_pairs={{32,0},{64,32},{96,64},{128,96},{160,128},{192,160},{224,192},{0,2... | collective-permute-start | bytes 786440 | tf_op jit(solution)/shard_map/ppermute | solution.py:19
  25.9 25.1 %copy-start.9 = (bf16[1,16,16,1024]{3,2,1,0:T(8,128)(2,1)}, bf16[1,16,16,1024]{3,2,1,0:T(8,128)(2,1)S(1)}, u32[]{:S(2)}) copy-start(bf16[1,16,16,1024]{3,2,1,0:T(8,128)(2,1)S(1)} %slice.310) | copy-start | bytes 1572868
  37.7 12.6 %copy-start.19 = (f32[8,17,17]{2,0,1:T(8,128)S(1)}, f32[8,17,17]{2,0,1:T(8,128)}, u32[]{:S(2)}) copy-start(f32[8,17,17]{2,0,1:T(8,128)} %param.16) | copy-start | bytes 27748
  53.1 20.4 %collective-permute-start.2 = (bf16[1,32,8,1024]{3,2,1,0:T(8,128)(2,1)}, bf16[1,32,8,1024]{3,2,1,0:T(8,128)(2,1)}, u32[]{:S(2)}, u32[]{:S(2)}) collective-permute-start(bf16[1,32,8,1024]{3,2,1,0:T(8,128)(2,1)} %get-tuple-element.159), channel_id=1, source_target_pairs={{0,4},{4,8},{8,12},{12,16},{16,20},{20,24},{24,28},{28,0},{1,5},{5... | collective-permute-start | bytes 1572872 | tf_op jit(solution)/shard_map/ppermute | solution.py:17
  54.4 19.2 %collective-permute-start.3 = (bf16[1,32,8,1024]{3,2,1,0:T(8,128)(2,1)}, bf16[1,32,8,1024]{3,2,1,0:T(8,128)(2,1)}, u32[]{:S(2)}, u32[]{:S(2)}) collective-permute-start(bf16[1,32,8,1024]{3,2,1,0:T(8,128)(2,1)} %get-tuple-element.160), channel_id=1, source_target_pairs={{4,0},{8,4},{12,8},{16,12},{20,16},{24,20},{28,24},{0,28},{5,1},{9... | collective-permute-start | bytes 1572872 | tf_op jit(solution)/shard_map/ppermute | solution.py:19
  132.5 1.5 copy-start.10
  134.0 1.7 copy-start.3
  134.0 2.0 copy-start.11
  140.2 1.6 copy-start.2
  189.5 1.7 copy-start.5
  191.2 1.7 copy-start.7
  192.8 1.7 copy-start.8
  194.5 1.7 copy-start.6
  196.8 6.0 %copy-start.1 = (f32[1,32,32,1024]{3,2,1,0:T(8,128)}, f32[1,32,32,1024]{3,2,1,0:T(8,128)S(1)}, u32[]{:S(2)}) copy-start(f32[1,32,32,1024]{3,2,1,0:T(8,128)S(1)} %add_dynamic-update-slice_fusion) | copy-start | bytes 12582916
  196.8 5.9 %copy-start.12 = (bf16[4,8,64,64]{3,2,1,0:T(8,128)(2,1)S(1)}, bf16[4,8,64,64]{3,2,1,0:T(8,128)(2,1)}, u32[]{:S(2)}) copy-start(bf16[4,8,64,64]{3,2,1,0:T(8,128)(2,1)} %get-tuple-element.172) | copy-start | bytes 786436
  197.9 17.1 %collective-permute-start.4 = (bf16[1,32,8,1024]{3,2,1,0:T(8,128)(2,1)}, bf16[1,32,8,1024]{3,2,1,0:T(8,128)(2,1)}, u32[]{:S(2)}, u32[]{:S(2)}) collective-permute-start(bf16[1,32,8,1024]{3,2,1,0:T(8,128)(2,1)} %get-tuple-element.155), channel_id=1, source_target_pairs={{0,4},{4,8},{8,12},{12,16},{16,20},{20,24},{24,28},{1,5},{5,9},{9,... | collective-permute-start | bytes 1572872 | tf_op jit(solution)/shard_map/ppermute | solution.py:17
  200.0 15.0 %collective-permute-start.5 = (bf16[1,32,8,1024]{3,2,1,0:T(8,128)(2,1)}, bf16[1,32,8,1024]{3,2,1,0:T(8,128)(2,1)}, u32[]{:S(2)}, u32[]{:S(2)}) collective-permute-start(bf16[1,32,8,1024]{3,2,1,0:T(8,128)(2,1)} %get-tuple-element.156), channel_id=1, source_target_pairs={{4,0},{8,4},{12,8},{16,12},{20,16},{24,20},{28,24},{5,1},{9,5},{13... | collective-permute-start | bytes 1572872 | tf_op jit(solution)/shard_map/ppermute | solution.py:19
  213.6 15.9 %copy-start.17 = (bf16[1,2,8,2,8,512]{5,4,3,2,1,0:T(8,128)(2,1)}, bf16[1,2,8,2,8,512]{5,4,3,2,1,0:T(8,128)(2,1)S(1)}, u32[]{:S(2)}) copy-start(bf16[1,2,8,2,8,512]{5,4,3,2,1,0:T(8,128)(2,1)S(1)} %copy.26) | copy-start | bytes 786436
  217.5 7.0 %copy-start.13 = (bf16[1,2,8,2,8,512]{5,4,3,2,1,0:T(8,128)(2,1)S(1)}, bf16[1,2,8,2,8,512]{5,4,3,2,1,0:T(8,128)(2,1)}, u32[]{:S(2)}) copy-start(bf16[1,2,8,2,8,512]{5,4,3,2,1,0:T(8,128)(2,1)} %copy.35) | copy-start | bytes 786436
  217.5 7.0 %copy-start.15 = (bf16[1,16,16,512]{3,2,1,0:T(8,128)(2,1)S(1)}, bf16[1,16,16,512]{3,2,1,0:T(8,128)(2,1)}, u32[]{:S(2)}) copy-start(bf16[1,16,16,512]{3,2,1,0:T(8,128)(2,1)} %param.17) | copy-start | bytes 786436
  220.1 5.7 %copy-start.4 = (f32[1,32,16,1024]{3,2,1,0:T(8,128)S(1)}, f32[1,32,16,1024]{3,2,1,0:T(8,128)}, u32[]{:S(2)}) copy-start(f32[1,32,16,1024]{3,2,1,0:T(8,128)} %fusion.34) | copy-start | bytes 6291460
  221.6 7.6 %collective-permute-start.6 = (bf16[1,8,16,1024]{3,2,1,0:T(8,128)(2,1)S(1)}, bf16[1,8,16,1024]{3,2,1,0:T(8,128)(2,1)S(1)}, u32[]{:S(2)}, u32[]{:S(2)}) collective-permute-start(bf16[1,8,16,1024]{3,2,1,0:T(8,128)(2,1)S(1)} %get-tuple-element.157), channel_id=1, source_target_pairs={{0,32},{32,64},{64,96},{96,128},{128,160},{160,192},{192,224},{224... | collective-permute-start | bytes 786440 | tf_op jit(solution)/shard_map/ppermute | solution.py:17
  221.7 7.5 %collective-permute-start.7 = (bf16[1,8,16,1024]{3,2,1,0:T(8,128)(2,1)S(1)}, bf16[1,8,16,1024]{3,2,1,0:T(8,128)(2,1)S(1)}, u32[]{:S(2)}, u32[]{:S(2)}) collective-permute-start(bf16[1,8,16,1024]{3,2,1,0:T(8,128)(2,1)S(1)} %get-tuple-element.158), channel_id=1, source_target_pairs={{32,0},{64,32},{96,64},{128,96},{160,128},{192,160},{224,192},{0,2... | collective-permute-start | bytes 786440 | tf_op jit(solution)/shard_map/ppermute | solution.py:19
  226.0 3.5 copy-start.16
  235.8 90.0 %copy-start.18 = (bf16[1,2,8,2,8,512]{5,4,3,2,1,0:T(8,128)(2,1)S(1)}, bf16[1,2,8,2,8,512]{5,4,3,2,1,0:T(8,128)(2,1)}, u32[]{:S(2)}) copy-start(bf16[1,2,8,2,8,512]{5,4,3,2,1,0:T(8,128)(2,1)} %copy-done.17) | copy-start | bytes 786436
Sparse Core Ops, SparseCore 0:
  231.9 273.5 all-reduce.2
where the time goes:
time: 525 us; the launch traced here: 516 us
  waiting for transfers between devices  182 us (35%)
  local copies, waits for them, and re-layouts  158 us (30%)
  blocking collectives  83.8 us (16%)
  matrix products  32.1 us (6%)
  between operations  22.6 us (4%)
  other arithmetic  21 us (4%)
  starting transfers between devices  16.8 us (3%)
    psum x1, waiting for transfers between devices, shards(): lax.psum((local_qkv, local_out, bias_local), ('az', 'rng', 'dp'))  178 us
    psum x1, blocking collectives, shards(): lax.psum((local_qkv, local_out, bias_local), ('az', 'rng', 'dp'))  83.8 us
    gather x36, local copies, waits for them, and re-layouts  35.3 us
    unnamed x47, local copies, waits for them, and re-layouts  24.1 us
    slice x4, local copies, waits for them, and re-layouts, query_turn(): terms[member]  23.1 us
    squeeze x4, local copies, waits for them, and re-layouts, query_turn(): terms[member]  20.1 us
    reshape x1, local copies, waits for them, and re-layouts, query_tile(): lax.dynamic_slice(key_ext, place, (1, ext_side, ext_side, 2 * width))  13.1 us
    ppermute x4, starting transfers between devices, extended(): lax.ppermute(head, axis, [((i + 1) % count, i) for i in range(ends)])  10.9 us
  transfers between devices with their start and end apart: 9, of which 2 were waited for; matrix products, arithmetic and copies ran while one was open for 13% of the time, Pallas kernels for 0%

commit v1 on v0

v1 whole, which is shorter than its diff:
```python
import functools
import math

import jax
import jax.numpy as jnp
from jax import lax
from jax.experimental import pallas as pl
from jax.experimental.pallas import tpu as pltpu
from jax.sharding import PartitionSpec as P

F32 = jnp.float32
BF16 = jnp.bfloat16
ABSENT = -1e30
NT = (((1,), (1,)), ((), ()))
VMEM_BYTES = 60 * 1024 * 1024


def dot(a, b, dims=(((1,), (0,)), ((), ()))):
    return lax.dot_general(a, b, dims, preferred_element_type=F32)


def row_slots(row):
    base = row // 8 * 256
    at = row % 8
    return (
        (0, 8, base + at * 8),
        (8, 24, base + 64 + at * 16),
        (24, 32, base + 192 + at * 8),
    )


def before_kernel(edge, x, cot, wt, wo, rows, q, q_t, da, da_t, table):
    xv = x[...]
    cv = cot[...]
    q[...] = (dot(xv, wt[0:512], NT).astype(BF16).astype(F32) * 0.125).astype(BF16)
    q_t[...] = (dot(wt[0:512], xv, NT).astype(BF16).astype(F32) * 0.125).astype(BF16)
    da[...] = dot(cv, wo[...], NT).astype(BF16)
    da_t[...] = dot(wo[...], cv, NT).astype(BF16)
    range_row = lax.broadcasted_iota(jnp.int32, (32, 512), 0)
    lane = lax.broadcasted_iota(jnp.int32, (32, 512), 1)
    gap = range_row - (lane & 15)
    first = jnp.where(edge[0] == 1, 8, 0)
    last = jnp.where(edge[1] == 1, 24, 32)
    present = (range_row >= first) & (range_row < last)

    def pair_step(pair, carry):
        for side in range(2):
            head_rows = rows[pair * 2 + side]
            spread = jnp.full((32, 512), ABSENT, F32)
            for j in range(17):
                spread = jnp.where(gap == j, head_rows[j : j + 1], spread)
            spread = jnp.where(present, spread, ABSENT)
            for v in range(8):
                turned = spread if v == 0 else pltpu.roll(spread, 512 - 16 * v, 1)
                for u in range(3):
                    block = turned[:, 128 * u : 128 * u + 128]
                    for low, high, at in row_slots(23 - 8 * u - v):
                        table[pair, at : at + high - low, side * 128 : side * 128 + 128] = block[
                            low:high
                        ]
        return carry

    lax.fori_loop(0, 4, pair_step, 0)


def main_kernel(
    core, own, top, bottom, left, right, tl, tr, bl, br, q, q_t, da, da_t, table, wt, cot,
    grad_own, g_top, g_bottom, g_left, g_right, g_tl, g_tr, g_bl, g_br, g_keep, g_send, g_bias,
    xs, k, v, k_t, v_t, dkv, att_t, dq_t, dsum, brow,
):
    pieces = (
        (tl, 0, 64, 0), (top, 0, 128, 64), (tr, 0, 64, 192),
        (left, 0, 64, 256), (own, 0, 128, 320), (right, 0, 64, 448),
        (left, 64, 64, 512), (own, 128, 128, 576), (right, 64, 64, 704),
        (bl, 0, 64, 768), (bottom, 0, 128, 832), (br, 0, 64, 960),
    )
    for ref, at, size, to in pieces:
        xs[to : to + size] = ref[at : at + size]

    def project(g, carry):
        at = pl.multiple_of(g * 256, 256)
        block = xs[pl.ds(at, 256)]
        k[pl.ds(at, 256)] = dot(block, wt[512:1024], NT).astype(BF16)
        v[pl.ds(at, 256)] = dot(block, wt[1024:1536], NT).astype(BF16)
        k_t[:, pl.ds(at, 256)] = dot(wt[512:1024], block, NT).astype(BF16)
        v_t[:, pl.ds(at, 256)] = dot(wt[1024:1536], block, NT).astype(BF16)
        return carry

    lax.fori_loop(0, 4, project, 0)

    upper_rows = lax.broadcasted_iota(jnp.int32, (128, 128), 0) < 64
    upper_lanes = lax.broadcasted_iota(jnp.int32, (128, 128), 1) < 64
    gap = lax.broadcasted_iota(jnp.int32, (32, 512), 0) - (
        lax.broadcasted_iota(jnp.int32, (32, 512), 1) & 15
    )

    def split_lanes(block):
        zero = jnp.zeros_like(block)
        return jnp.concatenate(
            [jnp.where(upper_rows, block, zero), jnp.where(upper_rows, zero, block)], axis=1
        )

    def split_rows(block):
        zero = jnp.zeros_like(block)
        return jnp.concatenate(
            [jnp.where(upper_lanes, block, zero), jnp.where(upper_lanes, zero, block)], axis=0
        )

    def pair_step(pair, carry):
        at = pl.multiple_of(pair * 128, 128)
        cols = pl.ds(at, 128)
        tails = []
        for t in range(2):
            keys = slice(t * 256, t * 256 + 768)
            mine = slice(t * 128, t * 128 + 128)
            score = dot(k[keys, cols], split_lanes(q_t[cols, mine])) + table[pair]
            top_score = jnp.max(score, axis=0, keepdims=True)
            weight = jnp.exp(score - top_score)
            prob = weight * (1.0 / jnp.sum(weight, axis=0, keepdims=True))
            prob_low = prob.astype(BF16)
            mixed = dot(v_t[cols, keys], prob_low)
            att = jnp.where(upper_rows, mixed[:, :128], mixed[:, 128:]).astype(BF16)
            att_t[cols, mine] = att
            da_block = da_t[cols, mine]
            product = att.astype(F32) * da_block.astype(F32)
            delta = jnp.concatenate(
                [
                    jnp.sum(product[:64], axis=0, keepdims=True),
                    jnp.sum(product[64:], axis=0, keepdims=True),
                ],
                axis=1,
            )
            d_score = prob * (dot(v[keys, cols], split_lanes(da_block)) - delta)
            if t == 0:
                dsum[...] = d_score
            else:
                dsum[...] += d_score
            score_low = d_score.astype(BF16)
            d_q = dot(k_t[cols, keys], score_low)
            dq_t[cols, mine] = (
                jnp.where(upper_rows, d_q[:, :128], d_q[:, 128:]) * 0.125
            ).astype(BF16)
            tails.append(
                (
                    dot(score_low, split_rows(q[mine, cols])),
                    dot(prob_low, split_rows(da[mine, cols])),
                )
            )
        for which in range(2):
            early, late = tails[0][which], tails[1][which]
            to = pl.ds(pl.multiple_of(which * 512 + at, 128), 128)
            dkv[0:256, to] = early[0:256].astype(BF16)
            dkv[256:768, to] = (early[256:768] + late[0:512]).astype(BF16)
            dkv[768:1024, to] = late[512:768].astype(BF16)
        for side in range(2):
            lanes = slice(side * 128, side * 128 + 128)
            total = None
            for turn in range(8):
                parts = [
                    jnp.concatenate(
                        [
                            dsum[to : to + high - low, lanes]
                            for low, high, to in row_slots(23 - 8 * u - turn)
                        ],
                        axis=0,
                    )
                    for u in range(3)
                ]
                strip = jnp.concatenate(parts + [jnp.zeros((32, 128), F32)], axis=1)
                if turn:
                    strip = pltpu.roll(strip, 16 * turn, 1)
                total = strip if total is None else total + strip
            for j in range(17):
                brow[pair * 2 + side, j : j + 1] = jnp.sum(
                    jnp.where(gap == j, total, 0.0), axis=0, keepdims=True
                )
            brow[pair * 2 + side, 17:24] = jnp.zeros((7, 512), F32)
        return carry

    lax.fori_loop(0, 4, pair_step, 0)

    fold = (
        lax.broadcasted_iota(jnp.int32, (512, 128), 0) // 16
        == lax.broadcasted_iota(jnp.int32, (512, 128), 1)
    ).astype(F32)
    folded = lax.dot_general(
        brow[...].reshape(192, 512), fold, (((1,), (0,)), ((), ())),
        precision=lax.Precision.HIGHEST, preferred_element_type=F32,
    )
    g_bias[...] = folded.reshape(8, 24, 128)

    x_t = xs[...].T
    own_t = jnp.concatenate([x_t[:, 320:448], x_t[:, 576:704]], axis=1)

    def hand_out(start, value):
        half, lanes = start // 1024, slice(start % 1024, start % 1024 + value.shape[1])
        value = value.astype(BF16)

        @pl.when(core[0] == half)
        def _():
            g_keep[:, lanes] = value

        @pl.when(core[0] != half)
        def _():
            g_send[:, lanes] = value

    hand_out(0, dot(own_t, dq_t[...], NT))
    for n in range(4):
        hand_out(512 + n * 256, dot(x_t, dkv[:, n * 256 : n * 256 + 256]))
    hand_out(1536, dot(att_t[...], cot[...]))
    d_q = dq_t[...].T
    homes = (
        ((g_tl, 0, 0, 64), (g_top, 0, 64, 128), (g_tr, 0, 192, 64)),
        ((g_left, 0, 0, 64), (None, 0, 64, 128), (g_right, 0, 192, 64)),
        ((g_left, 64, 0, 64), (None, 128, 64, 128), (g_right, 64, 192, 64)),
        ((g_bl, 0, 0, 64), (g_bottom, 0, 64, 128), (g_br, 0, 192, 64)),
    )
    for g in range(4):
        block = dot(dkv[g * 256 : g * 256 + 256], wt[512:1536])
        for ref, to, at, size in homes[g]:
            part = block[at : at + size]
            if ref is None:
                grad_own[to : to + size] = part + dot(d_q[to : to + size], wt[0:512])
            else:
                ref[to : to + size] = part.astype(BF16)


def after_kernel(own, up, down, west, east, nw, ne, sw, se, out):
    total = own[...]
    low = [up[...].astype(F32), down[...].astype(F32)]
    side = [west[...].astype(F32), east[...].astype(F32)]
    for half in range(2):
        rows = slice(half * 8, half * 8 + 8)
        corner = (nw, ne) if half == 0 else (sw, se)
        for col in range(2):
            cells = slice(col * 8, col * 8 + 8)
            out[rows, cells] = (
                total[rows, cells]
                + low[half][:, cells]
                + side[col][rows]
                + corner[col][...].astype(F32)
            ).astype(BF16)


def reduce_all(core, keep, send, bias):
    az, rng = lax.axis_size("az"), lax.axis_size("rng")

    def among(leaf, flip):
        return lax.ppermute(leaf, "dp", [(i, i ^ flip) for i in range(4)])

    half = (keep.astype(F32) + among(send, 1).astype(F32)).astype(BF16)
    rows = 512 // (az * rng)
    cols = -(-bias.size // (rows * 128)) * 128
    flat = jnp.pad(bias.reshape(-1), (0, rows * cols - bias.size)).astype(BF16)
    flat = jnp.broadcast_to(flat.reshape(1, rows, cols), (az * rng, rows, cols))
    parcel = jnp.concatenate([half.reshape(az * rng, rows, 1024), flat], axis=2)
    parcel = lax.all_to_all(parcel, ("az", "rng"), 0, 0, tiled=True)
    mine = jnp.sum(parcel.astype(F32), axis=0)
    near, other, far = among(mine, 2), among(mine, 1), among(mine, 3)
    here = mine + near
    there = other + far
    total_bias = (here[:, 1024:] + there[:, 1024:]).reshape(-1)[: bias.size].reshape(bias.shape)
    here, there = here[:, :1024], there[:, :1024]
    low = jnp.where(core == 0, here, there)
    high = jnp.where(core == 0, there, here)
    return jnp.concatenate([low, high[:, :512]], axis=1), high[:, 512:], total_bias


def whole(shape, dtype):
    return jax.ShapeDtypeStruct(shape, dtype)


def call(kernel, operands, outs, scratch=(), prefetch=0, flops=0, name=None):
    spec = pl.BlockSpec(memory_space=pltpu.VMEM)
    scalar = pl.BlockSpec(memory_space=pltpu.SMEM)
    size = sum(leaf.size * leaf.dtype.itemsize for leaf in tuple(operands) + tuple(outs))
    return pl.pallas_call(
        kernel,
        out_shape=tuple(outs),
        in_specs=[scalar] * prefetch + [spec] * (len(operands) - prefetch),
        out_specs=tuple([spec] * len(outs)),
        scratch_shapes=list(scratch),
        compiler_params=pltpu.CompilerParams(vmem_limit_bytes=VMEM_BYTES),
        cost_estimate=pl.CostEstimate(flops=flops, bytes_accessed=size, transcendentals=0),
        name=name,
    )(*operands)


def ring(count, step, closed):
    pairs = [(i, i + step) for i in range(count)]
    if closed:
        return [(a, b % count) for a, b in pairs]
    return [(a, b) for a, b in pairs if 0 <= b < count]


def diagonal(rows, cols, down, over):
    return [
        (a * cols + b, (a + down) % rows * cols + b + over)
        for a in range(rows)
        for b in range(cols)
        if 0 <= b + over < cols
    ]


def shards(tokens, qkv_weight, out_weight, relative_bias, cotangent):
    az, rng = lax.axis_size("az"), lax.axis_size("rng")
    width = tokens.shape[3]
    cells = tokens[0]
    own = cells.reshape(256, width)
    cot = cotangent.reshape(256, width)

    def along(leaf, axis, step):
        return lax.ppermute(leaf, axis, ring(az if axis == "az" else rng, step, axis == "az"))

    def across(leaf, down, over):
        return lax.ppermute(leaf, ("az", "rng"), diagonal(az, rng, down, over))

    halo = (
        along(cells[8:], "az", 1),
        along(cells[:8], "az", -1),
        along(cells[:, 8:], "rng", 1),
        along(cells[:, :8], "rng", -1),
        across(cells[8:, 8:], 1, 1),
        across(cells[8:, :8], 1, -1),
        across(cells[:8, 8:], -1, 1),
        across(cells[:8, :8], -1, -1),
    )
    halo = [leaf.reshape(-1, width) for leaf in halo]

    core = (lax.axis_index("dp") % 2).astype(jnp.int32)[None]
    at_range = lax.axis_index("rng")
    edge = jnp.stack([at_range == 0, at_range == rng - 1]).astype(jnp.int32)
    flipped = jnp.transpose(relative_bias[:, ::-1], (0, 2, 1))
    spread = jnp.pad(flipped, ((0, 0), (0, 7), (7, 8)), constant_values=ABSENT)
    bias_rows = jnp.repeat(spread, 16, axis=2)
    turned = qkv_weight.T

    q, q_t, da, da_t, table = call(
        before_kernel,
        (edge, own, cot, turned, out_weight, bias_rows),
        (
            whole((256, 512), BF16), whole((512, 256), BF16),
            whole((256, 512), BF16), whole((512, 256), BF16),
            whole((4, 768, 256), F32),
        ),
        prefetch=1,
        flops=600_000_000,
        name="before",
    )
    outs = call(
        main_kernel,
        (core, own, *halo, q, q_t, da, da_t, table, turned, cot),
        (
            whole((256, 512), F32),
            *[whole((128, 512), BF16)] * 4,
            *[whole((64, 512), BF16)] * 4,
            whole((512, 1024), BF16), whole((512, 1024), BF16),
            whole((8, 24, 128), F32),
        ),
        scratch=(
            pltpu.VMEM((1024, 512), BF16), pltpu.VMEM((1024, 512), BF16),
            pltpu.VMEM((1024, 512), BF16), pltpu.VMEM((512, 1024), BF16),
            pltpu.VMEM((512, 1024), BF16), pltpu.VMEM((1024, 1024), BF16),
            pltpu.VMEM((512, 256), BF16), pltpu.VMEM((512, 256), BF16),
            pltpu.VMEM((768, 256), F32), pltpu.VMEM((8, 24, 512), F32),
        ),
        prefetch=1,
        flops=10_000_000_000,
        name="attention",
    )
    grad_own, g_top, g_bottom, g_left, g_right, g_tl, g_tr, g_bl, g_br = outs[:9]
    g_keep, g_send, g_bias = outs[9:]
    arrived = (
        along(g_bottom.reshape(8, 16, width), "az", 1),
        along(g_top.reshape(8, 16, width), "az", -1),
        along(g_right.reshape(16, 8, width), "rng", 1),
        along(g_left.reshape(16, 8, width), "rng", -1),
        across(g_br.reshape(8, 8, width), 1, 1),
        across(g_bl.reshape(8, 8, width), 1, -1),
        across(g_tr.reshape(8, 8, width), -1, 1),
        across(g_tl.reshape(8, 8, width), -1, -1),
    )
    (grad_tokens,) = call(
        after_kernel,
        (grad_own.reshape(16, 16, width), *arrived),
        (whole((16, 16, width), BF16),),
        flops=1_000_000,
        name="after",
    )
    bias_local = jnp.transpose(g_bias[:, :17, 7:24], (0, 2, 1))[:, ::-1]
    rows_qkv, rows_out, total_bias = reduce_all(core[0], g_keep, g_send, bias_local)
    return (grad_tokens[None], rows_qkv, rows_out, total_bias)


def solution(mesh):
    placed = (P("dp", "az", "rng", None), P(), P(), P(), P("dp", "az", "rng", None))
    return jax.shard_map(
        shards,
        mesh=mesh,
        in_specs=placed,
        out_specs=(P("dp", "az", "rng", None), P(("az", "rng"), None), P(("az", "rng"), None), P()),
        check_vma=False,
    )
```

time: 525 us -> 148 us (0.28); the launches traced: 516 us -> 146 us
  waiting for transfers between devices: 182 us -> 25.2 us
  local copies, waits for them, and re-layouts: 158 us -> 14.9 us
  blocking collectives: 83.8 us -> 0 us
  starting transfers between devices: 16.8 us -> 69.6 us
  matrix products: 32.1 us -> 0 us
  Pallas kernels: 0 us -> 31.3 us
  between operations: 22.6 us -> 1.04 us
  other arithmetic: 21 us -> 4.39 us
    psum x1 -> x0, waiting for transfers between devices: 178 us -> none  [shards(): lax.psum((local_qkv, local_out, bias_local), ('az', 'rng', 'dp'))]
    psum x1 -> x0, blocking collectives: 83.8 us -> none  [shards(): lax.psum((local_qkv, local_out, bias_local), ('az', 'rng', 'dp'))]
    ppermute x8 -> x20, starting transfers between devices: 16.7 us -> 56.1 us  [the longest x8 30.4 us: across(): return lax.ppermute(leaf, ('az', 'rng'), diagonal(az, rng, down, over))]
    gather x36 -> x0, local copies, waits for them, and re-layouts: 35.3 us -> none
    slice x14 -> x4, local copies, waits for them, and re-layouts: 37.9 us -> 4.95 us  [the longest x1 1.7 us: shards(): cells[:8, :8]]
    dot_general x15 -> x0, matrix products: 32.1 us -> none  [the longest x1 4.99 us: bias_grad(): jnp.einsum('hijkl,ikx->hxjl', shaped, along, precision=lax.Precision.HIGH...]
    pallas_call x0 -> x3, Pallas kernels: none -> 31.3 us  [call(): pl.pallas_call(kernel, out_shape=tuple(outs), in_specs=[scalar] * prefetc...]
    ppermute x8 -> x20, waiting for transfers between devices: 3.19 us -> 25.2 us  [the longest x8 22.1 us: across(): return lax.ppermute(leaf, ('az', 'rng'), diagonal(az, rng, down, over))]
  transfers between devices with their start and end apart: 9 -> 21, of which waited for: 2 -> 5; matrix products, arithmetic and copies ran while one was open for 13% -> 8% of each run, Pallas kernels for 0% -> 5%
where the time goes in v1:
time: 148 us; the launch traced here: 146 us
  starting transfers between devices  69.6 us (47%)
  Pallas kernels  31.3 us (21%)
  waiting for transfers between devices  25.2 us (17%)
  local copies, waits for them, and re-layouts  14.9 us (10%)
  other arithmetic  4.39 us (3%)
    pallas_call x3, Pallas kernels, call(): pl.pallas_call(kernel, out_shape=tuple(outs), in_specs=[scalar] * prefetc...  31.3 us
    ppermute x8, starting transfers between devices, across(): return lax.ppermute(leaf, ('az', 'rng'), diagonal(az, rng, down, over))  30.4 us
    ppermute x8, waiting for transfers between devices, across(): return lax.ppermute(leaf, ('az', 'rng'), diagonal(az, rng, down, over))  22.1 us
    ppermute x8, starting transfers between devices, along(): lax.ppermute(leaf, axis, ring(az if axis == 'az' else rng, step, axis ==...  16.9 us
    all_to_all x1, starting transfers between devices, reduce_all(): parcel = lax.all_to_all(parcel, ('az', 'rng'), 0, 0, tiled=True)  13.5 us
    ppermute x4, starting transfers between devices, among(): return lax.ppermute(leaf, 'dp', [(i, i ^ flip) for i in range(4)])  8.74 us
    reshape x1, local copies, waits for them, and re-layouts, shards(): bias_rows = jnp.repeat(spread, 16, axis=2)  3.27 us
    unnamed x43, local copies, waits for them, and re-layouts  3.1 us
  transfers between devices with their start and end apart: 21, of which 5 were waited for; matrix products, arithmetic and copies ran while one was open for 8% of the time, Pallas kernels for 5%

profile of v1, /device:TPU:1, one launch (start us, length us, event | category | flops | bytes accessed | tf_op | source)
XLA Modules:
  0.0 146.4 jit_solution(4866080588000698981)
XLA Ops:
  0.6 1.7 %fusion.1 = (bf16[8,8,512]{2,1,0:T(8,128)(2,1)S(1)}, bf16[8,8,512]{2,1,0:T(8,128)(2,1)S(1)}, bf16[8,8,512]{2,1,0:T(8,128)(2,1)S(1)}, bf16[8,8,512]{2,1,0:T(8,128)(2,1)}) fusion(bf16[16,16,512]{2,1,0:T(8,128)(2,1)} %bitcast.40), kind=kLoop, calls=%fused_computation.13 | loop fusion | bytes 524288 | tf_op jit(solution)/shard_map/slice | solution.py:326
  2.3 1.3 collective-permute-start.5
  3.6 9.9 %collective-permute-start.6 = (bf16[8,8,512]{2,1,0:T(8,128)(2,1)S(1)}, bf16[8,8,512]{2,1,0:T(8,128)(2,1)S(1)}, u32[]{:S(2)}, u32[]{:S(2)}) collective-permute-start(bf16[8,8,512]{2,1,0:T(8,128)(2,1)S(1)} %get-tuple-element.47), channel_id=1, source_target_pairs={{0,228},{4,232},{8,236},{12,240},{16,244},{20,248},{24,252},{32,4}... | collective-permute-start | bytes 196616 | tf_op jit(solution)/shard_map/ppermute | solution.py:316
  13.5 1.3 collective-permute-start.7
  14.8 5.5 %collective-permute-start.4 = (bf16[8,8,512]{2,1,0:T(8,128)(2,1)}, bf16[8,8,512]{2,1,0:T(8,128)(2,1)}, u32[]{:S(2)}, u32[]{:S(2)}) collective-permute-start(bf16[8,8,512]{2,1,0:T(8,128)(2,1)} %get-tuple-element.49), channel_id=1, source_target_pairs={{0,36},{4,40},{8,44},{12,48},{16,52},{20,56},{24,60},{32,68},{36,7... | collective-permute-start | bytes 196616 | tf_op jit(solution)/shard_map/ppermute | solution.py:316
  20.3 1.0 fusion.2
  21.3 3.2 %collective-permute-start.2 = (bf16[16,8,512]{2,1,0:T(8,128)(2,1)S(1)}, bf16[16,8,512]{2,1,0:T(8,128)(2,1)}, u32[]{:S(2)}, u32[]{:S(2)}) collective-permute-start(bf16[16,8,512]{2,1,0:T(8,128)(2,1)S(1)} %get-tuple-element.51), channel_id=1, source_target_pairs={{0,4},{4,8},{8,12},{12,16},{16,20},{20,24},{24,28},{1,5},{5,9},{9,... | collective-permute-start | bytes 393224 | tf_op jit(solution)/shard_map/ppermute | solution.py:313
  24.5 1.6 %slice_bitcast_fusion = (bf16[8,16,512]{2,1,0:T(8,128)(2,1)S(1)}, bf16[8,16,512]{2,1,0:T(8,128)(2,1)}) fusion(bf16[1,16,16,512]{3,2,1,0:T(8,128)(2,1)} %param.5), kind=kLoop, calls=%fused_computation.4 | loop fusion | bytes 524288 | tf_op jit(solution)/shard_map/slice | solution.py:320
  26.1 0.9 reverse_bitcast_fusion
  27.0 1.3 collective-permute-start.3
  28.3 0.1 collective-permute-start
  28.5 2.7 %collective-permute-start.1 = (bf16[8,16,512]{2,1,0:T(8,128)(2,1)S(1)}, bf16[8,16,512]{2,1,0:T(8,128)(2,1)}, u32[]{:S(2)}, u32[]{:S(2)}) collective-permute-start(bf16[8,16,512]{2,1,0:T(8,128)(2,1)S(1)} %get-tuple-element.52), channel_id=1, source_target_pairs={{0,224},{32,0},{64,32},{96,64},{128,96},{160,128},{192,160},{224,1... | collective-permute-start | bytes 393224 | tf_op jit(solution)/shard_map/ppermute | solution.py:313
  31.2 0.6 add_convert_fusion.1.edge
  31.8 1.6 %copy.15 = bf16[512,1536]{0,1:T(8,128)(2,1)} copy(bf16[512,1536]{1,0:T(8,128)(2,1)S(1)} %copy-done) | data formatting | bytes 3145728 | tf_op args[1]
  33.4 0.1 copy.19
  33.6 0.1 pad.9.clone
  33.6 0.9 broadcast_in_dim.17
  34.5 3.3 %reshape.91.rows = f32[8,24,512]{2,1,0:T(8,128)} reshape(f32[8,24,32,16]{3,2,1,0:T(8,128)S(1)} %broadcast_in_dim.17) | data formatting | bytes 786432 | tf_op jit(solution)/shard_map/reshape | solution.py:335
  37.8 5.6 %before.1 = (bf16[256,512]{1,0:T(8,128)(2,1)}, bf16[512,256]{1,0:T(8,128)(2,1)}, bf16[256,512]{1,0:T(8,128)(2,1)}, bf16[512,256]{1,0:T(8,128)(2,1)}, f32[4,768,256]{2,1,0:T(8,128)}) custom-call(s32[2]{0:T(128)} %add_convert_fusion.1.edge, bf16[256,512]{1,0:T(8,128)(2,1)} %bitcast.42, bf16[256,512]{1,0:T(8,128)(2,1)} %bitcast.45, bf16[1536,512]{1,0:T(8,128)(2,1)} %bitcast.38, ...), custom_call_target="tpu_custom_call" | custom-call | flops 600000000 | bytes 7208968 | tf_op jit(solution)/shard_map/before/pallas_call | solution.py:277
  43.4 0.0 collective-permute-done.4
  43.4 0.0 collective-permute-done.2
  43.4 0.0 collective-permute-done
  43.4 0.0 collective-permute-done.1
  43.5 23.6 %attention.1 = (f32[256,512]{1,0:T(8,128)}, bf16[128,512]{1,0:T(8,128)(2,1)}, bf16[128,512]{1,0:T(8,128)(2,1)}, bf16[128,512]{1,0:T(8,128)(2,1)}, bf16[128,512]{...) custom-call(s32[1]{0:T(128)} %bitcast.core, ...), custom_call_target="tpu_custom_call" | custom-call | flops 10000000000 | bytes 10584068 | tf_op jit(solution)/shard_map/attention/pallas_call | solution.py:277
  67.0 2.4 %collective-permute-start.16 = (bf16[512,1024]{1,0:T(8,128)(2,1)}, bf16[512,1024]{1,0:T(8,128)(2,1)S(1)}, u32[]{:S(2)}, u32[]{:S(2)}) collective-permute-start(bf16[512,1024]{1,0:T(8,128)(2,1)} %get-tuple-element.36), channel_id=1, source_target_pairs={{0,1},{1,0},{2,3},{3,2},{4,5},{5,4},{6,7},{7,6},{8,9},{9,8},{10,11... | collective-permute-start | bytes 3145736 | tf_op jit(solution)/shard_map/ppermute | solution.py:249
  69.5 1.0 slice_bitcast_fusion.2
  70.5 0.1 rev.7
  70.6 0.1 copy.17
  70.7 0.2 reshape.102
  71.0 1.0 collective-permute-done.16
  72.0 1.6 %fusion = bf16[64,8,1024]{2,1,0:T(8,128)(2,1)S(1)} fusion(bf16[512,1024]{1,0:T(8,128)(2,1)S(1)} %collective-permute-done.16, bf16[512,1024]{1,0:T(8,128)(2,1)} %get-tuple-element.35), kind=kLoop, calls=%fused_computation.3 | loop fusion | flops 2097152 | bytes 3145728 | tf_op jit(solution)/shard_map/reshape | solution.py:256
  73.6 1.3 pad_maximum_fusion
  74.9 0.0 copy-start.16
  75.0 13.5 %all-to-all-start = ((bf16[64,8,1408]{2,1,0:T(8,128)(2,1)}), bf16[64,8,1408]{2,1,0:T(8,128)(2,1)S(1)}, u32[]{:S(2)}, u32[]{:S(2)}) async-start(bf16[64,8,1408]{2,1,0:T(8,128)(2,1)} %pad_maximum_fusion), calls=%async_computation | async-start | bytes 2883584 | tf_op jit(solution)/shard_map/all_to_all | solution.py:257
  88.5 3.8 %collective-permute-start.12 = (bf16[8,8,512]{2,1,0:T(8,128)(2,1)S(1)}, bf16[8,8,512]{2,1,0:T(8,128)(2,1)S(1)}, u32[]{:S(2)}, u32[]{:S(2)}) collective-permute-start(bf16[8,8,512]{2,1,0:T(8,128)(2,1)S(1)} %bitcast.59), channel_id=1, source_target_pairs={{0,36},{4,40},{8,44},{12,48},{16,52},{20,56},{24,60},{32,68},{36,7... | collective-permute-start | bytes 196616 | tf_op jit(solution)/shard_map/ppermute | solution.py:316
  92.3 1.3 collective-permute-start.13
  93.7 6.1 %collective-permute-start.14 = (bf16[8,8,512]{2,1,0:T(8,128)(2,1)S(1)}, bf16[8,8,512]{2,1,0:T(8,128)(2,1)S(1)}, u32[]{:S(2)}, u32[]{:S(2)}) collective-permute-start(bf16[8,8,512]{2,1,0:T(8,128)(2,1)S(1)} %bitcast.57), channel_id=1, source_target_pairs={{0,228},{4,232},{8,236},{12,240},{16,244},{20,248},{24,252},{32,4}... | collective-permute-start | bytes 196616 | tf_op jit(solution)/shard_map/ppermute | solution.py:316
  99.8 3.1 %collective-permute-start.10 = (bf16[16,8,512]{2,1,0:T(8,128)(2,1)S(1)}, bf16[16,8,512]{2,1,0:T(8,128)(2,1)S(1)}, u32[]{:S(2)}, u32[]{:S(2)}) collective-permute-start(bf16[16,8,512]{2,1,0:T(8,128)(2,1)S(1)} %bitcast.52), channel_id=1, source_target_pairs={{0,4},{4,8},{8,12},{12,16},{16,20},{20,24},{24,28},{1,5},{5,9},{9,... | collective-permute-start | bytes 393224 | tf_op jit(solution)/shard_map/ppermute | solution.py:313
  102.9 1.3 collective-permute-start.11
  104.2 13.0 %collective-permute-done.12.nw = bf16[8,8,512]{2,1,0:T(8,128)(2,1)S(1)} collective-permute-done((bf16[8,8,512]{2,1,0:T(8,128)(2,1)S(1)}, bf16[8,8,512]{2,1,0:T(8,128)(2,1)S(1)}, u32[]{:S(2)}, u32[]{:S(2)}) %collective-permute-start.12) | collective-permute-done | bytes 65568 | tf_op jit(solution)/shard_map/ppermute | solution.py:316
  117.2 4.0 %collective-permute-start.8 = (bf16[8,16,512]{2,1,0:T(8,128)(2,1)S(1)}, bf16[8,16,512]{2,1,0:T(8,128)(2,1)S(1)}, u32[]{:S(2)}, u32[]{:S(2)}) collective-permute-start(bf16[8,16,512]{2,1,0:T(8,128)(2,1)S(1)} %bitcast.50), channel_id=1, source_target_pairs={{0,32},{32,64},{64,96},{96,128},{128,160},{160,192},{192,224},{224... | collective-permute-start | bytes 393224 | tf_op jit(solution)/shard_map/ppermute | solution.py:313
  121.2 4.0 %collective-permute-done.13.ne = bf16[8,8,512]{2,1,0:T(8,128)(2,1)S(1)} collective-permute-done((bf16[8,8,512]{2,1,0:T(8,128)(2,1)S(1)}, bf16[8,8,512]{2,1,0:T(8,128)(2,1)S(1)}, u32[]{:S(2)}, u32[]{:S(2)}) %collective-permute-start.13) | collective-permute-done | bytes 65568 | tf_op jit(solution)/shard_map/ppermute | solution.py:316
  125.3 1.2 collective-permute-start.9
  126.5 0.0 collective-permute-done.14.sw
  126.5 1.3 collective-permute-start.15
  127.8 0.0 all-to-all-done
  127.8 0.2 convert_reduce_fusion
  128.0 5.1 %collective-permute-done.15.se = bf16[8,8,512]{2,1,0:T(8,128)(2,1)S(1)} collective-permute-done((bf16[8,8,512]{2,1,0:T(8,128)(2,1)S(1)}, bf16[8,8,512]{2,1,0:T(8,128)(2,1)S(1)}, u32[]{:S(2)}, u32[]{:S(2)}) %collective-permute-start.15) | collective-permute-done | bytes 65568 | tf_op jit(solution)/shard_map/ppermute | solution.py:316
  133.1 2.9 %collective-permute-start.17 = (f32[8,1408]{1,0:T(8,128)S(1)}, f32[8,1408]{1,0:T(8,128)S(1)}, u32[]{:S(2)}, u32[]{:S(2)}) collective-permute-start(f32[8,1408]{1,0:T(8,128)S(1)} %convert_reduce_fusion), channel_id=1, source_target_pairs={{0,2},{1,3},{2,0},{3,1},{4,6},{5,7},{6,4},{7,5},{8,10},{9,11},{10,... | collective-permute-start | bytes 135176 | tf_op jit(solution)/shard_map/ppermute | solution.py:249
  136.0 0.0 collective-permute-done.10.west
  136.0 3.3 %collective-permute-start.18 = (f32[8,1408]{1,0:T(8,128)S(1)}, f32[8,1408]{1,0:T(8,128)S(1)}, u32[]{:S(2)}, u32[]{:S(2)}) collective-permute-start(f32[8,1408]{1,0:T(8,128)S(1)} %convert_reduce_fusion), channel_id=1, source_target_pairs={{0,1},{1,0},{2,3},{3,2},{4,5},{5,4},{6,7},{7,6},{8,9},{9,8},{10,11... | collective-permute-start | bytes 135176 | tf_op jit(solution)/shard_map/ppermute | solution.py:249
  139.4 0.0 collective-permute-start.19
  139.4 0.0 collective-permute-done.9.down
  139.5 0.5 copy-done.2
  140.0 0.1 copy-done.3
  140.1 0.1 copy-done.4
  140.1 2.1 %after.1 = bf16[16,16,512]{2,1,0:T(8,128)(2,1)} custom-call(f32[16,16,512]{2,1,0:T(8,128)} %bitcast.44, bf16[8,16,512]{2,1,0:T(8,128)(2,1)} %copy-done.3, bf16[8,16,512]{2,1,0:T(8,128)(2,1)} %copy-done.4, bf16[16,8,512]{2,1,0:T(8,128)(2,1)} %copy-done.1, bf16[16,8,512]{2,1,0:T(8,128)(2,1)} %copy-done.2, bf16[8,8,512]{2,1,0:T(8,128)(2,1)} %copy-done.5, ...), custom_call_target="tpu_custom_call" | custom-call | flops 1000000 | bytes 1572864 | tf_op jit(solution)/shard_map/after/pallas_call | solution.py:277
  142.2 0.0 collective-permute-done.17
  142.2 0.0 collective-permute-done.18
  142.3 2.1 %collective-permute-done.19 = f32[8,1408]{1,0:T(8,128)S(1)} collective-permute-done((f32[8,1408]{1,0:T(8,128)S(1)}, f32[8,1408]{1,0:T(8,128)S(1)}, u32[]{:S(2)}, u32[]{:S(2)}) %collective-permute-start.19) | collective-permute-done | bytes 45088 | tf_op jit(solution)/shard_map/ppermute | solution.py:249
  144.4 0.2 reshape.104
  144.6 0.6 copy.18
  145.2 0.6 fusion.3
  145.8 0.6 pad_maximum_fusion.1
  (50 shorter events, 0.2 us)
Async XLA Ops:
  0.6 31.2 %copy-start = (bf16[512,1536]{1,0:T(8,128)(2,1)S(1)}, bf16[512,1536]{1,0:T(8,128)(2,1)}, u32[]{:S(2)}) copy-start(bf16[512,1536]{1,0:T(8,128)(2,1)} %param.6) | copy-start | bytes 4718596
  2.3 24.7 %collective-permute-start.5 = (bf16[8,8,512]{2,1,0:T(8,128)(2,1)S(1)}, bf16[8,8,512]{2,1,0:T(8,128)(2,1)S(1)}, u32[]{:S(2)}, u32[]{:S(2)}) collective-permute-start(bf16[8,8,512]{2,1,0:T(8,128)(2,1)S(1)} %get-tuple-element.48), channel_id=1, source_target_pairs={{4,32},{8,36},{12,40},{16,44},{20,48},{24,52},{28,56},{36,64},{40,... | collective-permute-start | bytes 196616 | tf_op jit(solution)/shard_map/ppermute | solution.py:316
  3.6 24.7 %collective-permute-start.6 = (bf16[8,8,512]{2,1,0:T(8,128)(2,1)S(1)}, bf16[8,8,512]{2,1,0:T(8,128)(2,1)S(1)}, u32[]{:S(2)}, u32[]{:S(2)}) collective-permute-start(bf16[8,8,512]{2,1,0:T(8,128)(2,1)S(1)} %get-tuple-element.47), channel_id=1, source_target_pairs={{0,228},{4,232},{8,236},{12,240},{16,244},{20,248},{24,252},{32,4}... | collective-permute-start | bytes 196616 | tf_op jit(solution)/shard_map/ppermute | solution.py:316
  13.5 14.9 %collective-permute-start.7 = (bf16[8,8,512]{2,1,0:T(8,128)(2,1)S(1)}, bf16[8,8,512]{2,1,0:T(8,128)(2,1)S(1)}, u32[]{:S(2)}, u32[]{:S(2)}) collective-permute-start(bf16[8,8,512]{2,1,0:T(8,128)(2,1)S(1)} %get-tuple-element.46), channel_id=1, source_target_pairs={{4,224},{8,228},{12,232},{16,236},{20,240},{24,244},{28,248},{36,0... | collective-permute-start | bytes 196616 | tf_op jit(solution)/shard_map/ppermute | solution.py:316
  14.8 28.6 %collective-permute-start.4 = (bf16[8,8,512]{2,1,0:T(8,128)(2,1)}, bf16[8,8,512]{2,1,0:T(8,128)(2,1)}, u32[]{:S(2)}, u32[]{:S(2)}) collective-permute-start(bf16[8,8,512]{2,1,0:T(8,128)(2,1)} %get-tuple-element.49), channel_id=1, source_target_pairs={{0,36},{4,40},{8,44},{12,48},{16,52},{20,56},{24,60},{32,68},{36,7... | collective-permute-start | bytes 196616 | tf_op jit(solution)/shard_map/ppermute | solution.py:316
  21.3 22.1 %collective-permute-start.2 = (bf16[16,8,512]{2,1,0:T(8,128)(2,1)S(1)}, bf16[16,8,512]{2,1,0:T(8,128)(2,1)}, u32[]{:S(2)}, u32[]{:S(2)}) collective-permute-start(bf16[16,8,512]{2,1,0:T(8,128)(2,1)S(1)} %get-tuple-element.51), channel_id=1, source_target_pairs={{0,4},{4,8},{8,12},{12,16},{16,20},{20,24},{24,28},{1,5},{5,9},{9,... | collective-permute-start | bytes 393224 | tf_op jit(solution)/shard_map/ppermute | solution.py:313
  27.0 6.5 %copy-start.13 = (bf16[8,8,512]{2,1,0:T(8,128)(2,1)}, bf16[8,8,512]{2,1,0:T(8,128)(2,1)S(1)}, u32[]{:S(2)}) copy-start(bf16[8,8,512]{2,1,0:T(8,128)(2,1)S(1)} %collective-permute-done.5) | copy-start | bytes 196612
  27.0 16.4 %collective-permute-start.3 = (bf16[16,8,512]{2,1,0:T(8,128)(2,1)S(1)}, bf16[16,8,512]{2,1,0:T(8,128)(2,1)}, u32[]{:S(2)}, u32[]{:S(2)}) collective-permute-start(bf16[16,8,512]{2,1,0:T(8,128)(2,1)S(1)} %get-tuple-element.50), channel_id=1, source_target_pairs={{4,0},{8,4},{12,8},{16,12},{20,16},{24,20},{28,24},{5,1},{9,5},{13... | collective-permute-start | bytes 393224 | tf_op jit(solution)/shard_map/ppermute | solution.py:313
  28.3 5.2 %copy-start.14 = (bf16[8,8,512]{2,1,0:T(8,128)(2,1)}, bf16[8,8,512]{2,1,0:T(8,128)(2,1)S(1)}, u32[]{:S(2)}) copy-start(bf16[8,8,512]{2,1,0:T(8,128)(2,1)S(1)} %collective-permute-done.6) | copy-start | bytes 196612
  28.3 15.1 %collective-permute-start = (bf16[8,16,512]{2,1,0:T(8,128)(2,1)}, bf16[8,16,512]{2,1,0:T(8,128)(2,1)}, u32[]{:S(2)}, u32[]{:S(2)}) collective-permute-start(bf16[8,16,512]{2,1,0:T(8,128)(2,1)} %get-tuple-element.53), channel_id=1, source_target_pairs={{0,32},{32,64},{64,96},{96,128},{128,160},{160,192},{192,224},{224... | collective-permute-start | bytes 393224 | tf_op jit(solution)/shard_map/ppermute | solution.py:313
  28.4 5.1 %copy-start.15 = (bf16[8,8,512]{2,1,0:T(8,128)(2,1)}, bf16[8,8,512]{2,1,0:T(8,128)(2,1)S(1)}, u32[]{:S(2)}) copy-start(bf16[8,8,512]{2,1,0:T(8,128)(2,1)S(1)} %collective-permute-done.7) | copy-start | bytes 196612
  28.5 15.0 %collective-permute-start.1 = (bf16[8,16,512]{2,1,0:T(8,128)(2,1)S(1)}, bf16[8,16,512]{2,1,0:T(8,128)(2,1)}, u32[]{:S(2)}, u32[]{:S(2)}) collective-permute-start(bf16[8,16,512]{2,1,0:T(8,128)(2,1)S(1)} %get-tuple-element.52), channel_id=1, source_target_pairs={{0,224},{32,0},{64,32},{96,64},{128,96},{160,128},{192,160},{224,1... | collective-permute-start | bytes 393224 | tf_op jit(solution)/shard_map/ppermute | solution.py:313
  67.0 4.9 %collective-permute-start.16 = (bf16[512,1024]{1,0:T(8,128)(2,1)}, bf16[512,1024]{1,0:T(8,128)(2,1)S(1)}, u32[]{:S(2)}, u32[]{:S(2)}) collective-permute-start(bf16[512,1024]{1,0:T(8,128)(2,1)} %get-tuple-element.36), channel_id=1, source_target_pairs={{0,1},{1,0},{2,3},{3,2},{4,5},{5,4},{6,7},{7,6},{8,9},{9,8},{10,11... | collective-permute-start | bytes 3145736 | tf_op jit(solution)/shard_map/ppermute | solution.py:249
  74.9 13.6 %copy-start.19 = (bf16[64,512]{1,0:T(8,128)(2,1)S(1)}, bf16[64,512]{1,0:T(8,128)(2,1)}, u32[]{:S(2)}) copy-start(bf16[64,512]{1,0:T(8,128)(2,1)} %get-tuple-element.31) | copy-start | bytes 196612
  74.9 17.4 %copy-start.18 = (bf16[64,512]{1,0:T(8,128)(2,1)S(1)}, bf16[64,512]{1,0:T(8,128)(2,1)}, u32[]{:S(2)}) copy-start(bf16[64,512]{1,0:T(8,128)(2,1)} %get-tuple-element.32) | copy-start | bytes 196612
  74.9 18.7 %copy-start.17 = (bf16[64,512]{1,0:T(8,128)(2,1)S(1)}, bf16[64,512]{1,0:T(8,128)(2,1)}, u32[]{:S(2)}) copy-start(bf16[64,512]{1,0:T(8,128)(2,1)} %get-tuple-element.33) | copy-start | bytes 196612
  74.9 24.9 %copy-start.12 = (bf16[128,512]{1,0:T(8,128)(2,1)S(1)}, bf16[128,512]{1,0:T(8,128)(2,1)}, u32[]{:S(2)}) copy-start(bf16[128,512]{1,0:T(8,128)(2,1)} %get-tuple-element.29) | copy-start | bytes 393220
  74.9 28.0 %copy-start.11 = (bf16[128,512]{1,0:T(8,128)(2,1)S(1)}, bf16[128,512]{1,0:T(8,128)(2,1)}, u32[]{:S(2)}) copy-start(bf16[128,512]{1,0:T(8,128)(2,1)} %get-tuple-element.30) | copy-start | bytes 393220
  74.9 42.2 %copy-start.10 = (bf16[128,512]{1,0:T(8,128)(2,1)S(1)}, bf16[128,512]{1,0:T(8,128)(2,1)}, u32[]{:S(2)}) copy-start(bf16[128,512]{1,0:T(8,128)(2,1)} %get-tuple-element.27) | copy-start | bytes 393220
  74.9 50.3 %copy-start.9 = (bf16[128,512]{1,0:T(8,128)(2,1)S(1)}, bf16[128,512]{1,0:T(8,128)(2,1)}, u32[]{:S(2)}) copy-start(bf16[128,512]{1,0:T(8,128)(2,1)} %get-tuple-element.28) | copy-start | bytes 393220
  74.9 51.5 %copy-start.16 = (bf16[64,512]{1,0:T(8,128)(2,1)S(1)}, bf16[64,512]{1,0:T(8,128)(2,1)}, u32[]{:S(2)}) copy-start(bf16[64,512]{1,0:T(8,128)(2,1)} %get-tuple-element.34) | copy-start | bytes 196612
  75.0 52.8 %all-to-all-start = ((bf16[64,8,1408]{2,1,0:T(8,128)(2,1)}), bf16[64,8,1408]{2,1,0:T(8,128)(2,1)S(1)}, u32[]{:S(2)}, u32[]{:S(2)}) async-start(bf16[64,8,1408]{2,1,0:T(8,128)(2,1)} %pad_maximum_fusion), calls=%async_computation | async-start | bytes 2883584 | tf_op jit(solution)/shard_map/all_to_all | solution.py:257
  88.5 28.7 %collective-permute-start.12 = (bf16[8,8,512]{2,1,0:T(8,128)(2,1)S(1)}, bf16[8,8,512]{2,1,0:T(8,128)(2,1)S(1)}, u32[]{:S(2)}, u32[]{:S(2)}) collective-permute-start(bf16[8,8,512]{2,1,0:T(8,128)(2,1)S(1)} %bitcast.59), channel_id=1, source_target_pairs={{0,36},{4,40},{8,44},{12,48},{16,52},{20,56},{24,60},{32,68},{36,7... | collective-permute-start | bytes 196616 | tf_op jit(solution)/shard_map/ppermute | solution.py:316
  92.3 32.9 %collective-permute-start.13 = (bf16[8,8,512]{2,1,0:T(8,128)(2,1)S(1)}, bf16[8,8,512]{2,1,0:T(8,128)(2,1)S(1)}, u32[]{:S(2)}, u32[]{:S(2)}) collective-permute-start(bf16[8,8,512]{2,1,0:T(8,128)(2,1)S(1)} %bitcast.58), channel_id=1, source_target_pairs={{4,32},{8,36},{12,40},{16,44},{20,48},{24,52},{28,56},{36,64},{40,... | collective-permute-start | bytes 196616 | tf_op jit(solution)/shard_map/ppermute | solution.py:316
  93.7 32.8 %collective-permute-start.14 = (bf16[8,8,512]{2,1,0:T(8,128)(2,1)S(1)}, bf16[8,8,512]{2,1,0:T(8,128)(2,1)S(1)}, u32[]{:S(2)}, u32[]{:S(2)}) collective-permute-start(bf16[8,8,512]{2,1,0:T(8,128)(2,1)S(1)} %bitcast.57), channel_id=1, source_target_pairs={{0,228},{4,232},{8,236},{12,240},{16,244},{20,248},{24,252},{32,4}... | collective-permute-start | bytes 196616 | tf_op jit(solution)/shard_map/ppermute | solution.py:316
  99.8 36.2 %collective-permute-start.10 = (bf16[16,8,512]{2,1,0:T(8,128)(2,1)S(1)}, bf16[16,8,512]{2,1,0:T(8,128)(2,1)S(1)}, u32[]{:S(2)}, u32[]{:S(2)}) collective-permute-start(bf16[16,8,512]{2,1,0:T(8,128)(2,1)S(1)} %bitcast.52), channel_id=1, source_target_pairs={{0,4},{4,8},{8,12},{12,16},{16,20},{20,24},{24,28},{1,5},{5,9},{9,... | collective-permute-start | bytes 393224 | tf_op jit(solution)/shard_map/ppermute | solution.py:313
  102.9 36.5 %collective-permute-start.11 = (bf16[16,8,512]{2,1,0:T(8,128)(2,1)S(1)}, bf16[16,8,512]{2,1,0:T(8,128)(2,1)S(1)}, u32[]{:S(2)}, u32[]{:S(2)}) collective-permute-start(bf16[16,8,512]{2,1,0:T(8,128)(2,1)S(1)} %bitcast.51), channel_id=1, source_target_pairs={{4,0},{8,4},{12,8},{16,12},{20,16},{24,20},{28,24},{5,1},{9,5},{13... | collective-permute-start | bytes 393224 | tf_op jit(solution)/shard_map/ppermute | solution.py:313
  117.2 22.3 %copy-start.5 = (bf16[8,8,512]{2,1,0:T(8,128)(2,1)}, bf16[8,8,512]{2,1,0:T(8,128)(2,1)S(1)}, u32[]{:S(2)}) copy-start(bf16[8,8,512]{2,1,0:T(8,128)(2,1)S(1)} %collective-permute-done.12.nw) | copy-start | bytes 196612
  117.2 22.2 %collective-permute-start.8 = (bf16[8,16,512]{2,1,0:T(8,128)(2,1)S(1)}, bf16[8,16,512]{2,1,0:T(8,128)(2,1)S(1)}, u32[]{:S(2)}, u32[]{:S(2)}) collective-permute-start(bf16[8,16,512]{2,1,0:T(8,128)(2,1)S(1)} %bitcast.50), channel_id=1, source_target_pairs={{0,32},{32,64},{64,96},{96,128},{128,160},{160,192},{192,224},{224... | collective-permute-start | bytes 393224 | tf_op jit(solution)/shard_map/ppermute | solution.py:313
  125.2 14.2 %copy-start.6 = (bf16[8,8,512]{2,1,0:T(8,128)(2,1)}, bf16[8,8,512]{2,1,0:T(8,128)(2,1)S(1)}, u32[]{:S(2)}) copy-start(bf16[8,8,512]{2,1,0:T(8,128)(2,1)S(1)} %collective-permute-done.13.ne) | copy-start | bytes 196612
  125.3 14.2 %collective-permute-start.9 = (bf16[8,16,512]{2,1,0:T(8,128)(2,1)S(1)}, bf16[8,16,512]{2,1,0:T(8,128)(2,1)S(1)}, u32[]{:S(2)}, u32[]{:S(2)}) collective-permute-start(bf16[8,16,512]{2,1,0:T(8,128)(2,1)S(1)} %bitcast.49), channel_id=1, source_target_pairs={{0,224},{32,0},{64,32},{96,64},{128,96},{160,128},{192,160},{224,1... | collective-permute-start | bytes 393224 | tf_op jit(solution)/shard_map/ppermute | solution.py:313
  126.5 13.0 %copy-start.7 = (bf16[8,8,512]{2,1,0:T(8,128)(2,1)}, bf16[8,8,512]{2,1,0:T(8,128)(2,1)S(1)}, u32[]{:S(2)}) copy-start(bf16[8,8,512]{2,1,0:T(8,128)(2,1)S(1)} %collective-permute-done.14.sw) | copy-start | bytes 196612
  126.5 6.6 %collective-permute-start.15 = (bf16[8,8,512]{2,1,0:T(8,128)(2,1)S(1)}, bf16[8,8,512]{2,1,0:T(8,128)(2,1)S(1)}, u32[]{:S(2)}, u32[]{:S(2)}) collective-permute-start(bf16[8,8,512]{2,1,0:T(8,128)(2,1)S(1)} %bitcast.56), channel_id=1, source_target_pairs={{4,224},{8,228},{12,232},{16,236},{20,240},{24,244},{28,248},{36,0... | collective-permute-start | bytes 196616 | tf_op jit(solution)/shard_map/ppermute | solution.py:316
  133.1 6.4 %copy-start.8 = (bf16[8,8,512]{2,1,0:T(8,128)(2,1)}, bf16[8,8,512]{2,1,0:T(8,128)(2,1)S(1)}, u32[]{:S(2)}) copy-start(bf16[8,8,512]{2,1,0:T(8,128)(2,1)S(1)} %collective-permute-done.15.se) | copy-start | bytes 196612
  133.1 9.2 %collective-permute-start.17 = (f32[8,1408]{1,0:T(8,128)S(1)}, f32[8,1408]{1,0:T(8,128)S(1)}, u32[]{:S(2)}, u32[]{:S(2)}) collective-permute-start(f32[8,1408]{1,0:T(8,128)S(1)} %convert_reduce_fusion), channel_id=1, source_target_pairs={{0,2},{1,3},{2,0},{3,1},{4,6},{5,7},{6,4},{7,5},{8,10},{9,11},{10,... | collective-permute-start | bytes 135176 | tf_op jit(solution)/shard_map/ppermute | solution.py:249
  136.0 3.5 %copy-start.1 = (bf16[16,8,512]{2,1,0:T(8,128)(2,1)}, bf16[16,8,512]{2,1,0:T(8,128)(2,1)S(1)}, u32[]{:S(2)}) copy-start(bf16[16,8,512]{2,1,0:T(8,128)(2,1)S(1)} %collective-permute-done.10.west) | copy-start | bytes 393220
  136.0 6.3 %collective-permute-start.18 = (f32[8,1408]{1,0:T(8,128)S(1)}, f32[8,1408]{1,0:T(8,128)S(1)}, u32[]{:S(2)}, u32[]{:S(2)}) collective-permute-start(f32[8,1408]{1,0:T(8,128)S(1)} %convert_reduce_fusion), channel_id=1, source_target_pairs={{0,1},{1,0},{2,3},{3,2},{4,5},{5,4},{6,7},{7,6},{8,9},{9,8},{10,11... | collective-permute-start | bytes 135176 | tf_op jit(solution)/shard_map/ppermute | solution.py:249
  139.3 0.7 copy-start.2
  139.4 5.0 %collective-permute-start.19 = (f32[8,1408]{1,0:T(8,128)S(1)}, f32[8,1408]{1,0:T(8,128)S(1)}, u32[]{:S(2)}, u32[]{:S(2)}) collective-permute-start(f32[8,1408]{1,0:T(8,128)S(1)} %convert_reduce_fusion), channel_id=1, source_target_pairs={{0,3},{1,2},{2,1},{3,0},{4,7},{5,6},{6,5},{7,4},{8,11},{9,10},{10,... | collective-permute-start | bytes 135176 | tf_op jit(solution)/shard_map/ppermute | solution.py:249
  139.4 0.7 copy-start.3
  139.4 0.7 copy-start.4

commit v2 on v1

v2 whole, which is shorter than its diff:
```python
import jax
import jax.numpy as jnp
from jax import lax
from jax.experimental import pallas as pl
from jax.experimental.pallas import tpu as pltpu
from jax.sharding import PartitionSpec as P

F32 = jnp.float32
BF16 = jnp.bfloat16
ABSENT = -1e30
NT = (((1,), (1,)), ((), ()))
TN = (((0,), (0,)), ((), ()))
MIB = 1024 * 1024


def dot(a, b, dims=(((1,), (0,)), ((), ())), exact=False):
    precision = lax.Precision.HIGHEST if exact else None
    return lax.dot_general(a, b, dims, precision=precision, preferred_element_type=F32)


def iota(shape, axis):
    return lax.broadcasted_iota(jnp.int32, shape, axis)


def row_slots(row):
    base = row // 8 * 256
    at = row % 8
    return (
        (0, 8, base + at * 8),
        (8, 24, base + 64 + at * 16),
        (24, 32, base + 192 + at * 8),
    )


def before_kernel(edge, x, cot, wt, wo, bias, q, q_t, da, da_t, table):
    xv = x[...]
    cv = cot[...]
    q[...] = (dot(xv, wt[0:512], NT).astype(BF16).astype(F32) * 0.125).astype(BF16)
    q_t[...] = (dot(wt[0:512], xv, NT).astype(BF16).astype(F32) * 0.125).astype(BF16)
    da[...] = dot(cv, wo[...], NT).astype(BF16)
    da_t[...] = dot(wo[...], cv, NT).astype(BF16)
    pick = (iota((17, 512), 0) == 23 - (iota((17, 512), 1) >> 4)).astype(F32)
    range_row = iota((32, 512), 0)
    lane = iota((32, 512), 1)
    gap = range_row - (lane & 15)
    first = jnp.where(edge[0] == 1, 8, 0)
    last = jnp.where(edge[1] == 1, 24, 32)
    present = (range_row >= first) & (range_row < last) & (lane >= 112) & (lane < 384)

    def pair_step(pair, carry):
        for side in range(2):
            head_rows = dot(bias[pair * 2 + side], pick, TN, exact=True)
            spread = jnp.full((32, 512), ABSENT, F32)
            for j in range(17):
                spread = jnp.where(gap == j, head_rows[j : j + 1], spread)
            spread = jnp.where(present, spread, ABSENT)
            for v in range(8):
                turned = spread if v == 0 else pltpu.roll(spread, 512 - 16 * v, 1)
                for u in range(3):
                    block = turned[:, 128 * u : 128 * u + 128]
                    for low, high, at in row_slots(23 - 8 * u - v):
                        table[pair, at : at + high - low, side * 128 : side * 128 + 128] = block[
                            low:high
                        ]
        return carry

    lax.fori_loop(0, 4, pair_step, 0)


def project(block, wt, k, v, k_t, v_t, at):
    rows = pl.ds(at, 256)
    keys = dot(block, wt[512:1024], NT).astype(BF16)
    values = dot(block, wt[1024:1536], NT).astype(BF16)
    k[rows] = keys
    v[rows] = values
    k_t[:, rows] = keys.T
    v_t[:, rows] = values.T


def middle_kernel(upper, lower, wt, k, v, k_t, v_t):
    project(upper[...], wt, k, v, k_t, v_t, 0)
    project(lower[...], wt, k, v, k_t, v_t, 256)


def attention_kernel(
    core, above, upper, lower, below, q, q_t, da, da_t, table, k_mid, v_mid, kt_mid, vt_mid, wt, own, cot,
    dkv, dq_t, g_keep, g_send, g_bias,
    k, v, k_t, v_t, xs, att_t, dsum, bsum, lhs, rhs,
):
    project(above[...], wt, k, v, k_t, v_t, 0)
    project(below[...], wt, k, v, k_t, v_t, 768)
    k[256:768] = k_mid[...]
    v[256:768] = v_mid[...]
    k_t[:, 256:768] = kt_mid[...]
    v_t[:, 256:768] = vt_mid[...]
    for g, ref in enumerate((above, upper, lower, below)):
        xs[:, g * 256 : g * 256 + 256] = ref[...].T

    upper_rows = iota((128, 128), 0) < 64
    upper_lanes = iota((128, 128), 1) < 64
    corner = iota((16, 512), 0) == (iota((16, 512), 1) & 15)

    def split_lanes(block):
        zero = jnp.zeros_like(block)
        return jnp.concatenate(
            [jnp.where(upper_rows, block, zero), jnp.where(upper_rows, zero, block)], axis=1
        )

    def split_rows(block):
        zero = jnp.zeros_like(block)
        return jnp.concatenate(
            [jnp.where(upper_lanes, block, zero), jnp.where(upper_lanes, zero, block)], axis=0
        )

    def pair_step(pair, carry):
        at = pl.multiple_of(pair * 128, 128)
        cols = pl.ds(at, 128)
        tails = []
        for t in range(2):
            keys = slice(t * 256, t * 256 + 768)
            mine = slice(t * 128, t * 128 + 128)
            score = dot(k[keys, cols], split_lanes(q_t[cols, mine])) + table[pair]
            top_score = jnp.max(score, axis=0, keepdims=True)
            weight = jnp.exp(score - top_score)
            prob = weight * (1.0 / jnp.sum(weight, axis=0, keepdims=True))
            prob_low = prob.astype(BF16)
            mixed = dot(v_t[cols, keys], prob_low)
            att = jnp.where(upper_rows, mixed[:, :128], mixed[:, 128:]).astype(BF16)
            att_t[cols, mine] = att
            da_block = da_t[cols, mine]
            product = att.astype(F32) * da_block.astype(F32)
            delta = jnp.concatenate(
                [
                    jnp.sum(product[:64], axis=0, keepdims=True),
                    jnp.sum(product[64:], axis=0, keepdims=True),
                ],
                axis=1,
            )
            d_score = prob * (dot(v[keys, cols], split_lanes(da_block)) - delta)
            if t == 0:
                dsum[...] = d_score
            else:
                dsum[...] += d_score
            score_low = d_score.astype(BF16)
            d_q = dot(k_t[cols, keys], score_low)
            dq_t[cols, mine] = (
                jnp.where(upper_rows, d_q[:, :128], d_q[:, 128:]) * 0.125
            ).astype(BF16)
            tails.append(
                (
                    dot(score_low, split_rows(q[mine, cols])),
                    dot(prob_low, split_rows(da[mine, cols])),
                )
            )
        for which in range(2):
            early, late = tails[0][which], tails[1][which]
            to = pl.ds(pl.multiple_of(which * 512 + at, 128), 128)
            dkv[0:256, to] = early[0:256].astype(BF16)
            dkv[256:768, to] = (early[256:768] + late[0:512]).astype(BF16)
            dkv[768:1024, to] = late[512:768].astype(BF16)
        for side in range(2):
            lanes = slice(side * 128, side * 128 + 128)
            total = None
            for turn in range(8):
                parts = [
                    jnp.concatenate(
                        [
                            dsum[to : to + high - low, lanes]
                            for low, high, to in row_slots(23 - 8 * u - turn)
                        ],
                        axis=0,
                    )
                    for u in range(3)
                ]
                strip = jnp.concatenate(parts + [jnp.zeros((32, 128), F32)], axis=1)
                if turn:
                    strip = pltpu.roll(strip, 16 * turn, 1)
                total = strip if total is None else total + strip
            tail = total[16:32]
            last = jnp.where(corner, tail, 0.0)
            rest = jnp.where(corner, 0.0, tail)
            bsum[0, pair * 2 + side] = (
                total[0:8]
                + pltpu.roll(total[8:16], 504, 1)
                + pltpu.roll(rest[0:8], 496, 1)
                + pltpu.roll(rest[8:16], 488, 1)
            )
            bsum[1, pair * 2 + side] = pltpu.roll(last[0:8], 496, 1) + pltpu.roll(
                last[8:16], 488, 1
            )
        return carry

    lax.fori_loop(0, 4, pair_step, 0)

    spot = iota((512, 384), 0)
    place = iota((512, 384), 1)
    i = (place * 241) >> 12
    j = place - i * 17
    inside = place < 289
    flat = None
    for which in range(2):
        lanes = None
        for b in range(8):
            row = bsum[which, :, b, :]
            row = pltpu.roll(row, 512 - b, 1) if b else row
            lanes = row if lanes is None else lanes + row
        from_lane = 368 - 16 * i - j
        choose = inside & (spot == from_lane) & ((j < 16) if which == 0 else (j == 16))
        part = dot(lanes, choose.astype(F32), exact=True)
        flat = part if flat is None else flat + part
    g_bias[...] = flat

    lhs[0, :, 0:128] = xs[:, 320:448]
    lhs[0, :, 128:256] = xs[:, 576:704]
    lhs[1] = att_t[...]
    rhs[0] = dq_t[...].T
    rhs[1] = cot[...]
    for ref, who in ((g_send, 1 - core[0]), (g_keep, core[0])):
        ref[:, 0:512] = dot(lhs[who], rhs[who]).astype(BF16)
        for n in range(2):
            lanes = pl.ds(pl.multiple_of(who * 512 + n * 256, 256), 256)
            ref[:, 512 + n * 256 : 768 + n * 256] = dot(xs[...], dkv[:, lanes]).astype(BF16)


def tokens_kernel(dkv, dq_t, wt, g_above, g_upper, g_lower, g_below):
    d_q = dq_t[...].T
    for g, ref in enumerate((g_above, g_upper, g_lower, g_below)):
        block = dot(dkv[g * 256 : g * 256 + 256], wt[512:1536])
        if g in (0, 3):
            ref[...] = block.astype(BF16)
        else:
            half = (g - 1) * 128
            ref[0:64] = block[0:64]
            ref[64:192] = block[64:192] + dot(d_q[half : half + 128], wt[0:512])
            ref[192:256] = block[192:256]


def fold_kernel(g_upper, g_lower, up, down, west, own, east):
    for half, (ref, term) in enumerate(((g_upper, up), (g_lower, down))):
        total = ref[...] + term[...].astype(F32)
        west[half * 64 : half * 64 + 64] = total[0:64].astype(BF16)
        own[half * 128 : half * 128 + 128] = total[64:192]
        east[half * 64 : half * 64 + 64] = total[192:256].astype(BF16)


def after_kernel(own, west, east, out):
    out[:, 0:8] = (own[:, 0:8] + west[...].astype(F32)).astype(BF16)
    out[:, 8:16] = (own[:, 8:16] + east[...].astype(F32)).astype(BF16)


def pack_kernel(keep, came, bias, _, parcel):
    count, rows, _ = parcel.shape
    cols = bias.shape[1]
    both = keep[...].astype(F32) + came[...].astype(F32)
    parcel[:, :, 0:1024] = both.astype(BF16).reshape(count, rows, 1024)
    parcel[:, :, 1024 : 1024 + cols] = jnp.broadcast_to(
        bias[...].astype(BF16)[None], (count, rows, cols)
    )


def finish_kernel(core, mine, near, other, far, qkv, out, bias):
    here = mine[...] + near[...]
    there = other[...] + far[...]
    is_first = core[0] == 0
    low = jnp.where(is_first, here[:, 0:1024], there[:, 0:1024])
    high = jnp.where(is_first, there[:, 0:1024], here[:, 0:1024])
    qkv[:, 0:1024] = low
    qkv[:, 1024:1536] = high[:, 512:1024]
    out[...] = high[:, 0:512]
    total = here[:, 1024:] + there[:, 1024:]
    for i in range(17):
        bias[i] = total[:, i * 17 : i * 17 + 17]


def whole(shape, dtype):
    return jax.ShapeDtypeStruct(shape, dtype)


def call(kernel, operands, outs, scratch=(), prefetch=0, flops=0, limit=16):
    spec = pl.BlockSpec(memory_space=pltpu.VMEM)
    scalar = pl.BlockSpec(memory_space=pltpu.SMEM)
    size = sum(leaf.size * leaf.dtype.itemsize for leaf in tuple(operands) + tuple(outs))
    return pl.pallas_call(
        kernel,
        out_shape=tuple(outs),
        in_specs=[scalar] * prefetch + [spec] * (len(operands) - prefetch),
        out_specs=tuple([spec] * len(outs)),
        scratch_shapes=list(scratch),
        compiler_params=pltpu.CompilerParams(vmem_limit_bytes=limit * MIB),
        cost_estimate=pl.CostEstimate(flops=flops, bytes_accessed=size, transcendentals=0),
        name=kernel.__name__,
    )(*operands)


def shards(tokens, qkv_weight, out_weight, relative_bias, cotangent):
    az, rng = lax.axis_size("az"), lax.axis_size("rng")
    width = tokens.shape[3]
    cells = tokens[0]
    own = cells.reshape(256, width)
    cot = cotangent.reshape(256, width)

    def turn(leaf, step):
        return lax.ppermute(leaf, "az", [(i, (i + step) % az) for i in range(az)])

    def shift(leaf, step):
        pairs = [(i, i + step) for i in range(rng) if 0 <= i + step < rng]
        return lax.ppermute(leaf, "rng", pairs)

    def among(leaf, flip):
        return lax.ppermute(leaf, "dp", [(i, i ^ flip) for i in range(4)])

    left = shift(cells[:, 8:], 1).reshape(128, width)
    right = shift(cells[:, :8], -1).reshape(128, width)
    upper = jnp.concatenate([left[:64], own[:128], right[:64]], axis=0)
    lower = jnp.concatenate([left[64:], own[128:], right[64:]], axis=0)
    above = turn(lower, 1)
    below = turn(upper, -1)

    core = (lax.axis_index("dp") % 2).astype(jnp.int32)[None]
    at_range = lax.axis_index("rng")
    edge = jnp.stack([at_range == 0, at_range == rng - 1]).astype(jnp.int32)
    turned = qkv_weight.T

    q, q_t, da, da_t, table = call(
        before_kernel,
        (edge, own, cot, turned, out_weight, relative_bias),
        (
            whole((256, 512), BF16), whole((512, 256), BF16),
            whole((256, 512), BF16), whole((512, 256), BF16),
            whole((4, 768, 256), F32),
        ),
        prefetch=1,
        flops=600_000_000,
        limit=12,
    )
    middle = call(
        middle_kernel,
        (upper, lower, turned),
        (
            whole((512, 512), BF16), whole((512, 512), BF16),
            whole((512, 512), BF16), whole((512, 512), BF16),
        ),
        flops=1_000_000_000,
        limit=12,
    )
    dkv, dq_t, g_keep, g_send, g_bias = call(
        attention_kernel,
        (core, above, upper, lower, below, q, q_t, da, da_t, table, *middle, turned, own, cot),
        (
            whole((1024, 1024), BF16), whole((512, 256), BF16),
            whole((512, 1024), BF16), whole((512, 1024), BF16),
            whole((8, 384), F32),
        ),
        scratch=(
            pltpu.VMEM((1024, 512), BF16), pltpu.VMEM((1024, 512), BF16),
            pltpu.VMEM((512, 1024), BF16), pltpu.VMEM((512, 1024), BF16),
            pltpu.VMEM((512, 1024), BF16), pltpu.VMEM((512, 256), BF16),
            pltpu.VMEM((768, 256), F32), pltpu.VMEM((2, 8, 8, 512), F32),
            pltpu.VMEM((2, 512, 256), BF16), pltpu.VMEM((2, 256, 512), BF16),
        ),
        prefetch=1,
        flops=10_000_000_000,
        limit=20,
    )

    g_above, g_upper, g_lower, g_below = call(
        tokens_kernel,
        (dkv, dq_t, turned),
        (
            whole((256, 512), BF16), whole((256, 512), F32),
            whole((256, 512), F32), whole((256, 512), BF16),
        ),
        flops=1_200_000_000,
    )

    came = among(g_send, 1)
    rows = 512 // (az * rng)
    cols = 384
    if rows != 8:
        g_bias = jnp.pad(g_bias, ((0, rows - 8), (0, 0)))
    (parcel,) = call(
        pack_kernel,
        (g_keep, came, g_bias, g_above),
        (whole((az * rng, rows, 1024 + cols), BF16),),
        flops=1_000_000,
    )
    parcel = lax.all_to_all(parcel, ("az", "rng"), 0, 0, tiled=True)

    up = turn(g_below, 1)
    down = turn(g_above, -1)
    to_west, g_own, to_east = call(
        fold_kernel,
        (g_upper, g_lower, up, down),
        (whole((128, 512), BF16), whole((256, 512), F32), whole((128, 512), BF16)),
        flops=1_000_000,
    )
    east = shift(to_west.reshape(16, 8, width), -1)
    west = shift(to_east.reshape(16, 8, width), 1)
    (grad_tokens,) = call(
        after_kernel,
        (g_own.reshape(16, 16, width), west, east),
        (whole((16, 16, width), BF16),),
        flops=1_000_000,
    )

    mine = jnp.sum(parcel.astype(F32), axis=0)
    near, other, far = among(mine, 2), among(mine, 1), among(mine, 3)
    rows_qkv, rows_out, total_bias = call(
        finish_kernel,
        (core, mine, near, other, far),
        (whole((rows, 1536), F32), whole((rows, 512), F32), whole((17, rows, 17), F32)),
        prefetch=1,
        flops=1_000_000,
    )
    total_bias = jnp.transpose(total_bias[:, :8], (1, 0, 2))
    return (grad_tokens[None], rows_qkv, rows_out, total_bias)


def solution(mesh):
    placed = (P("dp", "az", "rng", None), P(), P(), P(), P("dp", "az", "rng", None))
    return jax.shard_map(
        shards,
        mesh=mesh,
        in_specs=placed,
        out_specs=(P("dp", "az", "rng", None), P(("az", "rng"), None), P(("az", "rng"), None), P()),
        check_vma=False,
    )
```

time: 148 us -> 111 us (0.75)
  the two profiles are of different devices: /device:TPU:1 before, /device:TPU:8 now
where the time goes in v2:
time: 111 us; the launch traced here: 110 us
  waiting for transfers between devices  42 us (38%)
  starting transfers between devices  39.3 us (35%)
  Pallas kernels  22.6 us (20%)
  local copies, waits for them, and re-layouts  3.71 us (3%)
  other arithmetic  1.7 us (2%)
    ppermute x4, waiting for transfers between devices, turn(): return lax.ppermute(leaf, 'az', [(i, (i + step) % az) for i in range(az)])  37.3 us
    pallas_call x8, Pallas kernels, call(): pl.pallas_call(kernel, out_shape=tuple(outs), in_specs=[scalar] * prefetc...  22.6 us
    ppermute x4, starting transfers between devices, shift(): return lax.ppermute(leaf, 'rng', pairs)  15.9 us
    all_to_all x1, starting transfers between devices, shards(): parcel = lax.all_to_all(parcel, ('az', 'rng'), 0, 0, tiled=True)  10.1 us
    ppermute x4, starting transfers between devices, turn(): return lax.ppermute(leaf, 'az', [(i, (i + step) % az) for i in range(az)])  9.52 us
    ppermute x4, waiting for transfers between devices, among(): return lax.ppermute(leaf, 'dp', [(i, i ^ flip) for i in range(4)])  4.76 us
    ppermute x4, starting transfers between devices, among(): return lax.ppermute(leaf, 'dp', [(i, i ^ flip) for i in range(4)])  3.82 us
    unnamed x8, local copies, waits for them, and re-layouts  2.68 us
  transfers between devices with their start and end apart: 13, of which 5 were waited for; matrix products, arithmetic and copies ran while one was open for 4% of the time, Pallas kernels for 6%

profile of v2, /device:TPU:8, one launch (start us, length us, event | category | flops | bytes accessed | tf_op | source)
XLA Modules:
  0.0 110.2 jit_solution(1750317843286738355)
XLA Ops:
  0.6 1.0 fusion.1
  1.6 3.4 %collective-permute-start = (bf16[16,8,512]{2,1,0:T(8,128)(2,1)S(1)}, bf16[16,8,512]{2,1,0:T(8,128)(2,1)S(1)}, u32[]{:S(2)}, u32[]{:S(2)}) collective-permute-start(bf16[16,8,512]{2,1,0:T(8,128)(2,1)S(1)} %get-tuple-element.54), channel_id=1, source_target_pairs={{0,4},{4,8},{8,12},{12,16},{16,20},{20,24},{24,28},{1,5},{5,9},{9,... | collective-permute-start | bytes 393224 | tf_op jit(solution)/shard_map/ppermute | solution.py:307
  5.0 4.6 %collective-permute-start.1 = (bf16[16,8,512]{2,1,0:T(8,128)(2,1)S(1)}, bf16[16,8,512]{2,1,0:T(8,128)(2,1)S(1)}, u32[]{:S(2)}, u32[]{:S(2)}) collective-permute-start(bf16[16,8,512]{2,1,0:T(8,128)(2,1)S(1)} %get-tuple-element.55), channel_id=1, source_target_pairs={{4,0},{8,4},{12,8},{16,12},{20,16},{24,20},{28,24},{5,1},{9,5},{13... | collective-permute-start | bytes 393224 | tf_op jit(solution)/shard_map/ppermute | solution.py:307
  9.6 0.9 copy.10.bias
  10.5 0.0 copy-start
  10.5 1.8 %copy.9 = bf16[512,1536]{0,1:T(8,128)(2,1)S(1)} copy(bf16[512,1536]{1,0:T(8,128)(2,1)} %param.6) | data formatting | bytes 3145728 | tf_op args[1]
  12.3 0.0 copy-start.1
  12.3 0.0 copy-start.2
  12.3 0.0 copy-done
  12.4 0.0 collective-permute-done
  12.4 0.0 collective-permute-done.1
  12.4 2.0 %collective-permute-start.2 = (bf16[256,512]{1,0:T(8,128)(2,1)S(1)}, bf16[256,512]{1,0:T(8,128)(2,1)S(1)}, u32[]{:S(2)}, u32[]{:S(2)}) collective-permute-start(bf16[256,512]{1,0:T(8,128)(2,1)S(1)} %pad_maximum_fusion.lower), channel_id=1, source_target_pairs={{0,32},{32,64},{64,96},{96,128},{128,160},{160,192},{192,224},{224... | collective-permute-start | bytes 786440 | tf_op jit(solution)/shard_map/ppermute | solution.py:303
  14.5 4.0 %collective-permute-start.3 = (bf16[256,512]{1,0:T(8,128)(2,1)S(1)}, bf16[256,512]{1,0:T(8,128)(2,1)S(1)}, u32[]{:S(2)}, u32[]{:S(2)}) collective-permute-start(bf16[256,512]{1,0:T(8,128)(2,1)S(1)} %pad_maximum_fusion.1.upper), channel_id=1, source_target_pairs={{0,224},{32,0},{64,32},{96,64},{128,96},{160,128},{192,160},{224,1... | collective-permute-start | bytes 786440 | tf_op jit(solution)/shard_map/ppermute | solution.py:303
  18.5 0.1 add_convert_fusion.edge
  18.6 0.0 copy-done.1
  18.6 0.0 copy-done.2
  18.6 3.6 %before_kernel.1 = (bf16[256,512]{1,0:T(8,128)(2,1)S(1)}, bf16[512,256]{1,0:T(8,128)(2,1)S(1)}, bf16[256,512]{1,0:T(8,128)(2,1)S(1)}, bf16[512,256]{1,0:T(8,128)(2,1)S(1)}, f32[4,768,256]{2,1,0:T(8,128)S(1)}) custom-call(s32[2]{0:T(128)S(1)} %add_convert_fusion.edge, bf16[256,512]{1,0:T(8,128)(2,1)S(1)} %bitcast.27, bf16[256,512]{1,0:T(8,128)(2,1)S(1)} %bitcast.30, ...), custom_call_target="tpu_custom_call" | custom-call | flops 600000000 | bytes 6825000 | tf_op jit(solution)/shard_map/before_kernel/pallas_call | solution.py:283
  22.1 0.8 middle_kernel.1
  23.0 1.2 %collective-permute-done.2.above = bf16[256,512]{1,0:T(8,128)(2,1)S(1)} collective-permute-done((bf16[256,512]{1,0:T(8,128)(2,1)S(1)}, bf16[256,512]{1,0:T(8,128)(2,1)S(1)}, u32[]{:S(2)}, u32[]{:S(2)}) %collective-permute-start.2) | collective-permute-done | bytes 262176 | tf_op jit(solution)/shard_map/ppermute | solution.py:303
  24.1 0.0 collective-permute-done.3.below
  24.1 13.8 %attention_kernel.1 = (bf16[1024,1024]{1,0:T(8,128)(2,1)S(1)}, bf16[512,256]{1,0:T(8,128)(2,1)S(1)}, bf16[512,1024]{1,0:T(8,128)(2,1)S(1)}, bf16[512,1024]{1,0:T(8,128)(2,1)S(1)}, f32[8,384]{1,0:T(8,128)S(1)}) custom-call(s32[1]{0:T(128)} %bitcast.core, bf16[256,512]{1,0:T(8,128)(2,1)S(1)} %collective-permute-done.2.above, ...), custom_call_target="tpu_custom_call" | custom-call | flops 10000000000 | bytes 13905924 | tf_op jit(solution)/shard_map/attention_kernel/pallas_call | solution.py:283
  38.0 0.1 collective-permute-start.8
  38.1 1.4 %tokens_kernel.1 = (bf16[256,512]{1,0:T(8,128)(2,1)S(1)}, f32[256,512]{1,0:T(8,128)S(1)}, f32[256,512]{1,0:T(8,128)S(1)}, bf16[256,512]{1,0:T(8,128)(2,1)S(1)}) custom-call(bf16[1024,1024]{1,0:T(8,128)(2,1)S(1)} %get-tuple-element.37.dkv, bf16[512,256]{1,0:T(8,128)(2,1)S(1)} %get-tuple-element.38.dq_t, bf16[1536,512]{1,0:T(8,128)(2,1)S(1)} %bitcast.25), custom_call_target="tpu_custom_call" | custom-call | flops 1200000000 | bytes 5505024 | tf_op jit(solution)/shard_map/tokens_kernel/pallas_call | solution.py:283
  39.5 1.2 %collective-permute-done.8.came = bf16[512,1024]{1,0:T(8,128)(2,1)S(1)} collective-permute-done((bf16[512,1024]{1,0:T(8,128)(2,1)S(1)}, bf16[512,1024]{1,0:T(8,128)(2,1)S(1)}, u32[]{:S(2)}, u32[]{:S(2)}) %collective-permute-start.8) | collective-permute-done | bytes 1048608 | tf_op jit(solution)/shard_map/ppermute | solution.py:310
  40.7 1.4 %pack_kernel.1 = bf16[64,8,1408]{2,1,0:T(8,128)(2,1)} custom-call(bf16[512,1024]{1,0:T(8,128)(2,1)S(1)} %get-tuple-element.46.keep, bf16[512,1024]{1,0:T(8,128)(2,1)S(1)} %collective-permute-done.8.came, f32[8,384]{1,0:T(8,128)S(1)} %get-tuple-element.48.bias, bf16[256,512]{1,0:T(8,128)(2,1)S(1)} %get-tuple-element.42._), custom_call_target="tpu_custom_call" | custom-call | flops 1000000 | bytes 3813376 | tf_op jit(solution)/shard_map/pack_kernel/pallas_call | solution.py:283
  42.1 10.1 %all-to-all-start = ((bf16[64,8,1408]{2,1,0:T(8,128)(2,1)}), bf16[64,8,1408]{2,1,0:T(8,128)(2,1)}, u32[]{:S(2)}, u32[]{:S(2)}) async-start(bf16[64,8,1408]{2,1,0:T(8,128)(2,1)} %pack_kernel.1), calls=%async_computation | async-start | bytes 2883584 | tf_op jit(solution)/shard_map/all_to_all | solution.py:387
  52.2 1.7 %collective-permute-start.4 = (bf16[256,512]{1,0:T(8,128)(2,1)S(1)}, bf16[256,512]{1,0:T(8,128)(2,1)S(1)}, u32[]{:S(2)}, u32[]{:S(2)}) collective-permute-start(bf16[256,512]{1,0:T(8,128)(2,1)S(1)} %get-tuple-element.41), channel_id=1, source_target_pairs={{0,32},{32,64},{64,96},{96,128},{128,160},{160,192},{192,224},{224... | collective-permute-start | bytes 786440 | tf_op jit(solution)/shard_map/ppermute | solution.py:303
  53.9 1.8 %collective-permute-start.5 = (bf16[256,512]{1,0:T(8,128)(2,1)S(1)}, bf16[256,512]{1,0:T(8,128)(2,1)S(1)}, u32[]{:S(2)}, u32[]{:S(2)}) collective-permute-start(bf16[256,512]{1,0:T(8,128)(2,1)S(1)} %get-tuple-element.42._), channel_id=1, source_target_pairs={{0,224},{32,0},{64,32},{96,64},{128,96},{160,128},{192,160},{224,1... | collective-permute-start | bytes 786440 | tf_op jit(solution)/shard_map/ppermute | solution.py:303
  55.7 36.1 %collective-permute-done.4.up = bf16[256,512]{1,0:T(8,128)(2,1)S(1)} collective-permute-done((bf16[256,512]{1,0:T(8,128)(2,1)S(1)}, bf16[256,512]{1,0:T(8,128)(2,1)S(1)}, u32[]{:S(2)}, u32[]{:S(2)}) %collective-permute-start.4) | collective-permute-done | bytes 262176 | tf_op jit(solution)/shard_map/ppermute | solution.py:303
  91.8 0.0 collective-permute-done.5.down
  91.8 0.1 fold_kernel.1
  91.8 3.4 %collective-permute-start.6 = (bf16[16,8,512]{2,1,0:T(8,128)(2,1)S(1)}, bf16[16,8,512]{2,1,0:T(8,128)(2,1)S(1)}, u32[]{:S(2)}, u32[]{:S(2)}) collective-permute-start(bf16[16,8,512]{2,1,0:T(8,128)(2,1)S(1)} %bitcast.33), channel_id=1, source_target_pairs={{0,4},{4,8},{8,12},{12,16},{16,20},{20,24},{24,28},{1,5},{5,9},{9,... | collective-permute-start | bytes 393224 | tf_op jit(solution)/shard_map/ppermute | solution.py:307
  95.2 4.6 %collective-permute-start.7 = (bf16[16,8,512]{2,1,0:T(8,128)(2,1)S(1)}, bf16[16,8,512]{2,1,0:T(8,128)(2,1)S(1)}, u32[]{:S(2)}, u32[]{:S(2)}) collective-permute-start(bf16[16,8,512]{2,1,0:T(8,128)(2,1)S(1)} %bitcast.32), channel_id=1, source_target_pairs={{4,0},{8,4},{12,8},{16,12},{20,16},{24,20},{28,24},{5,1},{9,5},{13... | collective-permute-start | bytes 393224 | tf_op jit(solution)/shard_map/ppermute | solution.py:307
  99.8 0.0 all-to-all-done
  99.8 1.6 %convert_reduce_fusion.mine = f32[8,1408]{1,0:T(8,128)S(1)} fusion(bf16[64,8,1408]{2,1,0:T(8,128)(2,1)} %all-to-all-done), kind=kLoop, calls=%fused_computation | loop fusion | flops 1430528 | bytes 1486848 | tf_op jit(solution)/shard_map/reduce_sum | solution.py:406
  101.4 0.4 collective-permute-start.11
  101.8 2.1 %collective-permute-start.10 = (f32[8,1408]{1,0:T(8,128)S(1)}, f32[8,1408]{1,0:T(8,128)S(1)}, u32[]{:S(2)}, u32[]{:S(2)}) collective-permute-start(f32[8,1408]{1,0:T(8,128)S(1)} %convert_reduce_fusion.mine), channel_id=1, source_target_pairs={{0,1},{1,0},{2,3},{3,2},{4,5},{5,4},{6,7},{7,6},{8,9},{9,8},{10,11... | collective-permute-start | bytes 135176 | tf_op jit(solution)/shard_map/ppermute | solution.py:310
  103.9 1.2 %collective-permute-start.9 = (f32[8,1408]{1,0:T(8,128)S(1)}, f32[8,1408]{1,0:T(8,128)S(1)}, u32[]{:S(2)}, u32[]{:S(2)}) collective-permute-start(f32[8,1408]{1,0:T(8,128)S(1)} %convert_reduce_fusion.mine), channel_id=1, source_target_pairs={{0,2},{1,3},{2,0},{3,1},{4,6},{5,7},{6,4},{7,5},{8,10},{9,11},{10,... | collective-permute-start | bytes 135176 | tf_op jit(solution)/shard_map/ppermute | solution.py:310
  105.1 0.0 collective-permute-done.6.west
  105.1 0.0 collective-permute-done.7.east
  105.2 0.7 after_kernel.1
  105.9 0.6 collective-permute-done.11.far
  106.5 0.0 collective-permute-done.10.other
  106.5 3.0 %collective-permute-done.9.near = f32[8,1408]{1,0:T(8,128)S(1)} collective-permute-done((f32[8,1408]{1,0:T(8,128)S(1)}, f32[8,1408]{1,0:T(8,128)S(1)}, u32[]{:S(2)}, u32[]{:S(2)}) %collective-permute-start.9) | collective-permute-done | bytes 45088 | tf_op jit(solution)/shard_map/ppermute | solution.py:310
  109.5 0.7 finish_kernel.1
  (5 shorter events, 0.1 us)
Async XLA Ops:
  1.6 10.7 %collective-permute-start = (bf16[16,8,512]{2,1,0:T(8,128)(2,1)S(1)}, bf16[16,8,512]{2,1,0:T(8,128)(2,1)S(1)}, u32[]{:S(2)}, u32[]{:S(2)}) collective-permute-start(bf16[16,8,512]{2,1,0:T(8,128)(2,1)S(1)} %get-tuple-element.54), channel_id=1, source_target_pairs={{0,4},{4,8},{8,12},{12,16},{16,20},{20,24},{24,28},{1,5},{5,9},{9,... | collective-permute-start | bytes 393224 | tf_op jit(solution)/shard_map/ppermute | solution.py:307
  5.0 7.4 %collective-permute-start.1 = (bf16[16,8,512]{2,1,0:T(8,128)(2,1)S(1)}, bf16[16,8,512]{2,1,0:T(8,128)(2,1)S(1)}, u32[]{:S(2)}, u32[]{:S(2)}) collective-permute-start(bf16[16,8,512]{2,1,0:T(8,128)(2,1)S(1)} %get-tuple-element.55), channel_id=1, source_target_pairs={{4,0},{8,4},{12,8},{16,12},{20,16},{24,20},{28,24},{5,1},{9,5},{13... | collective-permute-start | bytes 393224 | tf_op jit(solution)/shard_map/ppermute | solution.py:307
  10.5 1.8 %copy-start = (bf16[1,16,16,512]{3,2,1,0:T(8,128)(2,1)S(1)}, bf16[1,16,16,512]{3,2,1,0:T(8,128)(2,1)}, u32[]{:S(2)}) copy-start(bf16[1,16,16,512]{3,2,1,0:T(8,128)(2,1)} %param.5) | copy-start | bytes 786436
  12.3 6.3 %copy-start.1 = (bf16[512,512]{1,0:T(8,128)(2,1)S(1)}, bf16[512,512]{1,0:T(8,128)(2,1)}, u32[]{:S(2)}) copy-start(bf16[512,512]{1,0:T(8,128)(2,1)} %wo.1) | copy-start | bytes 1572868
  12.3 6.3 %copy-start.2 = (bf16[1,16,16,512]{3,2,1,0:T(8,128)(2,1)S(1)}, bf16[1,16,16,512]{3,2,1,0:T(8,128)(2,1)}, u32[]{:S(2)}) copy-start(bf16[1,16,16,512]{3,2,1,0:T(8,128)(2,1)} %param.9) | copy-start | bytes 786436
  12.4 11.7 %collective-permute-start.2 = (bf16[256,512]{1,0:T(8,128)(2,1)S(1)}, bf16[256,512]{1,0:T(8,128)(2,1)S(1)}, u32[]{:S(2)}, u32[]{:S(2)}) collective-permute-start(bf16[256,512]{1,0:T(8,128)(2,1)S(1)} %pad_maximum_fusion.lower), channel_id=1, source_target_pairs={{0,32},{32,64},{64,96},{96,128},{128,160},{160,192},{192,224},{224... | collective-permute-start | bytes 786440 | tf_op jit(solution)/shard_map/ppermute | solution.py:303
  14.5 9.7 %collective-permute-start.3 = (bf16[256,512]{1,0:T(8,128)(2,1)S(1)}, bf16[256,512]{1,0:T(8,128)(2,1)S(1)}, u32[]{:S(2)}, u32[]{:S(2)}) collective-permute-start(bf16[256,512]{1,0:T(8,128)(2,1)S(1)} %pad_maximum_fusion.1.upper), channel_id=1, source_target_pairs={{0,224},{32,0},{64,32},{96,64},{128,96},{160,128},{192,160},{224,1... | collective-permute-start | bytes 786440 | tf_op jit(solution)/shard_map/ppermute | solution.py:303
  38.0 2.7 %collective-permute-start.8 = (bf16[512,1024]{1,0:T(8,128)(2,1)S(1)}, bf16[512,1024]{1,0:T(8,128)(2,1)S(1)}, u32[]{:S(2)}, u32[]{:S(2)}) collective-permute-start(bf16[512,1024]{1,0:T(8,128)(2,1)S(1)} %get-tuple-element.47), channel_id=1, source_target_pairs={{0,1},{1,0},{2,3},{3,2},{4,5},{5,4},{6,7},{7,6},{8,9},{9,8},{10,11... | collective-permute-start | bytes 3145736 | tf_op jit(solution)/shard_map/ppermute | solution.py:310
  42.1 57.7 %all-to-all-start = ((bf16[64,8,1408]{2,1,0:T(8,128)(2,1)}), bf16[64,8,1408]{2,1,0:T(8,128)(2,1)}, u32[]{:S(2)}, u32[]{:S(2)}) async-start(bf16[64,8,1408]{2,1,0:T(8,128)(2,1)} %pack_kernel.1), calls=%async_computation | async-start | bytes 2883584 | tf_op jit(solution)/shard_map/all_to_all | solution.py:387
  52.2 39.6 %collective-permute-start.4 = (bf16[256,512]{1,0:T(8,128)(2,1)S(1)}, bf16[256,512]{1,0:T(8,128)(2,1)S(1)}, u32[]{:S(2)}, u32[]{:S(2)}) collective-permute-start(bf16[256,512]{1,0:T(8,128)(2,1)S(1)} %get-tuple-element.41), channel_id=1, source_target_pairs={{0,32},{32,64},{64,96},{96,128},{128,160},{160,192},{192,224},{224... | collective-permute-start | bytes 786440 | tf_op jit(solution)/shard_map/ppermute | solution.py:303
  53.9 37.9 %collective-permute-start.5 = (bf16[256,512]{1,0:T(8,128)(2,1)S(1)}, bf16[256,512]{1,0:T(8,128)(2,1)S(1)}, u32[]{:S(2)}, u32[]{:S(2)}) collective-permute-start(bf16[256,512]{1,0:T(8,128)(2,1)S(1)} %get-tuple-element.42._), channel_id=1, source_target_pairs={{0,224},{32,0},{64,32},{96,64},{128,96},{160,128},{192,160},{224,1... | collective-permute-start | bytes 786440 | tf_op jit(solution)/shard_map/ppermute | solution.py:303
  91.8 13.3 %collective-permute-start.6 = (bf16[16,8,512]{2,1,0:T(8,128)(2,1)S(1)}, bf16[16,8,512]{2,1,0:T(8,128)(2,1)S(1)}, u32[]{:S(2)}, u32[]{:S(2)}) collective-permute-start(bf16[16,8,512]{2,1,0:T(8,128)(2,1)S(1)} %bitcast.33), channel_id=1, source_target_pairs={{0,4},{4,8},{8,12},{12,16},{16,20},{20,24},{24,28},{1,5},{5,9},{9,... | collective-permute-start | bytes 393224 | tf_op jit(solution)/shard_map/ppermute | solution.py:307
  95.2 9.9 %collective-permute-start.7 = (bf16[16,8,512]{2,1,0:T(8,128)(2,1)S(1)}, bf16[16,8,512]{2,1,0:T(8,128)(2,1)S(1)}, u32[]{:S(2)}, u32[]{:S(2)}) collective-permute-start(bf16[16,8,512]{2,1,0:T(8,128)(2,1)S(1)} %bitcast.32), channel_id=1, source_target_pairs={{4,0},{8,4},{12,8},{16,12},{20,16},{24,20},{28,24},{5,1},{9,5},{13... | collective-permute-start | bytes 393224 | tf_op jit(solution)/shard_map/ppermute | solution.py:307
  101.4 5.1 %collective-permute-start.11 = (f32[8,1408]{1,0:T(8,128)S(1)}, f32[8,1408]{1,0:T(8,128)S(1)}, u32[]{:S(2)}, u32[]{:S(2)}) collective-permute-start(f32[8,1408]{1,0:T(8,128)S(1)} %convert_reduce_fusion.mine), channel_id=1, source_target_pairs={{0,3},{1,2},{2,1},{3,0},{4,7},{5,6},{6,5},{7,4},{8,11},{9,10},{10,... | collective-permute-start | bytes 135176 | tf_op jit(solution)/shard_map/ppermute | solution.py:310
  101.8 4.6 %collective-permute-start.10 = (f32[8,1408]{1,0:T(8,128)S(1)}, f32[8,1408]{1,0:T(8,128)S(1)}, u32[]{:S(2)}, u32[]{:S(2)}) collective-permute-start(f32[8,1408]{1,0:T(8,128)S(1)} %convert_reduce_fusion.mine), channel_id=1, source_target_pairs={{0,1},{1,0},{2,3},{3,2},{4,5},{5,4},{6,7},{7,6},{8,9},{9,8},{10,11... | collective-permute-start | bytes 135176 | tf_op jit(solution)/shard_map/ppermute | solution.py:310
  103.9 5.6 %collective-permute-start.9 = (f32[8,1408]{1,0:T(8,128)S(1)}, f32[8,1408]{1,0:T(8,128)S(1)}, u32[]{:S(2)}, u32[]{:S(2)}) collective-permute-start(f32[8,1408]{1,0:T(8,128)S(1)} %convert_reduce_fusion.mine), channel_id=1, source_target_pairs={{0,2},{1,3},{2,0},{3,1},{4,6},{5,7},{6,4},{7,5},{8,10},{9,11},{10,... | collective-permute-start | bytes 135176 | tf_op jit(solution)/shard_map/ppermute | solution.py:310

commit v3 on v2

--- a/solution.py
+++ b/solution.py
@@ -250,12 +250,41 @@
 
 def pack_kernel(keep, came, bias, _, parcel):
     count, rows, _ = parcel.shape
-    cols = bias.shape[1]
-    both = keep[...].astype(F32) + came[...].astype(F32)
-    parcel[:, :, 0:1024] = both.astype(BF16).reshape(count, rows, 1024)
-    parcel[:, :, 1024 : 1024 + cols] = jnp.broadcast_to(
-        bias[...].astype(BF16)[None], (count, rows, cols)
-    )
+    for a in range(rows // 8):
+        for r in range(count):
+            at = (a * count + r) * 8
+            both = keep[at : at + 8].astype(F32) + came[at : at + 8].astype(F32)
+            parcel[r, a * 8 : a * 8 + 8, 0:1024] = both.astype(BF16)
+    parcel[:, :, 1024:1152] = jnp.zeros((count, rows, 128), BF16)
+    for n in range(3):
+        part = bias[:, n * 128 : n * 128 + 128].astype(BF16)
+        for r in range(count):
+            parcel[r, n * 8 : n * 8 + 8, 1024:1152] = part
+
+
+def regroup_kernel(came, parcel):
+    count = parcel.shape[0]
+    for a in range(count):
+        rows = slice(a * 8, a * 8 + 8)
+        total = came[0, rows, 0:1024].astype(F32)
+        for r in range(1, came.shape[0]):
+            total += came[r, rows, 0:1024].astype(F32)
+        parcel[a, :, 0:1024] = total.astype(BF16)
+    for n in range(3):
+        rows = slice(n * 8, n * 8 + 8)
+        total = came[0, rows, 1024:1152].astype(F32)
+        for r in range(1, came.shape[0]):
+            total += came[r, rows, 1024:1152].astype(F32)
+        part = total.astype(BF16)
+        for a in range(count):
+            parcel[a, :, 1024 + n * 128 : 1152 + n * 128] = part
+
+
+def total_kernel(came, mine):
+    total = came[0].astype(F32)
+    for a in range(1, came.shape[0]):
+        total += came[a].astype(F32)
+    mine[...] = total
 
 
 def finish_kernel(core, mine, near, other, far, qkv, out, bias):
@@ -374,17 +403,18 @@
     )
 
     came = among(g_send, 1)
-    rows = 512 // (az * rng)
-    cols = 384
-    if rows != 8:
-        g_bias = jnp.pad(g_bias, ((0, rows - 8), (0, 0)))
     (parcel,) = call(
         pack_kernel,
         (g_keep, came, g_bias, g_above),
-        (whole((az * rng, rows, 1024 + cols), BF16),),
+        (whole((rng, 8 * az, 1152), BF16),),
         flops=1_000_000,
     )
-    parcel = lax.all_to_all(parcel, ("az", "rng"), 0, 0, tiled=True)
+    parcel = lax.all_to_all(parcel, "rng", 0, 0, tiled=True)
+    (parcel,) = call(
+        regroup_kernel, (parcel,), (whole((az, 8, 1408), BF16),), flops=1_000_000
+    )
+    parcel = lax.all_to_all(parcel, "az", 0, 0, tiled=True)
+    (mine,) = call(total_kernel, (parcel,), (whole((8, 1408), F32),), flops=1_000_000)
 
     up = turn(g_below, 1)
     down = turn(g_above, -1)
@@ -403,16 +433,15 @@
         flops=1_000_000,
     )
 
-    mine = jnp.sum(parcel.astype(F32), axis=0)
     near, other, far = among(mine, 2), among(mine, 1), among(mine, 3)
     rows_qkv, rows_out, total_bias = call(
         finish_kernel,
         (core, mine, near, other, far),
-        (whole((rows, 1536), F32), whole((rows, 512), F32), whole((17, rows, 17), F32)),
+        (whole((8, 1536), F32), whole((8, 512), F32), whole((17, 8, 17), F32)),
         prefetch=1,
         flops=1_000_000,
     )
-    total_bias = jnp.transpose(total_bias[:, :8], (1, 0, 2))
+    total_bias = jnp.transpose(total_bias, (1, 0, 2))
     return (grad_tokens[None], rows_qkv, rows_out, total_bias)
 
 

time: 111 us -> 90.7 us (0.82)
  the two profiles are of different devices: /device:TPU:8 before, /device:TPU:1 now
where the time goes in v3:
time: 90.7 us; the launch traced here: 90.3 us
  starting transfers between devices  37 us (41%)
  waiting for transfers between devices  25.3 us (28%)
  Pallas kernels  23.3 us (26%)
  local copies, waits for them, and re-layouts  3.71 us (4%)
    pallas_call x10, Pallas kernels, call(): pl.pallas_call(kernel, out_shape=tuple(outs), in_specs=[scalar] * prefetc...  23.3 us
    all_to_all x1, waiting for transfers between devices, shards(): parcel = lax.all_to_all(parcel, 'rng', 0, 0, tiled=True)  14.2 us
    ppermute x4, starting transfers between devices, turn(): return lax.ppermute(leaf, 'az', [(i, (i + step) % az) for i in range(az)])  8.79 us
    ppermute x4, starting transfers between devices, among(): return lax.ppermute(leaf, 'dp', [(i, i ^ flip) for i in range(4)])  8.32 us
    ppermute x4, starting transfers between devices, shift(): return lax.ppermute(leaf, 'rng', pairs)  8.29 us
    all_to_all x1, starting transfers between devices, shards(): parcel = lax.all_to_all(parcel, 'rng', 0, 0, tiled=True)  5.86 us
    all_to_all x1, starting transfers between devices, shards(): parcel = lax.all_to_all(parcel, 'az', 0, 0, tiled=True)  5.7 us
    all_to_all x1, waiting for transfers between devices, shards(): parcel = lax.all_to_all(parcel, 'az', 0, 0, tiled=True)  5.26 us
  transfers between devices with their start and end apart: 14, of which 6 were waited for; matrix products, arithmetic and copies ran while one was open for 3% of the time, Pallas kernels for 8%

profile of v3, /device:TPU:1, one launch (start us, length us, event | category | flops | bytes accessed | tf_op | source)
XLA Modules:
  0.0 90.3 jit_solution(12946845754130659240)
XLA Ops:
  0.6 1.0 %fusion.1 = (bf16[16,8,512]{2,1,0:T(8,128)(2,1)S(1)}, bf16[16,8,512]{2,1,0:T(8,128)(2,1)S(1)}) fusion(bf16[16,16,512]{2,1,0:T(8,128)(2,1)} %bitcast.26), kind=kLoop, calls=%fused_computation.8 | loop fusion | bytes 524288 | tf_op jit(solution)/shard_map/slice | solution.py:341
  1.6 3.9 %collective-permute-start = (bf16[16,8,512]{2,1,0:T(8,128)(2,1)S(1)}, bf16[16,8,512]{2,1,0:T(8,128)(2,1)S(1)}, u32[]{:S(2)}, u32[]{:S(2)}) collective-permute-start(bf16[16,8,512]{2,1,0:T(8,128)(2,1)S(1)} %get-tuple-element.54), channel_id=1, source_target_pairs={{0,4},{4,8},{8,12},{12,16},{16,20},{20,24},{24,28},{1,5},{5,9},{9,... | collective-permute-start | bytes 393224 | tf_op jit(solution)/shard_map/ppermute | solution.py:336
  5.6 1.3 %collective-permute-start.1 = (bf16[16,8,512]{2,1,0:T(8,128)(2,1)S(1)}, bf16[16,8,512]{2,1,0:T(8,128)(2,1)S(1)}, u32[]{:S(2)}, u32[]{:S(2)}) collective-permute-start(bf16[16,8,512]{2,1,0:T(8,128)(2,1)S(1)} %get-tuple-element.55), channel_id=1, source_target_pairs={{4,0},{8,4},{12,8},{16,12},{20,16},{24,20},{28,24},{5,1},{9,5},{13... | collective-permute-start | bytes 393224 | tf_op jit(solution)/shard_map/ppermute | solution.py:336
  6.9 0.9 copy.10.bias
  7.8 0.0 copy-start
  7.8 1.8 %copy.9 = bf16[512,1536]{0,1:T(8,128)(2,1)S(1)} copy(bf16[512,1536]{1,0:T(8,128)(2,1)} %param.6) | data formatting | bytes 3145728 | tf_op args[1]
  9.6 0.0 copy-start.1
  9.6 0.0 copy-start.2
  9.6 0.0 copy-done
  9.6 0.0 collective-permute-done
  9.7 1.6 %collective-permute-done.1 = bf16[16,8,512]{2,1,0:T(8,128)(2,1)S(1)} collective-permute-done((bf16[16,8,512]{2,1,0:T(8,128)(2,1)S(1)}, bf16[16,8,512]{2,1,0:T(8,128)(2,1)S(1)}, u32[]{:S(2)}, u32[]{:S(2)}) %collective-permute-start.1) | collective-permute-done | bytes 131104 | tf_op jit(solution)/shard_map/ppermute | solution.py:336
  11.3 1.7 %collective-permute-start.2 = (bf16[256,512]{1,0:T(8,128)(2,1)S(1)}, bf16[256,512]{1,0:T(8,128)(2,1)S(1)}, u32[]{:S(2)}, u32[]{:S(2)}) collective-permute-start(bf16[256,512]{1,0:T(8,128)(2,1)S(1)} %pad_maximum_fusion.lower), channel_id=1, source_target_pairs={{0,32},{32,64},{64,96},{96,128},{128,160},{160,192},{192,224},{224... | collective-permute-start | bytes 786440 | tf_op jit(solution)/shard_map/ppermute | solution.py:332
  13.1 4.0 %collective-permute-start.3 = (bf16[256,512]{1,0:T(8,128)(2,1)S(1)}, bf16[256,512]{1,0:T(8,128)(2,1)S(1)}, u32[]{:S(2)}, u32[]{:S(2)}) collective-permute-start(bf16[256,512]{1,0:T(8,128)(2,1)S(1)} %pad_maximum_fusion.1.upper), channel_id=1, source_target_pairs={{0,224},{32,0},{64,32},{96,64},{128,96},{160,128},{192,160},{224,1... | collective-permute-start | bytes 786440 | tf_op jit(solution)/shard_map/ppermute | solution.py:332
  17.1 0.1 add_convert_fusion.edge
  17.2 0.0 copy-done.1
  17.2 0.0 copy-done.2
  17.2 3.6 %before_kernel.1 = (bf16[256,512]{1,0:T(8,128)(2,1)S(1)}, bf16[512,256]{1,0:T(8,128)(2,1)S(1)}, bf16[256,512]{1,0:T(8,128)(2,1)S(1)}, bf16[512,256]{1,0:T(8,128)(2,1)S(1)}, f32[4,768,256]{2,1,0:T(8,128)S(1)}) custom-call(s32[2]{0:T(128)S(1)} %add_convert_fusion.edge, bf16[256,512]{1,0:T(8,128)(2,1)S(1)} %bitcast.27, bf16[256,512]{1,0:T(8,128)(2,1)S(1)} %bitcast.30, ...), custom_call_target="tpu_custom_call" | custom-call | flops 600000000 | bytes 6825000 | tf_op jit(solution)/shard_map/before_kernel/pallas_call | solution.py:312
  20.7 0.8 middle_kernel.1
  21.6 0.0 collective-permute-done.2.above
  21.6 0.0 collective-permute-done.3.below
  21.6 13.9 %attention_kernel.1 = (bf16[1024,1024]{1,0:T(8,128)(2,1)S(1)}, bf16[512,256]{1,0:T(8,128)(2,1)S(1)}, bf16[512,1024]{1,0:T(8,128)(2,1)S(1)}, bf16[512,1024]{1,0:T(8,128)(2,1)S(1)}, f32[8,384]{1,0:T(8,128)S(1)}) custom-call(s32[1]{0:T(128)} %bitcast.core, bf16[256,512]{1,0:T(8,128)(2,1)S(1)} %collective-permute-done.2.above, ...), custom_call_target="tpu_custom_call" | custom-call | flops 10000000000 | bytes 13905924 | tf_op jit(solution)/shard_map/attention_kernel/pallas_call | solution.py:312
  35.5 2.7 %collective-permute-start.8 = (bf16[512,1024]{1,0:T(8,128)(2,1)S(1)}, bf16[512,1024]{1,0:T(8,128)(2,1)S(1)}, u32[]{:S(2)}, u32[]{:S(2)}) collective-permute-start(bf16[512,1024]{1,0:T(8,128)(2,1)S(1)} %get-tuple-element.47), channel_id=1, source_target_pairs={{0,1},{1,0},{2,3},{3,2},{4,5},{5,4},{6,7},{7,6},{8,9},{9,8},{10,11... | collective-permute-start | bytes 3145736 | tf_op jit(solution)/shard_map/ppermute | solution.py:339
  38.2 1.4 %tokens_kernel.1 = (bf16[256,512]{1,0:T(8,128)(2,1)S(1)}, f32[256,512]{1,0:T(8,128)S(1)}, f32[256,512]{1,0:T(8,128)S(1)}, bf16[256,512]{1,0:T(8,128)(2,1)S(1)}) custom-call(bf16[1024,1024]{1,0:T(8,128)(2,1)S(1)} %get-tuple-element.37.dkv, bf16[512,256]{1,0:T(8,128)(2,1)S(1)} %get-tuple-element.38.dq_t, bf16[1536,512]{1,0:T(8,128)(2,1)S(1)} %bitcast.25), custom_call_target="tpu_custom_call" | custom-call | flops 1200000000 | bytes 5505024 | tf_op jit(solution)/shard_map/tokens_kernel/pallas_call | solution.py:312
  39.6 0.9 collective-permute-done.8.came
  40.5 1.3 %pack_kernel.1 = bf16[8,64,1152]{2,1,0:T(8,128)(2,1)} custom-call(bf16[512,1024]{1,0:T(8,128)(2,1)S(1)} %get-tuple-element.46.keep, bf16[512,1024]{1,0:T(8,128)(2,1)S(1)} %collective-permute-done.8.came, f32[8,384]{1,0:T(8,128)S(1)} %get-tuple-element.48.bias, bf16[256,512]{1,0:T(8,128)(2,1)S(1)} %get-tuple-element.42._), custom_call_target="tpu_custom_call" | custom-call | flops 1000000 | bytes 3551232 | tf_op jit(solution)/shard_map/pack_kernel/pallas_call | solution.py:312
  41.8 5.9 %all-to-all-start = ((bf16[8,64,1152]{2,1,0:T(8,128)(2,1)}), bf16[8,64,1152]{2,1,0:T(8,128)(2,1)S(1)}, u32[]{:S(2)}, u32[]{:S(2)}) async-start(bf16[8,64,1152]{2,1,0:T(8,128)(2,1)} %pack_kernel.1), calls=%async_computation | async-start | bytes 2359296 | tf_op jit(solution)/shard_map/all_to_all | solution.py:412
  47.7 0.0 collective-permute-start.4
  47.7 3.0 %collective-permute-start.5 = (bf16[256,512]{1,0:T(8,128)(2,1)S(1)}, bf16[256,512]{1,0:T(8,128)(2,1)S(1)}, u32[]{:S(2)}, u32[]{:S(2)}) collective-permute-start(bf16[256,512]{1,0:T(8,128)(2,1)S(1)} %get-tuple-element.42._), channel_id=1, source_target_pairs={{0,224},{32,0},{64,32},{96,64},{128,96},{160,128},{192,160},{224,1... | collective-permute-start | bytes 786440 | tf_op jit(solution)/shard_map/ppermute | solution.py:332
  50.7 14.2 %all-to-all-done.came = bf16[8,64,1152]{2,1,0:T(8,128)(2,1)S(1)} async-done(((bf16[8,64,1152]{2,1,0:T(8,128)(2,1)}), bf16[8,64,1152]{2,1,0:T(8,128)(2,1)S(1)}, u32[]{:S(2)}, u32[]{:S(2)}) %all-to-all-start) | async-done | bytes 1179680 | tf_op jit(solution)/shard_map/all_to_all | solution.py:412
  64.9 0.8 regroup_kernel.1
  65.8 5.7 %all-to-all-start.1 = ((bf16[8,8,1408]{2,1,0:T(8,128)(2,1)}), bf16[8,8,1408]{2,1,0:T(8,128)(2,1)S(1)}, u32[]{:S(2)}, u32[]{:S(2)}) async-start(bf16[8,8,1408]{2,1,0:T(8,128)(2,1)} %regroup_kernel.1), calls=%async_computation.1 | async-start | bytes 360448 | tf_op jit(solution)/shard_map/all_to_all | solution.py:416
  71.4 0.0 collective-permute-done.4.up
  71.5 0.0 collective-permute-done.5.down
  71.5 0.1 fold_kernel.1
  71.6 1.8 %collective-permute-start.6 = (bf16[16,8,512]{2,1,0:T(8,128)(2,1)S(1)}, bf16[16,8,512]{2,1,0:T(8,128)(2,1)S(1)}, u32[]{:S(2)}, u32[]{:S(2)}) collective-permute-start(bf16[16,8,512]{2,1,0:T(8,128)(2,1)S(1)} %bitcast.33), channel_id=1, source_target_pairs={{0,4},{4,8},{8,12},{12,16},{16,20},{20,24},{24,28},{1,5},{5,9},{9,... | collective-permute-start | bytes 393224 | tf_op jit(solution)/shard_map/ppermute | solution.py:336
  73.3 1.3 %collective-permute-start.7 = (bf16[16,8,512]{2,1,0:T(8,128)(2,1)S(1)}, bf16[16,8,512]{2,1,0:T(8,128)(2,1)S(1)}, u32[]{:S(2)}, u32[]{:S(2)}) collective-permute-start(bf16[16,8,512]{2,1,0:T(8,128)(2,1)S(1)} %bitcast.32), channel_id=1, source_target_pairs={{4,0},{8,4},{12,8},{16,12},{20,16},{24,20},{28,24},{5,1},{9,5},{13... | collective-permute-start | bytes 393224 | tf_op jit(solution)/shard_map/ppermute | solution.py:336
  74.6 5.3 %all-to-all-done.1.came = bf16[8,8,1408]{2,1,0:T(8,128)(2,1)S(1)} async-done(((bf16[8,8,1408]{2,1,0:T(8,128)(2,1)}), bf16[8,8,1408]{2,1,0:T(8,128)(2,1)S(1)}, u32[]{:S(2)}, u32[]{:S(2)}) %all-to-all-start.1) | async-done | bytes 180256 | tf_op jit(solution)/shard_map/all_to_all | solution.py:416
  79.9 5.2 %collective-permute-start.11 = (f32[8,1408]{1,0:T(8,128)S(1)}, f32[8,1408]{1,0:T(8,128)S(1)}, u32[]{:S(2)}, u32[]{:S(2)}) collective-permute-start(f32[8,1408]{1,0:T(8,128)S(1)} %total_kernel.1.mine), channel_id=1, source_target_pairs={{0,3},{1,2},{2,1},{3,0},{4,7},{5,6},{6,5},{7,4},{8,11},{9,10},{10,... | collective-permute-start | bytes 135176 | tf_op jit(solution)/shard_map/ppermute | solution.py:339
  85.1 0.0 collective-permute-start.10
  85.1 0.4 collective-permute-start.9
  85.5 0.0 collective-permute-done.6.west
  85.5 0.0 collective-permute-done.7.east
  85.5 0.7 after_kernel.1
  86.3 1.3 %collective-permute-done.11.far = f32[8,1408]{1,0:T(8,128)S(1)} collective-permute-done((f32[8,1408]{1,0:T(8,128)S(1)}, f32[8,1408]{1,0:T(8,128)S(1)}, u32[]{:S(2)}, u32[]{:S(2)}) %collective-permute-start.11) | collective-permute-done | bytes 45088 | tf_op jit(solution)/shard_map/ppermute | solution.py:339
  87.6 0.0 collective-permute-done.10.other
  87.6 1.9 %collective-permute-done.9.near = f32[8,1408]{1,0:T(8,128)S(1)} collective-permute-done((f32[8,1408]{1,0:T(8,128)S(1)}, f32[8,1408]{1,0:T(8,128)S(1)}, u32[]{:S(2)}, u32[]{:S(2)}) %collective-permute-start.9) | collective-permute-done | bytes 45088 | tf_op jit(solution)/shard_map/ppermute | solution.py:339
  89.5 0.7 finish_kernel.1
  (6 shorter events, 0.1 us)
Async XLA Ops:
  1.6 8.0 %collective-permute-start = (bf16[16,8,512]{2,1,0:T(8,128)(2,1)S(1)}, bf16[16,8,512]{2,1,0:T(8,128)(2,1)S(1)}, u32[]{:S(2)}, u32[]{:S(2)}) collective-permute-start(bf16[16,8,512]{2,1,0:T(8,128)(2,1)S(1)} %get-tuple-element.54), channel_id=1, source_target_pairs={{0,4},{4,8},{8,12},{12,16},{16,20},{20,24},{24,28},{1,5},{5,9},{9,... | collective-permute-start | bytes 393224 | tf_op jit(solution)/shard_map/ppermute | solution.py:336
  5.6 5.7 %collective-permute-start.1 = (bf16[16,8,512]{2,1,0:T(8,128)(2,1)S(1)}, bf16[16,8,512]{2,1,0:T(8,128)(2,1)S(1)}, u32[]{:S(2)}, u32[]{:S(2)}) collective-permute-start(bf16[16,8,512]{2,1,0:T(8,128)(2,1)S(1)} %get-tuple-element.55), channel_id=1, source_target_pairs={{4,0},{8,4},{12,8},{16,12},{20,16},{24,20},{28,24},{5,1},{9,5},{13... | collective-permute-start | bytes 393224 | tf_op jit(solution)/shard_map/ppermute | solution.py:336
  7.8 1.8 %copy-start = (bf16[1,16,16,512]{3,2,1,0:T(8,128)(2,1)S(1)}, bf16[1,16,16,512]{3,2,1,0:T(8,128)(2,1)}, u32[]{:S(2)}) copy-start(bf16[1,16,16,512]{3,2,1,0:T(8,128)(2,1)} %param.5) | copy-start | bytes 786436
  9.6 7.6 %copy-start.1 = (bf16[512,512]{1,0:T(8,128)(2,1)S(1)}, bf16[512,512]{1,0:T(8,128)(2,1)}, u32[]{:S(2)}) copy-start(bf16[512,512]{1,0:T(8,128)(2,1)} %wo.1) | copy-start | bytes 1572868
  9.6 7.6 %copy-start.2 = (bf16[1,16,16,512]{3,2,1,0:T(8,128)(2,1)S(1)}, bf16[1,16,16,512]{3,2,1,0:T(8,128)(2,1)}, u32[]{:S(2)}) copy-start(bf16[1,16,16,512]{3,2,1,0:T(8,128)(2,1)} %param.9) | copy-start | bytes 786436
  11.3 10.2 %collective-permute-start.2 = (bf16[256,512]{1,0:T(8,128)(2,1)S(1)}, bf16[256,512]{1,0:T(8,128)(2,1)S(1)}, u32[]{:S(2)}, u32[]{:S(2)}) collective-permute-start(bf16[256,512]{1,0:T(8,128)(2,1)S(1)} %pad_maximum_fusion.lower), channel_id=1, source_target_pairs={{0,32},{32,64},{64,96},{96,128},{128,160},{160,192},{192,224},{224... | collective-permute-start | bytes 786440 | tf_op jit(solution)/shard_map/ppermute | solution.py:332
  13.1 8.5 %collective-permute-start.3 = (bf16[256,512]{1,0:T(8,128)(2,1)S(1)}, bf16[256,512]{1,0:T(8,128)(2,1)S(1)}, u32[]{:S(2)}, u32[]{:S(2)}) collective-permute-start(bf16[256,512]{1,0:T(8,128)(2,1)S(1)} %pad_maximum_fusion.1.upper), channel_id=1, source_target_pairs={{0,224},{32,0},{64,32},{96,64},{128,96},{160,128},{192,160},{224,1... | collective-permute-start | bytes 786440 | tf_op jit(solution)/shard_map/ppermute | solution.py:332
  35.5 5.0 %collective-permute-start.8 = (bf16[512,1024]{1,0:T(8,128)(2,1)S(1)}, bf16[512,1024]{1,0:T(8,128)(2,1)S(1)}, u32[]{:S(2)}, u32[]{:S(2)}) collective-permute-start(bf16[512,1024]{1,0:T(8,128)(2,1)S(1)} %get-tuple-element.47), channel_id=1, source_target_pairs={{0,1},{1,0},{2,3},{3,2},{4,5},{5,4},{6,7},{7,6},{8,9},{9,8},{10,11... | collective-permute-start | bytes 3145736 | tf_op jit(solution)/shard_map/ppermute | solution.py:339
  41.8 23.1 %all-to-all-start = ((bf16[8,64,1152]{2,1,0:T(8,128)(2,1)}), bf16[8,64,1152]{2,1,0:T(8,128)(2,1)S(1)}, u32[]{:S(2)}, u32[]{:S(2)}) async-start(bf16[8,64,1152]{2,1,0:T(8,128)(2,1)} %pack_kernel.1), calls=%async_computation | async-start | bytes 2359296 | tf_op jit(solution)/shard_map/all_to_all | solution.py:412
  47.7 23.8 %collective-permute-start.4 = (bf16[256,512]{1,0:T(8,128)(2,1)S(1)}, bf16[256,512]{1,0:T(8,128)(2,1)S(1)}, u32[]{:S(2)}, u32[]{:S(2)}) collective-permute-start(bf16[256,512]{1,0:T(8,128)(2,1)S(1)} %get-tuple-element.41), channel_id=1, source_target_pairs={{0,32},{32,64},{64,96},{96,128},{128,160},{160,192},{192,224},{224... | collective-permute-start | bytes 786440 | tf_op jit(solution)/shard_map/ppermute | solution.py:332
  47.7 23.8 %collective-permute-start.5 = (bf16[256,512]{1,0:T(8,128)(2,1)S(1)}, bf16[256,512]{1,0:T(8,128)(2,1)S(1)}, u32[]{:S(2)}, u32[]{:S(2)}) collective-permute-start(bf16[256,512]{1,0:T(8,128)(2,1)S(1)} %get-tuple-element.42._), channel_id=1, source_target_pairs={{0,224},{32,0},{64,32},{96,64},{128,96},{160,128},{192,160},{224,1... | collective-permute-start | bytes 786440 | tf_op jit(solution)/shard_map/ppermute | solution.py:332
  65.8 14.1 %all-to-all-start.1 = ((bf16[8,8,1408]{2,1,0:T(8,128)(2,1)}), bf16[8,8,1408]{2,1,0:T(8,128)(2,1)S(1)}, u32[]{:S(2)}, u32[]{:S(2)}) async-start(bf16[8,8,1408]{2,1,0:T(8,128)(2,1)} %regroup_kernel.1), calls=%async_computation.1 | async-start | bytes 360448 | tf_op jit(solution)/shard_map/all_to_all | solution.py:416
  71.6 13.9 %collective-permute-start.6 = (bf16[16,8,512]{2,1,0:T(8,128)(2,1)S(1)}, bf16[16,8,512]{2,1,0:T(8,128)(2,1)S(1)}, u32[]{:S(2)}, u32[]{:S(2)}) collective-permute-start(bf16[16,8,512]{2,1,0:T(8,128)(2,1)S(1)} %bitcast.33), channel_id=1, source_target_pairs={{0,4},{4,8},{8,12},{12,16},{16,20},{20,24},{24,28},{1,5},{5,9},{9,... | collective-permute-start | bytes 393224 | tf_op jit(solution)/shard_map/ppermute | solution.py:336
  73.3 12.2 %collective-permute-start.7 = (bf16[16,8,512]{2,1,0:T(8,128)(2,1)S(1)}, bf16[16,8,512]{2,1,0:T(8,128)(2,1)S(1)}, u32[]{:S(2)}, u32[]{:S(2)}) collective-permute-start(bf16[16,8,512]{2,1,0:T(8,128)(2,1)S(1)} %bitcast.32), channel_id=1, source_target_pairs={{4,0},{8,4},{12,8},{16,12},{20,16},{24,20},{28,24},{5,1},{9,5},{13... | collective-permute-start | bytes 393224 | tf_op jit(solution)/shard_map/ppermute | solution.py:336
  79.9 7.7 %collective-permute-start.11 = (f32[8,1408]{1,0:T(8,128)S(1)}, f32[8,1408]{1,0:T(8,128)S(1)}, u32[]{:S(2)}, u32[]{:S(2)}) collective-permute-start(f32[8,1408]{1,0:T(8,128)S(1)} %total_kernel.1.mine), channel_id=1, source_target_pairs={{0,3},{1,2},{2,1},{3,0},{4,7},{5,6},{6,5},{7,4},{8,11},{9,10},{10,... | collective-permute-start | bytes 135176 | tf_op jit(solution)/shard_map/ppermute | solution.py:339
  85.1 2.5 %collective-permute-start.10 = (f32[8,1408]{1,0:T(8,128)S(1)}, f32[8,1408]{1,0:T(8,128)S(1)}, u32[]{:S(2)}, u32[]{:S(2)}) collective-permute-start(f32[8,1408]{1,0:T(8,128)S(1)} %total_kernel.1.mine), channel_id=1, source_target_pairs={{0,1},{1,0},{2,3},{3,2},{4,5},{5,4},{6,7},{7,6},{8,9},{9,8},{10,11... | collective-permute-start | bytes 135176 | tf_op jit(solution)/shard_map/ppermute | solution.py:339
  85.1 4.4 %collective-permute-start.9 = (f32[8,1408]{1,0:T(8,128)S(1)}, f32[8,1408]{1,0:T(8,128)S(1)}, u32[]{:S(2)}, u32[]{:S(2)}) collective-permute-start(f32[8,1408]{1,0:T(8,128)S(1)} %total_kernel.1.mine), channel_id=1, source_target_pairs={{0,2},{1,3},{2,0},{3,1},{4,6},{5,7},{6,4},{7,5},{8,10},{9,11},{10,... | collective-permute-start | bytes 135176 | tf_op jit(solution)/shard_map/ppermute | solution.py:339

commit v4 on v3

--- a/solution.py
+++ b/solution.py
@@ -77,15 +77,23 @@
     v_t[:, rows] = values.T
 
 
-def middle_kernel(upper, lower, wt, k, v, k_t, v_t):
-    project(upper[...], wt, k, v, k_t, v_t, 0)
-    project(lower[...], wt, k, v, k_t, v_t, 256)
+def middle_kernel(upper, lower, wt, k, v, k_t, v_t, x_t):
+    for at, ref in ((0, upper), (256, lower)):
+        project(ref[...], wt, k, v, k_t, v_t, at)
+        x_t[:, at : at + 256] = ref[...].T
+
+
+def weight_terms(ref, who, x_t, dkv, lhs, rhs):
+    ref[:, 0:512] = dot(lhs[who], rhs[who]).astype(BF16)
+    for n in range(2):
+        lanes = pl.ds(pl.multiple_of(who * 512 + n * 256, 256), 256)
+        ref[:, 512 + n * 256 : 768 + n * 256] = dot(x_t[...], dkv[:, lanes]).astype(BF16)
 
 
 def attention_kernel(
-    core, above, upper, lower, below, q, q_t, da, da_t, table, k_mid, v_mid, kt_mid, vt_mid, wt, own, cot,
-    dkv, dq_t, g_keep, g_send, g_bias,
-    k, v, k_t, v_t, xs, att_t, dsum, bsum, lhs, rhs,
+    core, above, below, q, q_t, da, da_t, table, k_mid, v_mid, kt_mid, vt_mid, xt_mid, wt, cot,
+    x_t, dkv, lhs, rhs, bsum, g_send,
+    k, v, k_t, v_t, dq_t, dsum,
 ):
     project(above[...], wt, k, v, k_t, v_t, 0)
     project(below[...], wt, k, v, k_t, v_t, 768)
@@ -93,8 +101,12 @@
     v[256:768] = v_mid[...]
     k_t[:, 256:768] = kt_mid[...]
     v_t[:, 256:768] = vt_mid[...]
-    for g, ref in enumerate((above, upper, lower, below)):
-        xs[:, g * 256 : g * 256 + 256] = ref[...].T
+    x_t[:, 0:256] = above[...].T
+    x_t[:, 256:768] = xt_mid[...]
+    x_t[:, 768:1024] = below[...].T
+    lhs[0, :, 0:128] = xt_mid[:, 64:192]
+    lhs[0, :, 128:256] = xt_mid[:, 320:448]
+    rhs[1] = cot[...]
 
     upper_rows = iota((128, 128), 0) < 64
     upper_lanes = iota((128, 128), 1) < 64
@@ -106,6 +118,9 @@
             [jnp.where(upper_rows, block, zero), jnp.where(upper_rows, zero, block)], axis=1
         )
 
+    def tall(ref, rows, cols, block):
+        return dot(ref[rows, cols], block)
+
     def split_rows(block):
         zero = jnp.zeros_like(block)
         return jnp.concatenate(
@@ -115,43 +130,44 @@
     def pair_step(pair, carry):
         at = pl.multiple_of(pair * 128, 128)
         cols = pl.ds(at, 128)
-        tails = []
+        keys = [slice(t * 256, t * 256 + 768) for t in range(2)]
+        mine = [slice(t * 128, t * 128 + 128) for t in range(2)]
+        da_block = [da_t[cols, mine[t]] for t in range(2)]
+        score = [
+            tall(k, keys[t], cols, split_lanes(q_t[cols, mine[t]])) + table[pair] for t in range(2)
+        ]
+        d_prob = [tall(v, keys[t], cols, split_lanes(da_block[t])) for t in range(2)]
+        prob, delta, d_value, d_key = [], [], [], []
         for t in range(2):
-            keys = slice(t * 256, t * 256 + 768)
-            mine = slice(t * 128, t * 128 + 128)
-            score = dot(k[keys, cols], split_lanes(q_t[cols, mine])) + table[pair]
-            top_score = jnp.max(score, axis=0, keepdims=True)
-            weight = jnp.exp(score - top_score)
-            prob = weight * (1.0 / jnp.sum(weight, axis=0, keepdims=True))
-            prob_low = prob.astype(BF16)
-            mixed = dot(v_t[cols, keys], prob_low)
+            top_score = jnp.max(score[t], axis=0, keepdims=True)
+            weight = jnp.exp(score[t] - top_score)
+            prob.append(weight * (1.0 / jnp.sum(weight, axis=0, keepdims=True)))
+        prob_low = [each.astype(BF16) for each in prob]
+        for t in range(2):
+            mixed = dot(v_t[cols, keys[t]], prob_low[t])
             att = jnp.where(upper_rows, mixed[:, :128], mixed[:, 128:]).astype(BF16)
-            att_t[cols, mine] = att
-            da_block = da_t[cols, mine]
-            product = att.astype(F32) * da_block.astype(F32)
-            delta = jnp.concatenate(
-                [
-                    jnp.sum(product[:64], axis=0, keepdims=True),
-                    jnp.sum(product[64:], axis=0, keepdims=True),
-                ],
-                axis=1,
+            lhs[1, cols, mine[t]] = att
+            product = att.astype(F32) * da_block[t].astype(F32)
+            delta.append(
+                jnp.concatenate(
+                    [
+                        jnp.sum(product[:64], axis=0, keepdims=True),
+                        jnp.sum(product[64:], axis=0, keepdims=True),
+                    ],
+                    axis=1,
+                )
             )
-            d_score = prob * (dot(v[keys, cols], split_lanes(da_block)) - delta)
-            if t == 0:
-                dsum[...] = d_score
-            else:
-                dsum[...] += d_score
-            score_low = d_score.astype(BF16)
-            d_q = dot(k_t[cols, keys], score_low)
-            dq_t[cols, mine] = (
+            d_value.append(dot(prob_low[t], split_rows(da[mine[t], cols])))
+        d_score = [prob[t] * (d_prob[t] - delta[t]) for t in range(2)]
+        dsum[...] = d_score[0] + d_score[1]
+        for t in range(2):
+            score_low = d_score[t].astype(BF16)
+            d_q = dot(k_t[cols, keys[t]], score_low)
+            dq_t[cols, mine[t]] = (
                 jnp.where(upper_rows, d_q[:, :128], d_q[:, 128:]) * 0.125
             ).astype(BF16)
-            tails.append(
-                (
-                    dot(score_low, split_rows(q[mine, cols])),
-                    dot(prob_low, split_rows(da[mine, cols])),
-                )
-            )
+            d_key.append(dot(score_low, split_rows(q[mine[t], cols])))
+        tails = ((d_key[0], d_value[0]), (d_key[1], d_value[1]))
         for which in range(2):
             early, late = tails[0][which], tails[1][which]
             to = pl.ds(pl.multiple_of(which * 512 + at, 128), 128)
@@ -192,6 +208,15 @@
 
     lax.fori_loop(0, 4, pair_step, 0)
 
+    rhs[0] = dq_t[...].T
+    weight_terms(g_send, 1 - core[0], x_t, dkv, lhs, rhs)
+
+
+def terms_kernel(
+    core, x_t, dkv, lhs, rhs, bsum, wt, g_keep, g_bias, g_above, g_upper, g_lower, g_below
+):
+    weight_terms(g_keep, core[0], x_t, dkv, lhs, rhs)
+
     spot = iota((512, 384), 0)
     place = iota((512, 384), 1)
     i = (place * 241) >> 12
@@ -206,24 +231,10 @@
             lanes = row if lanes is None else lanes + row
         from_lane = 368 - 16 * i - j
         choose = inside & (spot == from_lane) & ((j < 16) if which == 0 else (j == 16))
-        part = dot(lanes, choose.astype(F32), exact=True)
+        part = dot(lanes.astype(BF16), choose.astype(F32).astype(BF16))
         flat = part if flat is None else flat + part
     g_bias[...] = flat
 
-    lhs[0, :, 0:128] = xs[:, 320:448]
-    lhs[0, :, 128:256] = xs[:, 576:704]
-    lhs[1] = att_t[...]
-    rhs[0] = dq_t[...].T
-    rhs[1] = cot[...]
-    for ref, who in ((g_send, 1 - core[0]), (g_keep, core[0])):
-        ref[:, 0:512] = dot(lhs[who], rhs[who]).astype(BF16)
-        for n in range(2):
-            lanes = pl.ds(pl.multiple_of(who * 512 + n * 256, 256), 256)
-            ref[:, 512 + n * 256 : 768 + n * 256] = dot(xs[...], dkv[:, lanes]).astype(BF16)
-
-
-def tokens_kernel(dkv, dq_t, wt, g_above, g_upper, g_lower, g_below):
-    d_q = dq_t[...].T
     for g, ref in enumerate((g_above, g_upper, g_lower, g_below)):
         block = dot(dkv[g * 256 : g * 256 + 256], wt[512:1536])
         if g in (0, 3):
@@ -231,7 +242,7 @@
         else:
             half = (g - 1) * 128
             ref[0:64] = block[0:64]
-            ref[64:192] = block[64:192] + dot(d_q[half : half + 128], wt[0:512])
+            ref[64:192] = block[64:192] + dot(rhs[0, half : half + 128], wt[0:512])
             ref[192:256] = block[192:256]
 
 
@@ -248,7 +259,7 @@
     out[:, 8:16] = (own[:, 8:16] + east[...].astype(F32)).astype(BF16)
 
 
-def pack_kernel(keep, came, bias, _, parcel):
+def pack_kernel(keep, came, bias, parcel):
     count, rows, _ = parcel.shape
     for a in range(rows // 8):
         for r in range(count):
@@ -262,7 +273,7 @@
             parcel[r, n * 8 : n * 8 + 8, 1024:1152] = part
 
 
-def regroup_kernel(came, parcel):
+def regroup_kernel(came, _, parcel):
     count = parcel.shape[0]
     for a in range(count):
         rows = slice(a * 8, a * 8 + 8)
@@ -305,14 +316,16 @@
     return jax.ShapeDtypeStruct(shape, dtype)
 
 
-def call(kernel, operands, outs, scratch=(), prefetch=0, flops=0, limit=16):
+def call(kernel, operands, outs, scratch=(), prefetch=0, flops=0, limit=16, untouched=0):
     spec = pl.BlockSpec(memory_space=pltpu.VMEM)
     scalar = pl.BlockSpec(memory_space=pltpu.SMEM)
     size = sum(leaf.size * leaf.dtype.itemsize for leaf in tuple(operands) + tuple(outs))
     return pl.pallas_call(
         kernel,
         out_shape=tuple(outs),
-        in_specs=[scalar] * prefetch + [spec] * (len(operands) - prefetch),
+        in_specs=[scalar] * prefetch
+        + [spec] * (len(operands) - prefetch - untouched)
+        + [pl.BlockSpec(memory_space=pl.ANY)] * untouched,
         out_specs=tuple([spec] * len(outs)),
         scratch_shapes=list(scratch),
         compiler_params=pltpu.CompilerParams(vmem_limit_bytes=limit * MIB),
@@ -363,58 +376,45 @@
         limit=12,
     )
     middle = call(
-        middle_kernel,
-        (upper, lower, turned),
+        middle_kernel, (upper, lower, turned), (whole((512, 512), BF16),) * 5, flops=1_000_000_000, limit=12
+    )
+    x_t, dkv, lhs, rhs, bsum, g_send = call(
+        attention_kernel,
+        (core, above, below, q, q_t, da, da_t, table, *middle, turned, cot),
         (
-            whole((512, 512), BF16), whole((512, 512), BF16),
-            whole((512, 512), BF16), whole((512, 512), BF16),
-        ),
-        flops=1_000_000_000,
-        limit=12,
-    )
-    dkv, dq_t, g_keep, g_send, g_bias = call(
-        attention_kernel,
-        (core, above, upper, lower, below, q, q_t, da, da_t, table, *middle, turned, own, cot),
-        (
-            whole((1024, 1024), BF16), whole((512, 256), BF16),
-            whole((512, 1024), BF16), whole((512, 1024), BF16),
-            whole((8, 384), F32),
+            whole((512, 1024), BF16), whole((1024, 1024), BF16),
+            whole((2, 512, 256), BF16), whole((2, 256, 512), BF16),
+            whole((2, 8, 8, 512), F32), whole((512, 1024), BF16),
         ),
         scratch=(
             pltpu.VMEM((1024, 512), BF16), pltpu.VMEM((1024, 512), BF16),
             pltpu.VMEM((512, 1024), BF16), pltpu.VMEM((512, 1024), BF16),
-            pltpu.VMEM((512, 1024), BF16), pltpu.VMEM((512, 256), BF16),
-            pltpu.VMEM((768, 256), F32), pltpu.VMEM((2, 8, 8, 512), F32),
-            pltpu.VMEM((2, 512, 256), BF16), pltpu.VMEM((2, 256, 512), BF16),
+            pltpu.VMEM((512, 256), BF16), pltpu.VMEM((768, 256), F32),
         ),
         prefetch=1,
         flops=10_000_000_000,
         limit=20,
     )
-
-    g_above, g_upper, g_lower, g_below = call(
-        tokens_kernel,
-        (dkv, dq_t, turned),
+    came = among(g_send, 1)
+    g_keep, g_bias, g_above, g_upper, g_lower, g_below = call(
+        terms_kernel,
+        (core, x_t, dkv, lhs, rhs, bsum, turned),
         (
+            whole((512, 1024), BF16), whole((8, 384), F32),
             whole((256, 512), BF16), whole((256, 512), F32),
             whole((256, 512), F32), whole((256, 512), BF16),
         ),
-        flops=1_200_000_000,
-    )
-
-    came = among(g_send, 1)
+        prefetch=1,
+        flops=2_500_000_000,
+        limit=12,
+    )
     (parcel,) = call(
         pack_kernel,
-        (g_keep, came, g_bias, g_above),
+        (g_keep, came, g_bias),
         (whole((rng, 8 * az, 1152), BF16),),
         flops=1_000_000,
     )
     parcel = lax.all_to_all(parcel, "rng", 0, 0, tiled=True)
-    (parcel,) = call(
-        regroup_kernel, (parcel,), (whole((az, 8, 1408), BF16),), flops=1_000_000
-    )
-    parcel = lax.all_to_all(parcel, "az", 0, 0, tiled=True)
-    (mine,) = call(total_kernel, (parcel,), (whole((8, 1408), F32),), flops=1_000_000)
 
     up = turn(g_below, 1)
     down = turn(g_above, -1)
@@ -433,6 +433,15 @@
         flops=1_000_000,
     )
 
+    (parcel,) = call(
+        regroup_kernel,
+        (parcel, grad_tokens),
+        (whole((az, 8, 1408), BF16),),
+        flops=1_000_000,
+        untouched=1,
+    )
+    parcel = lax.all_to_all(parcel, "az", 0, 0, tiled=True)
+    (mine,) = call(total_kernel, (parcel,), (whole((8, 1408), F32),), flops=1_000_000)
     near, other, far = among(mine, 2), among(mine, 1), among(mine, 3)
     rows_qkv, rows_out, total_bias = call(
         finish_kernel,

time: 90.7 us -> 90.7 us (level)
  the two profiles are of different devices: /device:TPU:1 before, /device:TPU:6 now
where the time goes in v4:
time: 90.7 us; the launch traced here: 90.3 us
  starting transfers between devices  29.3 us (32%)
  waiting for transfers between devices  21.6 us (24%)
  Pallas kernels  18.5 us (20%)
  blocking collectives  15.3 us (17%)
  local copies, waits for them, and re-layouts  4.66 us (5%)
    pallas_call x10, Pallas kernels, call(): pl.pallas_call(kernel, out_shape=tuple(outs), in_specs=[scalar] * prefetc...  18.5 us
    all_to_all x1, blocking collectives, shards(): parcel = lax.all_to_all(parcel, 'az', 0, 0, tiled=True)  15.3 us
    ppermute x4, starting transfers between devices, shift(): return lax.ppermute(leaf, 'rng', pairs)  11.7 us
    ppermute x4, waiting for transfers between devices, shift(): return lax.ppermute(leaf, 'rng', pairs)  10.2 us
    ppermute x4, starting transfers between devices, turn(): return lax.ppermute(leaf, 'az', [(i, (i + step) % az) for i in range(az)])  9.26 us
    ppermute x4, waiting for transfers between devices, turn(): return lax.ppermute(leaf, 'az', [(i, (i + step) % az) for i in range(az)])  6.12 us
    ppermute x4, waiting for transfers between devices, among(): return lax.ppermute(leaf, 'dp', [(i, i ^ flip) for i in range(4)])  5.29 us
    all_to_all x1, starting transfers between devices, shards(): parcel = lax.all_to_all(parcel, 'rng', 0, 0, tiled=True)  4.51 us
  transfers between devices with their start and end apart: 13, of which 8 were waited for; matrix products, arithmetic and copies ran while one was open for 3% of the time, Pallas kernels for 8%

profile of v4, /device:TPU:6, one launch (start us, length us, event | category | flops | bytes accessed | tf_op | source)
XLA Modules:
  0.0 90.3 jit_solution(16282753554043093773)
XLA Ops:
  0.6 1.0 %fusion.1 = (bf16[16,8,512]{2,1,0:T(8,128)(2,1)S(1)}, bf16[16,8,512]{2,1,0:T(8,128)(2,1)S(1)}) fusion(bf16[16,16,512]{2,1,0:T(8,128)(2,1)} %bitcast.26), kind=kLoop, calls=%fused_computation.8 | loop fusion | bytes 524288 | tf_op jit(solution)/shard_map/slice | solution.py:354
  1.6 3.4 %collective-permute-start = (bf16[16,8,512]{2,1,0:T(8,128)(2,1)S(1)}, bf16[16,8,512]{2,1,0:T(8,128)(2,1)S(1)}, u32[]{:S(2)}, u32[]{:S(2)}) collective-permute-start(bf16[16,8,512]{2,1,0:T(8,128)(2,1)S(1)} %get-tuple-element.62), channel_id=1, source_target_pairs={{0,4},{4,8},{8,12},{12,16},{16,20},{20,24},{24,28},{1,5},{5,9},{9,... | collective-permute-start | bytes 393224 | tf_op jit(solution)/shard_map/ppermute | solution.py:349
  5.0 2.4 %collective-permute-start.1 = (bf16[16,8,512]{2,1,0:T(8,128)(2,1)S(1)}, bf16[16,8,512]{2,1,0:T(8,128)(2,1)S(1)}, u32[]{:S(2)}, u32[]{:S(2)}) collective-permute-start(bf16[16,8,512]{2,1,0:T(8,128)(2,1)S(1)} %get-tuple-element.63), channel_id=1, source_target_pairs={{4,0},{8,4},{12,8},{16,12},{20,16},{24,20},{28,24},{5,1},{9,5},{13... | collective-permute-start | bytes 393224 | tf_op jit(solution)/shard_map/ppermute | solution.py:349
  7.5 0.9 copy.10.bias
  8.4 0.0 copy-start
  8.4 1.8 %copy.9 = bf16[512,1536]{0,1:T(8,128)(2,1)S(1)} copy(bf16[512,1536]{1,0:T(8,128)(2,1)} %param.6) | data formatting | bytes 3145728 | tf_op args[1]
  10.2 0.0 copy-start.2
  10.2 0.0 copy-start.3
  10.2 0.0 copy-done
  10.2 0.0 collective-permute-done
  10.3 3.7 %collective-permute-done.1 = bf16[16,8,512]{2,1,0:T(8,128)(2,1)S(1)} collective-permute-done((bf16[16,8,512]{2,1,0:T(8,128)(2,1)S(1)}, bf16[16,8,512]{2,1,0:T(8,128)(2,1)S(1)}, u32[]{:S(2)}, u32[]{:S(2)}) %collective-permute-start.1) | collective-permute-done | bytes 131104 | tf_op jit(solution)/shard_map/ppermute | solution.py:349
  14.0 2.0 %collective-permute-start.2 = (bf16[256,512]{1,0:T(8,128)(2,1)S(1)}, bf16[256,512]{1,0:T(8,128)(2,1)S(1)}, u32[]{:S(2)}, u32[]{:S(2)}) collective-permute-start(bf16[256,512]{1,0:T(8,128)(2,1)S(1)} %pad_maximum_fusion.lower), channel_id=1, source_target_pairs={{0,32},{32,64},{64,96},{96,128},{128,160},{160,192},{192,224},{224... | collective-permute-start | bytes 786440 | tf_op jit(solution)/shard_map/ppermute | solution.py:345
  16.1 4.0 %collective-permute-start.3 = (bf16[256,512]{1,0:T(8,128)(2,1)S(1)}, bf16[256,512]{1,0:T(8,128)(2,1)S(1)}, u32[]{:S(2)}, u32[]{:S(2)}) collective-permute-start(bf16[256,512]{1,0:T(8,128)(2,1)S(1)} %pad_maximum_fusion.1.upper), channel_id=1, source_target_pairs={{0,224},{32,0},{64,32},{96,64},{128,96},{160,128},{192,160},{224,1... | collective-permute-start | bytes 786440 | tf_op jit(solution)/shard_map/ppermute | solution.py:345
  20.1 0.1 add_convert_fusion.edge
  20.2 0.0 copy-done.2
  20.2 0.0 copy-done.3
  20.2 3.6 %before_kernel.1 = (bf16[256,512]{1,0:T(8,128)(2,1)S(1)}, bf16[512,256]{1,0:T(8,128)(2,1)S(1)}, bf16[256,512]{1,0:T(8,128)(2,1)S(1)}, bf16[512,256]{1,0:T(8,128)(2,1)S(1)}, f32[4,768,256]{2,1,0:T(8,128)S(1)}) custom-call(s32[2]{0:T(128)S(1)} %add_convert_fusion.edge, bf16[256,512]{1,0:T(8,128)(2,1)S(1)} %bitcast.27, bf16[256,512]{1,0:T(8,128)(2,1)S(1)} %bitcast.30, ...), custom_call_target="tpu_custom_call" | custom-call | flops 600000000 | bytes 6825000 | tf_op jit(solution)/shard_map/before_kernel/pallas_call | solution.py:323
  23.7 0.9 middle_kernel.1
  24.6 0.3 collective-permute-done.2.above
  24.9 0.0 collective-permute-done.3.below
  24.9 8.8 %attention_kernel.1 = (bf16[512,1024]{1,0:T(8,128)(2,1)S(1)}, bf16[1024,1024]{1,0:T(8,128)(2,1)S(1)}, bf16[2,512,256]{2,1,0:T(8,128)(2,1)S(1)}, bf16[2,256,512]{...) custom-call(s32[1]{0:T(128)} %bitcast.core, ...), custom_call_target="tpu_custom_call" | custom-call | flops 10000000000 | bytes 14680068 | tf_op jit(solution)/shard_map/attention_kernel/pallas_call | solution.py:323
  33.7 0.1 collective-permute-start.8
  33.8 2.3 %terms_kernel.1 = (bf16[512,1024]{1,0:T(8,128)(2,1)S(1)}, f32[8,384]{1,0:T(8,128)S(1)}, bf16[256,512]{1,0:T(8,128)(2,1)S(1)}, f32[256,512]{1,0:T(8,128)S(1)}, f3...) custom-call(s32[1]{0:T(128)} %bitcast.core, bf16[512,1024]{1,0:T(8,128)(2,1)S(1)} %get-tuple-element.42.x_t, ...), custom_call_target="tpu_custom_call" | custom-call | flops 2500000000 | bytes 8663044 | tf_op jit(solution)/shard_map/terms_kernel/pallas_call | solution.py:323
  36.0 0.4 collective-permute-done.8.came
  36.4 1.3 %pack_kernel.1 = bf16[8,64,1152]{2,1,0:T(8,128)(2,1)} custom-call(bf16[512,1024]{1,0:T(8,128)(2,1)S(1)} %get-tuple-element.54.keep, bf16[512,1024]{1,0:T(8,128)(2,1)S(1)} %collective-permute-done.8.came, f32[8,384]{1,0:T(8,128)S(1)} %get-tuple-element.56.bias), custom_call_target="tpu_custom_call" | custom-call | flops 1000000 | bytes 3289088 | tf_op jit(solution)/shard_map/pack_kernel/pallas_call | solution.py:323
  37.7 4.5 %all-to-all-start = ((bf16[8,64,1152]{2,1,0:T(8,128)(2,1)}), bf16[8,64,1152]{2,1,0:T(8,128)(2,1)S(1)}, u32[]{:S(2)}, u32[]{:S(2)}) async-start(bf16[8,64,1152]{2,1,0:T(8,128)(2,1)} %pack_kernel.1), calls=%async_computation | async-start | bytes 2359296 | tf_op jit(solution)/shard_map/all_to_all | solution.py:417
  42.2 0.0 collective-permute-start.4
  42.2 3.2 %collective-permute-start.5 = (bf16[256,512]{1,0:T(8,128)(2,1)S(1)}, bf16[256,512]{1,0:T(8,128)(2,1)S(1)}, u32[]{:S(2)}, u32[]{:S(2)}) collective-permute-start(bf16[256,512]{1,0:T(8,128)(2,1)S(1)} %get-tuple-element.50), channel_id=1, source_target_pairs={{0,224},{32,0},{64,32},{96,64},{128,96},{160,128},{192,160},{224,1... | collective-permute-start | bytes 786440 | tf_op jit(solution)/shard_map/ppermute | solution.py:345
  45.5 5.9 %collective-permute-done.4.up = bf16[256,512]{1,0:T(8,128)(2,1)S(1)} collective-permute-done((bf16[256,512]{1,0:T(8,128)(2,1)S(1)}, bf16[256,512]{1,0:T(8,128)(2,1)S(1)}, u32[]{:S(2)}, u32[]{:S(2)}) %collective-permute-start.4) | collective-permute-done | bytes 262176 | tf_op jit(solution)/shard_map/ppermute | solution.py:345
  51.3 0.0 collective-permute-done.5.down
  51.3 0.1 fold_kernel.1
  51.4 3.4 %collective-permute-start.6 = (bf16[16,8,512]{2,1,0:T(8,128)(2,1)S(1)}, bf16[16,8,512]{2,1,0:T(8,128)(2,1)S(1)}, u32[]{:S(2)}, u32[]{:S(2)}) collective-permute-start(bf16[16,8,512]{2,1,0:T(8,128)(2,1)S(1)} %bitcast.33), channel_id=1, source_target_pairs={{0,4},{4,8},{8,12},{12,16},{16,20},{20,24},{24,28},{1,5},{5,9},{9,... | collective-permute-start | bytes 393224 | tf_op jit(solution)/shard_map/ppermute | solution.py:349
  54.8 2.5 %collective-permute-start.7 = (bf16[16,8,512]{2,1,0:T(8,128)(2,1)S(1)}, bf16[16,8,512]{2,1,0:T(8,128)(2,1)S(1)}, u32[]{:S(2)}, u32[]{:S(2)}) collective-permute-start(bf16[16,8,512]{2,1,0:T(8,128)(2,1)S(1)} %bitcast.32), channel_id=1, source_target_pairs={{4,0},{8,4},{12,8},{16,12},{20,16},{24,20},{28,24},{5,1},{9,5},{13... | collective-permute-start | bytes 393224 | tf_op jit(solution)/shard_map/ppermute | solution.py:349
  57.3 2.0 %collective-permute-done.6.west = bf16[16,8,512]{2,1,0:T(8,128)(2,1)S(1)} collective-permute-done((bf16[16,8,512]{2,1,0:T(8,128)(2,1)S(1)}, bf16[16,8,512]{2,1,0:T(8,128)(2,1)S(1)}, u32[]{:S(2)}, u32[]{:S(2)}) %collective-permute-start.6) | collective-permute-done | bytes 131104 | tf_op jit(solution)/shard_map/ppermute | solution.py:349
  59.3 4.5 %collective-permute-done.7.east = bf16[16,8,512]{2,1,0:T(8,128)(2,1)S(1)} collective-permute-done((bf16[16,8,512]{2,1,0:T(8,128)(2,1)S(1)}, bf16[16,8,512]{2,1,0:T(8,128)(2,1)S(1)}, u32[]{:S(2)}, u32[]{:S(2)}) %collective-permute-start.7) | collective-permute-done | bytes 131104 | tf_op jit(solution)/shard_map/ppermute | solution.py:349
  63.8 0.7 after_kernel.1._
  64.5 0.0 all-to-all-done.came
  64.5 0.0 copy-start.1
  64.5 0.9 %copy-done.1 = bf16[16,16,512]{2,1,0:T(8,128)(2,1)S(1)} copy-done((bf16[16,16,512]{2,1,0:T(8,128)(2,1)S(1)}, bf16[16,16,512]{2,1,0:T(8,128)(2,1)}, u32[]{:S(2)}) %copy-start.1) | copy-done | bytes 262168
  65.5 0.1 regroup_kernel.1
  65.6 15.3 %all_to_all.10.came = bf16[8,8,1408]{2,1,0:T(8,128)(2,1)S(1)} all-to-all(bf16[8,8,1408]{2,1,0:T(8,128)(2,1)S(1)} %regroup_kernel.1), channel_id=1, replica_groups=mesh['az'=8,'rng'=8,'dp'=4] {'az'}, dimensions={0} | all-to-all | bytes 360448 | tf_op jit(solution)/shard_map/all_to_all | solution.py:443
  80.9 0.1 collective-permute-start.11
  81.0 3.0 %collective-permute-start.10 = (f32[8,1408]{1,0:T(8,128)S(1)}, f32[8,1408]{1,0:T(8,128)S(1)}, u32[]{:S(2)}, u32[]{:S(2)}) collective-permute-start(f32[8,1408]{1,0:T(8,128)S(1)} %total_kernel.1.mine), channel_id=1, source_target_pairs={{0,1},{1,0},{2,3},{3,2},{4,5},{5,4},{6,7},{7,6},{8,9},{9,8},{10,11... | collective-permute-start | bytes 135176 | tf_op jit(solution)/shard_map/ppermute | solution.py:352
  84.0 0.6 collective-permute-start.9
  84.7 1.8 %collective-permute-done.11.far = f32[8,1408]{1,0:T(8,128)S(1)} collective-permute-done((f32[8,1408]{1,0:T(8,128)S(1)}, f32[8,1408]{1,0:T(8,128)S(1)}, u32[]{:S(2)}, u32[]{:S(2)}) %collective-permute-start.11) | collective-permute-done | bytes 45088 | tf_op jit(solution)/shard_map/ppermute | solution.py:352
  86.4 0.0 collective-permute-done.10.other
  86.4 3.2 %collective-permute-done.9.near = f32[8,1408]{1,0:T(8,128)S(1)} collective-permute-done((f32[8,1408]{1,0:T(8,128)S(1)}, f32[8,1408]{1,0:T(8,128)S(1)}, u32[]{:S(2)}, u32[]{:S(2)}) %collective-permute-start.9) | collective-permute-done | bytes 45088 | tf_op jit(solution)/shard_map/ppermute | solution.py:352
  89.6 0.7 finish_kernel.1
  (6 shorter events, 0.1 us)
Async XLA Ops:
  1.6 8.6 %collective-permute-start = (bf16[16,8,512]{2,1,0:T(8,128)(2,1)S(1)}, bf16[16,8,512]{2,1,0:T(8,128)(2,1)S(1)}, u32[]{:S(2)}, u32[]{:S(2)}) collective-permute-start(bf16[16,8,512]{2,1,0:T(8,128)(2,1)S(1)} %get-tuple-element.62), channel_id=1, source_target_pairs={{0,4},{4,8},{8,12},{12,16},{16,20},{20,24},{24,28},{1,5},{5,9},{9,... | collective-permute-start | bytes 393224 | tf_op jit(solution)/shard_map/ppermute | solution.py:349
  5.0 9.0 %collective-permute-start.1 = (bf16[16,8,512]{2,1,0:T(8,128)(2,1)S(1)}, bf16[16,8,512]{2,1,0:T(8,128)(2,1)S(1)}, u32[]{:S(2)}, u32[]{:S(2)}) collective-permute-start(bf16[16,8,512]{2,1,0:T(8,128)(2,1)S(1)} %get-tuple-element.63), channel_id=1, source_target_pairs={{4,0},{8,4},{12,8},{16,12},{20,16},{24,20},{28,24},{5,1},{9,5},{13... | collective-permute-start | bytes 393224 | tf_op jit(solution)/shard_map/ppermute | solution.py:349
  8.4 1.8 %copy-start = (bf16[1,16,16,512]{3,2,1,0:T(8,128)(2,1)S(1)}, bf16[1,16,16,512]{3,2,1,0:T(8,128)(2,1)}, u32[]{:S(2)}) copy-start(bf16[1,16,16,512]{3,2,1,0:T(8,128)(2,1)} %param.5) | copy-start | bytes 786436
  10.2 10.0 %copy-start.2 = (bf16[512,512]{1,0:T(8,128)(2,1)S(1)}, bf16[512,512]{1,0:T(8,128)(2,1)}, u32[]{:S(2)}) copy-start(bf16[512,512]{1,0:T(8,128)(2,1)} %wo.1) | copy-start | bytes 1572868
  10.2 10.0 %copy-start.3 = (bf16[1,16,16,512]{3,2,1,0:T(8,128)(2,1)S(1)}, bf16[1,16,16,512]{3,2,1,0:T(8,128)(2,1)}, u32[]{:S(2)}) copy-start(bf16[1,16,16,512]{3,2,1,0:T(8,128)(2,1)} %param.9) | copy-start | bytes 786436
  14.0 10.8 %collective-permute-start.2 = (bf16[256,512]{1,0:T(8,128)(2,1)S(1)}, bf16[256,512]{1,0:T(8,128)(2,1)S(1)}, u32[]{:S(2)}, u32[]{:S(2)}) collective-permute-start(bf16[256,512]{1,0:T(8,128)(2,1)S(1)} %pad_maximum_fusion.lower), channel_id=1, source_target_pairs={{0,32},{32,64},{64,96},{96,128},{128,160},{160,192},{192,224},{224... | collective-permute-start | bytes 786440 | tf_op jit(solution)/shard_map/ppermute | solution.py:345
  16.1 8.8 %collective-permute-start.3 = (bf16[256,512]{1,0:T(8,128)(2,1)S(1)}, bf16[256,512]{1,0:T(8,128)(2,1)S(1)}, u32[]{:S(2)}, u32[]{:S(2)}) collective-permute-start(bf16[256,512]{1,0:T(8,128)(2,1)S(1)} %pad_maximum_fusion.1.upper), channel_id=1, source_target_pairs={{0,224},{32,0},{64,32},{96,64},{128,96},{160,128},{192,160},{224,1... | collective-permute-start | bytes 786440 | tf_op jit(solution)/shard_map/ppermute | solution.py:345
  33.7 2.7 %collective-permute-start.8 = (bf16[512,1024]{1,0:T(8,128)(2,1)S(1)}, bf16[512,1024]{1,0:T(8,128)(2,1)S(1)}, u32[]{:S(2)}, u32[]{:S(2)}) collective-permute-start(bf16[512,1024]{1,0:T(8,128)(2,1)S(1)} %get-tuple-element.55), channel_id=1, source_target_pairs={{0,1},{1,0},{2,3},{3,2},{4,5},{5,4},{6,7},{7,6},{8,9},{9,8},{10,11... | collective-permute-start | bytes 3145736 | tf_op jit(solution)/shard_map/ppermute | solution.py:352
  37.7 26.8 %all-to-all-start = ((bf16[8,64,1152]{2,1,0:T(8,128)(2,1)}), bf16[8,64,1152]{2,1,0:T(8,128)(2,1)S(1)}, u32[]{:S(2)}, u32[]{:S(2)}) async-start(bf16[8,64,1152]{2,1,0:T(8,128)(2,1)} %pack_kernel.1), calls=%async_computation | async-start | bytes 2359296 | tf_op jit(solution)/shard_map/all_to_all | solution.py:417
  42.2 9.1 %collective-permute-start.4 = (bf16[256,512]{1,0:T(8,128)(2,1)S(1)}, bf16[256,512]{1,0:T(8,128)(2,1)S(1)}, u32[]{:S(2)}, u32[]{:S(2)}) collective-permute-start(bf16[256,512]{1,0:T(8,128)(2,1)S(1)} %get-tuple-element.49), channel_id=1, source_target_pairs={{0,32},{32,64},{64,96},{96,128},{128,160},{160,192},{192,224},{224... | collective-permute-start | bytes 786440 | tf_op jit(solution)/shard_map/ppermute | solution.py:345
  42.2 9.1 %collective-permute-start.5 = (bf16[256,512]{1,0:T(8,128)(2,1)S(1)}, bf16[256,512]{1,0:T(8,128)(2,1)S(1)}, u32[]{:S(2)}, u32[]{:S(2)}) collective-permute-start(bf16[256,512]{1,0:T(8,128)(2,1)S(1)} %get-tuple-element.50), channel_id=1, source_target_pairs={{0,224},{32,0},{64,32},{96,64},{128,96},{160,128},{192,160},{224,1... | collective-permute-start | bytes 786440 | tf_op jit(solution)/shard_map/ppermute | solution.py:345
  51.4 7.9 %collective-permute-start.6 = (bf16[16,8,512]{2,1,0:T(8,128)(2,1)S(1)}, bf16[16,8,512]{2,1,0:T(8,128)(2,1)S(1)}, u32[]{:S(2)}, u32[]{:S(2)}) collective-permute-start(bf16[16,8,512]{2,1,0:T(8,128)(2,1)S(1)} %bitcast.33), channel_id=1, source_target_pairs={{0,4},{4,8},{8,12},{12,16},{16,20},{20,24},{24,28},{1,5},{5,9},{9,... | collective-permute-start | bytes 393224 | tf_op jit(solution)/shard_map/ppermute | solution.py:349
  54.8 9.0 %collective-permute-start.7 = (bf16[16,8,512]{2,1,0:T(8,128)(2,1)S(1)}, bf16[16,8,512]{2,1,0:T(8,128)(2,1)S(1)}, u32[]{:S(2)}, u32[]{:S(2)}) collective-permute-start(bf16[16,8,512]{2,1,0:T(8,128)(2,1)S(1)} %bitcast.32), channel_id=1, source_target_pairs={{4,0},{8,4},{12,8},{16,12},{20,16},{24,20},{28,24},{5,1},{9,5},{13... | collective-permute-start | bytes 393224 | tf_op jit(solution)/shard_map/ppermute | solution.py:349
  64.5 1.0 %copy-start.1 = (bf16[16,16,512]{2,1,0:T(8,128)(2,1)S(1)}, bf16[16,16,512]{2,1,0:T(8,128)(2,1)}, u32[]{:S(2)}) copy-start(bf16[16,16,512]{2,1,0:T(8,128)(2,1)} %after_kernel.1._) | copy-start | bytes 786436
  80.9 5.5 %collective-permute-start.11 = (f32[8,1408]{1,0:T(8,128)S(1)}, f32[8,1408]{1,0:T(8,128)S(1)}, u32[]{:S(2)}, u32[]{:S(2)}) collective-permute-start(f32[8,1408]{1,0:T(8,128)S(1)} %total_kernel.1.mine), channel_id=1, source_target_pairs={{0,3},{1,2},{2,1},{3,0},{4,7},{5,6},{6,5},{7,4},{8,11},{9,10},{10,... | collective-permute-start | bytes 135176 | tf_op jit(solution)/shard_map/ppermute | solution.py:352
  81.0 5.4 %collective-permute-start.10 = (f32[8,1408]{1,0:T(8,128)S(1)}, f32[8,1408]{1,0:T(8,128)S(1)}, u32[]{:S(2)}, u32[]{:S(2)}) collective-permute-start(f32[8,1408]{1,0:T(8,128)S(1)} %total_kernel.1.mine), channel_id=1, source_target_pairs={{0,1},{1,0},{2,3},{3,2},{4,5},{5,4},{6,7},{7,6},{8,9},{9,8},{10,11... | collective-permute-start | bytes 135176 | tf_op jit(solution)/shard_map/ppermute | solution.py:352
  84.0 5.6 %collective-permute-start.9 = (f32[8,1408]{1,0:T(8,128)S(1)}, f32[8,1408]{1,0:T(8,128)S(1)}, u32[]{:S(2)}, u32[]{:S(2)}) collective-permute-start(f32[8,1408]{1,0:T(8,128)S(1)} %total_kernel.1.mine), channel_id=1, source_target_pairs={{0,2},{1,3},{2,0},{3,1},{4,6},{5,7},{6,4},{7,5},{8,10},{9,11},{10,... | collective-permute-start | bytes 135176 | tf_op jit(solution)/shard_map/ppermute | solution.py:352

commit v5 on v4

--- a/solution.py
+++ b/solution.py
@@ -1,9 +1,12 @@
+import functools
+
 import jax
 import jax.numpy as jnp
 from jax import lax
 from jax.experimental import pallas as pl
 from jax.experimental.pallas import tpu as pltpu
-from jax.sharding import PartitionSpec as P
+from jax.sharding import Mesh, PartitionSpec as P
+
 
 F32 = jnp.float32
 BF16 = jnp.bfloat16
@@ -83,15 +86,23 @@
         x_t[:, at : at + 256] = ref[...].T
 
 
-def weight_terms(ref, who, x_t, dkv, lhs, rhs):
-    ref[:, 0:512] = dot(lhs[who], rhs[who]).astype(BF16)
+def by_range(block, rng):
+    rows, cols = block.shape
+    turned = jnp.transpose(block.reshape(rows // (rng * 8), rng, 8, cols), (1, 0, 2, 3))
+    return turned.reshape(rows, cols)
+
+
+def weight_terms(ref, who, rng, x_t, dkv, lhs, rhs):
+    ref[:, 0:512] = by_range(dot(lhs[who], rhs[who]), rng).astype(BF16)
     for n in range(2):
         lanes = pl.ds(pl.multiple_of(who * 512 + n * 256, 256), 256)
-        ref[:, 512 + n * 256 : 768 + n * 256] = dot(x_t[...], dkv[:, lanes]).astype(BF16)
+        ref[:, 512 + n * 256 : 768 + n * 256] = by_range(dot(x_t[...], dkv[:, lanes]), rng).astype(
+            BF16
+        )
 
 
 def attention_kernel(
-    core, above, below, q, q_t, da, da_t, table, k_mid, v_mid, kt_mid, vt_mid, xt_mid, wt, cot,
+    rng, core, above, below, q, q_t, da, da_t, table, k_mid, v_mid, kt_mid, vt_mid, xt_mid, wt, cot,
     x_t, dkv, lhs, rhs, bsum, g_send,
     k, v, k_t, v_t, dq_t, dsum,
 ):
@@ -209,13 +220,13 @@
     lax.fori_loop(0, 4, pair_step, 0)
 
     rhs[0] = dq_t[...].T
-    weight_terms(g_send, 1 - core[0], x_t, dkv, lhs, rhs)
+    weight_terms(g_send, 1 - core[0], rng, x_t, dkv, lhs, rhs)
 
 
 def terms_kernel(
-    core, x_t, dkv, lhs, rhs, bsum, wt, g_keep, g_bias, g_above, g_upper, g_lower, g_below
+    rng, core, x_t, dkv, lhs, rhs, bsum, wt, g_keep, g_bias, g_above, g_upper, g_lower, g_below
 ):
-    weight_terms(g_keep, core[0], x_t, dkv, lhs, rhs)
+    weight_terms(g_keep, core[0], rng, x_t, dkv, lhs, rhs)
 
     spot = iota((512, 384), 0)
     place = iota((512, 384), 1)
@@ -260,47 +271,41 @@
 
 
 def pack_kernel(keep, came, bias, parcel):
-    count, rows, _ = parcel.shape
-    for a in range(rows // 8):
-        for r in range(count):
-            at = (a * count + r) * 8
-            both = keep[at : at + 8].astype(F32) + came[at : at + 8].astype(F32)
-            parcel[r, a * 8 : a * 8 + 8, 0:1024] = both.astype(BF16)
-    parcel[:, :, 1024:1152] = jnp.zeros((count, rows, 128), BF16)
-    for n in range(3):
-        part = bias[:, n * 128 : n * 128 + 128].astype(BF16)
-        for r in range(count):
-            parcel[r, n * 8 : n * 8 + 8, 1024:1152] = part
+    rows = parcel.shape[1] - 8
+    for r in range(parcel.shape[0] // 2):
+        at = slice(r * rows, r * rows + rows)
+        both = (keep[at].astype(F32) + came[at].astype(F32)).astype(BF16)
+        for side in range(2):
+            parcel[r * 2 + side, 0:rows] = both[:, side * 512 : side * 512 + 512]
+    low = bias[...].astype(BF16)
+    for n in range(parcel.shape[0]):
+        parcel[n, rows : rows + 8, 0:384] = low
+        parcel[n, rows : rows + 8, 384:512] = jnp.zeros((8, 128), BF16)
 
 
 def regroup_kernel(came, _, parcel):
-    count = parcel.shape[0]
-    for a in range(count):
-        rows = slice(a * 8, a * 8 + 8)
-        total = came[0, rows, 0:1024].astype(F32)
-        for r in range(1, came.shape[0]):
-            total += came[r, rows, 0:1024].astype(F32)
-        parcel[a, :, 0:1024] = total.astype(BF16)
-    for n in range(3):
-        rows = slice(n * 8, n * 8 + 8)
-        total = came[0, rows, 1024:1152].astype(F32)
-        for r in range(1, came.shape[0]):
-            total += came[r, rows, 1024:1152].astype(F32)
-        part = total.astype(BF16)
-        for a in range(count):
-            parcel[a, :, 1024 + n * 128 : 1152 + n * 128] = part
+    total = came[0].astype(F32)
+    for n in range(1, came.shape[0]):
+        total += came[n].astype(F32)
+    rows = came.shape[1] - 8
+    low = total.astype(BF16)
+    for a in range(parcel.shape[0] // 2):
+        for side in range(2):
+            parcel[a * 2 + side, 0:8] = low[a * 8 : a * 8 + 8]
+            parcel[a * 2 + side, 8:16] = low[rows : rows + 8]
 
 
 def total_kernel(came, mine):
-    total = came[0].astype(F32)
-    for a in range(1, came.shape[0]):
-        total += came[a].astype(F32)
-    mine[...] = total
-
-
-def finish_kernel(core, mine, near, other, far, qkv, out, bias):
-    here = mine[...] + near[...]
-    there = other[...] + far[...]
+    for side in range(2):
+        total = came[side].astype(F32)
+        for a in range(1, came.shape[0] // 2):
+            total += came[a * 2 + side].astype(F32)
+        mine[:, side * 512 : side * 512 + 512] = total[0:8]
+        if side == 0:
+            mine[:, 1024:1408] = total[8:16, 0:384]
+
+
+def finish_kernel(core, here, there, qkv, out, bias):
     is_first = core[0] == 0
     low = jnp.where(is_first, here[:, 0:1024], there[:, 0:1024])
     high = jnp.where(is_first, there[:, 0:1024], here[:, 0:1024])
@@ -330,7 +335,6 @@
         scratch_shapes=list(scratch),
         compiler_params=pltpu.CompilerParams(vmem_limit_bytes=limit * MIB),
         cost_estimate=pl.CostEstimate(flops=flops, bytes_accessed=size, transcendentals=0),
-        name=kernel.__name__,
     )(*operands)
 
 
@@ -348,8 +352,8 @@
         pairs = [(i, i + step) for i in range(rng) if 0 <= i + step < rng]
         return lax.ppermute(leaf, "rng", pairs)
 
-    def among(leaf, flip):
-        return lax.ppermute(leaf, "dp", [(i, i ^ flip) for i in range(4)])
+    def swap(leaf):
+        return lax.ppermute(leaf, "core", [(0, 1), (1, 0)])
 
     left = shift(cells[:, 8:], 1).reshape(128, width)
     right = shift(cells[:, :8], -1).reshape(128, width)
@@ -358,7 +362,7 @@
     above = turn(lower, 1)
     below = turn(upper, -1)
 
-    core = (lax.axis_index("dp") % 2).astype(jnp.int32)[None]
+    core = lax.axis_index("core").astype(jnp.int32)[None]
     at_range = lax.axis_index("rng")
     edge = jnp.stack([at_range == 0, at_range == rng - 1]).astype(jnp.int32)
     turned = qkv_weight.T
@@ -379,7 +383,7 @@
         middle_kernel, (upper, lower, turned), (whole((512, 512), BF16),) * 5, flops=1_000_000_000, limit=12
     )
     x_t, dkv, lhs, rhs, bsum, g_send = call(
-        attention_kernel,
+        functools.partial(attention_kernel, rng),
         (core, above, below, q, q_t, da, da_t, table, *middle, turned, cot),
         (
             whole((512, 1024), BF16), whole((1024, 1024), BF16),
@@ -395,9 +399,9 @@
         flops=10_000_000_000,
         limit=20,
     )
-    came = among(g_send, 1)
+    came = swap(g_send)
     g_keep, g_bias, g_above, g_upper, g_lower, g_below = call(
-        terms_kernel,
+        functools.partial(terms_kernel, rng),
         (core, x_t, dkv, lhs, rhs, bsum, turned),
         (
             whole((512, 1024), BF16), whole((8, 384), F32),
@@ -411,10 +415,10 @@
     (parcel,) = call(
         pack_kernel,
         (g_keep, came, g_bias),
-        (whole((rng, 8 * az, 1152), BF16),),
+        (whole((rng * 2, 8 * az + 8, 512), BF16),),
         flops=1_000_000,
     )
-    parcel = lax.all_to_all(parcel, "rng", 0, 0, tiled=True)
+    parcel = lax.all_to_all(parcel, ("rng", "half"), 0, 0, tiled=True)
 
     up = turn(g_below, 1)
     down = turn(g_above, -1)
@@ -435,17 +439,16 @@
 
     (parcel,) = call(
         regroup_kernel,
-        (parcel, grad_tokens),
-        (whole((az, 8, 1408), BF16),),
+        (parcel, g_own),
+        (whole((az * 2, 16, 512), BF16),),
         flops=1_000_000,
         untouched=1,
     )
-    parcel = lax.all_to_all(parcel, "az", 0, 0, tiled=True)
+    parcel = lax.all_to_all(parcel, ("az", "half"), 0, 0, tiled=True)
     (mine,) = call(total_kernel, (parcel,), (whole((8, 1408), F32),), flops=1_000_000)
-    near, other, far = among(mine, 2), among(mine, 1), among(mine, 3)
     rows_qkv, rows_out, total_bias = call(
         finish_kernel,
-        (core, mine, near, other, far),
+        (core, mine, swap(mine)),
         (whole((8, 1536), F32), whole((8, 512), F32), whole((17, 8, 17), F32)),
         prefetch=1,
         flops=1_000_000,
@@ -455,11 +458,14 @@
 
 
 def solution(mesh):
-    placed = (P("dp", "az", "rng", None), P(), P(), P(), P("dp", "az", "rng", None))
+    az, rng, dp = mesh.devices.shape
+    split = Mesh(mesh.devices.reshape(az, rng, dp // 2, 2), ("az", "rng", "half", "core"))
+    cells = P(("half", "core"), "az", "rng", None)
+    rows = P(("az", "rng"), None)
     return jax.shard_map(
         shards,
-        mesh=mesh,
-        in_specs=placed,
-        out_specs=(P("dp", "az", "rng", None), P(("az", "rng"), None), P(("az", "rng"), None), P()),
+        mesh=split,
+        in_specs=(cells, P(), P(), P(), cells),
+        out_specs=(cells, rows, rows, P()),
         check_vma=False,
     )

time: 90.7 us -> 89.9 us (level)
  the two profiles are of different devices: /device:TPU:6 before, /device:TPU:1 now
where the time goes in v5:
time: 89.9 us; the launch traced here: 89.4 us
  starting transfers between devices  41.1 us (46%)
  waiting for transfers between devices  24.3 us (27%)
  Pallas kernels  19.3 us (21%)
  local copies, waits for them, and re-layouts  3.71 us (4%)
    pallas_call x10, Pallas kernels, call(): pl.pallas_call(kernel, out_shape=tuple(outs), in_specs=[scalar] * prefetc...  19.3 us
    ppermute x4, starting transfers between devices, shift(): return lax.ppermute(leaf, 'rng', pairs)  10.5 us
    all_to_all x1, waiting for transfers between devices, shards(): parcel = lax.all_to_all(parcel, ('rng', 'half'), 0, 0, tiled=True)  10.2 us
    ppermute x4, starting transfers between devices, turn(): return lax.ppermute(leaf, 'az', [(i, (i + step) % az) for i in range(az)])  8.69 us
    all_to_all x1, starting transfers between devices, shards(): parcel = lax.all_to_all(parcel, ('rng', 'half'), 0, 0, tiled=True)  8.3 us
    all_to_all x1, starting transfers between devices, shards(): parcel = lax.all_to_all(parcel, ('az', 'half'), 0, 0, tiled=True)  8.03 us
    all_to_all x1, waiting for transfers between devices, shards(): parcel = lax.all_to_all(parcel, ('az', 'half'), 0, 0, tiled=True)  6.55 us
    ppermute x4, waiting for transfers between devices, turn(): return lax.ppermute(leaf, 'az', [(i, (i + step) % az) for i in range(az)])  5.84 us
  transfers between devices with their start and end apart: 12, of which 5 were waited for; matrix products, arithmetic and copies ran while one was open for 3% of the time, Pallas kernels for 8%

profile of v5, /device:TPU:1, one launch (start us, length us, event | category | flops | bytes accessed | tf_op | source)
XLA Modules:
  0.0 89.4 jit_solution(7674438890425599499)
XLA Ops:
  0.6 1.0 %fusion.1 = (bf16[16,8,512]{2,1,0:T(8,128)(2,1)S(1)}, bf16[16,8,512]{2,1,0:T(8,128)(2,1)S(1)}) fusion(bf16[16,16,512]{2,1,0:T(8,128)(2,1)} %bitcast.26), kind=kLoop, calls=%fused_computation.8 | loop fusion | bytes 524288 | tf_op jit(solution)/shard_map/slice | solution.py:358
  1.6 3.9 %collective-permute-start = (bf16[16,8,512]{2,1,0:T(8,128)(2,1)S(1)}, bf16[16,8,512]{2,1,0:T(8,128)(2,1)S(1)}, u32[]{:S(2)}, u32[]{:S(2)}) collective-permute-start(bf16[16,8,512]{2,1,0:T(8,128)(2,1)S(1)} %get-tuple-element.62), channel_id=1, source_target_pairs={{0,4},{4,8},{8,12},{12,16},{16,20},{20,24},{24,28},{1,5},{5,9},{9,... | collective-permute-start | bytes 393224 | tf_op jit(solution)/shard_map/ppermute | solution.py:353
  5.6 1.3 %collective-permute-start.1 = (bf16[16,8,512]{2,1,0:T(8,128)(2,1)S(1)}, bf16[16,8,512]{2,1,0:T(8,128)(2,1)S(1)}, u32[]{:S(2)}, u32[]{:S(2)}) collective-permute-start(bf16[16,8,512]{2,1,0:T(8,128)(2,1)S(1)} %get-tuple-element.63), channel_id=1, source_target_pairs={{4,0},{8,4},{12,8},{16,12},{20,16},{24,20},{28,24},{5,1},{9,5},{13... | collective-permute-start | bytes 393224 | tf_op jit(solution)/shard_map/ppermute | solution.py:353
  6.9 0.9 %copy.10.bias = f32[8,17,17]{2,1,0:T(8,128)S(1)} copy(f32[8,17,17]{2,0,1:T(8,128)} %param.8) | data formatting | bytes 18496 | tf_op args[3]
  7.8 0.0 copy-start
  7.8 1.8 %copy.9 = bf16[512,1536]{0,1:T(8,128)(2,1)S(1)} copy(bf16[512,1536]{1,0:T(8,128)(2,1)} %param.6) | data formatting | bytes 3145728 | tf_op args[1]
  9.6 0.0 copy-done
  9.6 0.0 copy-start.1
  9.6 0.0 copy-start.2
  9.6 0.0 collective-permute-done
  9.7 1.6 %collective-permute-done.1 = bf16[16,8,512]{2,1,0:T(8,128)(2,1)S(1)} collective-permute-done((bf16[16,8,512]{2,1,0:T(8,128)(2,1)S(1)}, bf16[16,8,512]{2,1,0:T(8,128)(2,1)S(1)}, u32[]{:S(2)}, u32[]{:S(2)}) %collective-permute-start.1) | collective-permute-done | bytes 131104 | tf_op jit(solution)/shard_map/ppermute | solution.py:353
  11.3 1.7 %collective-permute-start.2 = (bf16[256,512]{1,0:T(8,128)(2,1)S(1)}, bf16[256,512]{1,0:T(8,128)(2,1)S(1)}, u32[]{:S(2)}, u32[]{:S(2)}) collective-permute-start(bf16[256,512]{1,0:T(8,128)(2,1)S(1)} %pad_maximum_fusion.lower), channel_id=1, source_target_pairs={{0,32},{32,64},{64,96},{96,128},{128,160},{160,192},{192,224},{224... | collective-permute-start | bytes 786440 | tf_op jit(solution)/shard_map/ppermute | solution.py:349
  13.1 4.0 %collective-permute-start.3 = (bf16[256,512]{1,0:T(8,128)(2,1)S(1)}, bf16[256,512]{1,0:T(8,128)(2,1)S(1)}, u32[]{:S(2)}, u32[]{:S(2)}) collective-permute-start(bf16[256,512]{1,0:T(8,128)(2,1)S(1)} %pad_maximum_fusion.1.upper), channel_id=1, source_target_pairs={{0,224},{32,0},{64,32},{96,64},{128,96},{160,128},{192,160},{224,1... | collective-permute-start | bytes 786440 | tf_op jit(solution)/shard_map/ppermute | solution.py:349
  17.1 0.1 add_convert_fusion.edge
  17.2 0.0 copy-done.1
  17.2 0.0 copy-done.2
  17.2 3.6 %shard_map.84 = (bf16[256,512]{1,0:T(8,128)(2,1)S(1)}, bf16[512,256]{1,0:T(8,128)(2,1)S(1)}, bf16[256,512]{1,0:T(8,128)(2,1)S(1)}, bf16[512,256]{1,0:T(8,128)(2,1)S(1)}, f32[4,768,256]{2,1,0:T(8,128)S(1)}) custom-call(s32[2]{0:T(128)S(1)} %add_convert_fusion.edge, bf16[256,512]{1,0:T(8,128)(2,1)S(1)} %bitcast.27, bf16[256,512]{1,0:T(8,128)(2,1)S(1)} %bitcast.29, ...), custom_call_target="tpu_custom_call" | custom-call | flops 600000000 | bytes 6825000 | tf_op jit(solution)/shard_map/pallas_call | solution.py:328
  20.7 0.8 shard_map.85
  21.6 0.0 collective-permute-done.2.above
  21.6 0.0 collective-permute-done.3.below
  21.6 8.9 %shard_map.86 = (bf16[512,1024]{1,0:T(8,128)(2,1)S(1)}, bf16[1024,1024]{1,0:T(8,128)(2,1)S(1)}, bf16[2,512,256]{2,1,0:T(8,128)(2,1)S(1)}, bf16[2,256,512]{2,1,0:...) custom-call(s32[1]{0:T(128)} %bitcast.core, ...), custom_call_target="tpu_custom_call" | custom-call | flops 10000000000 | bytes 14680068 | tf_op jit(solution)/shard_map/pallas_call | solution.py:328
  30.5 2.7 %collective-permute-start.8 = (bf16[512,1024]{1,0:T(8,128)(2,1)S(1)}, bf16[512,1024]{1,0:T(8,128)(2,1)S(1)}, u32[]{:S(2)}, u32[]{:S(2)}) collective-permute-start(bf16[512,1024]{1,0:T(8,128)(2,1)S(1)} %get-tuple-element.55), channel_id=1, source_target_pairs={{0,1},{1,0},{2,3},{3,2},{4,5},{5,4},{6,7},{7,6},{8,9},{9,8},{10,11... | collective-permute-start | bytes 3145736 | tf_op jit(solution)/shard_map/ppermute | solution.py:356
  33.2 2.3 %shard_map.87 = (bf16[512,1024]{1,0:T(8,128)(2,1)S(1)}, f32[8,384]{1,0:T(8,128)S(1)}, bf16[256,512]{1,0:T(8,128)(2,1)S(1)}, f32[256,512]{1,0:T(8,128)S(1)}, f32[...) custom-call(s32[1]{0:T(128)} %bitcast.core, bf16[512,1024]{1,0:T(8,128)(2,1)S(1)} %get-tuple-element.42.x_t, ...), custom_call_target="tpu_custom_call" | custom-call | flops 2500000000 | bytes 8663044 | tf_op jit(solution)/shard_map/pallas_call | solution.py:328
  35.5 0.0 collective-permute-done.8.came
  35.5 1.3 %shard_map.90 = bf16[16,72,512]{2,1,0:T(8,128)(2,1)} custom-call(bf16[512,1024]{1,0:T(8,128)(2,1)S(1)} %get-tuple-element.54.keep, bf16[512,1024]{1,0:T(8,128)(2,1)S(1)} %collective-permute-done.8.came, f32[8,384]{1,0:T(8,128)S(1)} %get-tuple-element.56.bias), custom_call_target="tpu_custom_call" | custom-call | flops 1000000 | bytes 3289088 | tf_op jit(solution)/shard_map/pallas_call | solution.py:328
  36.8 8.3 %all-to-all-start = ((bf16[16,72,512]{2,1,0:T(8,128)(2,1)}), bf16[16,72,512]{2,1,0:T(8,128)(2,1)S(1)}, u32[]{:S(2)}, u32[]{:S(2)}) async-start(bf16[16,72,512]{2,1,0:T(8,128)(2,1)} %shard_map.90), calls=%async_computation | async-start | bytes 2359296 | tf_op jit(solution)/shard_map/all_to_all | solution.py:421
  45.1 0.1 collective-permute-start.4
  45.2 2.9 %collective-permute-start.5 = (bf16[256,512]{1,0:T(8,128)(2,1)S(1)}, bf16[256,512]{1,0:T(8,128)(2,1)S(1)}, u32[]{:S(2)}, u32[]{:S(2)}) collective-permute-start(bf16[256,512]{1,0:T(8,128)(2,1)S(1)} %get-tuple-element.50), channel_id=1, source_target_pairs={{0,224},{32,0},{64,32},{96,64},{128,96},{160,128},{192,160},{224,1... | collective-permute-start | bytes 786440 | tf_op jit(solution)/shard_map/ppermute | solution.py:349
  48.1 5.8 %collective-permute-done.4.up = bf16[256,512]{1,0:T(8,128)(2,1)S(1)} collective-permute-done((bf16[256,512]{1,0:T(8,128)(2,1)S(1)}, bf16[256,512]{1,0:T(8,128)(2,1)S(1)}, u32[]{:S(2)}, u32[]{:S(2)}) %collective-permute-start.4) | collective-permute-done | bytes 262176 | tf_op jit(solution)/shard_map/ppermute | solution.py:349
  53.9 0.0 collective-permute-done.5.down
  53.9 0.1 shard_map.88
  54.0 10.2 %all-to-all-done.came = bf16[16,72,512]{2,1,0:T(8,128)(2,1)S(1)} async-done(((bf16[16,72,512]{2,1,0:T(8,128)(2,1)}), bf16[16,72,512]{2,1,0:T(8,128)(2,1)S(1)}, u32[]{:S(2)}, u32[]{:S(2)}) %all-to-all-start) | async-done | bytes 1179680 | tf_op jit(solution)/shard_map/all_to_all | solution.py:421
  64.2 0.9 shard_map.91
  65.1 8.0 %all-to-all-start.1 = ((bf16[16,16,512]{2,1,0:T(8,128)(2,1)}), bf16[16,16,512]{2,1,0:T(8,128)(2,1)S(1)}, u32[]{:S(2)}, u32[]{:S(2)}) async-start(bf16[16,16,512]{2,1,0:T(8,128)(2,1)} %shard_map.91), calls=%async_computation.1 | async-start | bytes 524288 | tf_op jit(solution)/shard_map/all_to_all | solution.py:447
  73.1 1.3 %collective-permute-start.7 = (bf16[16,8,512]{2,1,0:T(8,128)(2,1)S(1)}, bf16[16,8,512]{2,1,0:T(8,128)(2,1)S(1)}, u32[]{:S(2)}, u32[]{:S(2)}) collective-permute-start(bf16[16,8,512]{2,1,0:T(8,128)(2,1)S(1)} %bitcast.32), channel_id=1, source_target_pairs={{4,0},{8,4},{12,8},{16,12},{20,16},{24,20},{28,24},{5,1},{9,5},{13... | collective-permute-start | bytes 393224 | tf_op jit(solution)/shard_map/ppermute | solution.py:353
  74.4 4.0 %collective-permute-start.6 = (bf16[16,8,512]{2,1,0:T(8,128)(2,1)S(1)}, bf16[16,8,512]{2,1,0:T(8,128)(2,1)S(1)}, u32[]{:S(2)}, u32[]{:S(2)}) collective-permute-start(bf16[16,8,512]{2,1,0:T(8,128)(2,1)S(1)} %bitcast.31), channel_id=1, source_target_pairs={{0,4},{4,8},{8,12},{12,16},{16,20},{20,24},{24,28},{1,5},{5,9},{9,... | collective-permute-start | bytes 393224 | tf_op jit(solution)/shard_map/ppermute | solution.py:353
  78.4 6.5 %all-to-all-done.1.came = bf16[16,16,512]{2,1,0:T(8,128)(2,1)S(1)} async-done(((bf16[16,16,512]{2,1,0:T(8,128)(2,1)}), bf16[16,16,512]{2,1,0:T(8,128)(2,1)S(1)}, u32[]{:S(2)}, u32[]{:S(2)}) %all-to-all-start.1) | async-done | bytes 262176 | tf_op jit(solution)/shard_map/all_to_all | solution.py:447
  85.0 2.8 %collective-permute-start.9 = (f32[8,1408]{1,0:T(8,128)S(1)}, f32[8,1408]{1,0:T(8,128)S(1)}, u32[]{:S(2)}, u32[]{:S(2)}) collective-permute-start(f32[8,1408]{1,0:T(8,128)S(1)} %shard_map.92.here), channel_id=1, source_target_pairs={{0,1},{1,0},{2,3},{3,2},{4,5},{5,4},{6,7},{7,6},{8,9},{9,8},{10,11... | collective-permute-start | bytes 135176 | tf_op jit(solution)/shard_map/ppermute | solution.py:356
  87.8 0.0 collective-permute-done.7.east
  87.8 0.0 collective-permute-done.6.west
  87.8 0.7 shard_map.89
  88.6 0.1 collective-permute-done.9.there
  88.7 0.7 shard_map.93
  (6 shorter events, 0.1 us)
Async XLA Ops:
  1.6 8.0 %collective-permute-start = (bf16[16,8,512]{2,1,0:T(8,128)(2,1)S(1)}, bf16[16,8,512]{2,1,0:T(8,128)(2,1)S(1)}, u32[]{:S(2)}, u32[]{:S(2)}) collective-permute-start(bf16[16,8,512]{2,1,0:T(8,128)(2,1)S(1)} %get-tuple-element.62), channel_id=1, source_target_pairs={{0,4},{4,8},{8,12},{12,16},{16,20},{20,24},{24,28},{1,5},{5,9},{9,... | collective-permute-start | bytes 393224 | tf_op jit(solution)/shard_map/ppermute | solution.py:353
  5.6 5.7 %collective-permute-start.1 = (bf16[16,8,512]{2,1,0:T(8,128)(2,1)S(1)}, bf16[16,8,512]{2,1,0:T(8,128)(2,1)S(1)}, u32[]{:S(2)}, u32[]{:S(2)}) collective-permute-start(bf16[16,8,512]{2,1,0:T(8,128)(2,1)S(1)} %get-tuple-element.63), channel_id=1, source_target_pairs={{4,0},{8,4},{12,8},{16,12},{20,16},{24,20},{28,24},{5,1},{9,5},{13... | collective-permute-start | bytes 393224 | tf_op jit(solution)/shard_map/ppermute | solution.py:353
  7.8 1.8 %copy-start = (bf16[1,16,16,512]{3,2,1,0:T(8,128)(2,1)S(1)}, bf16[1,16,16,512]{3,2,1,0:T(8,128)(2,1)}, u32[]{:S(2)}) copy-start(bf16[1,16,16,512]{3,2,1,0:T(8,128)(2,1)} %param.5) | copy-start | bytes 786436
  9.6 7.6 %copy-start.1 = (bf16[512,512]{1,0:T(8,128)(2,1)S(1)}, bf16[512,512]{1,0:T(8,128)(2,1)}, u32[]{:S(2)}) copy-start(bf16[512,512]{1,0:T(8,128)(2,1)} %wo.1) | copy-start | bytes 1572868
  9.6 7.6 %copy-start.2 = (bf16[1,16,16,512]{3,2,1,0:T(8,128)(2,1)S(1)}, bf16[1,16,16,512]{3,2,1,0:T(8,128)(2,1)}, u32[]{:S(2)}) copy-start(bf16[1,16,16,512]{3,2,1,0:T(8,128)(2,1)} %param.9) | copy-start | bytes 786436
  11.3 10.3 %collective-permute-start.2 = (bf16[256,512]{1,0:T(8,128)(2,1)S(1)}, bf16[256,512]{1,0:T(8,128)(2,1)S(1)}, u32[]{:S(2)}, u32[]{:S(2)}) collective-permute-start(bf16[256,512]{1,0:T(8,128)(2,1)S(1)} %pad_maximum_fusion.lower), channel_id=1, source_target_pairs={{0,32},{32,64},{64,96},{96,128},{128,160},{160,192},{192,224},{224... | collective-permute-start | bytes 786440 | tf_op jit(solution)/shard_map/ppermute | solution.py:349
  13.1 8.5 %collective-permute-start.3 = (bf16[256,512]{1,0:T(8,128)(2,1)S(1)}, bf16[256,512]{1,0:T(8,128)(2,1)S(1)}, u32[]{:S(2)}, u32[]{:S(2)}) collective-permute-start(bf16[256,512]{1,0:T(8,128)(2,1)S(1)} %pad_maximum_fusion.1.upper), channel_id=1, source_target_pairs={{0,224},{32,0},{64,32},{96,64},{128,96},{160,128},{192,160},{224,1... | collective-permute-start | bytes 786440 | tf_op jit(solution)/shard_map/ppermute | solution.py:349
  30.5 5.1 %collective-permute-start.8 = (bf16[512,1024]{1,0:T(8,128)(2,1)S(1)}, bf16[512,1024]{1,0:T(8,128)(2,1)S(1)}, u32[]{:S(2)}, u32[]{:S(2)}) collective-permute-start(bf16[512,1024]{1,0:T(8,128)(2,1)S(1)} %get-tuple-element.55), channel_id=1, source_target_pairs={{0,1},{1,0},{2,3},{3,2},{4,5},{5,4},{6,7},{7,6},{8,9},{9,8},{10,11... | collective-permute-start | bytes 3145736 | tf_op jit(solution)/shard_map/ppermute | solution.py:356
  36.8 27.4 %all-to-all-start = ((bf16[16,72,512]{2,1,0:T(8,128)(2,1)}), bf16[16,72,512]{2,1,0:T(8,128)(2,1)S(1)}, u32[]{:S(2)}, u32[]{:S(2)}) async-start(bf16[16,72,512]{2,1,0:T(8,128)(2,1)} %shard_map.90), calls=%async_computation | async-start | bytes 2359296 | tf_op jit(solution)/shard_map/all_to_all | solution.py:421
  45.1 8.8 %collective-permute-start.4 = (bf16[256,512]{1,0:T(8,128)(2,1)S(1)}, bf16[256,512]{1,0:T(8,128)(2,1)S(1)}, u32[]{:S(2)}, u32[]{:S(2)}) collective-permute-start(bf16[256,512]{1,0:T(8,128)(2,1)S(1)} %get-tuple-element.49), channel_id=1, source_target_pairs={{0,32},{32,64},{64,96},{96,128},{128,160},{160,192},{192,224},{224... | collective-permute-start | bytes 786440 | tf_op jit(solution)/shard_map/ppermute | solution.py:349
  45.2 8.7 %collective-permute-start.5 = (bf16[256,512]{1,0:T(8,128)(2,1)S(1)}, bf16[256,512]{1,0:T(8,128)(2,1)S(1)}, u32[]{:S(2)}, u32[]{:S(2)}) collective-permute-start(bf16[256,512]{1,0:T(8,128)(2,1)S(1)} %get-tuple-element.50), channel_id=1, source_target_pairs={{0,224},{32,0},{64,32},{96,64},{128,96},{160,128},{192,160},{224,1... | collective-permute-start | bytes 786440 | tf_op jit(solution)/shard_map/ppermute | solution.py:349
  65.1 19.9 %all-to-all-start.1 = ((bf16[16,16,512]{2,1,0:T(8,128)(2,1)}), bf16[16,16,512]{2,1,0:T(8,128)(2,1)S(1)}, u32[]{:S(2)}, u32[]{:S(2)}) async-start(bf16[16,16,512]{2,1,0:T(8,128)(2,1)} %shard_map.91), calls=%async_computation.1 | async-start | bytes 524288 | tf_op jit(solution)/shard_map/all_to_all | solution.py:447
  73.1 14.7 %collective-permute-start.7 = (bf16[16,8,512]{2,1,0:T(8,128)(2,1)S(1)}, bf16[16,8,512]{2,1,0:T(8,128)(2,1)S(1)}, u32[]{:S(2)}, u32[]{:S(2)}) collective-permute-start(bf16[16,8,512]{2,1,0:T(8,128)(2,1)S(1)} %bitcast.32), channel_id=1, source_target_pairs={{4,0},{8,4},{12,8},{16,12},{20,16},{24,20},{28,24},{5,1},{9,5},{13... | collective-permute-start | bytes 393224 | tf_op jit(solution)/shard_map/ppermute | solution.py:353
  74.4 13.4 %collective-permute-start.6 = (bf16[16,8,512]{2,1,0:T(8,128)(2,1)S(1)}, bf16[16,8,512]{2,1,0:T(8,128)(2,1)S(1)}, u32[]{:S(2)}, u32[]{:S(2)}) collective-permute-start(bf16[16,8,512]{2,1,0:T(8,128)(2,1)S(1)} %bitcast.31), channel_id=1, source_target_pairs={{0,4},{4,8},{8,12},{12,16},{16,20},{20,24},{24,28},{1,5},{5,9},{9,... | collective-permute-start | bytes 393224 | tf_op jit(solution)/shard_map/ppermute | solution.py:353
  85.0 3.7 %collective-permute-start.9 = (f32[8,1408]{1,0:T(8,128)S(1)}, f32[8,1408]{1,0:T(8,128)S(1)}, u32[]{:S(2)}, u32[]{:S(2)}) collective-permute-start(f32[8,1408]{1,0:T(8,128)S(1)} %shard_map.92.here), channel_id=1, source_target_pairs={{0,1},{1,0},{2,3},{3,2},{4,5},{5,4},{6,7},{7,6},{8,9},{9,8},{10,11... | collective-permute-start | bytes 135176 | tf_op jit(solution)/shard_map/ppermute | solution.py:356

commit v6 on v5

--- a/solution.py
+++ b/solution.py
@@ -6,7 +6,6 @@
 from jax.experimental import pallas as pl
 from jax.experimental.pallas import tpu as pltpu
 from jax.sharding import Mesh, PartitionSpec as P
-
 
 F32 = jnp.float32
 BF16 = jnp.bfloat16
@@ -272,15 +271,12 @@
 
 def pack_kernel(keep, came, bias, parcel):
     rows = parcel.shape[1] - 8
-    for r in range(parcel.shape[0] // 2):
+    low = bias[...].astype(BF16)
+    for r in range(parcel.shape[0]):
         at = slice(r * rows, r * rows + rows)
-        both = (keep[at].astype(F32) + came[at].astype(F32)).astype(BF16)
-        for side in range(2):
-            parcel[r * 2 + side, 0:rows] = both[:, side * 512 : side * 512 + 512]
-    low = bias[...].astype(BF16)
-    for n in range(parcel.shape[0]):
-        parcel[n, rows : rows + 8, 0:384] = low
-        parcel[n, rows : rows + 8, 384:512] = jnp.zeros((8, 128), BF16)
+        parcel[r, 0:rows] = (keep[at].astype(F32) + came[at].astype(F32)).astype(BF16)
+        parcel[r, rows : rows + 8, 0:384] = low
+        parcel[r, rows : rows + 8, 384:1024] = jnp.zeros((8, 640), BF16)
 
 
 def regroup_kernel(came, _, parcel):
@@ -289,20 +285,20 @@
         total += came[n].astype(F32)
     rows = came.shape[1] - 8
     low = total.astype(BF16)
-    for a in range(parcel.shape[0] // 2):
-        for side in range(2):
-            parcel[a * 2 + side, 0:8] = low[a * 8 : a * 8 + 8]
-            parcel[a * 2 + side, 8:16] = low[rows : rows + 8]
+    for a in range(parcel.shape[0]):
+        parcel[a, :, 0:1024] = low[a * 8 : a * 8 + 8]
+        parcel[a, :, 1024:1408] = low[rows : rows + 8, 0:384]
 
 
 def total_kernel(came, mine):
-    for side in range(2):
-        total = came[side].astype(F32)
-        for a in range(1, came.shape[0] // 2):
-            total += came[a * 2 + side].astype(F32)
-        mine[:, side * 512 : side * 512 + 512] = total[0:8]
-        if side == 0:
-            mine[:, 1024:1408] = total[8:16, 0:384]
+    total = came[0].astype(F32)
+    for a in range(1, came.shape[0]):
+        total += came[a].astype(F32)
+    mine[...] = total
+
+
+def add_kernel(mine, came, both):
+    both[...] = mine[...] + came[...]
 
 
 def finish_kernel(core, here, there, qkv, out, bias):
@@ -335,6 +331,7 @@
         scratch_shapes=list(scratch),
         compiler_params=pltpu.CompilerParams(vmem_limit_bytes=limit * MIB),
         cost_estimate=pl.CostEstimate(flops=flops, bytes_accessed=size, transcendentals=0),
+        name=getattr(kernel, "func", kernel).__name__,
     )(*operands)
 
 
@@ -352,8 +349,8 @@
         pairs = [(i, i + step) for i in range(rng) if 0 <= i + step < rng]
         return lax.ppermute(leaf, "rng", pairs)
 
-    def swap(leaf):
-        return lax.ppermute(leaf, "core", [(0, 1), (1, 0)])
+    def swap(leaf, axis="core"):
+        return lax.ppermute(leaf, axis, [(0, 1), (1, 0)])
 
     left = shift(cells[:, 8:], 1).reshape(128, width)
     right = shift(cells[:, :8], -1).reshape(128, width)
@@ -415,10 +412,10 @@
     (parcel,) = call(
         pack_kernel,
         (g_keep, came, g_bias),
-        (whole((rng * 2, 8 * az + 8, 512), BF16),),
+        (whole((rng, 8 * az + 8, 1024), BF16),),
         flops=1_000_000,
     )
-    parcel = lax.all_to_all(parcel, ("rng", "half"), 0, 0, tiled=True)
+    parcel = lax.all_to_all(parcel, "rng", 0, 0, tiled=True)
 
     up = turn(g_below, 1)
     down = turn(g_above, -1)
@@ -440,12 +437,15 @@
     (parcel,) = call(
         regroup_kernel,
         (parcel, g_own),
-        (whole((az * 2, 16, 512), BF16),),
+        (whole((az, 8, 1408), BF16),),
         flops=1_000_000,
         untouched=1,
     )
-    parcel = lax.all_to_all(parcel, ("az", "half"), 0, 0, tiled=True)
+    parcel = lax.all_to_all(parcel, "az", 0, 0, tiled=True)
     (mine,) = call(total_kernel, (parcel,), (whole((8, 1408), F32),), flops=1_000_000)
+    (mine,) = call(
+        add_kernel, (mine, swap(mine, "half")), (whole((8, 1408), F32),), flops=1_000_000
+    )
     rows_qkv, rows_out, total_bias = call(
         finish_kernel,
         (core, mine, swap(mine)),

time: 89.9 us -> 85.3 us (0.949)
  starting transfers between devices: 41.1 us -> 38.4 us
  waiting for transfers between devices: 24.3 us -> 22.6 us
    all_to_all x2, waiting for transfers between devices: 16.7 us -> 11.6 us  [the longest x1 8.46 us: shards(): parcel = lax.all_to_all(parcel, 'rng', 0, 0, tiled=True)]
    all_to_all x2, starting transfers between devices: 16.3 us -> 11.6 us  [the longest x1 5.86 us: shards(): parcel = lax.all_to_all(parcel, 'rng', 0, 0, tiled=True)]
    ppermute x2 -> x3, waiting for transfers between devices: 0.12 us -> 3.46 us  [swap(): return lax.ppermute(leaf, axis, [(0, 1), (1, 0)])]
    ppermute x2 -> x3, starting transfers between devices: 5.55 us -> 7.71 us  [swap(): return lax.ppermute(leaf, axis, [(0, 1), (1, 0)])]
    pallas_call x10 -> x11, Pallas kernels: 19.3 us -> 19.3 us  [call(): pl.pallas_call(kernel, out_shape=tuple(outs), in_specs=[scalar] * prefetc...]
  transfers between devices with their start and end apart: 12 -> 13, of which waited for: 5 -> 6; matrix products, arithmetic and copies ran while one was open for 3% -> 3% of each run, Pallas kernels for 8% -> 9%
where the time goes in v6:
time: 85.3 us; the launch traced here: 84.9 us
  starting transfers between devices  38.4 us (45%)
  waiting for transfers between devices  22.6 us (26%)
  Pallas kernels  19.3 us (23%)
  local copies, waits for them, and re-layouts  3.71 us (4%)
    pallas_call x11, Pallas kernels, call(): pl.pallas_call(kernel, out_shape=tuple(outs), in_specs=[scalar] * prefetc...  19.3 us
    ppermute x4, starting transfers between devices, shift(): return lax.ppermute(leaf, 'rng', pairs)  10.5 us
    ppermute x4, starting transfers between devices, turn(): return lax.ppermute(leaf, 'az', [(i, (i + step) % az) for i in range(az)])  8.62 us
    all_to_all x1, waiting for transfers between devices, shards(): parcel = lax.all_to_all(parcel, 'rng', 0, 0, tiled=True)  8.46 us
    ppermute x3, starting transfers between devices, swap(): return lax.ppermute(leaf, axis, [(0, 1), (1, 0)])  7.71 us
    all_to_all x1, starting transfers between devices, shards(): parcel = lax.all_to_all(parcel, 'rng', 0, 0, tiled=True)  5.86 us
    ppermute x4, waiting for transfers between devices, turn(): return lax.ppermute(leaf, 'az', [(i, (i + step) % az) for i in range(az)])  5.85 us
    all_to_all x1, starting transfers between devices, shards(): parcel = lax.all_to_all(parcel, 'az', 0, 0, tiled=True)  5.7 us
  transfers between devices with their start and end apart: 13, of which 6 were waited for; matrix products, arithmetic and copies ran while one was open for 3% of the time, Pallas kernels for 9%

profile of v6, /device:TPU:1, one launch (start us, length us, event | category | flops | bytes accessed | tf_op | source)
XLA Modules:
  0.0 84.9 jit_solution(2542128048987682545)
XLA Ops:
  0.6 1.0 %fusion.1 = (bf16[16,8,512]{2,1,0:T(8,128)(2,1)S(1)}, bf16[16,8,512]{2,1,0:T(8,128)(2,1)S(1)}) fusion(bf16[16,16,512]{2,1,0:T(8,128)(2,1)} %bitcast.26), kind=kLoop, calls=%fused_computation.8 | loop fusion | bytes 524288 | tf_op jit(solution)/shard_map/slice | solution.py:355
  1.6 3.9 %collective-permute-start = (bf16[16,8,512]{2,1,0:T(8,128)(2,1)S(1)}, bf16[16,8,512]{2,1,0:T(8,128)(2,1)S(1)}, u32[]{:S(2)}, u32[]{:S(2)}) collective-permute-start(bf16[16,8,512]{2,1,0:T(8,128)(2,1)S(1)} %get-tuple-element.62), channel_id=1, source_target_pairs={{0,4},{4,8},{8,12},{12,16},{16,20},{20,24},{24,28},{1,5},{5,9},{9,... | collective-permute-start | bytes 393224 | tf_op jit(solution)/shard_map/ppermute | solution.py:350
  5.6 1.3 %collective-permute-start.1 = (bf16[16,8,512]{2,1,0:T(8,128)(2,1)S(1)}, bf16[16,8,512]{2,1,0:T(8,128)(2,1)S(1)}, u32[]{:S(2)}, u32[]{:S(2)}) collective-permute-start(bf16[16,8,512]{2,1,0:T(8,128)(2,1)S(1)} %get-tuple-element.63), channel_id=1, source_target_pairs={{4,0},{8,4},{12,8},{16,12},{20,16},{24,20},{28,24},{5,1},{9,5},{13... | collective-permute-start | bytes 393224 | tf_op jit(solution)/shard_map/ppermute | solution.py:350
  6.9 0.9 %copy.10.bias = f32[8,17,17]{2,1,0:T(8,128)S(1)} copy(f32[8,17,17]{2,0,1:T(8,128)} %param.8) | data formatting | bytes 18496 | tf_op args[3]
  7.8 0.0 copy-start
  7.8 1.8 %copy.9 = bf16[512,1536]{0,1:T(8,128)(2,1)S(1)} copy(bf16[512,1536]{1,0:T(8,128)(2,1)} %param.6) | data formatting | bytes 3145728 | tf_op args[1]
  9.6 0.0 copy-done
  9.6 0.0 copy-start.1
  9.6 0.0 copy-start.2
  9.6 0.0 collective-permute-done
  9.7 1.6 %collective-permute-done.1 = bf16[16,8,512]{2,1,0:T(8,128)(2,1)S(1)} collective-permute-done((bf16[16,8,512]{2,1,0:T(8,128)(2,1)S(1)}, bf16[16,8,512]{2,1,0:T(8,128)(2,1)S(1)}, u32[]{:S(2)}, u32[]{:S(2)}) %collective-permute-start.1) | collective-permute-done | bytes 131104 | tf_op jit(solution)/shard_map/ppermute | solution.py:350
  11.3 1.7 %collective-permute-start.2 = (bf16[256,512]{1,0:T(8,128)(2,1)S(1)}, bf16[256,512]{1,0:T(8,128)(2,1)S(1)}, u32[]{:S(2)}, u32[]{:S(2)}) collective-permute-start(bf16[256,512]{1,0:T(8,128)(2,1)S(1)} %pad_maximum_fusion.lower), channel_id=1, source_target_pairs={{0,32},{32,64},{64,96},{96,128},{128,160},{160,192},{192,224},{224... | collective-permute-start | bytes 786440 | tf_op jit(solution)/shard_map/ppermute | solution.py:346
  13.1 4.0 %collective-permute-start.3 = (bf16[256,512]{1,0:T(8,128)(2,1)S(1)}, bf16[256,512]{1,0:T(8,128)(2,1)S(1)}, u32[]{:S(2)}, u32[]{:S(2)}) collective-permute-start(bf16[256,512]{1,0:T(8,128)(2,1)S(1)} %pad_maximum_fusion.1.upper), channel_id=1, source_target_pairs={{0,224},{32,0},{64,32},{96,64},{128,96},{160,128},{192,160},{224,1... | collective-permute-start | bytes 786440 | tf_op jit(solution)/shard_map/ppermute | solution.py:346
  17.1 0.1 add_convert_fusion.edge
  17.2 0.0 copy-done.1
  17.2 0.0 copy-done.2
  17.2 3.6 %before_kernel.1 = (bf16[256,512]{1,0:T(8,128)(2,1)S(1)}, bf16[512,256]{1,0:T(8,128)(2,1)S(1)}, bf16[256,512]{1,0:T(8,128)(2,1)S(1)}, bf16[512,256]{1,0:T(8,128)(2,1)S(1)}, f32[4,768,256]{2,1,0:T(8,128)S(1)}) custom-call(s32[2]{0:T(128)S(1)} %add_convert_fusion.edge, bf16[256,512]{1,0:T(8,128)(2,1)S(1)} %bitcast.27, bf16[256,512]{1,0:T(8,128)(2,1)S(1)} %bitcast.29, ...), custom_call_target="tpu_custom_call" | custom-call | flops 600000000 | bytes 6825000 | tf_op jit(solution)/shard_map/before_kernel/pallas_call | solution.py:324
  20.7 0.8 middle_kernel.1
  21.6 0.0 collective-permute-done.2.above
  21.6 0.0 collective-permute-done.3.below
  21.6 8.9 %attention_kernel.1 = (bf16[512,1024]{1,0:T(8,128)(2,1)S(1)}, bf16[1024,1024]{1,0:T(8,128)(2,1)S(1)}, bf16[2,512,256]{2,1,0:T(8,128)(2,1)S(1)}, bf16[2,256,512]{...) custom-call(s32[1]{0:T(128)} %bitcast.core, ...), custom_call_target="tpu_custom_call" | custom-call | flops 10000000000 | bytes 14680068 | tf_op jit(solution)/shard_map/attention_kernel/pallas_call | solution.py:324
  30.5 2.7 %collective-permute-start.8 = (bf16[512,1024]{1,0:T(8,128)(2,1)S(1)}, bf16[512,1024]{1,0:T(8,128)(2,1)S(1)}, u32[]{:S(2)}, u32[]{:S(2)}) collective-permute-start(bf16[512,1024]{1,0:T(8,128)(2,1)S(1)} %get-tuple-element.55), channel_id=1, source_target_pairs={{0,1},{1,0},{2,3},{3,2},{4,5},{5,4},{6,7},{7,6},{8,9},{9,8},{10,11... | collective-permute-start | bytes 3145736 | tf_op jit(solution)/shard_map/ppermute | solution.py:353
  33.2 2.3 %terms_kernel.1 = (bf16[512,1024]{1,0:T(8,128)(2,1)S(1)}, f32[8,384]{1,0:T(8,128)S(1)}, bf16[256,512]{1,0:T(8,128)(2,1)S(1)}, f32[256,512]{1,0:T(8,128)S(1)}, f3...) custom-call(s32[1]{0:T(128)} %bitcast.core, bf16[512,1024]{1,0:T(8,128)(2,1)S(1)} %get-tuple-element.42.x_t, ...), custom_call_target="tpu_custom_call" | custom-call | flops 2500000000 | bytes 8663044 | tf_op jit(solution)/shard_map/terms_kernel/pallas_call | solution.py:324
  35.5 0.0 collective-permute-done.8.came
  35.5 1.3 %pack_kernel.1 = bf16[8,72,1024]{2,1,0:T(8,128)(2,1)} custom-call(bf16[512,1024]{1,0:T(8,128)(2,1)S(1)} %get-tuple-element.54.keep, bf16[512,1024]{1,0:T(8,128)(2,1)S(1)} %collective-permute-done.8.came, f32[8,384]{1,0:T(8,128)S(1)} %get-tuple-element.56.bias), custom_call_target="tpu_custom_call" | custom-call | flops 1000000 | bytes 3289088 | tf_op jit(solution)/shard_map/pack_kernel/pallas_call | solution.py:324
  36.8 5.9 %all-to-all-start = ((bf16[8,72,1024]{2,1,0:T(8,128)(2,1)}), bf16[8,72,1024]{2,1,0:T(8,128)(2,1)S(1)}, u32[]{:S(2)}, u32[]{:S(2)}) async-start(bf16[8,72,1024]{2,1,0:T(8,128)(2,1)} %pack_kernel.1), calls=%async_computation | async-start | bytes 2359296 | tf_op jit(solution)/shard_map/all_to_all | solution.py:418
  42.7 0.0 collective-permute-start.4
  42.7 2.9 %collective-permute-start.5 = (bf16[256,512]{1,0:T(8,128)(2,1)S(1)}, bf16[256,512]{1,0:T(8,128)(2,1)S(1)}, u32[]{:S(2)}, u32[]{:S(2)}) collective-permute-start(bf16[256,512]{1,0:T(8,128)(2,1)S(1)} %get-tuple-element.50), channel_id=1, source_target_pairs={{0,224},{32,0},{64,32},{96,64},{128,96},{160,128},{192,160},{224,1... | collective-permute-start | bytes 786440 | tf_op jit(solution)/shard_map/ppermute | solution.py:346
  45.6 5.8 %collective-permute-done.4.up = bf16[256,512]{1,0:T(8,128)(2,1)S(1)} collective-permute-done((bf16[256,512]{1,0:T(8,128)(2,1)S(1)}, bf16[256,512]{1,0:T(8,128)(2,1)S(1)}, u32[]{:S(2)}, u32[]{:S(2)}) %collective-permute-start.4) | collective-permute-done | bytes 262176 | tf_op jit(solution)/shard_map/ppermute | solution.py:346
  51.4 0.0 collective-permute-done.5.down
  51.4 0.1 fold_kernel.1
  51.5 8.5 %all-to-all-done.came = bf16[8,72,1024]{2,1,0:T(8,128)(2,1)S(1)} async-done(((bf16[8,72,1024]{2,1,0:T(8,128)(2,1)}), bf16[8,72,1024]{2,1,0:T(8,128)(2,1)S(1)}, u32[]{:S(2)}, u32[]{:S(2)}) %all-to-all-start) | async-done | bytes 1179680 | tf_op jit(solution)/shard_map/all_to_all | solution.py:418
  60.0 0.8 regroup_kernel.1
  60.8 5.7 %all-to-all-start.1 = ((bf16[8,8,1408]{2,1,0:T(8,128)(2,1)}), bf16[8,8,1408]{2,1,0:T(8,128)(2,1)S(1)}, u32[]{:S(2)}, u32[]{:S(2)}) async-start(bf16[8,8,1408]{2,1,0:T(8,128)(2,1)} %regroup_kernel.1), calls=%async_computation.1 | async-start | bytes 360448 | tf_op jit(solution)/shard_map/all_to_all | solution.py:444
  66.5 1.3 %collective-permute-start.7 = (bf16[16,8,512]{2,1,0:T(8,128)(2,1)S(1)}, bf16[16,8,512]{2,1,0:T(8,128)(2,1)S(1)}, u32[]{:S(2)}, u32[]{:S(2)}) collective-permute-start(bf16[16,8,512]{2,1,0:T(8,128)(2,1)S(1)} %bitcast.32), channel_id=1, source_target_pairs={{4,0},{8,4},{12,8},{16,12},{20,16},{24,20},{28,24},{5,1},{9,5},{13... | collective-permute-start | bytes 393224 | tf_op jit(solution)/shard_map/ppermute | solution.py:350
  67.7 4.0 %collective-permute-start.6 = (bf16[16,8,512]{2,1,0:T(8,128)(2,1)S(1)}, bf16[16,8,512]{2,1,0:T(8,128)(2,1)S(1)}, u32[]{:S(2)}, u32[]{:S(2)}) collective-permute-start(bf16[16,8,512]{2,1,0:T(8,128)(2,1)S(1)} %bitcast.31), channel_id=1, source_target_pairs={{0,4},{4,8},{8,12},{12,16},{16,20},{20,24},{24,28},{1,5},{5,9},{9,... | collective-permute-start | bytes 393224 | tf_op jit(solution)/shard_map/ppermute | solution.py:350
  71.8 3.1 %all-to-all-done.1.came = bf16[8,8,1408]{2,1,0:T(8,128)(2,1)S(1)} async-done(((bf16[8,8,1408]{2,1,0:T(8,128)(2,1)}), bf16[8,8,1408]{2,1,0:T(8,128)(2,1)S(1)}, u32[]{:S(2)}, u32[]{:S(2)}) %all-to-all-start.1) | async-done | bytes 180256 | tf_op jit(solution)/shard_map/all_to_all | solution.py:444
  74.9 2.7 %collective-permute-start.9 = (f32[8,1408]{1,0:T(8,128)S(1)}, f32[8,1408]{1,0:T(8,128)S(1)}, u32[]{:S(2)}, u32[]{:S(2)}) collective-permute-start(f32[8,1408]{1,0:T(8,128)S(1)} %total_kernel.1.mine), channel_id=1, source_target_pairs={{0,2},{2,0},{1,3},{3,1},{4,6},{6,4},{5,7},{7,5},{8,10},{10,8},{9,1... | collective-permute-start | bytes 135176 | tf_op jit(solution)/shard_map/ppermute | solution.py:353
  77.6 3.3 %collective-permute-done.9.came = f32[8,1408]{1,0:T(8,128)S(1)} collective-permute-done((f32[8,1408]{1,0:T(8,128)S(1)}, f32[8,1408]{1,0:T(8,128)S(1)}, u32[]{:S(2)}, u32[]{:S(2)}) %collective-permute-start.9) | collective-permute-done | bytes 45088 | tf_op jit(solution)/shard_map/ppermute | solution.py:353
  81.0 2.3 %collective-permute-start.10 = (f32[8,1408]{1,0:T(8,128)S(1)}, f32[8,1408]{1,0:T(8,128)S(1)}, u32[]{:S(2)}, u32[]{:S(2)}) collective-permute-start(f32[8,1408]{1,0:T(8,128)S(1)} %add_kernel.1.here), channel_id=1, source_target_pairs={{0,1},{1,0},{2,3},{3,2},{4,5},{5,4},{6,7},{7,6},{8,9},{9,8},{10,11... | collective-permute-start | bytes 135176 | tf_op jit(solution)/shard_map/ppermute | solution.py:353
  83.3 0.0 collective-permute-done.7.east
  83.3 0.0 collective-permute-done.6.west
  83.3 0.8 after_kernel.1
  84.1 0.1 collective-permute-done.10.there
  84.2 0.7 finish_kernel.1
  (7 shorter events, 0.1 us)
Async XLA Ops:
  1.6 8.0 %collective-permute-start = (bf16[16,8,512]{2,1,0:T(8,128)(2,1)S(1)}, bf16[16,8,512]{2,1,0:T(8,128)(2,1)S(1)}, u32[]{:S(2)}, u32[]{:S(2)}) collective-permute-start(bf16[16,8,512]{2,1,0:T(8,128)(2,1)S(1)} %get-tuple-element.62), channel_id=1, source_target_pairs={{0,4},{4,8},{8,12},{12,16},{16,20},{20,24},{24,28},{1,5},{5,9},{9,... | collective-permute-start | bytes 393224 | tf_op jit(solution)/shard_map/ppermute | solution.py:350
  5.6 5.7 %collective-permute-start.1 = (bf16[16,8,512]{2,1,0:T(8,128)(2,1)S(1)}, bf16[16,8,512]{2,1,0:T(8,128)(2,1)S(1)}, u32[]{:S(2)}, u32[]{:S(2)}) collective-permute-start(bf16[16,8,512]{2,1,0:T(8,128)(2,1)S(1)} %get-tuple-element.63), channel_id=1, source_target_pairs={{4,0},{8,4},{12,8},{16,12},{20,16},{24,20},{28,24},{5,1},{9,5},{13... | collective-permute-start | bytes 393224 | tf_op jit(solution)/shard_map/ppermute | solution.py:350
  7.8 1.8 %copy-start = (bf16[1,16,16,512]{3,2,1,0:T(8,128)(2,1)S(1)}, bf16[1,16,16,512]{3,2,1,0:T(8,128)(2,1)}, u32[]{:S(2)}) copy-start(bf16[1,16,16,512]{3,2,1,0:T(8,128)(2,1)} %param.5) | copy-start | bytes 786436
  9.6 7.6 %copy-start.1 = (bf16[512,512]{1,0:T(8,128)(2,1)S(1)}, bf16[512,512]{1,0:T(8,128)(2,1)}, u32[]{:S(2)}) copy-start(bf16[512,512]{1,0:T(8,128)(2,1)} %wo.1) | copy-start | bytes 1572868
  9.6 7.6 %copy-start.2 = (bf16[1,16,16,512]{3,2,1,0:T(8,128)(2,1)S(1)}, bf16[1,16,16,512]{3,2,1,0:T(8,128)(2,1)}, u32[]{:S(2)}) copy-start(bf16[1,16,16,512]{3,2,1,0:T(8,128)(2,1)} %param.9) | copy-start | bytes 786436
  11.3 10.3 %collective-permute-start.2 = (bf16[256,512]{1,0:T(8,128)(2,1)S(1)}, bf16[256,512]{1,0:T(8,128)(2,1)S(1)}, u32[]{:S(2)}, u32[]{:S(2)}) collective-permute-start(bf16[256,512]{1,0:T(8,128)(2,1)S(1)} %pad_maximum_fusion.lower), channel_id=1, source_target_pairs={{0,32},{32,64},{64,96},{96,128},{128,160},{160,192},{192,224},{224... | collective-permute-start | bytes 786440 | tf_op jit(solution)/shard_map/ppermute | solution.py:346
  13.1 8.5 %collective-permute-start.3 = (bf16[256,512]{1,0:T(8,128)(2,1)S(1)}, bf16[256,512]{1,0:T(8,128)(2,1)S(1)}, u32[]{:S(2)}, u32[]{:S(2)}) collective-permute-start(bf16[256,512]{1,0:T(8,128)(2,1)S(1)} %pad_maximum_fusion.1.upper), channel_id=1, source_target_pairs={{0,224},{32,0},{64,32},{96,64},{128,96},{160,128},{192,160},{224,1... | collective-permute-start | bytes 786440 | tf_op jit(solution)/shard_map/ppermute | solution.py:346
  30.5 5.1 %collective-permute-start.8 = (bf16[512,1024]{1,0:T(8,128)(2,1)S(1)}, bf16[512,1024]{1,0:T(8,128)(2,1)S(1)}, u32[]{:S(2)}, u32[]{:S(2)}) collective-permute-start(bf16[512,1024]{1,0:T(8,128)(2,1)S(1)} %get-tuple-element.55), channel_id=1, source_target_pairs={{0,1},{1,0},{2,3},{3,2},{4,5},{5,4},{6,7},{7,6},{8,9},{9,8},{10,11... | collective-permute-start | bytes 3145736 | tf_op jit(solution)/shard_map/ppermute | solution.py:353
  36.8 23.1 %all-to-all-start = ((bf16[8,72,1024]{2,1,0:T(8,128)(2,1)}), bf16[8,72,1024]{2,1,0:T(8,128)(2,1)S(1)}, u32[]{:S(2)}, u32[]{:S(2)}) async-start(bf16[8,72,1024]{2,1,0:T(8,128)(2,1)} %pack_kernel.1), calls=%async_computation | async-start | bytes 2359296 | tf_op jit(solution)/shard_map/all_to_all | solution.py:418
  42.7 8.7 %collective-permute-start.4 = (bf16[256,512]{1,0:T(8,128)(2,1)S(1)}, bf16[256,512]{1,0:T(8,128)(2,1)S(1)}, u32[]{:S(2)}, u32[]{:S(2)}) collective-permute-start(bf16[256,512]{1,0:T(8,128)(2,1)S(1)} %get-tuple-element.49), channel_id=1, source_target_pairs={{0,32},{32,64},{64,96},{96,128},{128,160},{160,192},{192,224},{224... | collective-permute-start | bytes 786440 | tf_op jit(solution)/shard_map/ppermute | solution.py:346
  42.7 8.7 %collective-permute-start.5 = (bf16[256,512]{1,0:T(8,128)(2,1)S(1)}, bf16[256,512]{1,0:T(8,128)(2,1)S(1)}, u32[]{:S(2)}, u32[]{:S(2)}) collective-permute-start(bf16[256,512]{1,0:T(8,128)(2,1)S(1)} %get-tuple-element.50), channel_id=1, source_target_pairs={{0,224},{32,0},{64,32},{96,64},{128,96},{160,128},{192,160},{224,1... | collective-permute-start | bytes 786440 | tf_op jit(solution)/shard_map/ppermute | solution.py:346
  60.8 14.1 %all-to-all-start.1 = ((bf16[8,8,1408]{2,1,0:T(8,128)(2,1)}), bf16[8,8,1408]{2,1,0:T(8,128)(2,1)S(1)}, u32[]{:S(2)}, u32[]{:S(2)}) async-start(bf16[8,8,1408]{2,1,0:T(8,128)(2,1)} %regroup_kernel.1), calls=%async_computation.1 | async-start | bytes 360448 | tf_op jit(solution)/shard_map/all_to_all | solution.py:444
  66.5 16.8 %collective-permute-start.7 = (bf16[16,8,512]{2,1,0:T(8,128)(2,1)S(1)}, bf16[16,8,512]{2,1,0:T(8,128)(2,1)S(1)}, u32[]{:S(2)}, u32[]{:S(2)}) collective-permute-start(bf16[16,8,512]{2,1,0:T(8,128)(2,1)S(1)} %bitcast.32), channel_id=1, source_target_pairs={{4,0},{8,4},{12,8},{16,12},{20,16},{24,20},{28,24},{5,1},{9,5},{13... | collective-permute-start | bytes 393224 | tf_op jit(solution)/shard_map/ppermute | solution.py:350
  67.7 15.6 %collective-permute-start.6 = (bf16[16,8,512]{2,1,0:T(8,128)(2,1)S(1)}, bf16[16,8,512]{2,1,0:T(8,128)(2,1)S(1)}, u32[]{:S(2)}, u32[]{:S(2)}) collective-permute-start(bf16[16,8,512]{2,1,0:T(8,128)(2,1)S(1)} %bitcast.31), channel_id=1, source_target_pairs={{0,4},{4,8},{8,12},{12,16},{16,20},{20,24},{24,28},{1,5},{5,9},{9,... | collective-permute-start | bytes 393224 | tf_op jit(solution)/shard_map/ppermute | solution.py:350
  74.9 6.1 %collective-permute-start.9 = (f32[8,1408]{1,0:T(8,128)S(1)}, f32[8,1408]{1,0:T(8,128)S(1)}, u32[]{:S(2)}, u32[]{:S(2)}) collective-permute-start(f32[8,1408]{1,0:T(8,128)S(1)} %total_kernel.1.mine), channel_id=1, source_target_pairs={{0,2},{2,0},{1,3},{3,1},{4,6},{6,4},{5,7},{7,5},{8,10},{10,8},{9,1... | collective-permute-start | bytes 135176 | tf_op jit(solution)/shard_map/ppermute | solution.py:353
  81.0 3.2 %collective-permute-start.10 = (f32[8,1408]{1,0:T(8,128)S(1)}, f32[8,1408]{1,0:T(8,128)S(1)}, u32[]{:S(2)}, u32[]{:S(2)}) collective-permute-start(f32[8,1408]{1,0:T(8,128)S(1)} %add_kernel.1.here), channel_id=1, source_target_pairs={{0,1},{1,0},{2,3},{3,2},{4,5},{5,4},{6,7},{7,6},{8,9},{9,8},{10,11... | collective-permute-start | bytes 135176 | tf_op jit(solution)/shard_map/ppermute | solution.py:353

commit v7 on v6

--- a/solution.py
+++ b/solution.py
@@ -34,13 +34,13 @@
     )
 
 
-def before_kernel(edge, x, cot, wt, wo, bias, q, q_t, da, da_t, table):
-    xv = x[...]
-    cv = cot[...]
-    q[...] = (dot(xv, wt[0:512], NT).astype(BF16).astype(F32) * 0.125).astype(BF16)
-    q_t[...] = (dot(wt[0:512], xv, NT).astype(BF16).astype(F32) * 0.125).astype(BF16)
-    da[...] = dot(cv, wo[...], NT).astype(BF16)
-    da_t[...] = dot(wo[...], cv, NT).astype(BF16)
+def before_kernel(edge, x, cot, w, wo, bias, q, q_t, da, da_t, table):
+    queries = (dot(x[...], w[:, 0:512]).astype(BF16).astype(F32) * 0.125).astype(BF16)
+    q[...] = queries
+    q_t[...] = queries.T
+    d_attended = dot(cot[...], wo[...], NT).astype(BF16)
+    da[...] = d_attended
+    da_t[...] = d_attended.T
     pick = (iota((17, 512), 0) == 23 - (iota((17, 512), 1) >> 4)).astype(F32)
     range_row = iota((32, 512), 0)
     lane = iota((32, 512), 1)
@@ -69,20 +69,29 @@
     lax.fori_loop(0, 4, pair_step, 0)
 
 
-def project(block, wt, k, v, k_t, v_t, at):
-    rows = pl.ds(at, 256)
-    keys = dot(block, wt[512:1024], NT).astype(BF16)
-    values = dot(block, wt[1024:1536], NT).astype(BF16)
+def project(block, w, k, v, k_t, v_t, x_t, at):
+    rows = slice(at, at + 256)
+    keys = dot(block, w[:, 512:1024]).astype(BF16)
+    values = dot(block, w[:, 1024:1536]).astype(BF16)
     k[rows] = keys
     v[rows] = values
     k_t[:, rows] = keys.T
     v_t[:, rows] = values.T
-
-
-def middle_kernel(upper, lower, wt, k, v, k_t, v_t, x_t):
-    for at, ref in ((0, upper), (256, lower)):
-        project(ref[...], wt, k, v, k_t, v_t, at)
-        x_t[:, at : at + 256] = ref[...].T
+    x_t[:, rows] = block.T
+
+
+def sides_kernel(left, right, upper, lower):
+    for half, ref in enumerate((upper, lower)):
+        ref[0:64] = left[half * 64 : half * 64 + 64]
+        ref[64:128] = right[half * 64 : half * 64 + 64]
+
+
+def middle_kernel(left, own, right, w, k, v, k_t, v_t, x_t):
+    for half in range(2):
+        side = slice(half * 64, half * 64 + 64)
+        mine = slice(half * 128, half * 128 + 128)
+        block = jnp.concatenate([left[side], own[mine], right[side]], axis=0)
+        project(block, w, k, v, k_t, v_t, x_t, half * 256)
 
 
 def by_range(block, rng):
@@ -101,19 +110,19 @@
 
 
 def attention_kernel(
-    rng, core, above, below, q, q_t, da, da_t, table, k_mid, v_mid, kt_mid, vt_mid, xt_mid, wt, cot,
+    rng, core, top, above, bottom, below, q, q_t, da, da_t, table,
+    k_mid, v_mid, kt_mid, vt_mid, xt_mid, w, cot,
     x_t, dkv, lhs, rhs, bsum, g_send,
     k, v, k_t, v_t, dq_t, dsum,
 ):
-    project(above[...], wt, k, v, k_t, v_t, 0)
-    project(below[...], wt, k, v, k_t, v_t, 768)
+    for at, own, sides in ((0, top, above), (768, bottom, below)):
+        block = jnp.concatenate([sides[0:64], own[...], sides[64:128]], axis=0)
+        project(block, w, k, v, k_t, v_t, x_t, at)
     k[256:768] = k_mid[...]
     v[256:768] = v_mid[...]
     k_t[:, 256:768] = kt_mid[...]
     v_t[:, 256:768] = vt_mid[...]
-    x_t[:, 0:256] = above[...].T
     x_t[:, 256:768] = xt_mid[...]
-    x_t[:, 768:1024] = below[...].T
     lhs[0, :, 0:128] = xt_mid[:, 64:192]
     lhs[0, :, 128:256] = xt_mid[:, 320:448]
     rhs[1] = cot[...]
@@ -216,14 +225,14 @@
             )
         return carry
 
-    lax.fori_loop(0, 4, pair_step, 0)
+    lax.fori_loop(0, 4, pair_step, 0, unroll=True)
 
     rhs[0] = dq_t[...].T
     weight_terms(g_send, 1 - core[0], rng, x_t, dkv, lhs, rhs)
 
 
 def terms_kernel(
-    rng, core, x_t, dkv, lhs, rhs, bsum, wt, g_keep, g_bias, g_above, g_upper, g_lower, g_below
+    rng, core, x_t, dkv, lhs, rhs, bsum, w, g_keep, g_bias, g_above, g_upper, g_lower, g_below
 ):
     weight_terms(g_keep, core[0], rng, x_t, dkv, lhs, rhs)
 
@@ -246,13 +255,13 @@
     g_bias[...] = flat
 
     for g, ref in enumerate((g_above, g_upper, g_lower, g_below)):
-        block = dot(dkv[g * 256 : g * 256 + 256], wt[512:1536])
+        block = dot(dkv[g * 256 : g * 256 + 256], w[:, 512:1536], NT)
         if g in (0, 3):
             ref[...] = block.astype(BF16)
         else:
             half = (g - 1) * 128
             ref[0:64] = block[0:64]
-            ref[64:192] = block[64:192] + dot(rhs[0, half : half + 128], wt[0:512])
+            ref[64:192] = block[64:192] + dot(rhs[0, half : half + 128], w[:, 0:512], NT)
             ref[192:256] = block[192:256]
 
 
@@ -270,24 +279,31 @@
 
 
 def pack_kernel(keep, came, bias, parcel):
-    rows = parcel.shape[1] - 8
+    count = parcel.shape[0]
+    rows = keep.shape[0] // count
     low = bias[...].astype(BF16)
-    for r in range(parcel.shape[0]):
+    for r in range(count):
         at = slice(r * rows, r * rows + rows)
-        parcel[r, 0:rows] = (keep[at].astype(F32) + came[at].astype(F32)).astype(BF16)
-        parcel[r, rows : rows + 8, 0:384] = low
-        parcel[r, rows : rows + 8, 384:1024] = jnp.zeros((8, 640), BF16)
+        both = (keep[at].astype(F32) + came[at].astype(F32)).astype(BF16)
+        for n in range(8):
+            parcel[r, n * rows : n * rows + rows] = both[:, n * 128 : n * 128 + 128]
+        for n in range(3):
+            to = 8 * rows + n * 8
+            parcel[r, to : to + 8] = low[:, n * 128 : n * 128 + 128]
 
 
 def regroup_kernel(came, _, parcel):
     total = came[0].astype(F32)
     for n in range(1, came.shape[0]):
         total += came[n].astype(F32)
-    rows = came.shape[1] - 8
-    low = total.astype(BF16)
-    for a in range(parcel.shape[0]):
-        parcel[a, :, 0:1024] = low[a * 8 : a * 8 + 8]
-        parcel[a, :, 1024:1408] = low[rows : rows + 8, 0:384]
+    count = parcel.shape[0]
+    for a in range(count):
+        for n in range(8):
+            at = (n * count + a) * 8
+            parcel[a, :, n * 128 : n * 128 + 128] = total[at : at + 8].astype(BF16)
+        for n in range(3):
+            at = count * 64 + n * 8
+            parcel[a, :, 1024 + n * 128 : 1152 + n * 128] = total[at : at + 8].astype(BF16)
 
 
 def total_kernel(came, mine):
@@ -354,19 +370,21 @@
 
     left = shift(cells[:, 8:], 1).reshape(128, width)
     right = shift(cells[:, :8], -1).reshape(128, width)
-    upper = jnp.concatenate([left[:64], own[:128], right[:64]], axis=0)
-    lower = jnp.concatenate([left[64:], own[128:], right[64:]], axis=0)
+    top = turn(own[128:], 1)
+    bottom = turn(own[:128], -1)
+    upper, lower = call(
+        sides_kernel, (left, right), (whole((128, 512), BF16),) * 2, flops=1_000_000
+    )
     above = turn(lower, 1)
     below = turn(upper, -1)
 
     core = lax.axis_index("core").astype(jnp.int32)[None]
     at_range = lax.axis_index("rng")
     edge = jnp.stack([at_range == 0, at_range == rng - 1]).astype(jnp.int32)
-    turned = qkv_weight.T
 
     q, q_t, da, da_t, table = call(
         before_kernel,
-        (edge, own, cot, turned, out_weight, relative_bias),
+        (edge, own, cot, qkv_weight, out_weight, relative_bias),
         (
             whole((256, 512), BF16), whole((512, 256), BF16),
             whole((256, 512), BF16), whole((512, 256), BF16),
@@ -377,11 +395,11 @@
         limit=12,
     )
     middle = call(
-        middle_kernel, (upper, lower, turned), (whole((512, 512), BF16),) * 5, flops=1_000_000_000, limit=12
+        middle_kernel, (left, own, right, qkv_weight), (whole((512, 512), BF16),) * 5, flops=1_000_000_000, limit=12
     )
     x_t, dkv, lhs, rhs, bsum, g_send = call(
         functools.partial(attention_kernel, rng),
-        (core, above, below, q, q_t, da, da_t, table, *middle, turned, cot),
+        (core, top, above, bottom, below, q, q_t, da, da_t, table, *middle, qkv_weight, cot),
         (
             whole((512, 1024), BF16), whole((1024, 1024), BF16),
             whole((2, 512, 256), BF16), whole((2, 256, 512), BF16),
@@ -399,7 +417,7 @@
     came = swap(g_send)
     g_keep, g_bias, g_above, g_upper, g_lower, g_below = call(
         functools.partial(terms_kernel, rng),
-        (core, x_t, dkv, lhs, rhs, bsum, turned),
+        (core, x_t, dkv, lhs, rhs, bsum, qkv_weight),
         (
             whole((512, 1024), BF16), whole((8, 384), F32),
             whole((256, 512), BF16), whole((256, 512), F32),
@@ -412,7 +430,7 @@
     (parcel,) = call(
         pack_kernel,
         (g_keep, came, g_bias),
-        (whole((rng, 8 * az + 8, 1024), BF16),),
+        (whole((rng, 64 * az + 24, 128), BF16),),
         flops=1_000_000,
     )
     parcel = lax.all_to_all(parcel, "rng", 0, 0, tiled=True)

time: 85.3 us -> 85.2 us (level)
  starting transfers between devices: 38.4 us -> 41 us
  waiting for transfers between devices: 22.6 us -> 20.3 us
  Pallas kernels: 19.3 us -> 18.2 us
    ppermute x4 -> x6, starting transfers between devices: 8.62 us -> 11.4 us  [turn(): return lax.ppermute(leaf, 'az', [(i, (i + step) % az) for i in range(az)])]
    ppermute x4, waiting for transfers between devices: 1.64 us -> 0.01 us  [shift(): return lax.ppermute(leaf, 'rng', pairs)]
    pallas_call x11 -> x12, Pallas kernels: 19.3 us -> 18.2 us  [call(): pl.pallas_call(kernel, out_shape=tuple(outs), in_specs=[scalar] * prefetc...]
    slice x4 -> x2, local copies, waits for them, and re-layouts: 1.03 us -> 2.06 us  [the longest x1 1.07 us: shards(): right = shift(cells[:, :8], -1).reshape(128, width)]
    unnamed x8 -> x11, local copies, waits for them, and re-layouts: 2.68 us -> 2.32 us
    ppermute x4 -> x6, waiting for transfers between devices: 5.85 us -> 6 us  [turn(): return lax.ppermute(leaf, 'az', [(i, (i + step) % az) for i in range(az)])]
  transfers between devices with their start and end apart: 13 -> 15, of which waited for: 6 -> 5; matrix products, arithmetic and copies ran while one was open for 3% -> 2% of each run, Pallas kernels for 9% -> 9%
where the time goes in v7:
time: 85.2 us; the launch traced here: 84.8 us
  starting transfers between devices  41 us (48%)
  waiting for transfers between devices  20.3 us (24%)
  Pallas kernels  18.2 us (21%)
  local copies, waits for them, and re-layouts  4.38 us (5%)
    pallas_call x12, Pallas kernels, call(): pl.pallas_call(kernel, out_shape=tuple(outs), in_specs=[scalar] * prefetc...  18.2 us
    ppermute x6, starting transfers between devices, turn(): return lax.ppermute(leaf, 'az', [(i, (i + step) % az) for i in range(az)])  11.4 us
    ppermute x4, starting transfers between devices, shift(): return lax.ppermute(leaf, 'rng', pairs)  11.1 us
    all_to_all x1, waiting for transfers between devices, shards(): parcel = lax.all_to_all(parcel, 'rng', 0, 0, tiled=True)  7.64 us
    ppermute x3, starting transfers between devices, swap(): return lax.ppermute(leaf, axis, [(0, 1), (1, 0)])  7.15 us
    ppermute x6, waiting for transfers between devices, turn(): return lax.ppermute(leaf, 'az', [(i, (i + step) % az) for i in range(az)])  6 us
    all_to_all x1, starting transfers between devices, shards(): parcel = lax.all_to_all(parcel, 'rng', 0, 0, tiled=True)  5.86 us
    all_to_all x1, starting transfers between devices, shards(): parcel = lax.all_to_all(parcel, 'az', 0, 0, tiled=True)  5.48 us
  transfers between devices with their start and end apart: 15, of which 5 were waited for; matrix products, arithmetic and copies ran while one was open for 2% of the time, Pallas kernels for 9%

profile of v7, /device:TPU:1, one launch (start us, length us, event | category | flops | bytes accessed | tf_op | source)
XLA Modules:
  0.0 84.8 jit_solution(7599816976649382318)
XLA Ops:
  0.6 0.0 copy-start
  0.6 0.0 copy-start.4
  0.7 0.0 copy-start.3
  0.7 1.1 %fusion.1 = (bf16[16,8,512]{2,1,0:T(8,128)(2,1)S(1)}, bf16[16,8,512]{2,1,0:T(8,128)(2,1)S(1)}) fusion(bf16[16,16,512]{2,1,0:T(8,128)(2,1)} %bitcast.15), kind=kLoop, calls=%fused_computation.2 | loop fusion | bytes 524288 | tf_op jit(solution)/shard_map/slice | solution.py:372
  1.7 1.3 %collective-permute-start.2 = (bf16[16,8,512]{2,1,0:T(8,128)(2,1)S(1)}, bf16[16,8,512]{2,1,0:T(8,128)(2,1)S(1)}, u32[]{:S(2)}, u32[]{:S(2)}) collective-permute-start(bf16[16,8,512]{2,1,0:T(8,128)(2,1)S(1)} %get-tuple-element.66), channel_id=1, source_target_pairs={{4,0},{8,4},{12,8},{16,12},{20,16},{24,20},{28,24},{5,1},{9,5},{13... | collective-permute-start | bytes 393224 | tf_op jit(solution)/shard_map/ppermute | solution.py:366
  3.0 4.6 %collective-permute-start.1 = (bf16[16,8,512]{2,1,0:T(8,128)(2,1)S(1)}, bf16[16,8,512]{2,1,0:T(8,128)(2,1)S(1)}, u32[]{:S(2)}, u32[]{:S(2)}) collective-permute-start(bf16[16,8,512]{2,1,0:T(8,128)(2,1)S(1)} %get-tuple-element.67), channel_id=1, source_target_pairs={{0,4},{4,8},{8,12},{12,16},{16,20},{20,24},{24,28},{1,5},{5,9},{9,... | collective-permute-start | bytes 393224 | tf_op jit(solution)/shard_map/ppermute | solution.py:366
  7.6 1.0 %fusion = (bf16[1,8,16,512]{3,2,1,0:T(8,128)(2,1)S(1)}, bf16[1,8,16,512]{3,2,1,0:T(8,128)(2,1)S(1)}) fusion(bf16[1,16,16,512]{3,2,1,0:T(8,128)(2,1)} %param.5), kind=kLoop, calls=%fused_computation.1 | loop fusion | bytes 524288 | tf_op jit(solution)/shard_map/slice | solution.py:374
  8.6 2.0 %collective-permute-start = (bf16[128,512]{1,0:T(8,128)(2,1)S(1)}, bf16[128,512]{1,0:T(8,128)(2,1)S(1)}, u32[]{:S(2)}, u32[]{:S(2)}) collective-permute-start(bf16[128,512]{1,0:T(8,128)(2,1)S(1)} %bitcast.29), channel_id=1, source_target_pairs={{0,32},{32,64},{64,96},{96,128},{128,160},{160,192},{192,224},{224... | collective-permute-start | bytes 393224 | tf_op jit(solution)/shard_map/ppermute | solution.py:362
  10.6 4.0 %collective-permute-start.4 = (bf16[128,512]{1,0:T(8,128)(2,1)S(1)}, bf16[128,512]{1,0:T(8,128)(2,1)S(1)}, u32[]{:S(2)}, u32[]{:S(2)}) collective-permute-start(bf16[128,512]{1,0:T(8,128)(2,1)S(1)} %bitcast.28), channel_id=1, source_target_pairs={{0,224},{32,0},{64,32},{96,64},{128,96},{160,128},{192,160},{224,1... | collective-permute-start | bytes 393224 | tf_op jit(solution)/shard_map/ppermute | solution.py:362
  14.6 0.9 %copy.9.bias = f32[8,17,17]{2,1,0:T(8,128)S(1)} copy(f32[8,17,17]{2,0,1:T(8,128)} %param.8) | data formatting | bytes 18496 | tf_op args[3]
  15.5 0.1 add_convert_fusion.edge
  15.6 0.0 collective-permute-done.2
  15.6 0.0 collective-permute-done.1
  15.6 0.1 collective-permute-start.3
  15.7 2.7 %collective-permute-start.5 = (bf16[128,512]{1,0:T(8,128)(2,1)S(1)}, bf16[128,512]{1,0:T(8,128)(2,1)S(1)}, u32[]{:S(2)}, u32[]{:S(2)}) collective-permute-start(bf16[128,512]{1,0:T(8,128)(2,1)S(1)} %get-tuple-element.35), channel_id=1, source_target_pairs={{0,224},{32,0},{64,32},{96,64},{128,96},{160,128},{192,160},{224,1... | collective-permute-start | bytes 393224 | tf_op jit(solution)/shard_map/ppermute | solution.py:362
  18.4 0.0 copy-done
  18.4 0.0 copy-done.4
  18.4 0.0 copy-done.3
  18.4 0.0 copy-start.1
  18.4 1.4 %copy-done.1 = bf16[512,1536]{1,0:T(8,128)(2,1)S(1)} copy-done((bf16[512,1536]{1,0:T(8,128)(2,1)S(1)}, bf16[512,1536]{1,0:T(8,128)(2,1)}, u32[]{:S(2)}) %copy-start.1) | copy-done | bytes 1572888
  19.8 0.0 copy-start.2
  19.8 3.3 %before_kernel.1 = (bf16[256,512]{1,0:T(8,128)(2,1)S(1)}, bf16[512,256]{1,0:T(8,128)(2,1)S(1)}, bf16[256,512]{1,0:T(8,128)(2,1)S(1)}, bf16[512,256]{1,0:T(8,128)(2,1)S(1)}, f32[4,768,256]{2,1,0:T(8,128)S(1)}) custom-call(s32[2]{0:T(128)S(1)} %add_convert_fusion.edge, bf16[256,512]{1,0:T(8,128)(2,1)S(1)} %bitcast.16, bf16[256,512]{1,0:T(8,128)(2,1)S(1)} %bitcast.19, ...), custom_call_target="tpu_custom_call" | custom-call | flops 600000000 | bytes 6825000 | tf_op jit(solution)/shard_map/before_kernel/pallas_call | solution.py:340
  23.1 0.0 copy-done.2
  23.1 0.8 middle_kernel.1
  23.9 0.0 collective-permute-done.top
  23.9 0.0 collective-permute-done.4.bottom
  24.0 0.0 collective-permute-done.3.above
  24.0 0.0 collective-permute-done.5.below
  24.0 7.8 %attention_kernel.1 = (bf16[512,1024]{1,0:T(8,128)(2,1)S(1)}, bf16[1024,1024]{1,0:T(8,128)(2,1)S(1)}, bf16[2,512,256]{2,1,0:T(8,128)(2,1)S(1)}, bf16[2,256,512]{...) custom-call(s32[1]{0:T(128)} %bitcast.core, ...), custom_call_target="tpu_custom_call" | custom-call | flops 10000000000 | bytes 14680068 | tf_op jit(solution)/shard_map/attention_kernel/pallas_call | solution.py:340
  31.8 2.2 %collective-permute-start.10 = (bf16[512,1024]{1,0:T(8,128)(2,1)S(1)}, bf16[512,1024]{1,0:T(8,128)(2,1)S(1)}, u32[]{:S(2)}, u32[]{:S(2)}) collective-permute-start(bf16[512,1024]{1,0:T(8,128)(2,1)S(1)} %get-tuple-element.59), channel_id=1, source_target_pairs={{0,1},{1,0},{2,3},{3,2},{4,5},{5,4},{6,7},{7,6},{8,9},{9,8},{10,11... | collective-permute-start | bytes 3145736 | tf_op jit(solution)/shard_map/ppermute | solution.py:369
  34.0 2.5 %terms_kernel.1 = (bf16[512,1024]{1,0:T(8,128)(2,1)S(1)}, f32[8,384]{1,0:T(8,128)S(1)}, bf16[256,512]{1,0:T(8,128)(2,1)S(1)}, f32[256,512]{1,0:T(8,128)S(1)}, f3...) custom-call(s32[1]{0:T(128)} %bitcast.core, bf16[512,1024]{1,0:T(8,128)(2,1)S(1)} %get-tuple-element.46.x_t, ...), custom_call_target="tpu_custom_call" | custom-call | flops 2500000000 | bytes 8663044 | tf_op jit(solution)/shard_map/terms_kernel/pallas_call | solution.py:340
  36.5 0.0 collective-permute-done.10.came
  36.5 1.3 %pack_kernel.1 = bf16[8,536,128]{2,1,0:T(8,128)(2,1)} custom-call(bf16[512,1024]{1,0:T(8,128)(2,1)S(1)} %get-tuple-element.58.keep, bf16[512,1024]{1,0:T(8,128)(2,1)S(1)} %collective-permute-done.10.came, f32[8,384]{1,0:T(8,128)S(1)} %get-tuple-element.60.bias), custom_call_target="tpu_custom_call" | custom-call | flops 1000000 | bytes 3207168 | tf_op jit(solution)/shard_map/pack_kernel/pallas_call | solution.py:340
  37.8 5.9 %all-to-all-start = ((bf16[8,536,128]{2,1,0:T(8,128)(2,1)}), bf16[8,536,128]{2,1,0:T(8,128)(2,1)S(1)}, u32[]{:S(2)}, u32[]{:S(2)}) async-start(bf16[8,536,128]{2,1,0:T(8,128)(2,1)} %pack_kernel.1), calls=%async_computation | async-start | bytes 2195456 | tf_op jit(solution)/shard_map/all_to_all | solution.py:436
  43.6 0.0 collective-permute-start.6
  43.7 2.7 %collective-permute-start.7 = (bf16[256,512]{1,0:T(8,128)(2,1)S(1)}, bf16[256,512]{1,0:T(8,128)(2,1)S(1)}, u32[]{:S(2)}, u32[]{:S(2)}) collective-permute-start(bf16[256,512]{1,0:T(8,128)(2,1)S(1)} %get-tuple-element.54), channel_id=1, source_target_pairs={{0,224},{32,0},{64,32},{96,64},{128,96},{160,128},{192,160},{224,1... | collective-permute-start | bytes 786440 | tf_op jit(solution)/shard_map/ppermute | solution.py:362
  46.3 6.0 %collective-permute-done.6.up = bf16[256,512]{1,0:T(8,128)(2,1)S(1)} collective-permute-done((bf16[256,512]{1,0:T(8,128)(2,1)S(1)}, bf16[256,512]{1,0:T(8,128)(2,1)S(1)}, u32[]{:S(2)}, u32[]{:S(2)}) %collective-permute-start.6) | collective-permute-done | bytes 262176 | tf_op jit(solution)/shard_map/ppermute | solution.py:362
  52.3 0.0 collective-permute-done.7.down
  52.3 0.1 fold_kernel.1
  52.4 7.6 %all-to-all-done.came = bf16[8,536,128]{2,1,0:T(8,128)(2,1)S(1)} async-done(((bf16[8,536,128]{2,1,0:T(8,128)(2,1)}), bf16[8,536,128]{2,1,0:T(8,128)(2,1)S(1)}, u32[]{:S(2)}, u32[]{:S(2)}) %all-to-all-start) | async-done | bytes 1097760 | tf_op jit(solution)/shard_map/all_to_all | solution.py:436
  60.0 0.8 regroup_kernel.1
  60.8 5.5 %all-to-all-start.1 = ((bf16[8,8,1408]{2,1,0:T(8,128)(2,1)}), bf16[8,8,1408]{2,1,0:T(8,128)(2,1)S(1)}, u32[]{:S(2)}, u32[]{:S(2)}) async-start(bf16[8,8,1408]{2,1,0:T(8,128)(2,1)} %regroup_kernel.1), calls=%async_computation.1 | async-start | bytes 360448 | tf_op jit(solution)/shard_map/all_to_all | solution.py:462
  66.3 1.3 %collective-permute-start.9 = (bf16[16,8,512]{2,1,0:T(8,128)(2,1)S(1)}, bf16[16,8,512]{2,1,0:T(8,128)(2,1)S(1)}, u32[]{:S(2)}, u32[]{:S(2)}) collective-permute-start(bf16[16,8,512]{2,1,0:T(8,128)(2,1)S(1)} %bitcast.26), channel_id=1, source_target_pairs={{4,0},{8,4},{12,8},{16,12},{20,16},{24,20},{28,24},{5,1},{9,5},{13... | collective-permute-start | bytes 393224 | tf_op jit(solution)/shard_map/ppermute | solution.py:366
  67.6 4.0 %collective-permute-start.8 = (bf16[16,8,512]{2,1,0:T(8,128)(2,1)S(1)}, bf16[16,8,512]{2,1,0:T(8,128)(2,1)S(1)}, u32[]{:S(2)}, u32[]{:S(2)}) collective-permute-start(bf16[16,8,512]{2,1,0:T(8,128)(2,1)S(1)} %bitcast.25), channel_id=1, source_target_pairs={{0,4},{4,8},{8,12},{12,16},{16,20},{20,24},{24,28},{1,5},{5,9},{9,... | collective-permute-start | bytes 393224 | tf_op jit(solution)/shard_map/ppermute | solution.py:366
  71.6 3.1 %all-to-all-done.1.came = bf16[8,8,1408]{2,1,0:T(8,128)(2,1)S(1)} async-done(((bf16[8,8,1408]{2,1,0:T(8,128)(2,1)}), bf16[8,8,1408]{2,1,0:T(8,128)(2,1)S(1)}, u32[]{:S(2)}, u32[]{:S(2)}) %all-to-all-start.1) | async-done | bytes 180256 | tf_op jit(solution)/shard_map/all_to_all | solution.py:462
  74.8 3.0 %collective-permute-start.11 = (f32[8,1408]{1,0:T(8,128)S(1)}, f32[8,1408]{1,0:T(8,128)S(1)}, u32[]{:S(2)}, u32[]{:S(2)}) collective-permute-start(f32[8,1408]{1,0:T(8,128)S(1)} %total_kernel.1.mine), channel_id=1, source_target_pairs={{0,2},{2,0},{1,3},{3,1},{4,6},{6,4},{5,7},{7,5},{8,10},{10,8},{9,1... | collective-permute-start | bytes 135176 | tf_op jit(solution)/shard_map/ppermute | solution.py:369
  77.8 3.4 %collective-permute-done.11.came = f32[8,1408]{1,0:T(8,128)S(1)} collective-permute-done((f32[8,1408]{1,0:T(8,128)S(1)}, f32[8,1408]{1,0:T(8,128)S(1)}, u32[]{:S(2)}, u32[]{:S(2)}) %collective-permute-start.11) | collective-permute-done | bytes 45088 | tf_op jit(solution)/shard_map/ppermute | solution.py:369
  81.2 2.0 %collective-permute-start.12 = (f32[8,1408]{1,0:T(8,128)S(1)}, f32[8,1408]{1,0:T(8,128)S(1)}, u32[]{:S(2)}, u32[]{:S(2)}) collective-permute-start(f32[8,1408]{1,0:T(8,128)S(1)} %add_kernel.1.here), channel_id=1, source_target_pairs={{0,1},{1,0},{2,3},{3,2},{4,5},{5,4},{6,7},{7,6},{8,9},{9,8},{10,11... | collective-permute-start | bytes 135176 | tf_op jit(solution)/shard_map/ppermute | solution.py:369
  83.2 0.0 collective-permute-done.9.east
  83.2 0.0 collective-permute-done.8.west
  83.2 0.8 after_kernel.1
  83.9 0.1 collective-permute-done.12.there
  84.0 0.7 finish_kernel.1
  (3 shorter events, 0.1 us)
Async XLA Ops:
  0.6 17.7 %copy-start = (bf16[1,16,16,512]{3,2,1,0:T(8,128)(2,1)S(1)}, bf16[1,16,16,512]{3,2,1,0:T(8,128)(2,1)}, u32[]{:S(2)}) copy-start(bf16[1,16,16,512]{3,2,1,0:T(8,128)(2,1)} %param.5) | copy-start | bytes 786436
  0.6 17.7 %copy-start.4 = (bf16[1,16,16,512]{3,2,1,0:T(8,128)(2,1)S(1)}, bf16[1,16,16,512]{3,2,1,0:T(8,128)(2,1)}, u32[]{:S(2)}) copy-start(bf16[1,16,16,512]{3,2,1,0:T(8,128)(2,1)} %param.9) | copy-start | bytes 786436
  0.7 17.7 %copy-start.3 = (bf16[512,512]{1,0:T(8,128)(2,1)S(1)}, bf16[512,512]{1,0:T(8,128)(2,1)}, u32[]{:S(2)}) copy-start(bf16[512,512]{1,0:T(8,128)(2,1)} %wo.1) | copy-start | bytes 1572868
  1.7 13.8 %collective-permute-start.2 = (bf16[16,8,512]{2,1,0:T(8,128)(2,1)S(1)}, bf16[16,8,512]{2,1,0:T(8,128)(2,1)S(1)}, u32[]{:S(2)}, u32[]{:S(2)}) collective-permute-start(bf16[16,8,512]{2,1,0:T(8,128)(2,1)S(1)} %get-tuple-element.66), channel_id=1, source_target_pairs={{4,0},{8,4},{12,8},{16,12},{20,16},{24,20},{28,24},{5,1},{9,5},{13... | collective-permute-start | bytes 393224 | tf_op jit(solution)/shard_map/ppermute | solution.py:366
  3.0 12.5 %collective-permute-start.1 = (bf16[16,8,512]{2,1,0:T(8,128)(2,1)S(1)}, bf16[16,8,512]{2,1,0:T(8,128)(2,1)S(1)}, u32[]{:S(2)}, u32[]{:S(2)}) collective-permute-start(bf16[16,8,512]{2,1,0:T(8,128)(2,1)S(1)} %get-tuple-element.67), channel_id=1, source_target_pairs={{0,4},{4,8},{8,12},{12,16},{16,20},{20,24},{24,28},{1,5},{5,9},{9,... | collective-permute-start | bytes 393224 | tf_op jit(solution)/shard_map/ppermute | solution.py:366
  8.6 15.3 %collective-permute-start = (bf16[128,512]{1,0:T(8,128)(2,1)S(1)}, bf16[128,512]{1,0:T(8,128)(2,1)S(1)}, u32[]{:S(2)}, u32[]{:S(2)}) collective-permute-start(bf16[128,512]{1,0:T(8,128)(2,1)S(1)} %bitcast.29), channel_id=1, source_target_pairs={{0,32},{32,64},{64,96},{96,128},{128,160},{160,192},{192,224},{224... | collective-permute-start | bytes 393224 | tf_op jit(solution)/shard_map/ppermute | solution.py:362
  10.6 13.4 %collective-permute-start.4 = (bf16[128,512]{1,0:T(8,128)(2,1)S(1)}, bf16[128,512]{1,0:T(8,128)(2,1)S(1)}, u32[]{:S(2)}, u32[]{:S(2)}) collective-permute-start(bf16[128,512]{1,0:T(8,128)(2,1)S(1)} %bitcast.28), channel_id=1, source_target_pairs={{0,224},{32,0},{64,32},{96,64},{128,96},{160,128},{192,160},{224,1... | collective-permute-start | bytes 393224 | tf_op jit(solution)/shard_map/ppermute | solution.py:362
  15.6 8.4 %collective-permute-start.3 = (bf16[128,512]{1,0:T(8,128)(2,1)S(1)}, bf16[128,512]{1,0:T(8,128)(2,1)S(1)}, u32[]{:S(2)}, u32[]{:S(2)}) collective-permute-start(bf16[128,512]{1,0:T(8,128)(2,1)S(1)} %get-tuple-element.34), channel_id=1, source_target_pairs={{0,32},{32,64},{64,96},{96,128},{128,160},{160,192},{192,224},{224... | collective-permute-start | bytes 393224 | tf_op jit(solution)/shard_map/ppermute | solution.py:362
  15.7 8.3 %collective-permute-start.5 = (bf16[128,512]{1,0:T(8,128)(2,1)S(1)}, bf16[128,512]{1,0:T(8,128)(2,1)S(1)}, u32[]{:S(2)}, u32[]{:S(2)}) collective-permute-start(bf16[128,512]{1,0:T(8,128)(2,1)S(1)} %get-tuple-element.35), channel_id=1, source_target_pairs={{0,224},{32,0},{64,32},{96,64},{128,96},{160,128},{192,160},{224,1... | collective-permute-start | bytes 393224 | tf_op jit(solution)/shard_map/ppermute | solution.py:362
  18.4 1.4 %copy-start.1 = (bf16[512,1536]{1,0:T(8,128)(2,1)S(1)}, bf16[512,1536]{1,0:T(8,128)(2,1)}, u32[]{:S(2)}) copy-start(bf16[512,1536]{1,0:T(8,128)(2,1)} %w.7) | copy-start | bytes 4718596
  19.8 3.3 %copy-start.2 = (bf16[512,1536]{1,0:T(8,128)(2,1)S(1)}, bf16[512,1536]{1,0:T(8,128)(2,1)}, u32[]{:S(2)}) copy-start(bf16[512,1536]{1,0:T(8,128)(2,1)} %w.7) | copy-start | bytes 4718596
  31.8 4.7 %collective-permute-start.10 = (bf16[512,1024]{1,0:T(8,128)(2,1)S(1)}, bf16[512,1024]{1,0:T(8,128)(2,1)S(1)}, u32[]{:S(2)}, u32[]{:S(2)}) collective-permute-start(bf16[512,1024]{1,0:T(8,128)(2,1)S(1)} %get-tuple-element.59), channel_id=1, source_target_pairs={{0,1},{1,0},{2,3},{3,2},{4,5},{5,4},{6,7},{7,6},{8,9},{9,8},{10,11... | collective-permute-start | bytes 3145736 | tf_op jit(solution)/shard_map/ppermute | solution.py:369
  37.8 22.3 %all-to-all-start = ((bf16[8,536,128]{2,1,0:T(8,128)(2,1)}), bf16[8,536,128]{2,1,0:T(8,128)(2,1)S(1)}, u32[]{:S(2)}, u32[]{:S(2)}) async-start(bf16[8,536,128]{2,1,0:T(8,128)(2,1)} %pack_kernel.1), calls=%async_computation | async-start | bytes 2195456 | tf_op jit(solution)/shard_map/all_to_all | solution.py:436
  43.6 8.7 %collective-permute-start.6 = (bf16[256,512]{1,0:T(8,128)(2,1)S(1)}, bf16[256,512]{1,0:T(8,128)(2,1)S(1)}, u32[]{:S(2)}, u32[]{:S(2)}) collective-permute-start(bf16[256,512]{1,0:T(8,128)(2,1)S(1)} %get-tuple-element.53), channel_id=1, source_target_pairs={{0,32},{32,64},{64,96},{96,128},{128,160},{160,192},{192,224},{224... | collective-permute-start | bytes 786440 | tf_op jit(solution)/shard_map/ppermute | solution.py:362
  43.7 8.7 %collective-permute-start.7 = (bf16[256,512]{1,0:T(8,128)(2,1)S(1)}, bf16[256,512]{1,0:T(8,128)(2,1)S(1)}, u32[]{:S(2)}, u32[]{:S(2)}) collective-permute-start(bf16[256,512]{1,0:T(8,128)(2,1)S(1)} %get-tuple-element.54), channel_id=1, source_target_pairs={{0,224},{32,0},{64,32},{96,64},{128,96},{160,128},{192,160},{224,1... | collective-permute-start | bytes 786440 | tf_op jit(solution)/shard_map/ppermute | solution.py:362
  60.8 13.9 %all-to-all-start.1 = ((bf16[8,8,1408]{2,1,0:T(8,128)(2,1)}), bf16[8,8,1408]{2,1,0:T(8,128)(2,1)S(1)}, u32[]{:S(2)}, u32[]{:S(2)}) async-start(bf16[8,8,1408]{2,1,0:T(8,128)(2,1)} %regroup_kernel.1), calls=%async_computation.1 | async-start | bytes 360448 | tf_op jit(solution)/shard_map/all_to_all | solution.py:462
  66.3 16.8 %collective-permute-start.9 = (bf16[16,8,512]{2,1,0:T(8,128)(2,1)S(1)}, bf16[16,8,512]{2,1,0:T(8,128)(2,1)S(1)}, u32[]{:S(2)}, u32[]{:S(2)}) collective-permute-start(bf16[16,8,512]{2,1,0:T(8,128)(2,1)S(1)} %bitcast.26), channel_id=1, source_target_pairs={{4,0},{8,4},{12,8},{16,12},{20,16},{24,20},{28,24},{5,1},{9,5},{13... | collective-permute-start | bytes 393224 | tf_op jit(solution)/shard_map/ppermute | solution.py:366
  67.6 15.6 %collective-permute-start.8 = (bf16[16,8,512]{2,1,0:T(8,128)(2,1)S(1)}, bf16[16,8,512]{2,1,0:T(8,128)(2,1)S(1)}, u32[]{:S(2)}, u32[]{:S(2)}) collective-permute-start(bf16[16,8,512]{2,1,0:T(8,128)(2,1)S(1)} %bitcast.25), channel_id=1, source_target_pairs={{0,4},{4,8},{8,12},{12,16},{16,20},{20,24},{24,28},{1,5},{5,9},{9,... | collective-permute-start | bytes 393224 | tf_op jit(solution)/shard_map/ppermute | solution.py:366
  74.8 6.4 %collective-permute-start.11 = (f32[8,1408]{1,0:T(8,128)S(1)}, f32[8,1408]{1,0:T(8,128)S(1)}, u32[]{:S(2)}, u32[]{:S(2)}) collective-permute-start(f32[8,1408]{1,0:T(8,128)S(1)} %total_kernel.1.mine), channel_id=1, source_target_pairs={{0,2},{2,0},{1,3},{3,1},{4,6},{6,4},{5,7},{7,5},{8,10},{10,8},{9,1... | collective-permute-start | bytes 135176 | tf_op jit(solution)/shard_map/ppermute | solution.py:369
  81.2 2.9 %collective-permute-start.12 = (f32[8,1408]{1,0:T(8,128)S(1)}, f32[8,1408]{1,0:T(8,128)S(1)}, u32[]{:S(2)}, u32[]{:S(2)}) collective-permute-start(f32[8,1408]{1,0:T(8,128)S(1)} %add_kernel.1.here), channel_id=1, source_target_pairs={{0,1},{1,0},{2,3},{3,2},{4,5},{5,4},{6,7},{7,6},{8,9},{9,8},{10,11... | collective-permute-start | bytes 135176 | tf_op jit(solution)/shard_map/ppermute | solution.py:369

commit v8 on v7

--- a/solution.py
+++ b/solution.py
@@ -6,6 +6,7 @@
 from jax.experimental import pallas as pl
 from jax.experimental.pallas import tpu as pltpu
 from jax.sharding import Mesh, PartitionSpec as P
+
 
 F32 = jnp.float32
 BF16 = jnp.bfloat16
@@ -34,13 +35,34 @@
     )
 
 
-def before_kernel(edge, x, cot, w, wo, bias, q, q_t, da, da_t, table):
+def slices_kernel(own, to_right, to_left, to_next, to_last, done):
+    copies = [
+        pltpu.make_async_copy(source, target, done.at[n])
+        for n, (source, target) in enumerate(
+            (
+                (own.at[:, pl.ds(8, 8)], to_right),
+                (own.at[:, pl.ds(0, 8)], to_left),
+                (own.at[pl.ds(8, 8)], to_next),
+                (own.at[pl.ds(0, 8)], to_last),
+            )
+        )
+    ]
+    for copy in copies:
+        copy.start()
+    for copy in copies:
+        copy.wait()
+
+
+def queries_kernel(x, cot, w, wo, q, q_t, da, da_t):
     queries = (dot(x[...], w[:, 0:512]).astype(BF16).astype(F32) * 0.125).astype(BF16)
     q[...] = queries
     q_t[...] = queries.T
     d_attended = dot(cot[...], wo[...], NT).astype(BF16)
     da[...] = d_attended
     da_t[...] = d_attended.T
+
+
+def table_kernel(edge, bias, table):
     pick = (iota((17, 512), 0) == 23 - (iota((17, 512), 1) >> 4)).astype(F32)
     range_row = iota((32, 512), 0)
     lane = iota((32, 512), 1)
@@ -48,25 +70,19 @@
     first = jnp.where(edge[0] == 1, 8, 0)
     last = jnp.where(edge[1] == 1, 24, 32)
     present = (range_row >= first) & (range_row < last) & (lane >= 112) & (lane < 384)
-
-    def pair_step(pair, carry):
-        for side in range(2):
-            head_rows = dot(bias[pair * 2 + side], pick, TN, exact=True)
-            spread = jnp.full((32, 512), ABSENT, F32)
-            for j in range(17):
-                spread = jnp.where(gap == j, head_rows[j : j + 1], spread)
-            spread = jnp.where(present, spread, ABSENT)
-            for v in range(8):
-                turned = spread if v == 0 else pltpu.roll(spread, 512 - 16 * v, 1)
-                for u in range(3):
-                    block = turned[:, 128 * u : 128 * u + 128]
-                    for low, high, at in row_slots(23 - 8 * u - v):
-                        table[pair, at : at + high - low, side * 128 : side * 128 + 128] = block[
-                            low:high
-                        ]
-        return carry
-
-    lax.fori_loop(0, 4, pair_step, 0)
+    for head in range(8):
+        pair, lanes = head // 2, slice(head % 2 * 128, head % 2 * 128 + 128)
+        head_rows = dot(bias[:, head, :], pick, TN, exact=True)
+        spread = jnp.full((32, 512), ABSENT, F32)
+        for j in range(17):
+            spread = jnp.where(gap == j, head_rows[j : j + 1], spread)
+        spread = jnp.where(present, spread, ABSENT)
+        for v in range(8):
+            turned = spread if v == 0 else pltpu.roll(spread, 512 - 16 * v, 1)
+            for u in range(3):
+                block = turned[:, 128 * u : 128 * u + 128]
+                for low, high, at in row_slots(23 - 8 * u - v):
+                    table[pair, at : at + high - low, lanes] = block[low:high]
 
 
 def project(block, w, k, v, k_t, v_t, x_t, at):
@@ -333,7 +349,7 @@
     return jax.ShapeDtypeStruct(shape, dtype)
 
 
-def call(kernel, operands, outs, scratch=(), prefetch=0, flops=0, limit=16, untouched=0):
+def call(kernel, operands, outs, scratch=(), prefetch=0, flops=0, limit=16, untouched=0, far=0):
     spec = pl.BlockSpec(memory_space=pltpu.VMEM)
     scalar = pl.BlockSpec(memory_space=pltpu.SMEM)
     size = sum(leaf.size * leaf.dtype.itemsize for leaf in tuple(operands) + tuple(outs))
@@ -341,13 +357,13 @@
         kernel,
         out_shape=tuple(outs),
         in_specs=[scalar] * prefetch
-        + [spec] * (len(operands) - prefetch - untouched)
-        + [pl.BlockSpec(memory_space=pl.ANY)] * untouched,
+        + [spec] * (len(operands) - prefetch - untouched - far)
+        + [pl.BlockSpec(memory_space=pl.ANY)] * untouched
+        + [pl.BlockSpec(memory_space=pltpu.HBM)] * far,
         out_specs=tuple([spec] * len(outs)),
         scratch_shapes=list(scratch),
         compiler_params=pltpu.CompilerParams(vmem_limit_bytes=limit * MIB),
         cost_estimate=pl.CostEstimate(flops=flops, bytes_accessed=size, transcendentals=0),
-        name=getattr(kernel, "func", kernel).__name__,
     )(*operands)
 
 
@@ -368,10 +384,18 @@
     def swap(leaf, axis="core"):
         return lax.ppermute(leaf, axis, [(0, 1), (1, 0)])
 
-    left = shift(cells[:, 8:], 1).reshape(128, width)
-    right = shift(cells[:, :8], -1).reshape(128, width)
-    top = turn(own[128:], 1)
-    bottom = turn(own[:128], -1)
+    to_right, to_left, to_next, to_last = call(
+        slices_kernel,
+        (cells,),
+        (whole((16, 8, width), BF16),) * 2 + (whole((8, 16, width), BF16),) * 2,
+        scratch=(pltpu.SemaphoreType.DMA((4,)),),
+        far=1,
+        flops=1_000_000,
+    )
+    left = shift(to_right, 1).reshape(128, width)
+    right = shift(to_left, -1).reshape(128, width)
+    top = turn(to_next, 1).reshape(128, width)
+    bottom = turn(to_last, -1).reshape(128, width)
     upper, lower = call(
         sides_kernel, (left, right), (whole((128, 512), BF16),) * 2, flops=1_000_000
     )
@@ -382,16 +406,22 @@
     at_range = lax.axis_index("rng")
     edge = jnp.stack([at_range == 0, at_range == rng - 1]).astype(jnp.int32)
 
-    q, q_t, da, da_t, table = call(
-        before_kernel,
-        (edge, own, cot, qkv_weight, out_weight, relative_bias),
+    (table,) = call(
+        table_kernel,
+        (edge, jnp.transpose(relative_bias, (1, 0, 2))),
+        (whole((4, 768, 256), F32),),
+        prefetch=1,
+        flops=100_000_000,
+        limit=12,
+    )
+    q, q_t, da, da_t = call(
+        queries_kernel,
+        (own, cot, qkv_weight, out_weight),
         (
             whole((256, 512), BF16), whole((512, 256), BF16),
             whole((256, 512), BF16), whole((512, 256), BF16),
-            whole((4, 768, 256), F32),
         ),
-        prefetch=1,
-        flops=600_000_000,
+        flops=300_000_000,
         limit=12,
     )
     middle = call(

time: 85.2 us -> 83.5 us (0.980)
  local copies, waits for them, and re-layouts: 4.38 us -> 1.84 us
  starting transfers between devices: 41 us -> 42.2 us
    slice x2 -> x0, local copies, waits for them, and re-layouts: 2.06 us -> none  [the longest x1 1.07 us: shards(): right = shift(cells[:, :8], -1).reshape(128, width)]
    ppermute x6, starting transfers between devices: 11.4 us -> 13.2 us  [turn(): return lax.ppermute(leaf, 'az', [(i, (i + step) % az) for i in range(az)])]
    unnamed x11 -> x12, local copies, waits for them, and re-layouts: 2.32 us -> 1.84 us
    pallas_call x12 -> x14, Pallas kernels: 18.2 us -> 17.8 us  [call(): pl.pallas_call(kernel, out_shape=tuple(outs), in_specs=[scalar] * prefetc...]
  transfers between devices with their start and end apart: 15 -> 15, of which waited for: 5 -> 5; matrix products, arithmetic and copies ran while one was open for 2% -> 0% of each run, Pallas kernels for 9% -> 8%
where the time goes in v8:
time: 83.5 us; the launch traced here: 83.1 us
  starting transfers between devices  42.2 us (51%)
  waiting for transfers between devices  20.3 us (24%)
  Pallas kernels  17.8 us (21%)
  local copies, waits for them, and re-layouts  1.84 us (2%)
    pallas_call x14, Pallas kernels, call(): pl.pallas_call(kernel, out_shape=tuple(outs), in_specs=[scalar] * prefetc...  17.8 us
    ppermute x6, starting transfers between devices, turn(): return lax.ppermute(leaf, 'az', [(i, (i + step) % az) for i in range(az)])  13.2 us
    ppermute x4, starting transfers between devices, shift(): return lax.ppermute(leaf, 'rng', pairs)  10.5 us
    all_to_all x1, waiting for transfers between devices, shards(): parcel = lax.all_to_all(parcel, 'rng', 0, 0, tiled=True)  7.63 us
    ppermute x3, starting transfers between devices, swap(): return lax.ppermute(leaf, axis, [(0, 1), (1, 0)])  7.37 us
    ppermute x6, waiting for transfers between devices, turn(): return lax.ppermute(leaf, 'az', [(i, (i + step) % az) for i in range(az)])  6.01 us
    all_to_all x1, starting transfers between devices, shards(): parcel = lax.all_to_all(parcel, 'rng', 0, 0, tiled=True)  5.86 us
    all_to_all x1, starting transfers between devices, shards(): parcel = lax.all_to_all(parcel, 'az', 0, 0, tiled=True)  5.29 us
  transfers between devices with their start and end apart: 15, of which 5 were waited for; matrix products, arithmetic and copies ran while one was open for 0% of the time, Pallas kernels for 8%

profile of v8, /device:TPU:1, one launch (start us, length us, event | category | flops | bytes accessed | tf_op | source)
XLA Modules:
  0.0 83.1 jit_solution(16052204231094222184)
XLA Ops:
  0.6 0.0 copy-start.1
  0.6 0.9 %copy-done.1 = bf16[1,16,16,512]{3,2,1,0:T(8,128)(2,1)S(1)} copy-done((bf16[1,16,16,512]{3,2,1,0:T(8,128)(2,1)S(1)}, bf16[1,16,16,512]{3,2,1,0:T(8,128)(2,1)}, u32[]{:S(2)}) %copy-start.1) | copy-done | bytes 262168
  1.6 0.4 shard_map.84
  2.0 3.9 %collective-permute-start.1 = (bf16[16,8,512]{2,1,0:T(8,128)(2,1)S(1)}, bf16[16,8,512]{2,1,0:T(8,128)(2,1)S(1)}, u32[]{:S(2)}, u32[]{:S(2)}) collective-permute-start(bf16[16,8,512]{2,1,0:T(8,128)(2,1)S(1)} %get-tuple-element.38), channel_id=1, source_target_pairs={{0,4},{4,8},{8,12},{12,16},{16,20},{20,24},{24,28},{1,5},{5,9},{9,... | collective-permute-start | bytes 393224 | tf_op jit(solution)/shard_map/ppermute | solution.py:382
  6.0 1.3 %collective-permute-start.2 = (bf16[16,8,512]{2,1,0:T(8,128)(2,1)S(1)}, bf16[16,8,512]{2,1,0:T(8,128)(2,1)S(1)}, u32[]{:S(2)}, u32[]{:S(2)}) collective-permute-start(bf16[16,8,512]{2,1,0:T(8,128)(2,1)S(1)} %get-tuple-element.39), channel_id=1, source_target_pairs={{4,0},{8,4},{12,8},{16,12},{20,16},{24,20},{28,24},{5,1},{9,5},{13... | collective-permute-start | bytes 393224 | tf_op jit(solution)/shard_map/ppermute | solution.py:382
  7.3 1.7 %collective-permute-start = (bf16[8,16,512]{2,1,0:T(8,128)(2,1)S(1)}, bf16[8,16,512]{2,1,0:T(8,128)(2,1)S(1)}, u32[]{:S(2)}, u32[]{:S(2)}) collective-permute-start(bf16[8,16,512]{2,1,0:T(8,128)(2,1)S(1)} %get-tuple-element.37), channel_id=1, source_target_pairs={{0,32},{32,64},{64,96},{96,128},{128,160},{160,192},{192,224},{224... | collective-permute-start | bytes 393224 | tf_op jit(solution)/shard_map/ppermute | solution.py:378
  9.0 4.0 %collective-permute-start.4 = (bf16[8,16,512]{2,1,0:T(8,128)(2,1)S(1)}, bf16[8,16,512]{2,1,0:T(8,128)(2,1)S(1)}, u32[]{:S(2)}, u32[]{:S(2)}) collective-permute-start(bf16[8,16,512]{2,1,0:T(8,128)(2,1)S(1)} %get-tuple-element.41), channel_id=1, source_target_pairs={{0,224},{32,0},{64,32},{96,64},{128,96},{160,128},{192,160},{224,1... | collective-permute-start | bytes 393224 | tf_op jit(solution)/shard_map/ppermute | solution.py:378
  13.0 0.1 add_convert_fusion.edge
  13.1 0.0 collective-permute-done.1
  13.1 0.0 collective-permute-done.2
  13.1 0.6 collective-permute-start.3
  13.7 4.2 %collective-permute-start.5 = (bf16[128,512]{1,0:T(8,128)(2,1)S(1)}, bf16[128,512]{1,0:T(8,128)(2,1)S(1)}, u32[]{:S(2)}, u32[]{:S(2)}) collective-permute-start(bf16[128,512]{1,0:T(8,128)(2,1)S(1)} %get-tuple-element.42), channel_id=1, source_target_pairs={{0,224},{32,0},{64,32},{96,64},{128,96},{160,128},{192,160},{224,1... | collective-permute-start | bytes 393224 | tf_op jit(solution)/shard_map/ppermute | solution.py:378
  17.9 0.0 copy-start.5
  17.9 0.9 %copy-done.5 = f32[8,17,17]{2,0,1:T(8,128)S(1)} copy-done((f32[8,17,17]{2,0,1:T(8,128)S(1)}, f32[8,17,17]{2,0,1:T(8,128)}, u32[]{:S(2)}) %copy-start.5) | copy-done | bytes 9272
  18.8 0.0 copy-start
  18.8 0.0 copy-start.2
  18.8 0.0 copy-start.3
  18.8 0.0 copy-start.4
  18.8 2.0 %shard_map.87.table = f32[4,768,256]{2,1,0:T(8,128)S(1)} custom-call(s32[2]{0:T(128)S(1)} %add_convert_fusion.edge, f32[17,8,17]{2,1,0:T(8,128)S(1)} %bitcast.26), custom_call_target="tpu_custom_call" | custom-call | flops 100000000 | bytes 3154984 | tf_op jit(solution)/shard_map/pallas_call | solution.py:356
  20.8 0.0 copy-done
  20.8 0.0 copy-done.2
  20.8 0.0 copy-done.3
  20.8 0.0 copy-done.4
  20.8 0.5 shard_map.86
  21.4 0.8 %shard_map.88 = (bf16[512,512]{1,0:T(8,128)(2,1)S(1)}, bf16[512,512]{1,0:T(8,128)(2,1)S(1)}, bf16[512,512]{1,0:T(8,128)(2,1)S(1)}, bf16[512,512]{1,0:T(8,128)(2,1)S(1)}, bf16[512,512]{1,0:T(8,128)(2,1)S(1)}) custom-call(bf16[128,512]{1,0:T(8,128)(2,1)S(1)} %bitcast.23, bf16[256,512]{1,0:T(8,128)(2,1)S(1)} %bitcast.19, bf16[128,512]{1,0:T(8,128)(2,1)S(1)} %bitcast.25, ...), custom_call_target="tpu_custom_call" | custom-call | flops 1000000000 | bytes 4718592 | tf_op jit(solution)/shard_map/pallas_call | solution.py:356
  22.2 0.0 collective-permute-done
  22.2 0.0 collective-permute-done.4
  22.2 0.0 collective-permute-done.3.above
  22.2 0.0 collective-permute-done.5.below
  22.2 7.9 %shard_map.89 = (bf16[512,1024]{1,0:T(8,128)(2,1)S(1)}, bf16[1024,1024]{1,0:T(8,128)(2,1)S(1)}, bf16[2,512,256]{2,1,0:T(8,128)(2,1)S(1)}, bf16[2,256,512]{2,1,0:...) custom-call(s32[1]{0:T(128)} %bitcast.core, bf16[128,512]{1,0:T(8,128)(2,1)S(1)} %bitcast.27, ...), custom_call_target="tpu_custom_call" | custom-call | flops 10000000000 | bytes 14680068 | tf_op jit(solution)/shard_map/pallas_call | solution.py:356
  30.1 2.4 %collective-permute-start.10 = (bf16[512,1024]{1,0:T(8,128)(2,1)S(1)}, bf16[512,1024]{1,0:T(8,128)(2,1)S(1)}, u32[]{:S(2)}, u32[]{:S(2)}) collective-permute-start(bf16[512,1024]{1,0:T(8,128)(2,1)S(1)} %get-tuple-element.65), channel_id=1, source_target_pairs={{0,1},{1,0},{2,3},{3,2},{4,5},{5,4},{6,7},{7,6},{8,9},{9,8},{10,11... | collective-permute-start | bytes 3145736 | tf_op jit(solution)/shard_map/ppermute | solution.py:385
  32.5 2.5 %shard_map.90 = (bf16[512,1024]{1,0:T(8,128)(2,1)S(1)}, f32[8,384]{1,0:T(8,128)S(1)}, bf16[256,512]{1,0:T(8,128)(2,1)S(1)}, f32[256,512]{1,0:T(8,128)S(1)}, f32[...) custom-call(s32[1]{0:T(128)} %bitcast.core, bf16[512,1024]{1,0:T(8,128)(2,1)S(1)} %get-tuple-element.52.x_t, ...), custom_call_target="tpu_custom_call" | custom-call | flops 2500000000 | bytes 8663044 | tf_op jit(solution)/shard_map/pallas_call | solution.py:356
  35.0 0.0 collective-permute-done.10.came
  35.0 1.3 %shard_map.93 = bf16[8,536,128]{2,1,0:T(8,128)(2,1)} custom-call(bf16[512,1024]{1,0:T(8,128)(2,1)S(1)} %get-tuple-element.64.keep, bf16[512,1024]{1,0:T(8,128)(2,1)S(1)} %collective-permute-done.10.came, f32[8,384]{1,0:T(8,128)S(1)} %get-tuple-element.66.bias), custom_call_target="tpu_custom_call" | custom-call | flops 1000000 | bytes 3207168 | tf_op jit(solution)/shard_map/pallas_call | solution.py:356
  36.3 5.9 %all-to-all-start = ((bf16[8,536,128]{2,1,0:T(8,128)(2,1)}), bf16[8,536,128]{2,1,0:T(8,128)(2,1)S(1)}, u32[]{:S(2)}, u32[]{:S(2)}) async-start(bf16[8,536,128]{2,1,0:T(8,128)(2,1)} %shard_map.93), calls=%async_computation | async-start | bytes 2195456 | tf_op jit(solution)/shard_map/all_to_all | solution.py:466
  42.1 0.0 collective-permute-start.6
  42.2 2.7 %collective-permute-start.7 = (bf16[256,512]{1,0:T(8,128)(2,1)S(1)}, bf16[256,512]{1,0:T(8,128)(2,1)S(1)}, u32[]{:S(2)}, u32[]{:S(2)}) collective-permute-start(bf16[256,512]{1,0:T(8,128)(2,1)S(1)} %get-tuple-element.60), channel_id=1, source_target_pairs={{0,224},{32,0},{64,32},{96,64},{128,96},{160,128},{192,160},{224,1... | collective-permute-start | bytes 786440 | tf_op jit(solution)/shard_map/ppermute | solution.py:378
  44.8 6.0 %collective-permute-done.6.up = bf16[256,512]{1,0:T(8,128)(2,1)S(1)} collective-permute-done((bf16[256,512]{1,0:T(8,128)(2,1)S(1)}, bf16[256,512]{1,0:T(8,128)(2,1)S(1)}, u32[]{:S(2)}, u32[]{:S(2)}) %collective-permute-start.6) | collective-permute-done | bytes 262176 | tf_op jit(solution)/shard_map/ppermute | solution.py:378
  50.8 0.0 collective-permute-done.7.down
  50.8 0.1 shard_map.91
  50.9 7.6 %all-to-all-done.came = bf16[8,536,128]{2,1,0:T(8,128)(2,1)S(1)} async-done(((bf16[8,536,128]{2,1,0:T(8,128)(2,1)}), bf16[8,536,128]{2,1,0:T(8,128)(2,1)S(1)}, u32[]{:S(2)}, u32[]{:S(2)}) %all-to-all-start) | async-done | bytes 1097760 | tf_op jit(solution)/shard_map/all_to_all | solution.py:466
  58.5 0.8 shard_map.94
  59.4 5.3 %all-to-all-start.1 = ((bf16[8,8,1408]{2,1,0:T(8,128)(2,1)}), bf16[8,8,1408]{2,1,0:T(8,128)(2,1)S(1)}, u32[]{:S(2)}, u32[]{:S(2)}) async-start(bf16[8,8,1408]{2,1,0:T(8,128)(2,1)} %shard_map.94), calls=%async_computation.1 | async-start | bytes 360448 | tf_op jit(solution)/shard_map/all_to_all | solution.py:492
  64.6 1.3 %collective-permute-start.9 = (bf16[16,8,512]{2,1,0:T(8,128)(2,1)S(1)}, bf16[16,8,512]{2,1,0:T(8,128)(2,1)S(1)}, u32[]{:S(2)}, u32[]{:S(2)}) collective-permute-start(bf16[16,8,512]{2,1,0:T(8,128)(2,1)S(1)} %bitcast.30), channel_id=1, source_target_pairs={{4,0},{8,4},{12,8},{16,12},{20,16},{24,20},{28,24},{5,1},{9,5},{13... | collective-permute-start | bytes 393224 | tf_op jit(solution)/shard_map/ppermute | solution.py:382
  65.9 4.0 %collective-permute-start.8 = (bf16[16,8,512]{2,1,0:T(8,128)(2,1)S(1)}, bf16[16,8,512]{2,1,0:T(8,128)(2,1)S(1)}, u32[]{:S(2)}, u32[]{:S(2)}) collective-permute-start(bf16[16,8,512]{2,1,0:T(8,128)(2,1)S(1)} %bitcast.29), channel_id=1, source_target_pairs={{0,4},{4,8},{8,12},{12,16},{16,20},{20,24},{24,28},{1,5},{5,9},{9,... | collective-permute-start | bytes 393224 | tf_op jit(solution)/shard_map/ppermute | solution.py:382
  69.9 3.1 %all-to-all-done.1.came = bf16[8,8,1408]{2,1,0:T(8,128)(2,1)S(1)} async-done(((bf16[8,8,1408]{2,1,0:T(8,128)(2,1)}), bf16[8,8,1408]{2,1,0:T(8,128)(2,1)S(1)}, u32[]{:S(2)}, u32[]{:S(2)}) %all-to-all-start.1) | async-done | bytes 180256 | tf_op jit(solution)/shard_map/all_to_all | solution.py:492
  73.1 2.7 %collective-permute-start.11 = (f32[8,1408]{1,0:T(8,128)S(1)}, f32[8,1408]{1,0:T(8,128)S(1)}, u32[]{:S(2)}, u32[]{:S(2)}) collective-permute-start(f32[8,1408]{1,0:T(8,128)S(1)} %shard_map.95.mine), channel_id=1, source_target_pairs={{0,2},{2,0},{1,3},{3,1},{4,6},{6,4},{5,7},{7,5},{8,10},{10,8},{9,1... | collective-permute-start | bytes 135176 | tf_op jit(solution)/shard_map/ppermute | solution.py:385
  75.8 3.4 %collective-permute-done.11.came = f32[8,1408]{1,0:T(8,128)S(1)} collective-permute-done((f32[8,1408]{1,0:T(8,128)S(1)}, f32[8,1408]{1,0:T(8,128)S(1)}, u32[]{:S(2)}, u32[]{:S(2)}) %collective-permute-start.11) | collective-permute-done | bytes 45088 | tf_op jit(solution)/shard_map/ppermute | solution.py:385
  79.2 2.3 %collective-permute-start.12 = (f32[8,1408]{1,0:T(8,128)S(1)}, f32[8,1408]{1,0:T(8,128)S(1)}, u32[]{:S(2)}, u32[]{:S(2)}) collective-permute-start(f32[8,1408]{1,0:T(8,128)S(1)} %shard_map.96.here), channel_id=1, source_target_pairs={{0,1},{1,0},{2,3},{3,2},{4,5},{5,4},{6,7},{7,6},{8,9},{9,8},{10,11... | collective-permute-start | bytes 135176 | tf_op jit(solution)/shard_map/ppermute | solution.py:385
  81.5 0.0 collective-permute-done.9.east
  81.5 0.0 collective-permute-done.8.west
  81.5 0.8 shard_map.92
  82.2 0.1 collective-permute-done.12.there
  82.3 0.7 shard_map.97
  (3 shorter events, 0.1 us)
Async XLA Ops:
  0.6 1.0 %copy-start.1 = (bf16[1,16,16,512]{3,2,1,0:T(8,128)(2,1)S(1)}, bf16[1,16,16,512]{3,2,1,0:T(8,128)(2,1)}, u32[]{:S(2)}) copy-start(bf16[1,16,16,512]{3,2,1,0:T(8,128)(2,1)} %param.5) | copy-start | bytes 786436
  2.0 11.1 %collective-permute-start.1 = (bf16[16,8,512]{2,1,0:T(8,128)(2,1)S(1)}, bf16[16,8,512]{2,1,0:T(8,128)(2,1)S(1)}, u32[]{:S(2)}, u32[]{:S(2)}) collective-permute-start(bf16[16,8,512]{2,1,0:T(8,128)(2,1)S(1)} %get-tuple-element.38), channel_id=1, source_target_pairs={{0,4},{4,8},{8,12},{12,16},{16,20},{20,24},{24,28},{1,5},{5,9},{9,... | collective-permute-start | bytes 393224 | tf_op jit(solution)/shard_map/ppermute | solution.py:382
  6.0 7.1 %collective-permute-start.2 = (bf16[16,8,512]{2,1,0:T(8,128)(2,1)S(1)}, bf16[16,8,512]{2,1,0:T(8,128)(2,1)S(1)}, u32[]{:S(2)}, u32[]{:S(2)}) collective-permute-start(bf16[16,8,512]{2,1,0:T(8,128)(2,1)S(1)} %get-tuple-element.39), channel_id=1, source_target_pairs={{4,0},{8,4},{12,8},{16,12},{20,16},{24,20},{28,24},{5,1},{9,5},{13... | collective-permute-start | bytes 393224 | tf_op jit(solution)/shard_map/ppermute | solution.py:382
  7.3 15.0 %collective-permute-start = (bf16[8,16,512]{2,1,0:T(8,128)(2,1)S(1)}, bf16[8,16,512]{2,1,0:T(8,128)(2,1)S(1)}, u32[]{:S(2)}, u32[]{:S(2)}) collective-permute-start(bf16[8,16,512]{2,1,0:T(8,128)(2,1)S(1)} %get-tuple-element.37), channel_id=1, source_target_pairs={{0,32},{32,64},{64,96},{96,128},{128,160},{160,192},{192,224},{224... | collective-permute-start | bytes 393224 | tf_op jit(solution)/shard_map/ppermute | solution.py:378
  9.0 13.3 %collective-permute-start.4 = (bf16[8,16,512]{2,1,0:T(8,128)(2,1)S(1)}, bf16[8,16,512]{2,1,0:T(8,128)(2,1)S(1)}, u32[]{:S(2)}, u32[]{:S(2)}) collective-permute-start(bf16[8,16,512]{2,1,0:T(8,128)(2,1)S(1)} %get-tuple-element.41), channel_id=1, source_target_pairs={{0,224},{32,0},{64,32},{96,64},{128,96},{160,128},{192,160},{224,1... | collective-permute-start | bytes 393224 | tf_op jit(solution)/shard_map/ppermute | solution.py:378
  13.1 9.1 %collective-permute-start.3 = (bf16[128,512]{1,0:T(8,128)(2,1)S(1)}, bf16[128,512]{1,0:T(8,128)(2,1)S(1)}, u32[]{:S(2)}, u32[]{:S(2)}) collective-permute-start(bf16[128,512]{1,0:T(8,128)(2,1)S(1)} %get-tuple-element.40), channel_id=1, source_target_pairs={{0,32},{32,64},{64,96},{96,128},{128,160},{160,192},{192,224},{224... | collective-permute-start | bytes 393224 | tf_op jit(solution)/shard_map/ppermute | solution.py:378
  13.7 8.5 %collective-permute-start.5 = (bf16[128,512]{1,0:T(8,128)(2,1)S(1)}, bf16[128,512]{1,0:T(8,128)(2,1)S(1)}, u32[]{:S(2)}, u32[]{:S(2)}) collective-permute-start(bf16[128,512]{1,0:T(8,128)(2,1)S(1)} %get-tuple-element.42), channel_id=1, source_target_pairs={{0,224},{32,0},{64,32},{96,64},{128,96},{160,128},{192,160},{224,1... | collective-permute-start | bytes 393224 | tf_op jit(solution)/shard_map/ppermute | solution.py:378
  17.9 0.9 %copy-start.5 = (f32[8,17,17]{2,0,1:T(8,128)S(1)}, f32[8,17,17]{2,0,1:T(8,128)}, u32[]{:S(2)}) copy-start(f32[8,17,17]{2,0,1:T(8,128)} %param.8) | copy-start | bytes 27748
  18.8 2.0 %copy-start = (bf16[512,1536]{1,0:T(8,128)(2,1)S(1)}, bf16[512,1536]{1,0:T(8,128)(2,1)}, u32[]{:S(2)}) copy-start(bf16[512,1536]{1,0:T(8,128)(2,1)} %w.7) | copy-start | bytes 4718596
  18.8 2.0 %copy-start.2 = (bf16[1,16,16,512]{3,2,1,0:T(8,128)(2,1)S(1)}, bf16[1,16,16,512]{3,2,1,0:T(8,128)(2,1)}, u32[]{:S(2)}) copy-start(bf16[1,16,16,512]{3,2,1,0:T(8,128)(2,1)} %param.5) | copy-start | bytes 786436
  18.8 2.0 %copy-start.3 = (bf16[512,512]{1,0:T(8,128)(2,1)S(1)}, bf16[512,512]{1,0:T(8,128)(2,1)}, u32[]{:S(2)}) copy-start(bf16[512,512]{1,0:T(8,128)(2,1)} %wo.1) | copy-start | bytes 1572868
  18.8 2.0 %copy-start.4 = (bf16[1,16,16,512]{3,2,1,0:T(8,128)(2,1)S(1)}, bf16[1,16,16,512]{3,2,1,0:T(8,128)(2,1)}, u32[]{:S(2)}) copy-start(bf16[1,16,16,512]{3,2,1,0:T(8,128)(2,1)} %param.9) | copy-start | bytes 786436
  30.1 4.9 %collective-permute-start.10 = (bf16[512,1024]{1,0:T(8,128)(2,1)S(1)}, bf16[512,1024]{1,0:T(8,128)(2,1)S(1)}, u32[]{:S(2)}, u32[]{:S(2)}) collective-permute-start(bf16[512,1024]{1,0:T(8,128)(2,1)S(1)} %get-tuple-element.65), channel_id=1, source_target_pairs={{0,1},{1,0},{2,3},{3,2},{4,5},{5,4},{6,7},{7,6},{8,9},{9,8},{10,11... | collective-permute-start | bytes 3145736 | tf_op jit(solution)/shard_map/ppermute | solution.py:385
  36.3 22.3 %all-to-all-start = ((bf16[8,536,128]{2,1,0:T(8,128)(2,1)}), bf16[8,536,128]{2,1,0:T(8,128)(2,1)S(1)}, u32[]{:S(2)}, u32[]{:S(2)}) async-start(bf16[8,536,128]{2,1,0:T(8,128)(2,1)} %shard_map.93), calls=%async_computation | async-start | bytes 2195456 | tf_op jit(solution)/shard_map/all_to_all | solution.py:466
  42.1 8.7 %collective-permute-start.6 = (bf16[256,512]{1,0:T(8,128)(2,1)S(1)}, bf16[256,512]{1,0:T(8,128)(2,1)S(1)}, u32[]{:S(2)}, u32[]{:S(2)}) collective-permute-start(bf16[256,512]{1,0:T(8,128)(2,1)S(1)} %get-tuple-element.59), channel_id=1, source_target_pairs={{0,32},{32,64},{64,96},{96,128},{128,160},{160,192},{192,224},{224... | collective-permute-start | bytes 786440 | tf_op jit(solution)/shard_map/ppermute | solution.py:378
  42.2 8.7 %collective-permute-start.7 = (bf16[256,512]{1,0:T(8,128)(2,1)S(1)}, bf16[256,512]{1,0:T(8,128)(2,1)S(1)}, u32[]{:S(2)}, u32[]{:S(2)}) collective-permute-start(bf16[256,512]{1,0:T(8,128)(2,1)S(1)} %get-tuple-element.60), channel_id=1, source_target_pairs={{0,224},{32,0},{64,32},{96,64},{128,96},{160,128},{192,160},{224,1... | collective-permute-start | bytes 786440 | tf_op jit(solution)/shard_map/ppermute | solution.py:378
  59.4 13.7 %all-to-all-start.1 = ((bf16[8,8,1408]{2,1,0:T(8,128)(2,1)}), bf16[8,8,1408]{2,1,0:T(8,128)(2,1)S(1)}, u32[]{:S(2)}, u32[]{:S(2)}) async-start(bf16[8,8,1408]{2,1,0:T(8,128)(2,1)} %shard_map.94), calls=%async_computation.1 | async-start | bytes 360448 | tf_op jit(solution)/shard_map/all_to_all | solution.py:492
  64.6 16.8 %collective-permute-start.9 = (bf16[16,8,512]{2,1,0:T(8,128)(2,1)S(1)}, bf16[16,8,512]{2,1,0:T(8,128)(2,1)S(1)}, u32[]{:S(2)}, u32[]{:S(2)}) collective-permute-start(bf16[16,8,512]{2,1,0:T(8,128)(2,1)S(1)} %bitcast.30), channel_id=1, source_target_pairs={{4,0},{8,4},{12,8},{16,12},{20,16},{24,20},{28,24},{5,1},{9,5},{13... | collective-permute-start | bytes 393224 | tf_op jit(solution)/shard_map/ppermute | solution.py:382
  65.9 15.6 %collective-permute-start.8 = (bf16[16,8,512]{2,1,0:T(8,128)(2,1)S(1)}, bf16[16,8,512]{2,1,0:T(8,128)(2,1)S(1)}, u32[]{:S(2)}, u32[]{:S(2)}) collective-permute-start(bf16[16,8,512]{2,1,0:T(8,128)(2,1)S(1)} %bitcast.29), channel_id=1, source_target_pairs={{0,4},{4,8},{8,12},{12,16},{16,20},{20,24},{24,28},{1,5},{5,9},{9,... | collective-permute-start | bytes 393224 | tf_op jit(solution)/shard_map/ppermute | solution.py:382
  73.1 6.1 %collective-permute-start.11 = (f32[8,1408]{1,0:T(8,128)S(1)}, f32[8,1408]{1,0:T(8,128)S(1)}, u32[]{:S(2)}, u32[]{:S(2)}) collective-permute-start(f32[8,1408]{1,0:T(8,128)S(1)} %shard_map.95.mine), channel_id=1, source_target_pairs={{0,2},{2,0},{1,3},{3,1},{4,6},{6,4},{5,7},{7,5},{8,10},{10,8},{9,1... | collective-permute-start | bytes 135176 | tf_op jit(solution)/shard_map/ppermute | solution.py:385
  79.2 3.2 %collective-permute-start.12 = (f32[8,1408]{1,0:T(8,128)S(1)}, f32[8,1408]{1,0:T(8,128)S(1)}, u32[]{:S(2)}, u32[]{:S(2)}) collective-permute-start(f32[8,1408]{1,0:T(8,128)S(1)} %shard_map.96.here), channel_id=1, source_target_pairs={{0,1},{1,0},{2,3},{3,2},{4,5},{5,4},{6,7},{7,6},{8,9},{9,8},{10,11... | collective-permute-start | bytes 135176 | tf_op jit(solution)/shard_map/ppermute | solution.py:385

commit v9 on v8

--- a/solution.py
+++ b/solution.py
@@ -491,9 +491,8 @@
     )
     parcel = lax.all_to_all(parcel, "az", 0, 0, tiled=True)
     (mine,) = call(total_kernel, (parcel,), (whole((8, 1408), F32),), flops=1_000_000)
-    (mine,) = call(
-        add_kernel, (mine, swap(mine, "half")), (whole((8, 1408), F32),), flops=1_000_000
-    )
+    near = swap(mine, "half")
+    (mine,) = call(add_kernel, (mine, near), (whole((8, 1408), F32),), flops=1_000_000)
     rows_qkv, rows_out, total_bias = call(
         finish_kernel,
         (core, mine, swap(mine)),

time: 83.5 us -> 83.5 us (level)
  no operation moved by 1% of the time
where the time goes in v9:
time: 83.5 us; the launch traced here: 83.1 us
  starting transfers between devices  42.2 us (51%)
  waiting for transfers between devices  20.3 us (24%)
  Pallas kernels  17.8 us (21%)
  local copies, waits for them, and re-layouts  1.84 us (2%)
    pallas_call x14, Pallas kernels, call(): pl.pallas_call(kernel, out_shape=tuple(outs), in_specs=[scalar] * prefetc...  17.8 us
    ppermute x6, starting transfers between devices, turn(): return lax.ppermute(leaf, 'az', [(i, (i + step) % az) for i in range(az)])  13.2 us
    ppermute x4, starting transfers between devices, shift(): return lax.ppermute(leaf, 'rng', pairs)  10.5 us
    all_to_all x1, waiting for transfers between devices, shards(): parcel = lax.all_to_all(parcel, 'rng', 0, 0, tiled=True)  7.63 us
    ppermute x3, starting transfers between devices, swap(): return lax.ppermute(leaf, axis, [(0, 1), (1, 0)])  7.37 us
    ppermute x6, waiting for transfers between devices, turn(): return lax.ppermute(leaf, 'az', [(i, (i + step) % az) for i in range(az)])  6.01 us
    all_to_all x1, starting transfers between devices, shards(): parcel = lax.all_to_all(parcel, 'rng', 0, 0, tiled=True)  5.86 us
    all_to_all x1, starting transfers between devices, shards(): parcel = lax.all_to_all(parcel, 'az', 0, 0, tiled=True)  5.29 us
  transfers between devices with their start and end apart: 15, of which 5 were waited for; matrix products, arithmetic and copies ran while one was open for 0% of the time, Pallas kernels for 8%

profile of v9, /device:TPU:1, one launch (start us, length us, event | category | flops | bytes accessed | tf_op | source)
XLA Modules:
  0.0 83.1 jit_solution(16052204231094222184)
XLA Ops:
  0.6 0.0 copy-start.1
  0.6 0.9 %copy-done.1 = bf16[1,16,16,512]{3,2,1,0:T(8,128)(2,1)S(1)} copy-done((bf16[1,16,16,512]{3,2,1,0:T(8,128)(2,1)S(1)}, bf16[1,16,16,512]{3,2,1,0:T(8,128)(2,1)}, u32[]{:S(2)}) %copy-start.1) | copy-done | bytes 262168
  1.6 0.4 shard_map.84
  2.0 3.9 %collective-permute-start.1 = (bf16[16,8,512]{2,1,0:T(8,128)(2,1)S(1)}, bf16[16,8,512]{2,1,0:T(8,128)(2,1)S(1)}, u32[]{:S(2)}, u32[]{:S(2)}) collective-permute-start(bf16[16,8,512]{2,1,0:T(8,128)(2,1)S(1)} %get-tuple-element.38), channel_id=1, source_target_pairs={{0,4},{4,8},{8,12},{12,16},{16,20},{20,24},{24,28},{1,5},{5,9},{9,... | collective-permute-start | bytes 393224 | tf_op jit(solution)/shard_map/ppermute | solution.py:382
  6.0 1.3 %collective-permute-start.2 = (bf16[16,8,512]{2,1,0:T(8,128)(2,1)S(1)}, bf16[16,8,512]{2,1,0:T(8,128)(2,1)S(1)}, u32[]{:S(2)}, u32[]{:S(2)}) collective-permute-start(bf16[16,8,512]{2,1,0:T(8,128)(2,1)S(1)} %get-tuple-element.39), channel_id=1, source_target_pairs={{4,0},{8,4},{12,8},{16,12},{20,16},{24,20},{28,24},{5,1},{9,5},{13... | collective-permute-start | bytes 393224 | tf_op jit(solution)/shard_map/ppermute | solution.py:382
  7.3 1.7 %collective-permute-start = (bf16[8,16,512]{2,1,0:T(8,128)(2,1)S(1)}, bf16[8,16,512]{2,1,0:T(8,128)(2,1)S(1)}, u32[]{:S(2)}, u32[]{:S(2)}) collective-permute-start(bf16[8,16,512]{2,1,0:T(8,128)(2,1)S(1)} %get-tuple-element.37), channel_id=1, source_target_pairs={{0,32},{32,64},{64,96},{96,128},{128,160},{160,192},{192,224},{224... | collective-permute-start | bytes 393224 | tf_op jit(solution)/shard_map/ppermute | solution.py:378
  9.0 4.0 %collective-permute-start.4 = (bf16[8,16,512]{2,1,0:T(8,128)(2,1)S(1)}, bf16[8,16,512]{2,1,0:T(8,128)(2,1)S(1)}, u32[]{:S(2)}, u32[]{:S(2)}) collective-permute-start(bf16[8,16,512]{2,1,0:T(8,128)(2,1)S(1)} %get-tuple-element.41), channel_id=1, source_target_pairs={{0,224},{32,0},{64,32},{96,64},{128,96},{160,128},{192,160},{224,1... | collective-permute-start | bytes 393224 | tf_op jit(solution)/shard_map/ppermute | solution.py:378
  13.0 0.1 add_convert_fusion.edge
  13.1 0.0 collective-permute-done.1
  13.1 0.0 collective-permute-done.2
  13.1 0.6 collective-permute-start.3
  13.7 4.2 %collective-permute-start.5 = (bf16[128,512]{1,0:T(8,128)(2,1)S(1)}, bf16[128,512]{1,0:T(8,128)(2,1)S(1)}, u32[]{:S(2)}, u32[]{:S(2)}) collective-permute-start(bf16[128,512]{1,0:T(8,128)(2,1)S(1)} %get-tuple-element.42), channel_id=1, source_target_pairs={{0,224},{32,0},{64,32},{96,64},{128,96},{160,128},{192,160},{224,1... | collective-permute-start | bytes 393224 | tf_op jit(solution)/shard_map/ppermute | solution.py:378
  17.9 0.0 copy-start.5
  17.9 0.9 %copy-done.5 = f32[8,17,17]{2,0,1:T(8,128)S(1)} copy-done((f32[8,17,17]{2,0,1:T(8,128)S(1)}, f32[8,17,17]{2,0,1:T(8,128)}, u32[]{:S(2)}) %copy-start.5) | copy-done | bytes 9272
  18.8 0.0 copy-start
  18.8 0.0 copy-start.2
  18.8 0.0 copy-start.3
  18.8 0.0 copy-start.4
  18.8 2.0 %shard_map.87.table = f32[4,768,256]{2,1,0:T(8,128)S(1)} custom-call(s32[2]{0:T(128)S(1)} %add_convert_fusion.edge, f32[17,8,17]{2,1,0:T(8,128)S(1)} %bitcast.26), custom_call_target="tpu_custom_call" | custom-call | flops 100000000 | bytes 3154984 | tf_op jit(solution)/shard_map/pallas_call | solution.py:356
  20.8 0.0 copy-done
  20.8 0.0 copy-done.2
  20.8 0.0 copy-done.3
  20.8 0.0 copy-done.4
  20.8 0.5 shard_map.86
  21.4 0.8 %shard_map.88 = (bf16[512,512]{1,0:T(8,128)(2,1)S(1)}, bf16[512,512]{1,0:T(8,128)(2,1)S(1)}, bf16[512,512]{1,0:T(8,128)(2,1)S(1)}, bf16[512,512]{1,0:T(8,128)(2,1)S(1)}, bf16[512,512]{1,0:T(8,128)(2,1)S(1)}) custom-call(bf16[128,512]{1,0:T(8,128)(2,1)S(1)} %bitcast.23, bf16[256,512]{1,0:T(8,128)(2,1)S(1)} %bitcast.19, bf16[128,512]{1,0:T(8,128)(2,1)S(1)} %bitcast.25, ...), custom_call_target="tpu_custom_call" | custom-call | flops 1000000000 | bytes 4718592 | tf_op jit(solution)/shard_map/pallas_call | solution.py:356
  22.2 0.0 collective-permute-done
  22.2 0.0 collective-permute-done.4
  22.2 0.0 collective-permute-done.3.above
  22.2 0.0 collective-permute-done.5.below
  22.2 7.9 %shard_map.89 = (bf16[512,1024]{1,0:T(8,128)(2,1)S(1)}, bf16[1024,1024]{1,0:T(8,128)(2,1)S(1)}, bf16[2,512,256]{2,1,0:T(8,128)(2,1)S(1)}, bf16[2,256,512]{2,1,0:...) custom-call(s32[1]{0:T(128)} %bitcast.core, bf16[128,512]{1,0:T(8,128)(2,1)S(1)} %bitcast.27, ...), custom_call_target="tpu_custom_call" | custom-call | flops 10000000000 | bytes 14680068 | tf_op jit(solution)/shard_map/pallas_call | solution.py:356
  30.1 2.4 %collective-permute-start.10 = (bf16[512,1024]{1,0:T(8,128)(2,1)S(1)}, bf16[512,1024]{1,0:T(8,128)(2,1)S(1)}, u32[]{:S(2)}, u32[]{:S(2)}) collective-permute-start(bf16[512,1024]{1,0:T(8,128)(2,1)S(1)} %get-tuple-element.65), channel_id=1, source_target_pairs={{0,1},{1,0},{2,3},{3,2},{4,5},{5,4},{6,7},{7,6},{8,9},{9,8},{10,11... | collective-permute-start | bytes 3145736 | tf_op jit(solution)/shard_map/ppermute | solution.py:385
  32.5 2.5 %shard_map.90 = (bf16[512,1024]{1,0:T(8,128)(2,1)S(1)}, f32[8,384]{1,0:T(8,128)S(1)}, bf16[256,512]{1,0:T(8,128)(2,1)S(1)}, f32[256,512]{1,0:T(8,128)S(1)}, f32[...) custom-call(s32[1]{0:T(128)} %bitcast.core, bf16[512,1024]{1,0:T(8,128)(2,1)S(1)} %get-tuple-element.52.x_t, ...), custom_call_target="tpu_custom_call" | custom-call | flops 2500000000 | bytes 8663044 | tf_op jit(solution)/shard_map/pallas_call | solution.py:356
  35.0 0.0 collective-permute-done.10.came
  35.0 1.3 %shard_map.93 = bf16[8,536,128]{2,1,0:T(8,128)(2,1)} custom-call(bf16[512,1024]{1,0:T(8,128)(2,1)S(1)} %get-tuple-element.64.keep, bf16[512,1024]{1,0:T(8,128)(2,1)S(1)} %collective-permute-done.10.came, f32[8,384]{1,0:T(8,128)S(1)} %get-tuple-element.66.bias), custom_call_target="tpu_custom_call" | custom-call | flops 1000000 | bytes 3207168 | tf_op jit(solution)/shard_map/pallas_call | solution.py:356
  36.3 5.9 %all-to-all-start = ((bf16[8,536,128]{2,1,0:T(8,128)(2,1)}), bf16[8,536,128]{2,1,0:T(8,128)(2,1)S(1)}, u32[]{:S(2)}, u32[]{:S(2)}) async-start(bf16[8,536,128]{2,1,0:T(8,128)(2,1)} %shard_map.93), calls=%async_computation | async-start | bytes 2195456 | tf_op jit(solution)/shard_map/all_to_all | solution.py:466
  42.1 0.0 collective-permute-start.6
  42.2 2.7 %collective-permute-start.7 = (bf16[256,512]{1,0:T(8,128)(2,1)S(1)}, bf16[256,512]{1,0:T(8,128)(2,1)S(1)}, u32[]{:S(2)}, u32[]{:S(2)}) collective-permute-start(bf16[256,512]{1,0:T(8,128)(2,1)S(1)} %get-tuple-element.60), channel_id=1, source_target_pairs={{0,224},{32,0},{64,32},{96,64},{128,96},{160,128},{192,160},{224,1... | collective-permute-start | bytes 786440 | tf_op jit(solution)/shard_map/ppermute | solution.py:378
  44.8 6.0 %collective-permute-done.6.up = bf16[256,512]{1,0:T(8,128)(2,1)S(1)} collective-permute-done((bf16[256,512]{1,0:T(8,128)(2,1)S(1)}, bf16[256,512]{1,0:T(8,128)(2,1)S(1)}, u32[]{:S(2)}, u32[]{:S(2)}) %collective-permute-start.6) | collective-permute-done | bytes 262176 | tf_op jit(solution)/shard_map/ppermute | solution.py:378
  50.8 0.0 collective-permute-done.7.down
  50.8 0.1 shard_map.91
  50.9 7.6 %all-to-all-done.came = bf16[8,536,128]{2,1,0:T(8,128)(2,1)S(1)} async-done(((bf16[8,536,128]{2,1,0:T(8,128)(2,1)}), bf16[8,536,128]{2,1,0:T(8,128)(2,1)S(1)}, u32[]{:S(2)}, u32[]{:S(2)}) %all-to-all-start) | async-done | bytes 1097760 | tf_op jit(solution)/shard_map/all_to_all | solution.py:466
  58.5 0.8 shard_map.94
  59.4 5.3 %all-to-all-start.1 = ((bf16[8,8,1408]{2,1,0:T(8,128)(2,1)}), bf16[8,8,1408]{2,1,0:T(8,128)(2,1)S(1)}, u32[]{:S(2)}, u32[]{:S(2)}) async-start(bf16[8,8,1408]{2,1,0:T(8,128)(2,1)} %shard_map.94), calls=%async_computation.1 | async-start | bytes 360448 | tf_op jit(solution)/shard_map/all_to_all | solution.py:492
  64.6 1.3 %collective-permute-start.9 = (bf16[16,8,512]{2,1,0:T(8,128)(2,1)S(1)}, bf16[16,8,512]{2,1,0:T(8,128)(2,1)S(1)}, u32[]{:S(2)}, u32[]{:S(2)}) collective-permute-start(bf16[16,8,512]{2,1,0:T(8,128)(2,1)S(1)} %bitcast.30), channel_id=1, source_target_pairs={{4,0},{8,4},{12,8},{16,12},{20,16},{24,20},{28,24},{5,1},{9,5},{13... | collective-permute-start | bytes 393224 | tf_op jit(solution)/shard_map/ppermute | solution.py:382
  65.9 4.0 %collective-permute-start.8 = (bf16[16,8,512]{2,1,0:T(8,128)(2,1)S(1)}, bf16[16,8,512]{2,1,0:T(8,128)(2,1)S(1)}, u32[]{:S(2)}, u32[]{:S(2)}) collective-permute-start(bf16[16,8,512]{2,1,0:T(8,128)(2,1)S(1)} %bitcast.29), channel_id=1, source_target_pairs={{0,4},{4,8},{8,12},{12,16},{16,20},{20,24},{24,28},{1,5},{5,9},{9,... | collective-permute-start | bytes 393224 | tf_op jit(solution)/shard_map/ppermute | solution.py:382
  69.9 3.1 %all-to-all-done.1.came = bf16[8,8,1408]{2,1,0:T(8,128)(2,1)S(1)} async-done(((bf16[8,8,1408]{2,1,0:T(8,128)(2,1)}), bf16[8,8,1408]{2,1,0:T(8,128)(2,1)S(1)}, u32[]{:S(2)}, u32[]{:S(2)}) %all-to-all-start.1) | async-done | bytes 180256 | tf_op jit(solution)/shard_map/all_to_all | solution.py:492
  73.1 2.7 %collective-permute-start.11 = (f32[8,1408]{1,0:T(8,128)S(1)}, f32[8,1408]{1,0:T(8,128)S(1)}, u32[]{:S(2)}, u32[]{:S(2)}) collective-permute-start(f32[8,1408]{1,0:T(8,128)S(1)} %shard_map.95.mine), channel_id=1, source_target_pairs={{0,2},{2,0},{1,3},{3,1},{4,6},{6,4},{5,7},{7,5},{8,10},{10,8},{9,1... | collective-permute-start | bytes 135176 | tf_op jit(solution)/shard_map/ppermute | solution.py:385
  75.8 3.4 %collective-permute-done.11.came = f32[8,1408]{1,0:T(8,128)S(1)} collective-permute-done((f32[8,1408]{1,0:T(8,128)S(1)}, f32[8,1408]{1,0:T(8,128)S(1)}, u32[]{:S(2)}, u32[]{:S(2)}) %collective-permute-start.11) | collective-permute-done | bytes 45088 | tf_op jit(solution)/shard_map/ppermute | solution.py:385
  79.2 2.3 %collective-permute-start.12 = (f32[8,1408]{1,0:T(8,128)S(1)}, f32[8,1408]{1,0:T(8,128)S(1)}, u32[]{:S(2)}, u32[]{:S(2)}) collective-permute-start(f32[8,1408]{1,0:T(8,128)S(1)} %shard_map.96.here), channel_id=1, source_target_pairs={{0,1},{1,0},{2,3},{3,2},{4,5},{5,4},{6,7},{7,6},{8,9},{9,8},{10,11... | collective-permute-start | bytes 135176 | tf_op jit(solution)/shard_map/ppermute | solution.py:385
  81.5 0.0 collective-permute-done.9.east
  81.5 0.0 collective-permute-done.8.west
  81.5 0.8 shard_map.92
  82.2 0.1 collective-permute-done.12.there
  82.3 0.7 shard_map.97
  (3 shorter events, 0.1 us)
Async XLA Ops:
  0.6 1.0 %copy-start.1 = (bf16[1,16,16,512]{3,2,1,0:T(8,128)(2,1)S(1)}, bf16[1,16,16,512]{3,2,1,0:T(8,128)(2,1)}, u32[]{:S(2)}) copy-start(bf16[1,16,16,512]{3,2,1,0:T(8,128)(2,1)} %param.5) | copy-start | bytes 786436
  2.0 11.1 %collective-permute-start.1 = (bf16[16,8,512]{2,1,0:T(8,128)(2,1)S(1)}, bf16[16,8,512]{2,1,0:T(8,128)(2,1)S(1)}, u32[]{:S(2)}, u32[]{:S(2)}) collective-permute-start(bf16[16,8,512]{2,1,0:T(8,128)(2,1)S(1)} %get-tuple-element.38), channel_id=1, source_target_pairs={{0,4},{4,8},{8,12},{12,16},{16,20},{20,24},{24,28},{1,5},{5,9},{9,... | collective-permute-start | bytes 393224 | tf_op jit(solution)/shard_map/ppermute | solution.py:382
  6.0 7.1 %collective-permute-start.2 = (bf16[16,8,512]{2,1,0:T(8,128)(2,1)S(1)}, bf16[16,8,512]{2,1,0:T(8,128)(2,1)S(1)}, u32[]{:S(2)}, u32[]{:S(2)}) collective-permute-start(bf16[16,8,512]{2,1,0:T(8,128)(2,1)S(1)} %get-tuple-element.39), channel_id=1, source_target_pairs={{4,0},{8,4},{12,8},{16,12},{20,16},{24,20},{28,24},{5,1},{9,5},{13... | collective-permute-start | bytes 393224 | tf_op jit(solution)/shard_map/ppermute | solution.py:382
  7.3 15.0 %collective-permute-start = (bf16[8,16,512]{2,1,0:T(8,128)(2,1)S(1)}, bf16[8,16,512]{2,1,0:T(8,128)(2,1)S(1)}, u32[]{:S(2)}, u32[]{:S(2)}) collective-permute-start(bf16[8,16,512]{2,1,0:T(8,128)(2,1)S(1)} %get-tuple-element.37), channel_id=1, source_target_pairs={{0,32},{32,64},{64,96},{96,128},{128,160},{160,192},{192,224},{224... | collective-permute-start | bytes 393224 | tf_op jit(solution)/shard_map/ppermute | solution.py:378
  9.0 13.3 %collective-permute-start.4 = (bf16[8,16,512]{2,1,0:T(8,128)(2,1)S(1)}, bf16[8,16,512]{2,1,0:T(8,128)(2,1)S(1)}, u32[]{:S(2)}, u32[]{:S(2)}) collective-permute-start(bf16[8,16,512]{2,1,0:T(8,128)(2,1)S(1)} %get-tuple-element.41), channel_id=1, source_target_pairs={{0,224},{32,0},{64,32},{96,64},{128,96},{160,128},{192,160},{224,1... | collective-permute-start | bytes 393224 | tf_op jit(solution)/shard_map/ppermute | solution.py:378
  13.1 9.1 %collective-permute-start.3 = (bf16[128,512]{1,0:T(8,128)(2,1)S(1)}, bf16[128,512]{1,0:T(8,128)(2,1)S(1)}, u32[]{:S(2)}, u32[]{:S(2)}) collective-permute-start(bf16[128,512]{1,0:T(8,128)(2,1)S(1)} %get-tuple-element.40), channel_id=1, source_target_pairs={{0,32},{32,64},{64,96},{96,128},{128,160},{160,192},{192,224},{224... | collective-permute-start | bytes 393224 | tf_op jit(solution)/shard_map/ppermute | solution.py:378
  13.7 8.5 %collective-permute-start.5 = (bf16[128,512]{1,0:T(8,128)(2,1)S(1)}, bf16[128,512]{1,0:T(8,128)(2,1)S(1)}, u32[]{:S(2)}, u32[]{:S(2)}) collective-permute-start(bf16[128,512]{1,0:T(8,128)(2,1)S(1)} %get-tuple-element.42), channel_id=1, source_target_pairs={{0,224},{32,0},{64,32},{96,64},{128,96},{160,128},{192,160},{224,1... | collective-permute-start | bytes 393224 | tf_op jit(solution)/shard_map/ppermute | solution.py:378
  17.9 0.9 %copy-start.5 = (f32[8,17,17]{2,0,1:T(8,128)S(1)}, f32[8,17,17]{2,0,1:T(8,128)}, u32[]{:S(2)}) copy-start(f32[8,17,17]{2,0,1:T(8,128)} %param.8) | copy-start | bytes 27748
  18.8 2.0 %copy-start = (bf16[512,1536]{1,0:T(8,128)(2,1)S(1)}, bf16[512,1536]{1,0:T(8,128)(2,1)}, u32[]{:S(2)}) copy-start(bf16[512,1536]{1,0:T(8,128)(2,1)} %w.7) | copy-start | bytes 4718596
  18.8 2.0 %copy-start.2 = (bf16[1,16,16,512]{3,2,1,0:T(8,128)(2,1)S(1)}, bf16[1,16,16,512]{3,2,1,0:T(8,128)(2,1)}, u32[]{:S(2)}) copy-start(bf16[1,16,16,512]{3,2,1,0:T(8,128)(2,1)} %param.5) | copy-start | bytes 786436
  18.8 2.0 %copy-start.3 = (bf16[512,512]{1,0:T(8,128)(2,1)S(1)}, bf16[512,512]{1,0:T(8,128)(2,1)}, u32[]{:S(2)}) copy-start(bf16[512,512]{1,0:T(8,128)(2,1)} %wo.1) | copy-start | bytes 1572868
  18.8 2.0 %copy-start.4 = (bf16[1,16,16,512]{3,2,1,0:T(8,128)(2,1)S(1)}, bf16[1,16,16,512]{3,2,1,0:T(8,128)(2,1)}, u32[]{:S(2)}) copy-start(bf16[1,16,16,512]{3,2,1,0:T(8,128)(2,1)} %param.9) | copy-start | bytes 786436
  30.1 4.9 %collective-permute-start.10 = (bf16[512,1024]{1,0:T(8,128)(2,1)S(1)}, bf16[512,1024]{1,0:T(8,128)(2,1)S(1)}, u32[]{:S(2)}, u32[]{:S(2)}) collective-permute-start(bf16[512,1024]{1,0:T(8,128)(2,1)S(1)} %get-tuple-element.65), channel_id=1, source_target_pairs={{0,1},{1,0},{2,3},{3,2},{4,5},{5,4},{6,7},{7,6},{8,9},{9,8},{10,11... | collective-permute-start | bytes 3145736 | tf_op jit(solution)/shard_map/ppermute | solution.py:385
  36.3 22.3 %all-to-all-start = ((bf16[8,536,128]{2,1,0:T(8,128)(2,1)}), bf16[8,536,128]{2,1,0:T(8,128)(2,1)S(1)}, u32[]{:S(2)}, u32[]{:S(2)}) async-start(bf16[8,536,128]{2,1,0:T(8,128)(2,1)} %shard_map.93), calls=%async_computation | async-start | bytes 2195456 | tf_op jit(solution)/shard_map/all_to_all | solution.py:466
  42.1 8.7 %collective-permute-start.6 = (bf16[256,512]{1,0:T(8,128)(2,1)S(1)}, bf16[256,512]{1,0:T(8,128)(2,1)S(1)}, u32[]{:S(2)}, u32[]{:S(2)}) collective-permute-start(bf16[256,512]{1,0:T(8,128)(2,1)S(1)} %get-tuple-element.59), channel_id=1, source_target_pairs={{0,32},{32,64},{64,96},{96,128},{128,160},{160,192},{192,224},{224... | collective-permute-start | bytes 786440 | tf_op jit(solution)/shard_map/ppermute | solution.py:378
  42.2 8.7 %collective-permute-start.7 = (bf16[256,512]{1,0:T(8,128)(2,1)S(1)}, bf16[256,512]{1,0:T(8,128)(2,1)S(1)}, u32[]{:S(2)}, u32[]{:S(2)}) collective-permute-start(bf16[256,512]{1,0:T(8,128)(2,1)S(1)} %get-tuple-element.60), channel_id=1, source_target_pairs={{0,224},{32,0},{64,32},{96,64},{128,96},{160,128},{192,160},{224,1... | collective-permute-start | bytes 786440 | tf_op jit(solution)/shard_map/ppermute | solution.py:378
  59.4 13.7 %all-to-all-start.1 = ((bf16[8,8,1408]{2,1,0:T(8,128)(2,1)}), bf16[8,8,1408]{2,1,0:T(8,128)(2,1)S(1)}, u32[]{:S(2)}, u32[]{:S(2)}) async-start(bf16[8,8,1408]{2,1,0:T(8,128)(2,1)} %shard_map.94), calls=%async_computation.1 | async-start | bytes 360448 | tf_op jit(solution)/shard_map/all_to_all | solution.py:492
  64.6 16.8 %collective-permute-start.9 = (bf16[16,8,512]{2,1,0:T(8,128)(2,1)S(1)}, bf16[16,8,512]{2,1,0:T(8,128)(2,1)S(1)}, u32[]{:S(2)}, u32[]{:S(2)}) collective-permute-start(bf16[16,8,512]{2,1,0:T(8,128)(2,1)S(1)} %bitcast.30), channel_id=1, source_target_pairs={{4,0},{8,4},{12,8},{16,12},{20,16},{24,20},{28,24},{5,1},{9,5},{13... | collective-permute-start | bytes 393224 | tf_op jit(solution)/shard_map/ppermute | solution.py:382
  65.9 15.6 %collective-permute-start.8 = (bf16[16,8,512]{2,1,0:T(8,128)(2,1)S(1)}, bf16[16,8,512]{2,1,0:T(8,128)(2,1)S(1)}, u32[]{:S(2)}, u32[]{:S(2)}) collective-permute-start(bf16[16,8,512]{2,1,0:T(8,128)(2,1)S(1)} %bitcast.29), channel_id=1, source_target_pairs={{0,4},{4,8},{8,12},{12,16},{16,20},{20,24},{24,28},{1,5},{5,9},{9,... | collective-permute-start | bytes 393224 | tf_op jit(solution)/shard_map/ppermute | solution.py:382
  73.1 6.1 %collective-permute-start.11 = (f32[8,1408]{1,0:T(8,128)S(1)}, f32[8,1408]{1,0:T(8,128)S(1)}, u32[]{:S(2)}, u32[]{:S(2)}) collective-permute-start(f32[8,1408]{1,0:T(8,128)S(1)} %shard_map.95.mine), channel_id=1, source_target_pairs={{0,2},{2,0},{1,3},{3,1},{4,6},{6,4},{5,7},{7,5},{8,10},{10,8},{9,1... | collective-permute-start | bytes 135176 | tf_op jit(solution)/shard_map/ppermute | solution.py:385
  79.2 3.2 %collective-permute-start.12 = (f32[8,1408]{1,0:T(8,128)S(1)}, f32[8,1408]{1,0:T(8,128)S(1)}, u32[]{:S(2)}, u32[]{:S(2)}) collective-permute-start(f32[8,1408]{1,0:T(8,128)S(1)} %shard_map.96.here), channel_id=1, source_target_pairs={{0,1},{1,0},{2,3},{3,2},{4,5},{5,4},{6,7},{7,6},{8,9},{9,8},{10,11... | collective-permute-start | bytes 135176 | tf_op jit(solution)/shard_map/ppermute | solution.py:385

commit v10 on v9

--- a/solution.py
+++ b/solution.py
@@ -62,7 +62,9 @@
     da_t[...] = d_attended.T
 
 
-def table_kernel(edge, bias, table):
+def table_kernel(edge, bias_far, table, bias, done):
+    copy = pltpu.make_async_copy(bias_far, bias, done)
+    copy.start()
     pick = (iota((17, 512), 0) == 23 - (iota((17, 512), 1) >> 4)).astype(F32)
     range_row = iota((32, 512), 0)
     lane = iota((32, 512), 1)
@@ -70,6 +72,7 @@
     first = jnp.where(edge[0] == 1, 8, 0)
     last = jnp.where(edge[1] == 1, 24, 32)
     present = (range_row >= first) & (range_row < last) & (lane >= 112) & (lane < 384)
+    copy.wait()
     for head in range(8):
         pair, lanes = head // 2, slice(head % 2 * 128, head % 2 * 128 + 128)
         head_rows = dot(bias[:, head, :], pick, TN, exact=True)
@@ -294,18 +297,23 @@
     out[:, 8:16] = (own[:, 8:16] + east[...].astype(F32)).astype(BF16)
 
 
-def pack_kernel(keep, came, bias, parcel):
+def pack_kernel(keep, came, bias, parcel, block, done):
     count = parcel.shape[0]
     rows = keep.shape[0] // count
     low = bias[...].astype(BF16)
+    copies = []
     for r in range(count):
         at = slice(r * rows, r * rows + rows)
         both = (keep[at].astype(F32) + came[at].astype(F32)).astype(BF16)
         for n in range(8):
-            parcel[r, n * rows : n * rows + rows] = both[:, n * 128 : n * 128 + 128]
+            block[r, n * rows : n * rows + rows] = both[:, n * 128 : n * 128 + 128]
         for n in range(3):
             to = 8 * rows + n * 8
-            parcel[r, to : to + 8] = low[:, n * 128 : n * 128 + 128]
+            block[r, to : to + 8] = low[:, n * 128 : n * 128 + 128]
+        copies.append(pltpu.make_async_copy(block.at[r], parcel.at[r], done.at[r]))
+        copies[-1].start()
+    for copy in copies:
+        copy.wait()
 
 
 def regroup_kernel(came, _, parcel):
@@ -349,7 +357,7 @@
     return jax.ShapeDtypeStruct(shape, dtype)
 
 
-def call(kernel, operands, outs, scratch=(), prefetch=0, flops=0, limit=16, untouched=0, far=0):
+def call(kernel, operands, outs, scratch=(), prefetch=0, flops=0, limit=16, untouched=0, far=0, outside=False):
     spec = pl.BlockSpec(memory_space=pltpu.VMEM)
     scalar = pl.BlockSpec(memory_space=pltpu.SMEM)
     size = sum(leaf.size * leaf.dtype.itemsize for leaf in tuple(operands) + tuple(outs))
@@ -360,7 +368,7 @@
         + [spec] * (len(operands) - prefetch - untouched - far)
         + [pl.BlockSpec(memory_space=pl.ANY)] * untouched
         + [pl.BlockSpec(memory_space=pltpu.HBM)] * far,
-        out_specs=tuple([spec] * len(outs)),
+        out_specs=tuple([pl.BlockSpec(memory_space=pl.ANY) if outside else spec] * len(outs)),
         scratch_shapes=list(scratch),
         compiler_params=pltpu.CompilerParams(vmem_limit_bytes=limit * MIB),
         cost_estimate=pl.CostEstimate(flops=flops, bytes_accessed=size, transcendentals=0),
@@ -386,7 +394,7 @@
 
     to_right, to_left, to_next, to_last = call(
         slices_kernel,
-        (cells,),
+        (pltpu.with_memory_space_constraint(cells, pltpu.HBM),),
         (whole((16, 8, width), BF16),) * 2 + (whole((8, 16, width), BF16),) * 2,
         scratch=(pltpu.SemaphoreType.DMA((4,)),),
         far=1,
@@ -408,9 +416,16 @@
 
     (table,) = call(
         table_kernel,
-        (edge, jnp.transpose(relative_bias, (1, 0, 2))),
+        (
+            edge,
+            pltpu.with_memory_space_constraint(
+                jnp.transpose(relative_bias, (1, 0, 2)), pltpu.HBM
+            ),
+        ),
         (whole((4, 768, 256), F32),),
+        scratch=(pltpu.VMEM((17, 8, 17), F32), pltpu.SemaphoreType.DMA(())),
         prefetch=1,
+        far=1,
         flops=100_000_000,
         limit=12,
     )
@@ -461,6 +476,10 @@
         pack_kernel,
         (g_keep, came, g_bias),
         (whole((rng, 64 * az + 24, 128), BF16),),
+        scratch=(
+            pltpu.VMEM((rng, 64 * az + 24, 128), BF16), pltpu.SemaphoreType.DMA((rng,)),
+        ),
+        outside=True,
         flops=1_000_000,
     )
     parcel = lax.all_to_all(parcel, "rng", 0, 0, tiled=True)

time: 83.5 us -> 83.3 us (level)
  local copies, waits for them, and re-layouts: 1.84 us -> 0.01 us
  Pallas kernels: 17.8 us -> 19.5 us
    unnamed x12 -> x8, local copies, waits for them, and re-layouts: 1.84 us -> 0.01 us
    pallas_call x14, Pallas kernels: 17.8 us -> 19.5 us  [call(): pl.pallas_call(kernel, out_shape=tuple(outs), in_specs=[scalar] * prefetc...]
  transfers between devices with their start and end apart: 15 -> 15, of which waited for: 5 -> 5; matrix products, arithmetic and copies ran while one was open for 0% -> 0% of each run, Pallas kernels for 8% -> 9%
where the time goes in v10:
time: 83.3 us; the launch traced here: 83 us
  starting transfers between devices  42.3 us (51%)
  waiting for transfers between devices  20.3 us (24%)
  Pallas kernels  19.5 us (23%)
    pallas_call x14, Pallas kernels, call(): pl.pallas_call(kernel, out_shape=tuple(outs), in_specs=[scalar] * prefetc...  19.5 us
    ppermute x6, starting transfers between devices, turn(): return lax.ppermute(leaf, 'az', [(i, (i + step) % az) for i in range(az)])  13.2 us
    ppermute x4, starting transfers between devices, shift(): return lax.ppermute(leaf, 'rng', pairs)  10.5 us
    all_to_all x1, waiting for transfers between devices, shards(): parcel = lax.all_to_all(parcel, 'rng', 0, 0, tiled=True)  7.64 us
    ppermute x3, starting transfers between devices, swap(): return lax.ppermute(leaf, axis, [(0, 1), (1, 0)])  7.39 us
    ppermute x6, waiting for transfers between devices, turn(): return lax.ppermute(leaf, 'az', [(i, (i + step) % az) for i in range(az)])  6 us
    all_to_all x1, starting transfers between devices, shards(): parcel = lax.all_to_all(parcel, 'rng', 0, 0, tiled=True)  5.87 us
    all_to_all x1, starting transfers between devices, shards(): parcel = lax.all_to_all(parcel, 'az', 0, 0, tiled=True)  5.3 us
  transfers between devices with their start and end apart: 15, of which 5 were waited for; matrix products, arithmetic and copies ran while one was open for 0% of the time, Pallas kernels for 9%

profile of v10, /device:TPU:1, one launch (start us, length us, event | category | flops | bytes accessed | tf_op | source)
XLA Modules:
  0.0 83.0 jit_solution(16892885154782458898)
XLA Ops:
  0.6 1.1 %shard_map.84 = (bf16[16,8,512]{2,1,0:T(8,128)(2,1)S(1)}, bf16[16,8,512]{2,1,0:T(8,128)(2,1)S(1)}, bf16[8,16,512]{2,1,0:T(8,128)(2,1)S(1)}, bf16[8,16,512]{2,1,0:T(8,128)(2,1)S(1)}) custom-call(bf16[16,16,512]{2,1,0:T(8,128)(2,1)} %bitcast.17), custom_call_target="tpu_custom_call" | custom-call | flops 1000000 | bytes 786432 | tf_op jit(solution)/shard_map/pallas_call | solution.py:364
  1.8 3.9 %collective-permute-start.1 = (bf16[16,8,512]{2,1,0:T(8,128)(2,1)S(1)}, bf16[16,8,512]{2,1,0:T(8,128)(2,1)S(1)}, u32[]{:S(2)}, u32[]{:S(2)}) collective-permute-start(bf16[16,8,512]{2,1,0:T(8,128)(2,1)S(1)} %get-tuple-element.38), channel_id=1, source_target_pairs={{0,4},{4,8},{8,12},{12,16},{16,20},{20,24},{24,28},{1,5},{5,9},{9,... | collective-permute-start | bytes 393224 | tf_op jit(solution)/shard_map/ppermute | solution.py:390
  5.7 1.3 %collective-permute-start.2 = (bf16[16,8,512]{2,1,0:T(8,128)(2,1)S(1)}, bf16[16,8,512]{2,1,0:T(8,128)(2,1)S(1)}, u32[]{:S(2)}, u32[]{:S(2)}) collective-permute-start(bf16[16,8,512]{2,1,0:T(8,128)(2,1)S(1)} %get-tuple-element.39), channel_id=1, source_target_pairs={{4,0},{8,4},{12,8},{16,12},{20,16},{24,20},{28,24},{5,1},{9,5},{13... | collective-permute-start | bytes 393224 | tf_op jit(solution)/shard_map/ppermute | solution.py:390
  7.0 1.7 %collective-permute-start = (bf16[8,16,512]{2,1,0:T(8,128)(2,1)S(1)}, bf16[8,16,512]{2,1,0:T(8,128)(2,1)S(1)}, u32[]{:S(2)}, u32[]{:S(2)}) collective-permute-start(bf16[8,16,512]{2,1,0:T(8,128)(2,1)S(1)} %get-tuple-element.37), channel_id=1, source_target_pairs={{0,32},{32,64},{64,96},{96,128},{128,160},{160,192},{192,224},{224... | collective-permute-start | bytes 393224 | tf_op jit(solution)/shard_map/ppermute | solution.py:386
  8.7 4.0 %collective-permute-start.4 = (bf16[8,16,512]{2,1,0:T(8,128)(2,1)S(1)}, bf16[8,16,512]{2,1,0:T(8,128)(2,1)S(1)}, u32[]{:S(2)}, u32[]{:S(2)}) collective-permute-start(bf16[8,16,512]{2,1,0:T(8,128)(2,1)S(1)} %get-tuple-element.41), channel_id=1, source_target_pairs={{0,224},{32,0},{64,32},{96,64},{128,96},{160,128},{192,160},{224,1... | collective-permute-start | bytes 393224 | tf_op jit(solution)/shard_map/ppermute | solution.py:386
  12.8 0.1 add_convert_fusion.edge
  12.8 0.0 collective-permute-done.1
  12.8 0.0 collective-permute-done.2
  12.9 0.6 collective-permute-start.3
  13.5 4.2 %collective-permute-start.5 = (bf16[128,512]{1,0:T(8,128)(2,1)S(1)}, bf16[128,512]{1,0:T(8,128)(2,1)S(1)}, u32[]{:S(2)}, u32[]{:S(2)}) collective-permute-start(bf16[128,512]{1,0:T(8,128)(2,1)S(1)} %get-tuple-element.42), channel_id=1, source_target_pairs={{0,224},{32,0},{64,32},{96,64},{128,96},{160,128},{192,160},{224,1... | collective-permute-start | bytes 393224 | tf_op jit(solution)/shard_map/ppermute | solution.py:386
  17.7 0.0 copy-start
  17.7 0.0 copy-start.1
  17.7 0.0 copy-start.2
  17.7 0.0 copy-start.3
  17.7 3.1 %shard_map.87.table = f32[4,768,256]{2,1,0:T(8,128)S(1)} custom-call(s32[2]{0:T(128)S(1)} %add_convert_fusion.edge, f32[17,8,17]{2,1,0:T(8,128)} %bitcast.31), custom_call_target="tpu_custom_call" | custom-call | flops 100000000 | bytes 3154984 | tf_op jit(solution)/shard_map/pallas_call | solution.py:364
  20.8 0.0 copy-done
  20.8 0.0 copy-done.1
  20.8 0.0 copy-done.2
  20.8 0.0 copy-done.3
  20.9 0.5 shard_map.86
  21.4 0.8 shard_map.88
  22.2 0.0 collective-permute-done
  22.2 0.0 collective-permute-done.4
  22.2 0.0 collective-permute-done.3.above
  22.2 0.0 collective-permute-done.5.below
  22.3 7.8 %shard_map.89 = (bf16[512,1024]{1,0:T(8,128)(2,1)S(1)}, bf16[1024,1024]{1,0:T(8,128)(2,1)S(1)}, bf16[2,512,256]{2,1,0:T(8,128)(2,1)S(1)}, bf16[2,256,512]{2,1,0:...) custom-call(s32[1]{0:T(128)} %bitcast.core, bf16[128,512]{1,0:T(8,128)(2,1)S(1)} %bitcast.26, ...), custom_call_target="tpu_custom_call" | custom-call | flops 10000000000 | bytes 14680068 | tf_op jit(solution)/shard_map/pallas_call | solution.py:364
  30.1 2.4 %collective-permute-start.10 = (bf16[512,1024]{1,0:T(8,128)(2,1)S(1)}, bf16[512,1024]{1,0:T(8,128)(2,1)S(1)}, u32[]{:S(2)}, u32[]{:S(2)}) collective-permute-start(bf16[512,1024]{1,0:T(8,128)(2,1)S(1)} %get-tuple-element.65), channel_id=1, source_target_pairs={{0,1},{1,0},{2,3},{3,2},{4,5},{5,4},{6,7},{7,6},{8,9},{9,8},{10,11... | collective-permute-start | bytes 3145736 | tf_op jit(solution)/shard_map/ppermute | solution.py:393
  32.5 2.5 %shard_map.90 = (bf16[512,1024]{1,0:T(8,128)(2,1)S(1)}, f32[8,384]{1,0:T(8,128)S(1)}, bf16[256,512]{1,0:T(8,128)(2,1)S(1)}, f32[256,512]{1,0:T(8,128)S(1)}, f32[...) custom-call(s32[1]{0:T(128)} %bitcast.core, bf16[512,1024]{1,0:T(8,128)(2,1)S(1)} %get-tuple-element.52.x_t, ...), custom_call_target="tpu_custom_call" | custom-call | flops 2500000000 | bytes 8663044 | tf_op jit(solution)/shard_map/pallas_call | solution.py:364
  35.0 0.0 collective-permute-done.10.came
  35.0 1.1 %shard_map.93 = bf16[8,536,128]{2,1,0:T(8,128)(2,1)} custom-call(bf16[512,1024]{1,0:T(8,128)(2,1)S(1)} %get-tuple-element.64.keep, bf16[512,1024]{1,0:T(8,128)(2,1)S(1)} %collective-permute-done.10.came, f32[8,384]{1,0:T(8,128)S(1)} %get-tuple-element.66.bias), custom_call_target="tpu_custom_call" | custom-call | flops 1000000 | bytes 3207168 | tf_op jit(solution)/shard_map/pallas_call | solution.py:364
  36.2 5.9 %all-to-all-start = ((bf16[8,536,128]{2,1,0:T(8,128)(2,1)}), bf16[8,536,128]{2,1,0:T(8,128)(2,1)S(1)}, u32[]{:S(2)}, u32[]{:S(2)}) async-start(bf16[8,536,128]{2,1,0:T(8,128)(2,1)} %shard_map.93), calls=%async_computation | async-start | bytes 2195456 | tf_op jit(solution)/shard_map/all_to_all | solution.py:485
  42.0 0.0 collective-permute-start.6
  42.0 2.7 %collective-permute-start.7 = (bf16[256,512]{1,0:T(8,128)(2,1)S(1)}, bf16[256,512]{1,0:T(8,128)(2,1)S(1)}, u32[]{:S(2)}, u32[]{:S(2)}) collective-permute-start(bf16[256,512]{1,0:T(8,128)(2,1)S(1)} %get-tuple-element.60), channel_id=1, source_target_pairs={{0,224},{32,0},{64,32},{96,64},{128,96},{160,128},{192,160},{224,1... | collective-permute-start | bytes 786440 | tf_op jit(solution)/shard_map/ppermute | solution.py:386
  44.7 6.0 %collective-permute-done.6.up = bf16[256,512]{1,0:T(8,128)(2,1)S(1)} collective-permute-done((bf16[256,512]{1,0:T(8,128)(2,1)S(1)}, bf16[256,512]{1,0:T(8,128)(2,1)S(1)}, u32[]{:S(2)}, u32[]{:S(2)}) %collective-permute-start.6) | collective-permute-done | bytes 262176 | tf_op jit(solution)/shard_map/ppermute | solution.py:386
  50.7 0.0 collective-permute-done.7.down
  50.7 0.1 shard_map.91
  50.8 7.6 %all-to-all-done.came = bf16[8,536,128]{2,1,0:T(8,128)(2,1)S(1)} async-done(((bf16[8,536,128]{2,1,0:T(8,128)(2,1)}), bf16[8,536,128]{2,1,0:T(8,128)(2,1)S(1)}, u32[]{:S(2)}, u32[]{:S(2)}) %all-to-all-start) | async-done | bytes 1097760 | tf_op jit(solution)/shard_map/all_to_all | solution.py:485
  58.4 0.8 shard_map.94
  59.2 5.3 %all-to-all-start.1 = ((bf16[8,8,1408]{2,1,0:T(8,128)(2,1)}), bf16[8,8,1408]{2,1,0:T(8,128)(2,1)S(1)}, u32[]{:S(2)}, u32[]{:S(2)}) async-start(bf16[8,8,1408]{2,1,0:T(8,128)(2,1)} %shard_map.94), calls=%async_computation.1 | async-start | bytes 360448 | tf_op jit(solution)/shard_map/all_to_all | solution.py:511
  64.5 1.3 %collective-permute-start.9 = (bf16[16,8,512]{2,1,0:T(8,128)(2,1)S(1)}, bf16[16,8,512]{2,1,0:T(8,128)(2,1)S(1)}, u32[]{:S(2)}, u32[]{:S(2)}) collective-permute-start(bf16[16,8,512]{2,1,0:T(8,128)(2,1)S(1)} %bitcast.29), channel_id=1, source_target_pairs={{4,0},{8,4},{12,8},{16,12},{20,16},{24,20},{28,24},{5,1},{9,5},{13... | collective-permute-start | bytes 393224 | tf_op jit(solution)/shard_map/ppermute | solution.py:390
  65.8 4.0 %collective-permute-start.8 = (bf16[16,8,512]{2,1,0:T(8,128)(2,1)S(1)}, bf16[16,8,512]{2,1,0:T(8,128)(2,1)S(1)}, u32[]{:S(2)}, u32[]{:S(2)}) collective-permute-start(bf16[16,8,512]{2,1,0:T(8,128)(2,1)S(1)} %bitcast.28), channel_id=1, source_target_pairs={{0,4},{4,8},{8,12},{12,16},{16,20},{20,24},{24,28},{1,5},{5,9},{9,... | collective-permute-start | bytes 393224 | tf_op jit(solution)/shard_map/ppermute | solution.py:390
  69.8 3.1 %all-to-all-done.1.came = bf16[8,8,1408]{2,1,0:T(8,128)(2,1)S(1)} async-done(((bf16[8,8,1408]{2,1,0:T(8,128)(2,1)}), bf16[8,8,1408]{2,1,0:T(8,128)(2,1)S(1)}, u32[]{:S(2)}, u32[]{:S(2)}) %all-to-all-start.1) | async-done | bytes 180256 | tf_op jit(solution)/shard_map/all_to_all | solution.py:511
  73.0 2.7 %collective-permute-start.11 = (f32[8,1408]{1,0:T(8,128)S(1)}, f32[8,1408]{1,0:T(8,128)S(1)}, u32[]{:S(2)}, u32[]{:S(2)}) collective-permute-start(f32[8,1408]{1,0:T(8,128)S(1)} %shard_map.95.mine), channel_id=1, source_target_pairs={{0,2},{2,0},{1,3},{3,1},{4,6},{6,4},{5,7},{7,5},{8,10},{10,8},{9,1... | collective-permute-start | bytes 135176 | tf_op jit(solution)/shard_map/ppermute | solution.py:393
  75.7 3.4 %collective-permute-done.11.came = f32[8,1408]{1,0:T(8,128)S(1)} collective-permute-done((f32[8,1408]{1,0:T(8,128)S(1)}, f32[8,1408]{1,0:T(8,128)S(1)}, u32[]{:S(2)}, u32[]{:S(2)}) %collective-permute-start.11) | collective-permute-done | bytes 45088 | tf_op jit(solution)/shard_map/ppermute | solution.py:393
  79.1 2.3 %collective-permute-start.12 = (f32[8,1408]{1,0:T(8,128)S(1)}, f32[8,1408]{1,0:T(8,128)S(1)}, u32[]{:S(2)}, u32[]{:S(2)}) collective-permute-start(f32[8,1408]{1,0:T(8,128)S(1)} %shard_map.96.here), channel_id=1, source_target_pairs={{0,1},{1,0},{2,3},{3,2},{4,5},{5,4},{6,7},{7,6},{8,9},{9,8},{10,11... | collective-permute-start | bytes 135176 | tf_op jit(solution)/shard_map/ppermute | solution.py:393
  81.4 0.0 collective-permute-done.9.east
  81.4 0.0 collective-permute-done.8.west
  81.4 0.8 shard_map.92
  82.1 0.1 collective-permute-done.12.there
  82.2 0.7 shard_map.97
  (3 shorter events, 0.1 us)
Async XLA Ops:
  1.8 11.1 %collective-permute-start.1 = (bf16[16,8,512]{2,1,0:T(8,128)(2,1)S(1)}, bf16[16,8,512]{2,1,0:T(8,128)(2,1)S(1)}, u32[]{:S(2)}, u32[]{:S(2)}) collective-permute-start(bf16[16,8,512]{2,1,0:T(8,128)(2,1)S(1)} %get-tuple-element.38), channel_id=1, source_target_pairs={{0,4},{4,8},{8,12},{12,16},{16,20},{20,24},{24,28},{1,5},{5,9},{9,... | collective-permute-start | bytes 393224 | tf_op jit(solution)/shard_map/ppermute | solution.py:390
  5.7 7.1 %collective-permute-start.2 = (bf16[16,8,512]{2,1,0:T(8,128)(2,1)S(1)}, bf16[16,8,512]{2,1,0:T(8,128)(2,1)S(1)}, u32[]{:S(2)}, u32[]{:S(2)}) collective-permute-start(bf16[16,8,512]{2,1,0:T(8,128)(2,1)S(1)} %get-tuple-element.39), channel_id=1, source_target_pairs={{4,0},{8,4},{12,8},{16,12},{20,16},{24,20},{28,24},{5,1},{9,5},{13... | collective-permute-start | bytes 393224 | tf_op jit(solution)/shard_map/ppermute | solution.py:390
  7.0 15.2 %collective-permute-start = (bf16[8,16,512]{2,1,0:T(8,128)(2,1)S(1)}, bf16[8,16,512]{2,1,0:T(8,128)(2,1)S(1)}, u32[]{:S(2)}, u32[]{:S(2)}) collective-permute-start(bf16[8,16,512]{2,1,0:T(8,128)(2,1)S(1)} %get-tuple-element.37), channel_id=1, source_target_pairs={{0,32},{32,64},{64,96},{96,128},{128,160},{160,192},{192,224},{224... | collective-permute-start | bytes 393224 | tf_op jit(solution)/shard_map/ppermute | solution.py:386
  8.7 13.5 %collective-permute-start.4 = (bf16[8,16,512]{2,1,0:T(8,128)(2,1)S(1)}, bf16[8,16,512]{2,1,0:T(8,128)(2,1)S(1)}, u32[]{:S(2)}, u32[]{:S(2)}) collective-permute-start(bf16[8,16,512]{2,1,0:T(8,128)(2,1)S(1)} %get-tuple-element.41), channel_id=1, source_target_pairs={{0,224},{32,0},{64,32},{96,64},{128,96},{160,128},{192,160},{224,1... | collective-permute-start | bytes 393224 | tf_op jit(solution)/shard_map/ppermute | solution.py:386
  12.9 9.4 %collective-permute-start.3 = (bf16[128,512]{1,0:T(8,128)(2,1)S(1)}, bf16[128,512]{1,0:T(8,128)(2,1)S(1)}, u32[]{:S(2)}, u32[]{:S(2)}) collective-permute-start(bf16[128,512]{1,0:T(8,128)(2,1)S(1)} %get-tuple-element.40), channel_id=1, source_target_pairs={{0,32},{32,64},{64,96},{96,128},{128,160},{160,192},{192,224},{224... | collective-permute-start | bytes 393224 | tf_op jit(solution)/shard_map/ppermute | solution.py:386
  13.5 8.8 %collective-permute-start.5 = (bf16[128,512]{1,0:T(8,128)(2,1)S(1)}, bf16[128,512]{1,0:T(8,128)(2,1)S(1)}, u32[]{:S(2)}, u32[]{:S(2)}) collective-permute-start(bf16[128,512]{1,0:T(8,128)(2,1)S(1)} %get-tuple-element.42), channel_id=1, source_target_pairs={{0,224},{32,0},{64,32},{96,64},{128,96},{160,128},{192,160},{224,1... | collective-permute-start | bytes 393224 | tf_op jit(solution)/shard_map/ppermute | solution.py:386
  17.7 3.1 %copy-start = (bf16[512,1536]{1,0:T(8,128)(2,1)S(1)}, bf16[512,1536]{1,0:T(8,128)(2,1)}, u32[]{:S(2)}) copy-start(bf16[512,1536]{1,0:T(8,128)(2,1)} %w.7) | copy-start | bytes 4718596
  17.7 3.2 %copy-start.1 = (bf16[1,16,16,512]{3,2,1,0:T(8,128)(2,1)S(1)}, bf16[1,16,16,512]{3,2,1,0:T(8,128)(2,1)}, u32[]{:S(2)}) copy-start(bf16[1,16,16,512]{3,2,1,0:T(8,128)(2,1)} %param.5) | copy-start | bytes 786436
  17.7 3.2 %copy-start.2 = (bf16[512,512]{1,0:T(8,128)(2,1)S(1)}, bf16[512,512]{1,0:T(8,128)(2,1)}, u32[]{:S(2)}) copy-start(bf16[512,512]{1,0:T(8,128)(2,1)} %wo.1) | copy-start | bytes 1572868
  17.7 3.2 %copy-start.3 = (bf16[1,16,16,512]{3,2,1,0:T(8,128)(2,1)S(1)}, bf16[1,16,16,512]{3,2,1,0:T(8,128)(2,1)}, u32[]{:S(2)}) copy-start(bf16[1,16,16,512]{3,2,1,0:T(8,128)(2,1)} %param.9) | copy-start | bytes 786436
  30.1 4.9 %collective-permute-start.10 = (bf16[512,1024]{1,0:T(8,128)(2,1)S(1)}, bf16[512,1024]{1,0:T(8,128)(2,1)S(1)}, u32[]{:S(2)}, u32[]{:S(2)}) collective-permute-start(bf16[512,1024]{1,0:T(8,128)(2,1)S(1)} %get-tuple-element.65), channel_id=1, source_target_pairs={{0,1},{1,0},{2,3},{3,2},{4,5},{5,4},{6,7},{7,6},{8,9},{9,8},{10,11... | collective-permute-start | bytes 3145736 | tf_op jit(solution)/shard_map/ppermute | solution.py:393
  36.2 22.3 %all-to-all-start = ((bf16[8,536,128]{2,1,0:T(8,128)(2,1)}), bf16[8,536,128]{2,1,0:T(8,128)(2,1)S(1)}, u32[]{:S(2)}, u32[]{:S(2)}) async-start(bf16[8,536,128]{2,1,0:T(8,128)(2,1)} %shard_map.93), calls=%async_computation | async-start | bytes 2195456 | tf_op jit(solution)/shard_map/all_to_all | solution.py:485
  42.0 8.7 %collective-permute-start.6 = (bf16[256,512]{1,0:T(8,128)(2,1)S(1)}, bf16[256,512]{1,0:T(8,128)(2,1)S(1)}, u32[]{:S(2)}, u32[]{:S(2)}) collective-permute-start(bf16[256,512]{1,0:T(8,128)(2,1)S(1)} %get-tuple-element.59), channel_id=1, source_target_pairs={{0,32},{32,64},{64,96},{96,128},{128,160},{160,192},{192,224},{224... | collective-permute-start | bytes 786440 | tf_op jit(solution)/shard_map/ppermute | solution.py:386
  42.0 8.7 %collective-permute-start.7 = (bf16[256,512]{1,0:T(8,128)(2,1)S(1)}, bf16[256,512]{1,0:T(8,128)(2,1)S(1)}, u32[]{:S(2)}, u32[]{:S(2)}) collective-permute-start(bf16[256,512]{1,0:T(8,128)(2,1)S(1)} %get-tuple-element.60), channel_id=1, source_target_pairs={{0,224},{32,0},{64,32},{96,64},{128,96},{160,128},{192,160},{224,1... | collective-permute-start | bytes 786440 | tf_op jit(solution)/shard_map/ppermute | solution.py:386
  59.2 13.7 %all-to-all-start.1 = ((bf16[8,8,1408]{2,1,0:T(8,128)(2,1)}), bf16[8,8,1408]{2,1,0:T(8,128)(2,1)S(1)}, u32[]{:S(2)}, u32[]{:S(2)}) async-start(bf16[8,8,1408]{2,1,0:T(8,128)(2,1)} %shard_map.94), calls=%async_computation.1 | async-start | bytes 360448 | tf_op jit(solution)/shard_map/all_to_all | solution.py:511
  64.5 16.8 %collective-permute-start.9 = (bf16[16,8,512]{2,1,0:T(8,128)(2,1)S(1)}, bf16[16,8,512]{2,1,0:T(8,128)(2,1)S(1)}, u32[]{:S(2)}, u32[]{:S(2)}) collective-permute-start(bf16[16,8,512]{2,1,0:T(8,128)(2,1)S(1)} %bitcast.29), channel_id=1, source_target_pairs={{4,0},{8,4},{12,8},{16,12},{20,16},{24,20},{28,24},{5,1},{9,5},{13... | collective-permute-start | bytes 393224 | tf_op jit(solution)/shard_map/ppermute | solution.py:390
  65.8 15.6 %collective-permute-start.8 = (bf16[16,8,512]{2,1,0:T(8,128)(2,1)S(1)}, bf16[16,8,512]{2,1,0:T(8,128)(2,1)S(1)}, u32[]{:S(2)}, u32[]{:S(2)}) collective-permute-start(bf16[16,8,512]{2,1,0:T(8,128)(2,1)S(1)} %bitcast.28), channel_id=1, source_target_pairs={{0,4},{4,8},{8,12},{12,16},{16,20},{20,24},{24,28},{1,5},{5,9},{9,... | collective-permute-start | bytes 393224 | tf_op jit(solution)/shard_map/ppermute | solution.py:390
  73.0 6.1 %collective-permute-start.11 = (f32[8,1408]{1,0:T(8,128)S(1)}, f32[8,1408]{1,0:T(8,128)S(1)}, u32[]{:S(2)}, u32[]{:S(2)}) collective-permute-start(f32[8,1408]{1,0:T(8,128)S(1)} %shard_map.95.mine), channel_id=1, source_target_pairs={{0,2},{2,0},{1,3},{3,1},{4,6},{6,4},{5,7},{7,5},{8,10},{10,8},{9,1... | collective-permute-start | bytes 135176 | tf_op jit(solution)/shard_map/ppermute | solution.py:393
  79.1 3.2 %collective-permute-start.12 = (f32[8,1408]{1,0:T(8,128)S(1)}, f32[8,1408]{1,0:T(8,128)S(1)}, u32[]{:S(2)}, u32[]{:S(2)}) collective-permute-start(f32[8,1408]{1,0:T(8,128)S(1)} %shard_map.96.here), channel_id=1, source_target_pairs={{0,1},{1,0},{2,3},{3,2},{4,5},{5,4},{6,7},{7,6},{8,9},{9,8},{10,11... | collective-permute-start | bytes 135176 | tf_op jit(solution)/shard_map/ppermute | solution.py:393

commit v11 on v10

--- a/solution.py
+++ b/solution.py
@@ -35,11 +35,12 @@
     )
 
 
-def slices_kernel(own, to_right, to_left, to_next, to_last, done):
+def slices_kernel(own, bias, to_right, to_left, to_next, to_last, bias_near, done):
     copies = [
         pltpu.make_async_copy(source, target, done.at[n])
         for n, (source, target) in enumerate(
             (
+                (bias, bias_near),
                 (own.at[:, pl.ds(8, 8)], to_right),
                 (own.at[:, pl.ds(0, 8)], to_left),
                 (own.at[pl.ds(8, 8)], to_next),
@@ -62,9 +63,7 @@
     da_t[...] = d_attended.T
 
 
-def table_kernel(edge, bias_far, table, bias, done):
-    copy = pltpu.make_async_copy(bias_far, bias, done)
-    copy.start()
+def table_kernel(edge, bias, table):
     pick = (iota((17, 512), 0) == 23 - (iota((17, 512), 1) >> 4)).astype(F32)
     range_row = iota((32, 512), 0)
     lane = iota((32, 512), 1)
@@ -72,7 +71,6 @@
     first = jnp.where(edge[0] == 1, 8, 0)
     last = jnp.where(edge[1] == 1, 24, 32)
     present = (range_row >= first) & (range_row < last) & (lane >= 112) & (lane < 384)
-    copy.wait()
     for head in range(8):
         pair, lanes = head // 2, slice(head % 2 * 128, head % 2 * 128 + 128)
         head_rows = dot(bias[:, head, :], pick, TN, exact=True)
@@ -392,12 +390,18 @@
     def swap(leaf, axis="core"):
         return lax.ppermute(leaf, axis, [(0, 1), (1, 0)])
 
-    to_right, to_left, to_next, to_last = call(
+    bias = jnp.transpose(relative_bias, (1, 0, 2))
+    to_right, to_left, to_next, to_last, bias = call(
         slices_kernel,
-        (pltpu.with_memory_space_constraint(cells, pltpu.HBM),),
-        (whole((16, 8, width), BF16),) * 2 + (whole((8, 16, width), BF16),) * 2,
-        scratch=(pltpu.SemaphoreType.DMA((4,)),),
-        far=1,
+        (
+            pltpu.with_memory_space_constraint(cells, pltpu.HBM),
+            pltpu.with_memory_space_constraint(bias, pltpu.HBM),
+        ),
+        (whole((16, 8, width), BF16),) * 2
+        + (whole((8, 16, width), BF16),) * 2
+        + (whole(bias.shape, F32),),
+        scratch=(pltpu.SemaphoreType.DMA((5,)),),
+        far=2,
         flops=1_000_000,
     )
     left = shift(to_right, 1).reshape(128, width)
@@ -416,16 +420,9 @@
 
     (table,) = call(
         table_kernel,
-        (
-            edge,
-            pltpu.with_memory_space_constraint(
-                jnp.transpose(relative_bias, (1, 0, 2)), pltpu.HBM
-            ),
-        ),
+        (edge, bias),
         (whole((4, 768, 256), F32),),
-        scratch=(pltpu.VMEM((17, 8, 17), F32), pltpu.SemaphoreType.DMA(())),
         prefetch=1,
-        far=1,
         flops=100_000_000,
         limit=12,
     )

time: 83.3 us -> 82.3 us (0.988)
  Pallas kernels: 19.5 us -> 18.4 us
    pallas_call x14, Pallas kernels: 19.5 us -> 18.4 us  [call(): pl.pallas_call(kernel, out_shape=tuple(outs), in_specs=[scalar] * prefetc...]
  transfers between devices with their start and end apart: 15 -> 15, of which waited for: 5 -> 5; matrix products, arithmetic and copies ran while one was open for 0% -> 0% of each run, Pallas kernels for 9% -> 8%
where the time goes in v11:
time: 82.3 us; the launch traced here: 81.9 us
  starting transfers between devices  42.3 us (51%)
  waiting for transfers between devices  20.3 us (25%)
  Pallas kernels  18.4 us (22%)
    pallas_call x14, Pallas kernels, call(): pl.pallas_call(kernel, out_shape=tuple(outs), in_specs=[scalar] * prefetc...  18.4 us
    ppermute x6, starting transfers between devices, turn(): return lax.ppermute(leaf, 'az', [(i, (i + step) % az) for i in range(az)])  13.2 us
    ppermute x4, starting transfers between devices, shift(): return lax.ppermute(leaf, 'rng', pairs)  10.5 us
    all_to_all x1, waiting for transfers between devices, shards(): parcel = lax.all_to_all(parcel, 'rng', 0, 0, tiled=True)  7.63 us
    ppermute x3, starting transfers between devices, swap(): return lax.ppermute(leaf, axis, [(0, 1), (1, 0)])  7.39 us
    ppermute x6, waiting for transfers between devices, turn(): return lax.ppermute(leaf, 'az', [(i, (i + step) % az) for i in range(az)])  6.01 us
    all_to_all x1, starting transfers between devices, shards(): parcel = lax.all_to_all(parcel, 'rng', 0, 0, tiled=True)  5.87 us
    all_to_all x1, starting transfers between devices, shards(): parcel = lax.all_to_all(parcel, 'az', 0, 0, tiled=True)  5.33 us
  transfers between devices with their start and end apart: 15, of which 5 were waited for; matrix products, arithmetic and copies ran while one was open for 0% of the time, Pallas kernels for 8%

profile of v11, /device:TPU:1, one launch (start us, length us, event | category | flops | bytes accessed | tf_op | source)
XLA Modules:
  0.0 81.9 jit_solution(18304225973049455487)
XLA Ops:
  0.6 1.2 %shard_map.84 = (bf16[16,8,512]{2,1,0:T(8,128)(2,1)S(1)}, bf16[16,8,512]{2,1,0:T(8,128)(2,1)S(1)}, bf16[8,16,512]{2,1,0:T(8,128)(2,1)S(1)}, bf16[8,16,512]{2,1,0:T(8,128)(2,1)S(1)}, f32[17,8,17]{2,1,0:T(8,128)S(1)}) custom-call(bf16[16,16,512]{2,1,0:T(8,128)(2,1)} %bitcast.17, f32[17,8,17]{2,1,0:T(8,128)} %bitcast.31), custom_call_target="tpu_custom_call" | custom-call | flops 1000000 | bytes 804928 | tf_op jit(solution)/shard_map/pallas_call | solution.py:362
  1.8 3.9 %collective-permute-start.1 = (bf16[16,8,512]{2,1,0:T(8,128)(2,1)S(1)}, bf16[16,8,512]{2,1,0:T(8,128)(2,1)S(1)}, u32[]{:S(2)}, u32[]{:S(2)}) collective-permute-start(bf16[16,8,512]{2,1,0:T(8,128)(2,1)S(1)} %get-tuple-element.39), channel_id=1, source_target_pairs={{0,4},{4,8},{8,12},{12,16},{16,20},{20,24},{24,28},{1,5},{5,9},{9,... | collective-permute-start | bytes 393224 | tf_op jit(solution)/shard_map/ppermute | solution.py:388
  5.8 1.3 %collective-permute-start.2 = (bf16[16,8,512]{2,1,0:T(8,128)(2,1)S(1)}, bf16[16,8,512]{2,1,0:T(8,128)(2,1)S(1)}, u32[]{:S(2)}, u32[]{:S(2)}) collective-permute-start(bf16[16,8,512]{2,1,0:T(8,128)(2,1)S(1)} %get-tuple-element.40), channel_id=1, source_target_pairs={{4,0},{8,4},{12,8},{16,12},{20,16},{24,20},{28,24},{5,1},{9,5},{13... | collective-permute-start | bytes 393224 | tf_op jit(solution)/shard_map/ppermute | solution.py:388
  7.1 1.7 %collective-permute-start = (bf16[8,16,512]{2,1,0:T(8,128)(2,1)S(1)}, bf16[8,16,512]{2,1,0:T(8,128)(2,1)S(1)}, u32[]{:S(2)}, u32[]{:S(2)}) collective-permute-start(bf16[8,16,512]{2,1,0:T(8,128)(2,1)S(1)} %get-tuple-element.38), channel_id=1, source_target_pairs={{0,32},{32,64},{64,96},{96,128},{128,160},{160,192},{192,224},{224... | collective-permute-start | bytes 393224 | tf_op jit(solution)/shard_map/ppermute | solution.py:384
  8.8 4.0 %collective-permute-start.4 = (bf16[8,16,512]{2,1,0:T(8,128)(2,1)S(1)}, bf16[8,16,512]{2,1,0:T(8,128)(2,1)S(1)}, u32[]{:S(2)}, u32[]{:S(2)}) collective-permute-start(bf16[8,16,512]{2,1,0:T(8,128)(2,1)S(1)} %get-tuple-element.42), channel_id=1, source_target_pairs={{0,224},{32,0},{64,32},{96,64},{128,96},{160,128},{192,160},{224,1... | collective-permute-start | bytes 393224 | tf_op jit(solution)/shard_map/ppermute | solution.py:384
  12.8 0.1 add_convert_fusion.edge
  12.9 0.0 collective-permute-done.1
  12.9 0.0 collective-permute-done.2
  12.9 0.6 collective-permute-start.3
  13.5 4.2 %collective-permute-start.5 = (bf16[128,512]{1,0:T(8,128)(2,1)S(1)}, bf16[128,512]{1,0:T(8,128)(2,1)S(1)}, u32[]{:S(2)}, u32[]{:S(2)}) collective-permute-start(bf16[128,512]{1,0:T(8,128)(2,1)S(1)} %get-tuple-element.43), channel_id=1, source_target_pairs={{0,224},{32,0},{64,32},{96,64},{128,96},{160,128},{192,160},{224,1... | collective-permute-start | bytes 393224 | tf_op jit(solution)/shard_map/ppermute | solution.py:384
  17.7 0.0 copy-start
  17.7 0.0 copy-start.1
  17.7 0.0 copy-start.2
  17.7 0.0 copy-start.3
  17.7 2.0 %shard_map.87.table = f32[4,768,256]{2,1,0:T(8,128)S(1)} custom-call(s32[2]{0:T(128)S(1)} %add_convert_fusion.edge, f32[17,8,17]{2,1,0:T(8,128)S(1)} %get-tuple-element.48.bias), custom_call_target="tpu_custom_call" | custom-call | flops 100000000 | bytes 3154984 | tf_op jit(solution)/shard_map/pallas_call | solution.py:362
  19.7 0.0 copy-done
  19.7 0.0 copy-done.1
  19.8 0.0 copy-done.2
  19.8 0.0 copy-done.3
  19.8 0.5 shard_map.86
  20.3 0.8 %shard_map.88 = (bf16[512,512]{1,0:T(8,128)(2,1)S(1)}, bf16[512,512]{1,0:T(8,128)(2,1)S(1)}, bf16[512,512]{1,0:T(8,128)(2,1)S(1)}, bf16[512,512]{1,0:T(8,128)(2,1)S(1)}, bf16[512,512]{1,0:T(8,128)(2,1)S(1)}) custom-call(bf16[128,512]{1,0:T(8,128)(2,1)S(1)} %bitcast.23, bf16[256,512]{1,0:T(8,128)(2,1)S(1)} %bitcast.19, bf16[128,512]{1,0:T(8,128)(2,1)S(1)} %bitcast.25, ...), custom_call_target="tpu_custom_call" | custom-call | flops 1000000000 | bytes 4718592 | tf_op jit(solution)/shard_map/pallas_call | solution.py:362
  21.1 0.0 collective-permute-done
  21.1 0.0 collective-permute-done.4
  21.1 0.0 collective-permute-done.3.above
  21.2 0.0 collective-permute-done.5.below
  21.2 7.9 %shard_map.89 = (bf16[512,1024]{1,0:T(8,128)(2,1)S(1)}, bf16[1024,1024]{1,0:T(8,128)(2,1)S(1)}, bf16[2,512,256]{2,1,0:T(8,128)(2,1)S(1)}, bf16[2,256,512]{2,1,0:...) custom-call(s32[1]{0:T(128)} %bitcast.core, bf16[128,512]{1,0:T(8,128)(2,1)S(1)} %bitcast.26, ...), custom_call_target="tpu_custom_call" | custom-call | flops 10000000000 | bytes 14680068 | tf_op jit(solution)/shard_map/pallas_call | solution.py:362
  29.0 2.4 %collective-permute-start.10 = (bf16[512,1024]{1,0:T(8,128)(2,1)S(1)}, bf16[512,1024]{1,0:T(8,128)(2,1)S(1)}, u32[]{:S(2)}, u32[]{:S(2)}) collective-permute-start(bf16[512,1024]{1,0:T(8,128)(2,1)S(1)} %get-tuple-element.67), channel_id=1, source_target_pairs={{0,1},{1,0},{2,3},{3,2},{4,5},{5,4},{6,7},{7,6},{8,9},{9,8},{10,11... | collective-permute-start | bytes 3145736 | tf_op jit(solution)/shard_map/ppermute | solution.py:391
  31.4 2.5 %shard_map.90 = (bf16[512,1024]{1,0:T(8,128)(2,1)S(1)}, f32[8,384]{1,0:T(8,128)S(1)}, bf16[256,512]{1,0:T(8,128)(2,1)S(1)}, f32[256,512]{1,0:T(8,128)S(1)}, f32[...) custom-call(s32[1]{0:T(128)} %bitcast.core, bf16[512,1024]{1,0:T(8,128)(2,1)S(1)} %get-tuple-element.54.x_t, ...), custom_call_target="tpu_custom_call" | custom-call | flops 2500000000 | bytes 8663044 | tf_op jit(solution)/shard_map/pallas_call | solution.py:362
  34.0 0.0 collective-permute-done.10.came
  34.0 1.1 %shard_map.93 = bf16[8,536,128]{2,1,0:T(8,128)(2,1)} custom-call(bf16[512,1024]{1,0:T(8,128)(2,1)S(1)} %get-tuple-element.66.keep, bf16[512,1024]{1,0:T(8,128)(2,1)S(1)} %collective-permute-done.10.came, f32[8,384]{1,0:T(8,128)S(1)} %get-tuple-element.68.bias), custom_call_target="tpu_custom_call" | custom-call | flops 1000000 | bytes 3207168 | tf_op jit(solution)/shard_map/pallas_call | solution.py:362
  35.1 5.9 %all-to-all-start = ((bf16[8,536,128]{2,1,0:T(8,128)(2,1)}), bf16[8,536,128]{2,1,0:T(8,128)(2,1)S(1)}, u32[]{:S(2)}, u32[]{:S(2)}) async-start(bf16[8,536,128]{2,1,0:T(8,128)(2,1)} %shard_map.93), calls=%async_computation | async-start | bytes 2195456 | tf_op jit(solution)/shard_map/all_to_all | solution.py:482
  41.0 0.0 collective-permute-start.6
  41.0 2.7 %collective-permute-start.7 = (bf16[256,512]{1,0:T(8,128)(2,1)S(1)}, bf16[256,512]{1,0:T(8,128)(2,1)S(1)}, u32[]{:S(2)}, u32[]{:S(2)}) collective-permute-start(bf16[256,512]{1,0:T(8,128)(2,1)S(1)} %get-tuple-element.62), channel_id=1, source_target_pairs={{0,224},{32,0},{64,32},{96,64},{128,96},{160,128},{192,160},{224,1... | collective-permute-start | bytes 786440 | tf_op jit(solution)/shard_map/ppermute | solution.py:384
  43.6 6.0 %collective-permute-done.6.up = bf16[256,512]{1,0:T(8,128)(2,1)S(1)} collective-permute-done((bf16[256,512]{1,0:T(8,128)(2,1)S(1)}, bf16[256,512]{1,0:T(8,128)(2,1)S(1)}, u32[]{:S(2)}, u32[]{:S(2)}) %collective-permute-start.6) | collective-permute-done | bytes 262176 | tf_op jit(solution)/shard_map/ppermute | solution.py:384
  49.6 0.0 collective-permute-done.7.down
  49.6 0.1 shard_map.91
  49.7 7.6 %all-to-all-done.came = bf16[8,536,128]{2,1,0:T(8,128)(2,1)S(1)} async-done(((bf16[8,536,128]{2,1,0:T(8,128)(2,1)}), bf16[8,536,128]{2,1,0:T(8,128)(2,1)S(1)}, u32[]{:S(2)}, u32[]{:S(2)}) %all-to-all-start) | async-done | bytes 1097760 | tf_op jit(solution)/shard_map/all_to_all | solution.py:482
  57.4 0.8 shard_map.94
  58.2 5.3 %all-to-all-start.1 = ((bf16[8,8,1408]{2,1,0:T(8,128)(2,1)}), bf16[8,8,1408]{2,1,0:T(8,128)(2,1)S(1)}, u32[]{:S(2)}, u32[]{:S(2)}) async-start(bf16[8,8,1408]{2,1,0:T(8,128)(2,1)} %shard_map.94), calls=%async_computation.1 | async-start | bytes 360448 | tf_op jit(solution)/shard_map/all_to_all | solution.py:508
  63.5 1.3 %collective-permute-start.9 = (bf16[16,8,512]{2,1,0:T(8,128)(2,1)S(1)}, bf16[16,8,512]{2,1,0:T(8,128)(2,1)S(1)}, u32[]{:S(2)}, u32[]{:S(2)}) collective-permute-start(bf16[16,8,512]{2,1,0:T(8,128)(2,1)S(1)} %bitcast.29), channel_id=1, source_target_pairs={{4,0},{8,4},{12,8},{16,12},{20,16},{24,20},{28,24},{5,1},{9,5},{13... | collective-permute-start | bytes 393224 | tf_op jit(solution)/shard_map/ppermute | solution.py:388
  64.8 4.0 %collective-permute-start.8 = (bf16[16,8,512]{2,1,0:T(8,128)(2,1)S(1)}, bf16[16,8,512]{2,1,0:T(8,128)(2,1)S(1)}, u32[]{:S(2)}, u32[]{:S(2)}) collective-permute-start(bf16[16,8,512]{2,1,0:T(8,128)(2,1)S(1)} %bitcast.28), channel_id=1, source_target_pairs={{0,4},{4,8},{8,12},{12,16},{16,20},{20,24},{24,28},{1,5},{5,9},{9,... | collective-permute-start | bytes 393224 | tf_op jit(solution)/shard_map/ppermute | solution.py:388
  68.8 3.1 %all-to-all-done.1.came = bf16[8,8,1408]{2,1,0:T(8,128)(2,1)S(1)} async-done(((bf16[8,8,1408]{2,1,0:T(8,128)(2,1)}), bf16[8,8,1408]{2,1,0:T(8,128)(2,1)S(1)}, u32[]{:S(2)}, u32[]{:S(2)}) %all-to-all-start.1) | async-done | bytes 180256 | tf_op jit(solution)/shard_map/all_to_all | solution.py:508
  72.0 2.7 %collective-permute-start.11 = (f32[8,1408]{1,0:T(8,128)S(1)}, f32[8,1408]{1,0:T(8,128)S(1)}, u32[]{:S(2)}, u32[]{:S(2)}) collective-permute-start(f32[8,1408]{1,0:T(8,128)S(1)} %shard_map.95.mine), channel_id=1, source_target_pairs={{0,2},{2,0},{1,3},{3,1},{4,6},{6,4},{5,7},{7,5},{8,10},{10,8},{9,1... | collective-permute-start | bytes 135176 | tf_op jit(solution)/shard_map/ppermute | solution.py:391
  74.7 3.4 %collective-permute-done.11.came = f32[8,1408]{1,0:T(8,128)S(1)} collective-permute-done((f32[8,1408]{1,0:T(8,128)S(1)}, f32[8,1408]{1,0:T(8,128)S(1)}, u32[]{:S(2)}, u32[]{:S(2)}) %collective-permute-start.11) | collective-permute-done | bytes 45088 | tf_op jit(solution)/shard_map/ppermute | solution.py:391
  78.0 2.3 %collective-permute-start.12 = (f32[8,1408]{1,0:T(8,128)S(1)}, f32[8,1408]{1,0:T(8,128)S(1)}, u32[]{:S(2)}, u32[]{:S(2)}) collective-permute-start(f32[8,1408]{1,0:T(8,128)S(1)} %shard_map.96.here), channel_id=1, source_target_pairs={{0,1},{1,0},{2,3},{3,2},{4,5},{5,4},{6,7},{7,6},{8,9},{9,8},{10,11... | collective-permute-start | bytes 135176 | tf_op jit(solution)/shard_map/ppermute | solution.py:391
  80.3 0.0 collective-permute-done.9.east
  80.3 0.0 collective-permute-done.8.west
  80.3 0.8 shard_map.92
  81.1 0.1 collective-permute-done.12.there
  81.2 0.7 shard_map.97
  (3 shorter events, 0.1 us)
Async XLA Ops:
  1.8 11.1 %collective-permute-start.1 = (bf16[16,8,512]{2,1,0:T(8,128)(2,1)S(1)}, bf16[16,8,512]{2,1,0:T(8,128)(2,1)S(1)}, u32[]{:S(2)}, u32[]{:S(2)}) collective-permute-start(bf16[16,8,512]{2,1,0:T(8,128)(2,1)S(1)} %get-tuple-element.39), channel_id=1, source_target_pairs={{0,4},{4,8},{8,12},{12,16},{16,20},{20,24},{24,28},{1,5},{5,9},{9,... | collective-permute-start | bytes 393224 | tf_op jit(solution)/shard_map/ppermute | solution.py:388
  5.8 7.1 %collective-permute-start.2 = (bf16[16,8,512]{2,1,0:T(8,128)(2,1)S(1)}, bf16[16,8,512]{2,1,0:T(8,128)(2,1)S(1)}, u32[]{:S(2)}, u32[]{:S(2)}) collective-permute-start(bf16[16,8,512]{2,1,0:T(8,128)(2,1)S(1)} %get-tuple-element.40), channel_id=1, source_target_pairs={{4,0},{8,4},{12,8},{16,12},{20,16},{24,20},{28,24},{5,1},{9,5},{13... | collective-permute-start | bytes 393224 | tf_op jit(solution)/shard_map/ppermute | solution.py:388
  7.1 14.1 %collective-permute-start = (bf16[8,16,512]{2,1,0:T(8,128)(2,1)S(1)}, bf16[8,16,512]{2,1,0:T(8,128)(2,1)S(1)}, u32[]{:S(2)}, u32[]{:S(2)}) collective-permute-start(bf16[8,16,512]{2,1,0:T(8,128)(2,1)S(1)} %get-tuple-element.38), channel_id=1, source_target_pairs={{0,32},{32,64},{64,96},{96,128},{128,160},{160,192},{192,224},{224... | collective-permute-start | bytes 393224 | tf_op jit(solution)/shard_map/ppermute | solution.py:384
  8.8 12.4 %collective-permute-start.4 = (bf16[8,16,512]{2,1,0:T(8,128)(2,1)S(1)}, bf16[8,16,512]{2,1,0:T(8,128)(2,1)S(1)}, u32[]{:S(2)}, u32[]{:S(2)}) collective-permute-start(bf16[8,16,512]{2,1,0:T(8,128)(2,1)S(1)} %get-tuple-element.42), channel_id=1, source_target_pairs={{0,224},{32,0},{64,32},{96,64},{128,96},{160,128},{192,160},{224,1... | collective-permute-start | bytes 393224 | tf_op jit(solution)/shard_map/ppermute | solution.py:384
  12.9 8.2 %collective-permute-start.3 = (bf16[128,512]{1,0:T(8,128)(2,1)S(1)}, bf16[128,512]{1,0:T(8,128)(2,1)S(1)}, u32[]{:S(2)}, u32[]{:S(2)}) collective-permute-start(bf16[128,512]{1,0:T(8,128)(2,1)S(1)} %get-tuple-element.41), channel_id=1, source_target_pairs={{0,32},{32,64},{64,96},{96,128},{128,160},{160,192},{192,224},{224... | collective-permute-start | bytes 393224 | tf_op jit(solution)/shard_map/ppermute | solution.py:384
  13.5 7.7 %collective-permute-start.5 = (bf16[128,512]{1,0:T(8,128)(2,1)S(1)}, bf16[128,512]{1,0:T(8,128)(2,1)S(1)}, u32[]{:S(2)}, u32[]{:S(2)}) collective-permute-start(bf16[128,512]{1,0:T(8,128)(2,1)S(1)} %get-tuple-element.43), channel_id=1, source_target_pairs={{0,224},{32,0},{64,32},{96,64},{128,96},{160,128},{192,160},{224,1... | collective-permute-start | bytes 393224 | tf_op jit(solution)/shard_map/ppermute | solution.py:384
  17.7 2.0 %copy-start = (bf16[512,1536]{1,0:T(8,128)(2,1)S(1)}, bf16[512,1536]{1,0:T(8,128)(2,1)}, u32[]{:S(2)}) copy-start(bf16[512,1536]{1,0:T(8,128)(2,1)} %w.7) | copy-start | bytes 4718596
  17.7 2.0 %copy-start.1 = (bf16[1,16,16,512]{3,2,1,0:T(8,128)(2,1)S(1)}, bf16[1,16,16,512]{3,2,1,0:T(8,128)(2,1)}, u32[]{:S(2)}) copy-start(bf16[1,16,16,512]{3,2,1,0:T(8,128)(2,1)} %param.5) | copy-start | bytes 786436
  17.7 2.0 %copy-start.2 = (bf16[512,512]{1,0:T(8,128)(2,1)S(1)}, bf16[512,512]{1,0:T(8,128)(2,1)}, u32[]{:S(2)}) copy-start(bf16[512,512]{1,0:T(8,128)(2,1)} %wo.1) | copy-start | bytes 1572868
  17.7 2.0 %copy-start.3 = (bf16[1,16,16,512]{3,2,1,0:T(8,128)(2,1)S(1)}, bf16[1,16,16,512]{3,2,1,0:T(8,128)(2,1)}, u32[]{:S(2)}) copy-start(bf16[1,16,16,512]{3,2,1,0:T(8,128)(2,1)} %param.9) | copy-start | bytes 786436
  29.0 4.9 %collective-permute-start.10 = (bf16[512,1024]{1,0:T(8,128)(2,1)S(1)}, bf16[512,1024]{1,0:T(8,128)(2,1)S(1)}, u32[]{:S(2)}, u32[]{:S(2)}) collective-permute-start(bf16[512,1024]{1,0:T(8,128)(2,1)S(1)} %get-tuple-element.67), channel_id=1, source_target_pairs={{0,1},{1,0},{2,3},{3,2},{4,5},{5,4},{6,7},{7,6},{8,9},{9,8},{10,11... | collective-permute-start | bytes 3145736 | tf_op jit(solution)/shard_map/ppermute | solution.py:391
  35.1 22.3 %all-to-all-start = ((bf16[8,536,128]{2,1,0:T(8,128)(2,1)}), bf16[8,536,128]{2,1,0:T(8,128)(2,1)S(1)}, u32[]{:S(2)}, u32[]{:S(2)}) async-start(bf16[8,536,128]{2,1,0:T(8,128)(2,1)} %shard_map.93), calls=%async_computation | async-start | bytes 2195456 | tf_op jit(solution)/shard_map/all_to_all | solution.py:482
  41.0 8.7 %collective-permute-start.6 = (bf16[256,512]{1,0:T(8,128)(2,1)S(1)}, bf16[256,512]{1,0:T(8,128)(2,1)S(1)}, u32[]{:S(2)}, u32[]{:S(2)}) collective-permute-start(bf16[256,512]{1,0:T(8,128)(2,1)S(1)} %get-tuple-element.61), channel_id=1, source_target_pairs={{0,32},{32,64},{64,96},{96,128},{128,160},{160,192},{192,224},{224... | collective-permute-start | bytes 786440 | tf_op jit(solution)/shard_map/ppermute | solution.py:384
  41.0 8.7 %collective-permute-start.7 = (bf16[256,512]{1,0:T(8,128)(2,1)S(1)}, bf16[256,512]{1,0:T(8,128)(2,1)S(1)}, u32[]{:S(2)}, u32[]{:S(2)}) collective-permute-start(bf16[256,512]{1,0:T(8,128)(2,1)S(1)} %get-tuple-element.62), channel_id=1, source_target_pairs={{0,224},{32,0},{64,32},{96,64},{128,96},{160,128},{192,160},{224,1... | collective-permute-start | bytes 786440 | tf_op jit(solution)/shard_map/ppermute | solution.py:384
  58.2 13.8 %all-to-all-start.1 = ((bf16[8,8,1408]{2,1,0:T(8,128)(2,1)}), bf16[8,8,1408]{2,1,0:T(8,128)(2,1)S(1)}, u32[]{:S(2)}, u32[]{:S(2)}) async-start(bf16[8,8,1408]{2,1,0:T(8,128)(2,1)} %shard_map.94), calls=%async_computation.1 | async-start | bytes 360448 | tf_op jit(solution)/shard_map/all_to_all | solution.py:508
  63.5 16.8 %collective-permute-start.9 = (bf16[16,8,512]{2,1,0:T(8,128)(2,1)S(1)}, bf16[16,8,512]{2,1,0:T(8,128)(2,1)S(1)}, u32[]{:S(2)}, u32[]{:S(2)}) collective-permute-start(bf16[16,8,512]{2,1,0:T(8,128)(2,1)S(1)} %bitcast.29), channel_id=1, source_target_pairs={{4,0},{8,4},{12,8},{16,12},{20,16},{24,20},{28,24},{5,1},{9,5},{13... | collective-permute-start | bytes 393224 | tf_op jit(solution)/shard_map/ppermute | solution.py:388
  64.8 15.6 %collective-permute-start.8 = (bf16[16,8,512]{2,1,0:T(8,128)(2,1)S(1)}, bf16[16,8,512]{2,1,0:T(8,128)(2,1)S(1)}, u32[]{:S(2)}, u32[]{:S(2)}) collective-permute-start(bf16[16,8,512]{2,1,0:T(8,128)(2,1)S(1)} %bitcast.28), channel_id=1, source_target_pairs={{0,4},{4,8},{8,12},{12,16},{16,20},{20,24},{24,28},{1,5},{5,9},{9,... | collective-permute-start | bytes 393224 | tf_op jit(solution)/shard_map/ppermute | solution.py:388
  72.0 6.1 %collective-permute-start.11 = (f32[8,1408]{1,0:T(8,128)S(1)}, f32[8,1408]{1,0:T(8,128)S(1)}, u32[]{:S(2)}, u32[]{:S(2)}) collective-permute-start(f32[8,1408]{1,0:T(8,128)S(1)} %shard_map.95.mine), channel_id=1, source_target_pairs={{0,2},{2,0},{1,3},{3,1},{4,6},{6,4},{5,7},{7,5},{8,10},{10,8},{9,1... | collective-permute-start | bytes 135176 | tf_op jit(solution)/shard_map/ppermute | solution.py:391
  78.0 3.2 %collective-permute-start.12 = (f32[8,1408]{1,0:T(8,128)S(1)}, f32[8,1408]{1,0:T(8,128)S(1)}, u32[]{:S(2)}, u32[]{:S(2)}) collective-permute-start(f32[8,1408]{1,0:T(8,128)S(1)} %shard_map.96.here), channel_id=1, source_target_pairs={{0,1},{1,0},{2,3},{3,2},{4,5},{5,4},{6,7},{7,6},{8,9},{9,8},{10,11... | collective-permute-start | bytes 135176 | tf_op jit(solution)/shard_map/ppermute | solution.py:391

commit v12 on v11

--- a/solution.py
+++ b/solution.py
@@ -335,18 +335,14 @@
     mine[...] = total
 
 
-def add_kernel(mine, came, both):
-    both[...] = mine[...] + came[...]
-
-
-def finish_kernel(core, here, there, qkv, out, bias):
-    is_first = core[0] == 0
-    low = jnp.where(is_first, here[:, 0:1024], there[:, 0:1024])
-    high = jnp.where(is_first, there[:, 0:1024], here[:, 0:1024])
+def finish_kernel(parts, qkv, out, bias):
+    first = parts[0] + parts[2]
+    second = parts[1] + parts[3]
+    low, high = first[:, 0:1024], second[:, 0:1024]
     qkv[:, 0:1024] = low
     qkv[:, 1024:1536] = high[:, 512:1024]
     out[...] = high[:, 0:512]
-    total = here[:, 1024:] + there[:, 1024:]
+    total = first[:, 1024:] + second[:, 1024:]
     for i in range(17):
         bias[i] = total[:, i * 17 : i * 17 + 17]
 
@@ -507,13 +503,11 @@
     )
     parcel = lax.all_to_all(parcel, "az", 0, 0, tiled=True)
     (mine,) = call(total_kernel, (parcel,), (whole((8, 1408), F32),), flops=1_000_000)
-    near = swap(mine, "half")
-    (mine,) = call(add_kernel, (mine, near), (whole((8, 1408), F32),), flops=1_000_000)
+    parts = lax.all_gather(mine, ("half", "core"))
     rows_qkv, rows_out, total_bias = call(
         finish_kernel,
-        (core, mine, swap(mine)),
+        (parts,),
         (whole((8, 1536), F32), whole((8, 512), F32), whole((17, 8, 17), F32)),
-        prefetch=1,
         flops=1_000_000,
     )
     total_bias = jnp.transpose(total_bias, (1, 0, 2))

time: 82.3 us -> 84 us (1.021)
  the two profiles are of different devices: /device:TPU:1 before, /device:TPU:57 now
where the time goes in v12:
time: 84 us; the launch traced here: 83.7 us
  starting transfers between devices  36.5 us (43%)
  Pallas kernels  18.4 us (22%)
  waiting for transfers between devices  18.4 us (22%)
  blocking collectives  9.44 us (11%)
    pallas_call x13, Pallas kernels, call(): pl.pallas_call(kernel, out_shape=tuple(outs), in_specs=[scalar] * prefetc...  18.4 us
    ppermute x4, starting transfers between devices, shift(): return lax.ppermute(leaf, 'rng', pairs)  12.7 us
    all_gather x1, blocking collectives, shards(): parts = lax.all_gather(mine, ('half', 'core'))  9.44 us
    ppermute x6, waiting for transfers between devices, turn(): return lax.ppermute(leaf, 'az', [(i, (i + step) % az) for i in range(az)])  8.67 us
    ppermute x6, starting transfers between devices, turn(): return lax.ppermute(leaf, 'az', [(i, (i + step) % az) for i in range(az)])  8.55 us
    all_to_all x1, starting transfers between devices, shards(): parcel = lax.all_to_all(parcel, 'az', 0, 0, tiled=True)  7.87 us
    ppermute x4, waiting for transfers between devices, shift(): return lax.ppermute(leaf, 'rng', pairs)  6.02 us
    all_to_all x1, starting transfers between devices, shards(): parcel = lax.all_to_all(parcel, 'rng', 0, 0, tiled=True)  5.15 us
  transfers between devices with their start and end apart: 13, of which 6 were waited for; matrix products, arithmetic and copies ran while one was open for 0% of the time, Pallas kernels for 8%

profile of v12, /device:TPU:57, one launch (start us, length us, event | category | flops | bytes accessed | tf_op | source)
XLA Modules:
  0.0 83.7 jit_solution(10532746902804415163)
XLA Ops:
  0.6 1.2 %shard_map.84 = (bf16[16,8,512]{2,1,0:T(8,128)(2,1)S(1)}, bf16[16,8,512]{2,1,0:T(8,128)(2,1)S(1)}, bf16[8,16,512]{2,1,0:T(8,128)(2,1)S(1)}, bf16[8,16,512]{2,1,0:T(8,128)(2,1)S(1)}, f32[17,8,17]{2,1,0:T(8,128)S(1)}) custom-call(bf16[16,16,512]{2,1,0:T(8,128)(2,1)} %bitcast.18, f32[17,8,17]{2,1,0:T(8,128)} %bitcast.33), custom_call_target="tpu_custom_call" | custom-call | flops 1000000 | bytes 804928 | tf_op jit(solution)/shard_map/pallas_call | solution.py:358
  1.8 3.1 %collective-permute-start.1 = (bf16[16,8,512]{2,1,0:T(8,128)(2,1)S(1)}, bf16[16,8,512]{2,1,0:T(8,128)(2,1)S(1)}, u32[]{:S(2)}, u32[]{:S(2)}) collective-permute-start(bf16[16,8,512]{2,1,0:T(8,128)(2,1)S(1)} %get-tuple-element.39), channel_id=1, source_target_pairs={{0,4},{4,8},{8,12},{12,16},{16,20},{20,24},{24,28},{1,5},{5,9},{9,... | collective-permute-start | bytes 393224 | tf_op jit(solution)/shard_map/ppermute | solution.py:384
  4.9 4.3 %collective-permute-start.2 = (bf16[16,8,512]{2,1,0:T(8,128)(2,1)S(1)}, bf16[16,8,512]{2,1,0:T(8,128)(2,1)S(1)}, u32[]{:S(2)}, u32[]{:S(2)}) collective-permute-start(bf16[16,8,512]{2,1,0:T(8,128)(2,1)S(1)} %get-tuple-element.40), channel_id=1, source_target_pairs={{4,0},{8,4},{12,8},{16,12},{20,16},{24,20},{28,24},{5,1},{9,5},{13... | collective-permute-start | bytes 393224 | tf_op jit(solution)/shard_map/ppermute | solution.py:384
  9.2 1.7 %collective-permute-start = (bf16[8,16,512]{2,1,0:T(8,128)(2,1)S(1)}, bf16[8,16,512]{2,1,0:T(8,128)(2,1)S(1)}, u32[]{:S(2)}, u32[]{:S(2)}) collective-permute-start(bf16[8,16,512]{2,1,0:T(8,128)(2,1)S(1)} %get-tuple-element.38), channel_id=1, source_target_pairs={{0,32},{32,64},{64,96},{96,128},{128,160},{160,192},{192,224},{224... | collective-permute-start | bytes 393224 | tf_op jit(solution)/shard_map/ppermute | solution.py:380
  10.9 0.0 collective-permute-start.4
  10.9 0.1 add_convert_fusion.edge
  11.0 0.0 collective-permute-done.1
  11.0 0.1 collective-permute-done.2
  11.2 1.7 %collective-permute-start.3 = (bf16[128,512]{1,0:T(8,128)(2,1)S(1)}, bf16[128,512]{1,0:T(8,128)(2,1)S(1)}, u32[]{:S(2)}, u32[]{:S(2)}) collective-permute-start(bf16[128,512]{1,0:T(8,128)(2,1)S(1)} %get-tuple-element.41), channel_id=1, source_target_pairs={{0,32},{32,64},{64,96},{96,128},{128,160},{160,192},{192,224},{224... | collective-permute-start | bytes 393224 | tf_op jit(solution)/shard_map/ppermute | solution.py:380
  12.9 2.4 %collective-permute-start.5 = (bf16[128,512]{1,0:T(8,128)(2,1)S(1)}, bf16[128,512]{1,0:T(8,128)(2,1)S(1)}, u32[]{:S(2)}, u32[]{:S(2)}) collective-permute-start(bf16[128,512]{1,0:T(8,128)(2,1)S(1)} %get-tuple-element.43), channel_id=1, source_target_pairs={{0,224},{32,0},{64,32},{96,64},{128,96},{160,128},{192,160},{224,1... | collective-permute-start | bytes 393224 | tf_op jit(solution)/shard_map/ppermute | solution.py:380
  15.2 0.0 copy-start
  15.2 0.0 copy-start.1
  15.2 0.0 copy-start.2
  15.3 0.0 copy-start.3
  15.3 2.0 %shard_map.87.table = f32[4,768,256]{2,1,0:T(8,128)S(1)} custom-call(s32[2]{0:T(128)S(1)} %add_convert_fusion.edge, f32[17,8,17]{2,1,0:T(8,128)S(1)} %get-tuple-element.48.bias), custom_call_target="tpu_custom_call" | custom-call | flops 100000000 | bytes 3154984 | tf_op jit(solution)/shard_map/pallas_call | solution.py:358
  17.3 0.0 copy-done
  17.3 0.0 copy-done.1
  17.3 0.0 copy-done.2
  17.3 0.0 copy-done.3
  17.3 0.5 shard_map.86
  17.8 0.8 shard_map.88
  18.7 0.0 collective-permute-done
  18.7 0.0 collective-permute-done.4
  18.7 0.0 collective-permute-done.3.above
  18.7 0.0 collective-permute-done.5.below
  18.7 7.9 %shard_map.89 = (bf16[512,1024]{1,0:T(8,128)(2,1)S(1)}, bf16[1024,1024]{1,0:T(8,128)(2,1)S(1)}, bf16[2,512,256]{2,1,0:T(8,128)(2,1)S(1)}, bf16[2,256,512]{2,1,0:...) custom-call(s32[1]{0:T(128)} %bitcast.core, bf16[128,512]{1,0:T(8,128)(2,1)S(1)} %bitcast.28, ...), custom_call_target="tpu_custom_call" | custom-call | flops 10000000000 | bytes 14680068 | tf_op jit(solution)/shard_map/pallas_call | solution.py:358
  26.6 2.2 %collective-permute-start.10 = (bf16[512,1024]{1,0:T(8,128)(2,1)S(1)}, bf16[512,1024]{1,0:T(8,128)(2,1)S(1)}, u32[]{:S(2)}, u32[]{:S(2)}) collective-permute-start(bf16[512,1024]{1,0:T(8,128)(2,1)S(1)} %get-tuple-element.67), channel_id=1, source_target_pairs={{0,1},{1,0},{2,3},{3,2},{4,5},{5,4},{6,7},{7,6},{8,9},{9,8},{10,11... | collective-permute-start | bytes 3145736 | tf_op jit(solution)/shard_map/ppermute | solution.py:387
  28.8 2.5 %shard_map.90 = (bf16[512,1024]{1,0:T(8,128)(2,1)S(1)}, f32[8,384]{1,0:T(8,128)S(1)}, bf16[256,512]{1,0:T(8,128)(2,1)S(1)}, f32[256,512]{1,0:T(8,128)S(1)}, f32[...) custom-call(s32[1]{0:T(128)} %bitcast.core, bf16[512,1024]{1,0:T(8,128)(2,1)S(1)} %get-tuple-element.54.x_t, ...), custom_call_target="tpu_custom_call" | custom-call | flops 2500000000 | bytes 8663044 | tf_op jit(solution)/shard_map/pallas_call | solution.py:358
  31.3 0.0 collective-permute-done.10.came
  31.3 1.1 %shard_map.93 = bf16[8,536,128]{2,1,0:T(8,128)(2,1)} custom-call(bf16[512,1024]{1,0:T(8,128)(2,1)S(1)} %get-tuple-element.66.keep, bf16[512,1024]{1,0:T(8,128)(2,1)S(1)} %collective-permute-done.10.came, f32[8,384]{1,0:T(8,128)S(1)} %get-tuple-element.68.bias), custom_call_target="tpu_custom_call" | custom-call | flops 1000000 | bytes 3207168 | tf_op jit(solution)/shard_map/pallas_call | solution.py:358
  32.4 5.1 %all-to-all-start = ((bf16[8,536,128]{2,1,0:T(8,128)(2,1)}), bf16[8,536,128]{2,1,0:T(8,128)(2,1)S(1)}, u32[]{:S(2)}, u32[]{:S(2)}) async-start(bf16[8,536,128]{2,1,0:T(8,128)(2,1)} %shard_map.93), calls=%async_computation | async-start | bytes 2195456 | tf_op jit(solution)/shard_map/all_to_all | solution.py:478
  37.6 2.8 %collective-permute-start.6 = (bf16[256,512]{1,0:T(8,128)(2,1)S(1)}, bf16[256,512]{1,0:T(8,128)(2,1)S(1)}, u32[]{:S(2)}, u32[]{:S(2)}) collective-permute-start(bf16[256,512]{1,0:T(8,128)(2,1)S(1)} %get-tuple-element.61), channel_id=1, source_target_pairs={{0,32},{32,64},{64,96},{96,128},{128,160},{160,192},{192,224},{224... | collective-permute-start | bytes 786440 | tf_op jit(solution)/shard_map/ppermute | solution.py:380
  40.4 0.0 collective-permute-start.7
  40.4 5.8 %collective-permute-done.6.up = bf16[256,512]{1,0:T(8,128)(2,1)S(1)} collective-permute-done((bf16[256,512]{1,0:T(8,128)(2,1)S(1)}, bf16[256,512]{1,0:T(8,128)(2,1)S(1)}, u32[]{:S(2)}, u32[]{:S(2)}) %collective-permute-start.6) | collective-permute-done | bytes 262176 | tf_op jit(solution)/shard_map/ppermute | solution.py:380
  46.1 2.9 %collective-permute-done.7.down = bf16[256,512]{1,0:T(8,128)(2,1)S(1)} collective-permute-done((bf16[256,512]{1,0:T(8,128)(2,1)S(1)}, bf16[256,512]{1,0:T(8,128)(2,1)S(1)}, u32[]{:S(2)}, u32[]{:S(2)}) %collective-permute-start.7) | collective-permute-done | bytes 262176 | tf_op jit(solution)/shard_map/ppermute | solution.py:380
  49.0 0.1 shard_map.91
  49.1 3.7 %all-to-all-done.came = bf16[8,536,128]{2,1,0:T(8,128)(2,1)S(1)} async-done(((bf16[8,536,128]{2,1,0:T(8,128)(2,1)}), bf16[8,536,128]{2,1,0:T(8,128)(2,1)S(1)}, u32[]{:S(2)}, u32[]{:S(2)}) %all-to-all-start) | async-done | bytes 1097760 | tf_op jit(solution)/shard_map/all_to_all | solution.py:478
  52.8 0.8 shard_map.94
  53.6 7.9 %all-to-all-start.1 = ((bf16[8,8,1408]{2,1,0:T(8,128)(2,1)}), bf16[8,8,1408]{2,1,0:T(8,128)(2,1)S(1)}, u32[]{:S(2)}, u32[]{:S(2)}) async-start(bf16[8,8,1408]{2,1,0:T(8,128)(2,1)} %shard_map.94), calls=%async_computation.1 | async-start | bytes 360448 | tf_op jit(solution)/shard_map/all_to_all | solution.py:504
  61.5 3.4 %collective-permute-start.9 = (bf16[16,8,512]{2,1,0:T(8,128)(2,1)S(1)}, bf16[16,8,512]{2,1,0:T(8,128)(2,1)S(1)}, u32[]{:S(2)}, u32[]{:S(2)}) collective-permute-start(bf16[16,8,512]{2,1,0:T(8,128)(2,1)S(1)} %bitcast.31), channel_id=1, source_target_pairs={{4,0},{8,4},{12,8},{16,12},{20,16},{24,20},{28,24},{5,1},{9,5},{13... | collective-permute-start | bytes 393224 | tf_op jit(solution)/shard_map/ppermute | solution.py:384
  64.9 1.9 %collective-permute-start.8 = (bf16[16,8,512]{2,1,0:T(8,128)(2,1)S(1)}, bf16[16,8,512]{2,1,0:T(8,128)(2,1)S(1)}, u32[]{:S(2)}, u32[]{:S(2)}) collective-permute-start(bf16[16,8,512]{2,1,0:T(8,128)(2,1)S(1)} %bitcast.30), channel_id=1, source_target_pairs={{0,4},{4,8},{8,12},{12,16},{16,20},{20,24},{24,28},{1,5},{5,9},{9,... | collective-permute-start | bytes 393224 | tf_op jit(solution)/shard_map/ppermute | solution.py:384
  66.8 0.7 collective-permute-done.9.east
  67.5 5.2 %collective-permute-done.8.west = bf16[16,8,512]{2,1,0:T(8,128)(2,1)S(1)} collective-permute-done((bf16[16,8,512]{2,1,0:T(8,128)(2,1)S(1)}, bf16[16,8,512]{2,1,0:T(8,128)(2,1)S(1)}, u32[]{:S(2)}, u32[]{:S(2)}) %collective-permute-start.8) | collective-permute-done | bytes 131104 | tf_op jit(solution)/shard_map/ppermute | solution.py:384
  72.7 0.7 shard_map.92
  73.5 0.0 all-to-all-done.1.came
  73.5 9.4 %all-gather = f32[32,1408]{1,0:T(8,128)S(1)} all-gather(f32[8,1408]{1,0:T(8,128)S(1)} %shard_map.95), channel_id=2, replica_groups=mesh['az'=8,'rng'=8,'half'=2,'core'=2] {'half','core'}, dimensions={0}, use_global_device_ids=true | all-gather | bytes 225280 | tf_op jit(solution)/shard_map/all_gather | solution.py:506
  82.9 0.7 shard_map.96
  (2 shorter events, 0.0 us)
Async XLA Ops:
  1.8 9.2 %collective-permute-start.1 = (bf16[16,8,512]{2,1,0:T(8,128)(2,1)S(1)}, bf16[16,8,512]{2,1,0:T(8,128)(2,1)S(1)}, u32[]{:S(2)}, u32[]{:S(2)}) collective-permute-start(bf16[16,8,512]{2,1,0:T(8,128)(2,1)S(1)} %get-tuple-element.39), channel_id=1, source_target_pairs={{0,4},{4,8},{8,12},{12,16},{16,20},{20,24},{24,28},{1,5},{5,9},{9,... | collective-permute-start | bytes 393224 | tf_op jit(solution)/shard_map/ppermute | solution.py:384
  4.9 6.2 %collective-permute-start.2 = (bf16[16,8,512]{2,1,0:T(8,128)(2,1)S(1)}, bf16[16,8,512]{2,1,0:T(8,128)(2,1)S(1)}, u32[]{:S(2)}, u32[]{:S(2)}) collective-permute-start(bf16[16,8,512]{2,1,0:T(8,128)(2,1)S(1)} %get-tuple-element.40), channel_id=1, source_target_pairs={{4,0},{8,4},{12,8},{16,12},{20,16},{24,20},{28,24},{5,1},{9,5},{13... | collective-permute-start | bytes 393224 | tf_op jit(solution)/shard_map/ppermute | solution.py:384
  9.2 9.4 %collective-permute-start = (bf16[8,16,512]{2,1,0:T(8,128)(2,1)S(1)}, bf16[8,16,512]{2,1,0:T(8,128)(2,1)S(1)}, u32[]{:S(2)}, u32[]{:S(2)}) collective-permute-start(bf16[8,16,512]{2,1,0:T(8,128)(2,1)S(1)} %get-tuple-element.38), channel_id=1, source_target_pairs={{0,32},{32,64},{64,96},{96,128},{128,160},{160,192},{192,224},{224... | collective-permute-start | bytes 393224 | tf_op jit(solution)/shard_map/ppermute | solution.py:380
  10.9 7.7 %collective-permute-start.4 = (bf16[8,16,512]{2,1,0:T(8,128)(2,1)S(1)}, bf16[8,16,512]{2,1,0:T(8,128)(2,1)S(1)}, u32[]{:S(2)}, u32[]{:S(2)}) collective-permute-start(bf16[8,16,512]{2,1,0:T(8,128)(2,1)S(1)} %get-tuple-element.42), channel_id=1, source_target_pairs={{0,224},{32,0},{64,32},{96,64},{128,96},{160,128},{192,160},{224,1... | collective-permute-start | bytes 393224 | tf_op jit(solution)/shard_map/ppermute | solution.py:380
  11.2 7.5 %collective-permute-start.3 = (bf16[128,512]{1,0:T(8,128)(2,1)S(1)}, bf16[128,512]{1,0:T(8,128)(2,1)S(1)}, u32[]{:S(2)}, u32[]{:S(2)}) collective-permute-start(bf16[128,512]{1,0:T(8,128)(2,1)S(1)} %get-tuple-element.41), channel_id=1, source_target_pairs={{0,32},{32,64},{64,96},{96,128},{128,160},{160,192},{192,224},{224... | collective-permute-start | bytes 393224 | tf_op jit(solution)/shard_map/ppermute | solution.py:380
  12.9 5.8 %collective-permute-start.5 = (bf16[128,512]{1,0:T(8,128)(2,1)S(1)}, bf16[128,512]{1,0:T(8,128)(2,1)S(1)}, u32[]{:S(2)}, u32[]{:S(2)}) collective-permute-start(bf16[128,512]{1,0:T(8,128)(2,1)S(1)} %get-tuple-element.43), channel_id=1, source_target_pairs={{0,224},{32,0},{64,32},{96,64},{128,96},{160,128},{192,160},{224,1... | collective-permute-start | bytes 393224 | tf_op jit(solution)/shard_map/ppermute | solution.py:380
  15.2 2.0 %copy-start = (bf16[512,1536]{1,0:T(8,128)(2,1)S(1)}, bf16[512,1536]{1,0:T(8,128)(2,1)}, u32[]{:S(2)}) copy-start(bf16[512,1536]{1,0:T(8,128)(2,1)} %w.7) | copy-start | bytes 4718596
  15.2 2.0 %copy-start.1 = (bf16[1,16,16,512]{3,2,1,0:T(8,128)(2,1)S(1)}, bf16[1,16,16,512]{3,2,1,0:T(8,128)(2,1)}, u32[]{:S(2)}) copy-start(bf16[1,16,16,512]{3,2,1,0:T(8,128)(2,1)} %param.5) | copy-start | bytes 786436
  15.2 2.0 %copy-start.2 = (bf16[512,512]{1,0:T(8,128)(2,1)S(1)}, bf16[512,512]{1,0:T(8,128)(2,1)}, u32[]{:S(2)}) copy-start(bf16[512,512]{1,0:T(8,128)(2,1)} %wo.1) | copy-start | bytes 1572868
  15.3 2.0 %copy-start.3 = (bf16[1,16,16,512]{3,2,1,0:T(8,128)(2,1)S(1)}, bf16[1,16,16,512]{3,2,1,0:T(8,128)(2,1)}, u32[]{:S(2)}) copy-start(bf16[1,16,16,512]{3,2,1,0:T(8,128)(2,1)} %param.9) | copy-start | bytes 786436
  26.6 4.8 %collective-permute-start.10 = (bf16[512,1024]{1,0:T(8,128)(2,1)S(1)}, bf16[512,1024]{1,0:T(8,128)(2,1)S(1)}, u32[]{:S(2)}, u32[]{:S(2)}) collective-permute-start(bf16[512,1024]{1,0:T(8,128)(2,1)S(1)} %get-tuple-element.67), channel_id=1, source_target_pairs={{0,1},{1,0},{2,3},{3,2},{4,5},{5,4},{6,7},{7,6},{8,9},{9,8},{10,11... | collective-permute-start | bytes 3145736 | tf_op jit(solution)/shard_map/ppermute | solution.py:387
  32.4 20.4 %all-to-all-start = ((bf16[8,536,128]{2,1,0:T(8,128)(2,1)}), bf16[8,536,128]{2,1,0:T(8,128)(2,1)S(1)}, u32[]{:S(2)}, u32[]{:S(2)}) async-start(bf16[8,536,128]{2,1,0:T(8,128)(2,1)} %shard_map.93), calls=%async_computation | async-start | bytes 2195456 | tf_op jit(solution)/shard_map/all_to_all | solution.py:478
  37.6 8.5 %collective-permute-start.6 = (bf16[256,512]{1,0:T(8,128)(2,1)S(1)}, bf16[256,512]{1,0:T(8,128)(2,1)S(1)}, u32[]{:S(2)}, u32[]{:S(2)}) collective-permute-start(bf16[256,512]{1,0:T(8,128)(2,1)S(1)} %get-tuple-element.61), channel_id=1, source_target_pairs={{0,32},{32,64},{64,96},{96,128},{128,160},{160,192},{192,224},{224... | collective-permute-start | bytes 786440 | tf_op jit(solution)/shard_map/ppermute | solution.py:380
  40.4 8.7 %collective-permute-start.7 = (bf16[256,512]{1,0:T(8,128)(2,1)S(1)}, bf16[256,512]{1,0:T(8,128)(2,1)S(1)}, u32[]{:S(2)}, u32[]{:S(2)}) collective-permute-start(bf16[256,512]{1,0:T(8,128)(2,1)S(1)} %get-tuple-element.62), channel_id=1, source_target_pairs={{0,224},{32,0},{64,32},{96,64},{128,96},{160,128},{192,160},{224,1... | collective-permute-start | bytes 786440 | tf_op jit(solution)/shard_map/ppermute | solution.py:380
  53.6 19.8 %all-to-all-start.1 = ((bf16[8,8,1408]{2,1,0:T(8,128)(2,1)}), bf16[8,8,1408]{2,1,0:T(8,128)(2,1)S(1)}, u32[]{:S(2)}, u32[]{:S(2)}) async-start(bf16[8,8,1408]{2,1,0:T(8,128)(2,1)} %shard_map.94), calls=%async_computation.1 | async-start | bytes 360448 | tf_op jit(solution)/shard_map/all_to_all | solution.py:504
  61.5 6.0 %collective-permute-start.9 = (bf16[16,8,512]{2,1,0:T(8,128)(2,1)S(1)}, bf16[16,8,512]{2,1,0:T(8,128)(2,1)S(1)}, u32[]{:S(2)}, u32[]{:S(2)}) collective-permute-start(bf16[16,8,512]{2,1,0:T(8,128)(2,1)S(1)} %bitcast.31), channel_id=1, source_target_pairs={{4,0},{8,4},{12,8},{16,12},{20,16},{24,20},{28,24},{5,1},{9,5},{13... | collective-permute-start | bytes 393224 | tf_op jit(solution)/shard_map/ppermute | solution.py:384
  64.9 7.8 %collective-permute-start.8 = (bf16[16,8,512]{2,1,0:T(8,128)(2,1)S(1)}, bf16[16,8,512]{2,1,0:T(8,128)(2,1)S(1)}, u32[]{:S(2)}, u32[]{:S(2)}) collective-permute-start(bf16[16,8,512]{2,1,0:T(8,128)(2,1)S(1)} %bitcast.30), channel_id=1, source_target_pairs={{0,4},{4,8},{8,12},{12,16},{16,20},{20,24},{24,28},{1,5},{5,9},{9,... | collective-permute-start | bytes 393224 | tf_op jit(solution)/shard_map/ppermute | solution.py:384
